TPU v7x, 32 devices: a whole 2x2x4 slice. The times are simulated.
32 devices in a mesh: ctx: 8 (over z, y), fsdp: 4 (over x, core).
Axes of the slice: x: 2, y: 2, z: 4, core: 2. Of those that a mesh axis runs over, the one named last changes fastest.
Arguments:
- hidden_in: bfloat16 [4, 2048, 1536], P('fsdp', 'ctx'), may hold values from -6 to 6
- out_grad: bfloat16 [4, 2048, 1536], P('fsdp', 'ctx'), may hold values from -6 to 6
- positions: int32 [4, 2048], P('fsdp'), may hold values from 0 to 2047, as said below
- attn_gain: bfloat16 [1536], P('fsdp'), may hold values from 0.5 to 1.5
- w_query: bfloat16 [1536, 1536], P('fsdp'), may hold values from -0.15625 to 0.15625
- w_key: bfloat16 [1536, 768], P('fsdp'), may hold values from -0.15625 to 0.15625
- w_value: bfloat16 [1536, 768], P('fsdp'), may hold values from -0.15625 to 0.15625
- w_out: bfloat16 [1536, 1536], P('fsdp'), may hold values from -3 to 3
- ffn_gain: bfloat16 [1536], P('fsdp'), may hold values from 0.5 to 1.5
- w_gate: bfloat16 [1536, 4096], P('fsdp'), may hold values from -0.15625 to 0.15625
- w_up: bfloat16 [1536, 4096], P('fsdp'), may hold values from -0.15625 to 0.15625
- w_down: bfloat16 [1536, 4096], P('fsdp'), may hold values from -0.09375 to 0.09375
Outputs:
- out: bfloat16 [4, 2048, 1536], P('fsdp', 'ctx')
- input_grad: float32 [4, 2048, 1536], P('fsdp', 'ctx')
- attn_gain_grad: float32 [1536], P('fsdp')
- w_query_grad: float32 [1536, 1536], P('fsdp')
- w_key_grad: float32 [1536, 768], P('fsdp')
- w_value_grad: float32 [1536, 768], P('fsdp')
- w_out_grad: float32 [1536, 1536], P('fsdp')
- ffn_gain_grad: float32 [1536], P('fsdp')
- w_gate_grad: float32 [1536, 4096], P('fsdp')
- w_up_grad: float32 [1536, 4096], P('fsdp')
- w_down_grad: float32 [1536, 4096], P('fsdp')
Inputs may be any that keep to these rules, and one draw needn't show every extreme that they name: In each sequence, the 256 rows of one ctx index hold the positions of causal block b followed by those of block 15 - b, each in increasing order, where b is that index's place in a permutation of the 8 pairs drawn for that sequence; each sequence's positions are a permutation of 0 to 2047.
All inputs are finite; a program needn't handle non-finite values.
Results may differ from a plain program's by a relative error of at most 0.022.
Values may be sent and summed in bfloat16 or wider, within the bound.
No kernel may reach another device: no remote copies, remote signals or barrier semaphores. Data moves between devices by JAX's collectives and lax.ppermute only.
A program may use at most 448 MiB of HBM per device.

v0:
```python
import math

import jax
import jax.numpy as jnp
from jax import lax
from jax.sharding import PartitionSpec as P

HQ = 16
HK = 8
HD = 96


epsilon = 1e-05
rope_base = 100000.0
masked_score = -1e30


def angles_of(places):
    frequency = jnp.exp(jnp.arange(HD // 2, dtype=jnp.float32) * (-2.0 * math.log(rope_base) / HD))
    turned = places.astype(jnp.float32)[:, None] * frequency[None, :]
    return (jnp.cos(turned)[:, None, :], jnp.sin(turned)[:, None, :])


def rotate(values, cosine, sine):
    half_size = values.shape[-1] // 2
    first_half = values[..., :half_size]
    second_half = values[..., half_size:]
    return jnp.concatenate(
        [first_half * cosine - second_half * sine, second_half * cosine + first_half * sine],
        axis=-1,
    )


def contract_last(left, right):
    return lax.dot_general(
        left, right, (((1,), (1,)), ((), ())), preferred_element_type=jnp.float32
    )


def contract_first(left, right):
    return lax.dot_general(
        left, right, (((0,), (0,)), ((), ())), preferred_element_type=jnp.float32
    )


def rms_back(values, inverse, gain, grad_normed):
    weighted = gain * grad_normed
    inner = jnp.mean(values * weighted, axis=1, keepdims=True)
    grad_values = inverse * weighted - values * inverse * inverse * inverse * inner
    return (grad_values, jnp.sum(grad_normed * values * inverse, axis=0))


def body(
    hidden_in,
    out_grad,
    positions,
    attn_gain,
    w_query,
    w_key,
    w_value,
    w_out,
    ffn_gain,
    w_gate,
    w_up,
    w_down,
):
    shards = (attn_gain, w_query, w_key, w_value, w_out, ffn_gain, w_gate, w_up, w_down)
    weights = (
        lax.all_gather(shards[0], "fsdp", axis=0, tiled=True),
        lax.all_gather(shards[1], "fsdp", axis=0, tiled=True),
        lax.all_gather(shards[2], "fsdp", axis=0, tiled=True),
        lax.all_gather(shards[3], "fsdp", axis=0, tiled=True),
        lax.all_gather(shards[4], "fsdp", axis=0, tiled=True),
        lax.all_gather(shards[5], "fsdp", axis=0, tiled=True),
        lax.all_gather(shards[6], "fsdp", axis=0, tiled=True),
        lax.all_gather(shards[7], "fsdp", axis=0, tiled=True),
        lax.all_gather(shards[8], "fsdp", axis=0, tiled=True),
    )
    gain_one = weights[0].astype(jnp.float32)
    gain_two = weights[5].astype(jnp.float32)
    rows_in = hidden_in[0].astype(jnp.float32)
    row_count = rows_in.shape[0]
    group_size = HQ // HK
    scale = 1.0 / math.sqrt(HD)
    all_places = positions[0]
    own_places = lax.dynamic_slice_in_dim(
        all_places, lax.axis_index("ctx") * row_count, row_count, 0
    )
    cosine, sine = angles_of(own_places)
    inverse_one = lax.rsqrt(jnp.mean(rows_in * rows_in, axis=1, keepdims=True) + epsilon)
    normed_one = (rows_in * inverse_one * gain_one).astype(jnp.bfloat16)
    query = jnp.dot(normed_one, weights[1], preferred_element_type=jnp.float32)
    keys = jnp.dot(normed_one, weights[2], preferred_element_type=jnp.float32)
    values = jnp.dot(normed_one, weights[3], preferred_element_type=jnp.float32).astype(
        jnp.bfloat16
    )
    query_rot = (
        rotate(query.reshape(row_count, HQ, HD), cosine, sine)
        .astype(jnp.bfloat16)
        .reshape(row_count, HK, group_size, HD)
    )
    keys_rot = (
        rotate(keys.reshape(row_count, HK, HD), cosine, sine)
        .astype(jnp.bfloat16)
        .reshape(row_count, HK * HD)
    )
    keys_all, values_all = (
        lax.all_gather(keys_rot, "ctx", axis=0, tiled=True),
        lax.all_gather(values, "ctx", axis=0, tiled=True),
    )
    key_total = keys_all.shape[0]
    keys_all = keys_all.reshape(key_total, HK, HD)
    values_all = values_all.reshape(key_total, HK, HD)
    block_size = math.gcd(key_total, 512)
    block_count = key_total // block_size

    def scores_at(start):
        key_block = lax.dynamic_slice_in_dim(keys_all, start, block_size, 0)
        key_places = lax.dynamic_slice_in_dim(all_places, start, block_size, 0)
        raw = (
            jnp.einsum("rkgd,skd->rkgs", query_rot, key_block, preferred_element_type=jnp.float32)
            * scale
        )
        allowed = key_places[None, None, None, :] <= own_places[:, None, None, None]
        return (jnp.where(allowed, raw, masked_score), key_block)

    def running_total(block_index, carry):
        top_score, total = carry
        scores, unused = scores_at(block_index * block_size)
        new_top = jnp.maximum(top_score, jnp.max(scores, axis=-1))
        total = total * jnp.exp(top_score - new_top) + jnp.sum(
            jnp.exp(scores - new_top[..., None]), axis=-1
        )
        return (new_top, total)

    start_top = jnp.full((row_count, HK, group_size), masked_score, jnp.float32)
    start_total = jnp.zeros((row_count, HK, group_size), jnp.float32)
    top_score, total = lax.fori_loop(0, block_count, running_total, (start_top, start_total))
    log_total = top_score + jnp.log(total)

    def add_values(block_index, mixed):
        start = block_index * block_size
        scores, unused = scores_at(start)
        value_block = lax.dynamic_slice_in_dim(values_all, start, block_size, 0)
        soft = jnp.exp(scores - log_total[..., None]).astype(jnp.bfloat16)
        return mixed + jnp.einsum(
            "rkgs,skd->rkgd", soft, value_block, preferred_element_type=jnp.float32
        )

    mixed_exact = lax.fori_loop(
        0, block_count, add_values, jnp.zeros((row_count, HK, group_size, HD), jnp.float32)
    )
    mixed_low = mixed_exact.reshape(row_count, HQ * HD).astype(jnp.bfloat16)
    middle = rows_in + contract_last(mixed_low, weights[4])
    inverse_two = lax.rsqrt(jnp.mean(middle * middle, axis=1, keepdims=True) + epsilon)
    normed_two = (middle * inverse_two * gain_two).astype(jnp.bfloat16)
    gate = jnp.dot(normed_two, weights[6], preferred_element_type=jnp.float32)
    upward = jnp.dot(normed_two, weights[7], preferred_element_type=jnp.float32)
    sigmoid_gate = jax.nn.sigmoid(gate)
    swish = gate * sigmoid_gate
    hidden = (swish * upward).astype(jnp.bfloat16)
    result = (middle + contract_last(hidden, weights[8])).astype(jnp.bfloat16)
    weights = (
        lax.all_gather(shards[0], "fsdp", axis=0, tiled=True),
        lax.all_gather(shards[1], "fsdp", axis=0, tiled=True),
        lax.all_gather(shards[2], "fsdp", axis=0, tiled=True),
        lax.all_gather(shards[3], "fsdp", axis=0, tiled=True),
        lax.all_gather(shards[4], "fsdp", axis=0, tiled=True),
        lax.all_gather(shards[5], "fsdp", axis=0, tiled=True),
        lax.all_gather(shards[6], "fsdp", axis=0, tiled=True),
        lax.all_gather(shards[7], "fsdp", axis=0, tiled=True),
        lax.all_gather(shards[8], "fsdp", axis=0, tiled=True),
    )
    grad_down = out_grad[0]
    grad_hidden = jnp.dot(grad_down, weights[8], preferred_element_type=jnp.float32)
    grad_gate = (grad_hidden * upward * sigmoid_gate * (1.0 + gate * (1.0 - sigmoid_gate))).astype(
        jnp.bfloat16
    )
    grad_up = (grad_hidden * swish).astype(jnp.bfloat16)
    grad_normed_two = contract_last(grad_gate, weights[6]) + contract_last(grad_up, weights[7])
    grad_middle_norm, grad_gain_two = rms_back(middle, inverse_two, gain_two, grad_normed_two)
    grad_middle = grad_down.astype(jnp.float32) + grad_middle_norm
    grad_branch = grad_middle.astype(jnp.bfloat16)
    grad_mixed = jnp.dot(grad_branch, weights[4], preferred_element_type=jnp.float32).astype(
        jnp.bfloat16
    )
    grad_mixed = grad_mixed.reshape(row_count, HK, group_size, HD)
    delta = jnp.sum(grad_mixed.astype(jnp.float32) * mixed_exact, axis=-1)

    def key_step(block_index, carry):
        grad_query, grad_keys, grad_values = carry
        start = block_index * block_size
        scores, key_block = scores_at(start)
        value_block = lax.dynamic_slice_in_dim(values_all, start, block_size, 0)
        soft = jnp.exp(scores - log_total[..., None])
        grad_soft = jnp.einsum(
            "rkgd,skd->rkgs", grad_mixed, value_block, preferred_element_type=jnp.float32
        )
        grad_scores = (soft * (grad_soft - delta[..., None])).astype(jnp.bfloat16)
        grad_query = grad_query + scale * jnp.einsum(
            "rkgs,skd->rkgd", grad_scores, key_block, preferred_element_type=jnp.float32
        )
        key_part = scale * jnp.einsum(
            "rkgs,rkgd->skd", grad_scores, query_rot, preferred_element_type=jnp.float32
        )
        value_part = jnp.einsum(
            "rkgs,rkgd->skd",
            soft.astype(jnp.bfloat16),
            grad_mixed,
            preferred_element_type=jnp.float32,
        )
        grad_keys = lax.dynamic_update_slice_in_dim(
            grad_keys, key_part.reshape(block_size, HK * HD), start, 0
        )
        grad_values = lax.dynamic_update_slice_in_dim(
            grad_values, value_part.reshape(block_size, HK * HD), start, 0
        )
        return (grad_query, grad_keys, grad_values)

    start_query = jnp.zeros((row_count, HK, group_size, HD), jnp.float32)
    start_keys = jnp.zeros((key_total, HK * HD), jnp.float32)
    grad_query, grad_keys, grad_values = lax.fori_loop(
        0, block_count, key_step, (start_query, start_keys, start_keys)
    )
    own_key_grads, own_value_grads = (
        lax.psum_scatter(
            grad_keys.astype(jnp.bfloat16), "ctx", scatter_dimension=0, tiled=True
        ).astype(jnp.float32),
        lax.psum_scatter(
            grad_values.astype(jnp.bfloat16), "ctx", scatter_dimension=0, tiled=True
        ).astype(jnp.float32),
    )
    grad_keys_raw = (
        rotate(own_key_grads.reshape(row_count, HK, HD), cosine, -sine)
        .reshape(row_count, HK * HD)
        .astype(jnp.bfloat16)
    )
    grad_values_low = own_value_grads.astype(jnp.bfloat16)
    grad_query_raw = (
        rotate(grad_query.reshape(row_count, HQ, HD), cosine, -sine)
        .reshape(row_count, HQ * HD)
        .astype(jnp.bfloat16)
    )
    grad_normed_one = (
        contract_last(grad_query_raw, weights[1])
        + contract_last(grad_keys_raw, weights[2])
        + contract_last(grad_values_low, weights[3])
    )
    grad_rows_norm, grad_gain_one = rms_back(rows_in, inverse_one, gain_one, grad_normed_one)
    input_grad = (grad_middle + grad_rows_norm)[None]
    down_part = lax.psum_scatter(
        contract_first(grad_down, hidden).astype(jnp.bfloat16),
        "fsdp",
        scatter_dimension=0,
        tiled=True,
    )
    gate_part, up_part, out_part, gain_two_part = (
        lax.psum_scatter(
            contract_first(normed_two, grad_gate).astype(jnp.bfloat16),
            "fsdp",
            scatter_dimension=0,
            tiled=True,
        ).astype(jnp.float32),
        lax.psum_scatter(
            contract_first(normed_two, grad_up).astype(jnp.bfloat16),
            "fsdp",
            scatter_dimension=0,
            tiled=True,
        ).astype(jnp.float32),
        lax.psum_scatter(
            contract_first(grad_branch, mixed_low).astype(jnp.bfloat16),
            "fsdp",
            scatter_dimension=0,
            tiled=True,
        ).astype(jnp.float32),
        lax.psum_scatter(
            grad_gain_two.astype(jnp.bfloat16), "fsdp", scatter_dimension=0, tiled=True
        ).astype(jnp.float32),
    )
    query_part, key_part, value_part, gain_one_part = (
        lax.psum_scatter(
            contract_first(normed_one, grad_query_raw).astype(jnp.bfloat16),
            "fsdp",
            scatter_dimension=0,
            tiled=True,
        ).astype(jnp.float32),
        lax.psum_scatter(
            contract_first(normed_one, grad_keys_raw).astype(jnp.bfloat16),
            "fsdp",
            scatter_dimension=0,
            tiled=True,
        ).astype(jnp.float32),
        lax.psum_scatter(
            contract_first(normed_one, grad_values_low).astype(jnp.bfloat16),
            "fsdp",
            scatter_dimension=0,
            tiled=True,
        ).astype(jnp.float32),
        lax.psum_scatter(
            grad_gain_one.astype(jnp.bfloat16), "fsdp", scatter_dimension=0, tiled=True
        ).astype(jnp.float32),
    )
    summed = (
        lax.psum(gain_one_part.astype(jnp.bfloat16), "ctx").astype(jnp.float32),
        lax.psum(query_part.astype(jnp.bfloat16), "ctx").astype(jnp.float32),
        lax.psum(key_part.astype(jnp.bfloat16), "ctx").astype(jnp.float32),
        lax.psum(value_part.astype(jnp.bfloat16), "ctx").astype(jnp.float32),
        lax.psum(out_part.astype(jnp.bfloat16), "ctx").astype(jnp.float32),
        lax.psum(gain_two_part.astype(jnp.bfloat16), "ctx").astype(jnp.float32),
        lax.psum(gate_part.astype(jnp.bfloat16), "ctx").astype(jnp.float32),
        lax.psum(up_part.astype(jnp.bfloat16), "ctx").astype(jnp.float32),
        lax.psum(down_part, "ctx").astype(jnp.float32),
    )
    return (
        result[None],
        input_grad,
        summed[0],
        summed[1],
        summed[2],
        summed[3],
        summed[4],
        summed[5],
        summed[6],
        summed[7],
        summed[8],
    )


def solution(mesh):
    placed = (
        P("fsdp", "ctx", None),
        P("fsdp", "ctx", None),
        P("fsdp", None),
        P("fsdp"),
        P("fsdp", None),
        P("fsdp", None),
        P("fsdp", None),
        P("fsdp", None),
        P("fsdp"),
        P("fsdp", None),
        P("fsdp", None),
        P("fsdp", None),
    )
    return jax.shard_map(
        body,
        mesh=mesh,
        in_specs=placed,
        out_specs=(
            P("fsdp", "ctx", None),
            P("fsdp", "ctx", None),
            P("fsdp"),
            P("fsdp", None),
            P("fsdp", None),
            P("fsdp", None),
            P("fsdp", None),
            P("fsdp"),
            P("fsdp", None),
            P("fsdp", None),
            P("fsdp", None),
        ),
        check_vma=False,
    )
```

profile of v0, /device:TPU:0, one launch (start us, length us, event | category | flops | bytes accessed | tf_op | source)
XLA Modules:
  0.0 1717.2 jit_solution(11761543956456879321)
XLA Ops:
  9.5 6.1 all-gather
  15.9 20.5 %all-gather.12.cloned.1.call-done = bf16[1536,768]{1,0:T(8,128)(2,1)} async-done(((bf16[384,768]{1,0:T(8,128)(2,1)}), bf16[1536,768]{1,0:T(8,128)(2,1)}) %all-gather.12.cloned.1.call-update) | async-done | bytes 2359312 | tf_op jit(solution)/shard_map/all_gather | solution.py:72
  40.6 21.4 %all-gather.16.cloned.1.call-done = bf16[1536,768]{1,0:T(8,128)(2,1)} async-done(((bf16[384,768]{1,0:T(8,128)(2,1)}), bf16[1536,768]{1,0:T(8,128)(2,1)}) %all-gather.16.cloned.1.call-update) | async-done | bytes 2359312 | tf_op jit(solution)/shard_map/all_gather | solution.py:71
  69.6 5.4 all-gather.1
  75.1 26.0 %all-gather.20.cloned.1.call-done = bf16[1536,1536]{1,0:T(8,128)(2,1)} async-done(((bf16[384,1536]{1,0:T(8,128)(2,1)}), bf16[1536,1536]{1,0:T(8,128)(2,1)}) %all-gather.20.cloned.1.call-update) | async-done | bytes 4718608 | tf_op jit(solution)/shard_map/all_gather | solution.py:70
  101.1 6.6 copy.51
  107.7 3.9 fusion.72
  111.9 52.3 %all-gather.14.cloned.1.call-done = bf16[2048,768]{1,0:T(8,128)(2,1)} async-done(((bf16[256,768]{1,0:T(8,128)(2,1)}), bf16[2048,768]{1,0:T(8,128)(2,1)}) %all-gather.14.cloned.1.call-update) | async-done | bytes 3145744 | tf_op jit(solution)/shard_map/all_gather | solution.py:109
  164.2 4.6 copy.49
  168.9 59.5 %all-gather.18.cloned.1.call-done = bf16[2048,768]{0,1:T(8,128)(2,1)} async-done(((bf16[256,768]{0,1:T(8,128)(2,1)}), bf16[2048,768]{0,1:T(8,128)(2,1)}) %all-gather.18.cloned.1.call-update) | async-done | bytes 3145744 | tf_op jit(solution)/shard_map/all_gather | solution.py:108
  228.4 46.4 %while.48 = (s32[]{:T(128)}, f32[256,8,2]{0,2,1:T(2,128)S(1)}, f32[256,8,2]{0,2,1:T(2,128)S(1)}, s32[2048]{0:T(1024)S(1)}, s32[256]{0:T(256)S(1)}, /*index=5*/bf...) while((s32[]{:T(128)}, f32[256,8,2]{0,2,1:T(2,128)S(1)}, ...), condition=%wide.region_4.5_spmd.clone, body=%wide.region_1.4_spmd.clone.sunk | while | flops 417484800 | bytes 18963636 | solution.py:138
  228.6 5.8 fusion.153
  234.5 6.3 exponential_reduce_fusion.2
  241.1 5.8 fusion.153
  247.0 5.2 exponential_reduce_fusion.2
  252.4 5.8 fusion.153
  258.3 5.1 exponential_reduce_fusion.2
  263.7 5.8 fusion.153
  269.6 5.2 exponential_reduce_fusion.2
  274.9 24.7 %while.49 = (s32[]{:T(128)}, f32[256,8,2,96]{0,3,2,1:T(8,128)}, bf16[2048,8,96]{0,2,1:T(8,128)(2,1)}, s32[2048]{0:T(1024)S(1)}, s32[256]{0:T(256)S(1)}, /*index=...) while((s32[]{:T(128)}, f32[256,8,2,96]{0,3,2,1:T(8,128)}, ...), condition=%wide.region_6.7_spmd.clone, body=%wide.region_5.6_spmd.clone.sunk | while | flops 814612480 | bytes 5792440 | solution.py:150
  275.1 5.7 bitcast_add_fusion.4
  281.0 6.2 bitcast_add_fusion.4
  287.4 5.9 bitcast_add_fusion.4
  293.6 5.9 bitcast_add_fusion.4
  301.9 4.1 multiply_reduce_fusion.3
  307.4 41.8 %all-gather.24.cloned.1.call-done = bf16[1536,4096]{1,0:T(8,128)(2,1)} async-done(((bf16[384,4096]{1,0:T(8,128)(2,1)}), bf16[1536,4096]{1,0:T(8,128)(2,1)}) %all-gather.24.cloned.1.call-update) | async-done | bytes 12582928 | tf_op jit(solution)/shard_map/all_gather | solution.py:75
  349.2 9.5 fusion.87
  358.7 74.2 %all-gather.26.cloned.1.call-done = bf16[1536,4096]{1,0:T(8,128)(2,1)} async-done(((bf16[384,4096]{1,0:T(8,128)(2,1)}), bf16[1536,4096]{1,0:T(8,128)(2,1)}) %all-gather.26.cloned.1.call-update) | async-done | bytes 12582928 | tf_op jit(solution)/shard_map/all_gather | solution.py:76
  432.9 10.0 fusion.88
  442.9 73.7 %all-gather.28.cloned.1.call-done = bf16[1536,4096]{1,0:T(8,128)(2,1)} async-done(((bf16[384,4096]{1,0:T(8,128)(2,1)}), bf16[1536,4096]{1,0:T(8,128)(2,1)}) %all-gather.28.cloned.1.call-update) | async-done | bytes 12582928 | tf_op jit(solution)/shard_map/all_gather | solution.py:77
  516.6 10.8 multiply_convert_fusion
  527.4 8.0 fusion.89
  535.4 7.5 multiply_reduce_fusion
  544.7 4.6 convolution_convert_fusion.7
  557.5 84.5 %while.50 = (s32[]{:T(128)}, f32[256,8,2,96]{0,3,2,1:T(8,128)S(1)}, bf16[2048,768]{0,1:T(8,128)(2,1)}, bf16[2048,768]{0,1:T(8,128)(2,1)}, bf16[2048,8,96]{0,2,1:...) while((s32[]{:T(128)}, f32[256,8,2,96]{0,3,2,1:T(8,128)S(1)}, ...), condition=%wide.region_11.12_spmd.clone, body=%wide.region_10.11_spmd.clone.sunk | while | flops 2036334592 | bytes 141745520 | solution.py:222
  563.4 5.4 fusion.171
  584.5 5.4 fusion.171
  589.9 3.5 bitcast_add_fusion.5
  605.5 5.4 fusion.171
  610.9 3.5 bitcast_add_fusion.5
  626.6 5.4 fusion.171
  632.0 3.5 bitcast_add_fusion.5
  643.1 8.5 fusion.47
  651.6 16.9 copy.65
  670.6 3.7 convolution_convert_fusion.4
  675.7 4.8 convolution_convert_fusion.3
  680.6 36.8 %reduce-scatter.12.cloned.1.call-done = bf16[256,768]{0,1:T(8,128)(2,1)} async-done(((bf16[2048,768]{0,1:T(8,128)(2,1)}), bf16[256,768]{0,1:T(8,128)(2,1)}) %reduce-scatter.12.cloned.1.call-update) | async-done | bytes 393232 | tf_op jit(solution)/shard_map/reduce_scatter | solution.py:226
  721.0 73.8 %reduce-scatter.14.cloned.1.call-done = bf16[256,768]{0,1:T(8,128)(2,1)} async-done(((bf16[2048,768]{0,1:T(8,128)(2,1)}), bf16[256,768]{0,1:T(8,128)(2,1)}) %reduce-scatter.14.cloned.1.call-update) | async-done | bytes 393232 | tf_op jit(solution)/shard_map/reduce_scatter | solution.py:229
  798.2 9.6 convolution_convert_fusion.2
  807.9 9.4 convolution_convert_fusion.1
  817.6 77.9 %reduce-scatter.28.cloned.1.call-done = bf16[384,4096]{1,0:T(8,128)(2,1)} async-done(((bf16[1536,4096]{1,0:T(8,128)(2,1)}), bf16[384,4096]{1,0:T(8,128)(2,1)}) %reduce-scatter.28.cloned.1.call-update) | async-done | bytes 3145744
  895.5 4.6 copy.66
  900.1 46.4 %reduce-scatter.16.cloned.1.call-done = bf16[384,1536]{1,0:T(8,128)(2,1)} async-done(((bf16[1536,1536]{1,0:T(8,128)(2,1)}), bf16[384,1536]{1,0:T(8,128)(2,1)}) %reduce-scatter.16.cloned.1.call-update) | async-done | bytes 1179664 | tf_op jit(solution)/shard_map/reduce_scatter | solution.py:281
  946.5 51.0 %reduce-scatter.22.cloned.1.call-done = bf16[384,1536]{1,0:T(8,128)(2,1)} async-done(((bf16[1536,1536]{1,0:T(8,128)(2,1)}), bf16[384,1536]{1,0:T(8,128)(2,1)}) %reduce-scatter.22.cloned.1.call-update) | async-done | bytes 1179664 | tf_op jit(solution)/shard_map/reduce_scatter | solution.py:270
  997.5 36.1 %reduce-scatter.18.cloned.1.call-done = bf16[384,768]{1,0:T(8,128)(2,1)} async-done(((bf16[1536,768]{1,0:T(8,128)(2,1)}), bf16[384,768]{1,0:T(8,128)(2,1)}) %reduce-scatter.18.cloned.1.call-update) | async-done | bytes 589840 | tf_op jit(solution)/shard_map/reduce_scatter | solution.py:287
  1033.6 36.2 %reduce-scatter.20.cloned.1.call-done = bf16[384,768]{1,0:T(8,128)(2,1)} async-done(((bf16[1536,768]{1,0:T(8,128)(2,1)}), bf16[384,768]{1,0:T(8,128)(2,1)}) %reduce-scatter.20.cloned.1.call-update) | async-done | bytes 589840 | tf_op jit(solution)/shard_map/reduce_scatter | solution.py:293
  1069.8 101.5 %reduce-scatter.24.cloned.1.call-done = bf16[384,4096]{1,0:T(8,128)(2,1)} async-done(((bf16[1536,4096]{1,0:T(8,128)(2,1)}), bf16[384,4096]{1,0:T(8,128)(2,1)}) %reduce-scatter.24.cloned.1.call-update) | async-done | bytes 3145744 | tf_op jit(solution)/shard_map/reduce_scatter | solution.py:258
  1171.3 101.5 %reduce-scatter.26.cloned.1.call-done = bf16[384,4096]{1,0:T(8,128)(2,1)} async-done(((bf16[1536,4096]{1,0:T(8,128)(2,1)}), bf16[384,4096]{1,0:T(8,128)(2,1)}) %reduce-scatter.26.cloned.1.call-update) | async-done | bytes 3145744 | tf_op jit(solution)/shard_map/reduce_scatter | solution.py:264
  1274.8 3.9 fusion.90
  1278.8 7.7 fusion.50
  1290.3 6.4 all-reduce.4
  1296.9 22.7 %all-reduce.2 = (bf16[384]{0:T(512)(128)(2,1)S(1)}, bf16[384]{0:T(512)(128)(2,1)S(1)}) all-reduce(bf16[384]{0:T(512)(128)(2,1)S(1)} %dynamic-slice.2, bf16[384]{0:T(512)(128)(2,1)S(1)} %dynamic-slice.4), channel_id=1, replica_groups=mesh['ctx'=8,'fsdp'=4] {'ctx'}, use_global_device_ids=true, to_apply=%region_17.18 | all-reduce | flops 768 | bytes 3072 | tf_op jit(solution)/shard_map/psum | solution.py:304
  1323.9 369.0 %all-reduce.7.cloned.1.call-done = (bf16[384,4096]{0,1:T(8,128)(2,1)}, bf16[384,1536]{1,0:T(8,128)(2,1)}, bf16[384,768]{1,0:T(8,128)(2,1)}, bf16[384,768]{1,0:T(...) async-done(((bf16[384,4096]{0,1:T(8,128)(2,1)}, bf16[384,1536]{1,0:T(8,128)(2,1)}, bf16[384,768]{1,0:T(8,128)(2,1)}, ...) | async-done | bytes 12976144 | tf_op jit(solution)/shard_map/psum | solution.py:312
  1706.8 3.6 copy.53
  (257 shorter events, 117.5 us)
Async XLA Ops:
  7.2 2.3 copy-start.37
  7.2 8.4 copy-start.3
  7.2 29.2 %all-gather.12.cloned.1.call-start = ((), (), s32[]{:S(2)}) async-start(), calls=%async_computation.9 | async-start | bytes 2949120 | tf_op jit(solution)/shard_map/all_gather | solution.py:72
  7.9 54.1 %all-gather.16.cloned.1.call-start = ((), (), s32[]{:S(2)}) async-start(), calls=%async_computation.11 | async-start | bytes 2949120 | tf_op jit(solution)/shard_map/all_gather | solution.py:71
  8.7 92.4 %all-gather.20.cloned.1.call-start = ((), (), s32[]{:S(2)}) async-start(), calls=%async_computation.13 | async-start | bytes 5898240 | tf_op jit(solution)/shard_map/all_gather | solution.py:70
  9.4 154.8 %all-gather.14.cloned.1.call-start = ((), (), s32[]{:S(2)}) async-start(), calls=%async_computation.10 | async-start | bytes 3538944 | tf_op jit(solution)/shard_map/all_gather | solution.py:109
  15.6 92.1 %copy-start.30 = (f32[1536]{0:T(1024)}, f32[1536]{0:T(1024)S(1)}, u32[]{:S(2)}) copy-start(f32[1536]{0:T(1024)S(1)} %reshape.350) | copy-start | bytes 18436
  15.9 91.9 %copy-start.34 = (f32[256]{0:T(256)}, f32[256]{0:T(256)S(1)}, u32[]{:S(2)}) copy-start(f32[256]{0:T(256)S(1)} %add_rsqrt_fusion.1) | copy-start | bytes 3076
  15.9 23.8 %copy-start.33 = (s32[1,2048]{1,0:T(1,128)S(1)}, s32[1,2048]{1,0:T(1,128)}, u32[]{:S(2)}) copy-start(s32[1,2048]{1,0:T(1,128)} %param.20) | copy-start | bytes 24580
  39.7 188.7 %all-gather.18.cloned.1.call-start = ((), (), s32[]{:S(2)}) async-start(), calls=%async_computation.12 | async-start | bytes 3538944 | tf_op jit(solution)/shard_map/all_gather | solution.py:108
  40.6 71.0 %copy-start.25 = (f32[256,48]{0,1:T(8,128)}, f32[256,48]{0,1:T(8,128)S(1)}, u32[]{:S(2)}) copy-start(f32[256,48]{0,1:T(8,128)S(1)} %get-tuple-element.719) | copy-start | bytes 147460
  66.7 235.2 %all-gather.22.cloned.1.call-start = ((), (), s32[]{:S(2)}) async-start(), calls=%async_computation.14 | async-start | bytes 5898240 | tf_op jit(solution)/shard_map/all_gather | solution.py:73
  67.3 281.9 %all-gather.24.cloned.1.call-start = ((), (), s32[]{:S(2)}) async-start(), calls=%async_computation.15 | async-start | bytes 15728640 | tf_op jit(solution)/shard_map/all_gather | solution.py:75
  68.0 364.8 %all-gather.26.cloned.1.call-start = ((), (), s32[]{:S(2)}) async-start(), calls=%async_computation.16 | async-start | bytes 15728640 | tf_op jit(solution)/shard_map/all_gather | solution.py:76
  68.8 447.8 %all-gather.28.cloned.1.call-start = ((), (), s32[]{:S(2)}) async-start(), calls=%async_computation.17 | async-start | bytes 15728640 | tf_op jit(solution)/shard_map/all_gather | solution.py:77
  69.5 647.8 %reduce-scatter.12.cloned.1.call-start = ((), (), s32[]{:S(2)}) async-start(), calls=%async_computation.18 | async-start | bytes 3538944 | tf_op jit(solution)/shard_map/reduce_scatter | solution.py:226
  527.4 8.0 copy-start.23
  527.4 8.1 copy-start.22
  527.4 8.1 copy-start.9
  535.4 7.6 copy-start.12
  557.6 5.7 copy-start.16
  560.2 3.2 copy-start.1
  568.8 4.9 copy-start.2
  568.8 5.0 copy-start.17
  573.8 2.2 copy-start
  578.8 5.7 copy-start.16
  581.3 3.2 copy-start.1
  589.9 4.9 copy-start.2
  589.9 5.0 copy-start.17
  594.9 2.2 copy-start
  599.8 5.7 copy-start.16
  602.3 3.2 copy-start.1
  610.9 4.9 copy-start.2
  610.9 5.0 copy-start.17
  615.9 2.2 copy-start
  620.9 5.7 copy-start.16
  623.4 3.2 copy-start.1
  632.0 4.9 copy-start.2
  632.0 5.0 copy-start.17
  637.0 2.2 copy-start
  642.0 152.8 %reduce-scatter.14.cloned.1.call-start = ((), (), s32[]{:S(2)}) async-start(), calls=%async_computation.19 | async-start | bytes 3538944 | tf_op jit(solution)/shard_map/reduce_scatter | solution.py:229
  642.7 252.7 %reduce-scatter.28.cloned.1.call-start = ((), (), s32[]{:S(2)}) async-start(), calls=%async_computation.26 | async-start | bytes 15728640
  668.6 2.0 copy-start.4
  668.6 2.0 copy-start.31
  668.6 2.0 copy-start.35
  668.6 277.8 %reduce-scatter.16.cloned.1.call-start = ((), (), s32[]{:S(2)}) async-start(), calls=%async_computation.20 | async-start | bytes 5898240 | tf_op jit(solution)/shard_map/reduce_scatter | solution.py:281
  674.3 323.1 %reduce-scatter.22.cloned.1.call-start = ((), (), s32[]{:S(2)}) async-start(), calls=%async_computation.23 | async-start | bytes 5898240 | tf_op jit(solution)/shard_map/reduce_scatter | solution.py:270
  680.5 353.0 %reduce-scatter.18.cloned.1.call-start = ((), (), s32[]{:S(2)}) async-start(), calls=%async_computation.21 | async-start | bytes 2949120 | tf_op jit(solution)/shard_map/reduce_scatter | solution.py:287
  720.9 348.9 %reduce-scatter.20.cloned.1.call-start = ((), (), s32[]{:S(2)}) async-start(), calls=%async_computation.22 | async-start | bytes 2949120 | tf_op jit(solution)/shard_map/reduce_scatter | solution.py:293
  798.2 373.2 %reduce-scatter.24.cloned.1.call-start = ((), (), s32[]{:S(2)}) async-start(), calls=%async_computation.24 | async-start | bytes 15728640 | tf_op jit(solution)/shard_map/reduce_scatter | solution.py:258
  807.9 465.0 %reduce-scatter.26.cloned.1.call-start = ((), (), s32[]{:S(2)}) async-start(), calls=%async_computation.25 | async-start | bytes 15728640 | tf_op jit(solution)/shard_map/reduce_scatter | solution.py:264
  817.3 875.5 %all-reduce.7.cloned.1.call-start = ((), (), s32[]{:S(2)}) async-start(), calls=%async_computation.27 | async-start | bytes 25952256 | tf_op jit(solution)/shard_map/psum | solution.py:312
  1272.9 1.9 copy-start.15
  1274.8 4.0 copy-start.10
  1274.8 4.0 copy-start.11
  1278.7 7.7 copy-start.7
  1286.4 1.7 copy-start.24
  1288.1 2.2 copy-start.36
  1692.9 3.1 copy-start.29
  1692.9 4.2 copy-start.28
  1695.9 2.2 copy-start.27
  1697.0 2.8 copy-start.20
  1699.8 3.5 copy-start.19
  1703.3 3.5 copy-start.18
  (10 other events, 10.6 us)
Sparse Core Ops, SparseCore 0:
  9.6 26.7 all-gather.11
  37.9 24.0 all-gather.15
  63.6 37.4 all-gather.19
  103.7 60.4 all-gather.13
  166.7 61.6 all-gather.17
  229.8 35.6 all-gather.21
  267.0 82.0 all-gather.23
  350.7 82.0 all-gather.25
  434.4 82.0 all-gather.27
  642.1 75.1 reduce-scatter.11
  721.0 73.8 reduce-scatter.13
  797.3 98.1 reduce-scatter.27
  898.6 47.8 reduce-scatter.15
  949.6 47.8 reduce-scatter.21
  1000.4 33.0 reduce-scatter.17
  1036.7 33.0 reduce-scatter.19
  1072.2 99.0 reduce-scatter.23
  1173.8 99.0 reduce-scatter.25
  1279.1 413.6 all-reduce.6
where the time goes:
time: 1720 us
  waiting for transfers between devices  1310 us (76%)
  matrix products  226 us (13%)
  local copies, waits for them, and re-layouts  77.6 us (5%)
  other arithmetic  50.7 us (3%)
  blocking collectives  40.7 us (2%)
    psum x1, waiting for transfers between devices, body(): lax.psum(down_part, 'ctx').astype(jnp.float32)  369 us
    reduce_scatter x1, waiting for transfers between devices, body(): lax.psum_scatter(contract_first(normed_two, grad_gate).astype(jnp.bfloat1...  102 us
    reduce_scatter x1, waiting for transfers between devices, body(): lax.psum_scatter(contract_first(normed_two, grad_up).astype(jnp.bfloat16)...  102 us
    unnamed x20, waiting for transfers between devices  83.4 us
    all_gather x1, waiting for transfers between devices, body(): lax.all_gather(shards[7], 'fsdp', axis=0, tiled=True)  74.2 us
    reduce_scatter x1, waiting for transfers between devices, body(): lax.psum_scatter(grad_values.astype(jnp.bfloat16), 'ctx', scatter_dimensi...  73.8 us
    all_gather x1, waiting for transfers between devices, body(): lax.all_gather(shards[8], 'fsdp', axis=0, tiled=True)  73.7 us
    all_gather x1, waiting for transfers between devices, body(): lax.all_gather(keys_rot, 'ctx', axis=0, tiled=True)  59.5 us
  transfers between devices with their start and end apart: 19, of which 18 were waited for; matrix products, arithmetic and copies ran while one was open for 12% of the time, Pallas kernels for 0%

commit v1 on v0

v1 whole, which is shorter than its diff:
```python
import functools
import math

import jax
import jax.numpy as jnp
from jax import lax
from jax.experimental import pallas as pl
from jax.experimental.pallas import tpu as pltpu
from jax.sharding import PartitionSpec as P

HQ = 16
HK = 8
HD = 96
GROUP = HQ // HK
BLK = 128

epsilon = 1e-05
rope_base = 100000.0
masked_score = -1e30
scale = 1.0 / math.sqrt(HD)
low = jnp.bfloat16
wide = jnp.float32


def angles_of(places):
    frequency = jnp.exp(jnp.arange(HD // 2, dtype=wide) * (-2.0 * math.log(rope_base) / HD))
    turned = places.astype(wide)[:, None] * frequency[None, :]
    return (jnp.cos(turned)[:, None, :], jnp.sin(turned)[:, None, :])


def rotate(values, cosine, sine):
    half_size = values.shape[-1] // 2
    first_half = values[..., :half_size]
    second_half = values[..., half_size:]
    return jnp.concatenate(
        [first_half * cosine - second_half * sine, second_half * cosine + first_half * sine],
        axis=-1,
    )


def product(left, right):
    return jnp.dot(left, right, preferred_element_type=wide)


def contract_last(left, right):
    return lax.dot_general(left, right, (((1,), (1,)), ((), ())), preferred_element_type=wide)


def contract_first(left, right):
    return lax.dot_general(left, right, (((0,), (0,)), ((), ())), preferred_element_type=wide)


def rms_back(values, inverse, gain, grad_normed):
    weighted = gain * grad_normed
    inner = jnp.mean(values * weighted, axis=1, keepdims=True)
    grad_values = inverse * weighted - values * inverse * inverse * inverse * inner
    return (grad_values, jnp.sum(grad_normed * values * inverse, axis=0))


def swap(array, axis, bits, size):
    return lax.ppermute(array, axis, [(i, i ^ bits) for i in range(size)])


def over_fsdp(array, bits):
    return swap(array, "fsdp", bits, 4)


def over_ctx(array, bits):
    return swap(array, "ctx", bits, 8)


def columns(array, index, width):
    return lax.dynamic_slice_in_dim(array, index * width, width, 1)


def rows(array, index, height):
    return lax.dynamic_slice_in_dim(array, index * height, height, 0)


def gather_fsdp(array):
    far = over_fsdp(array, 2)
    near = over_fsdp(array, 1)
    both = over_fsdp(far, 1)
    return (array, near, far, both)


def scatter_fsdp(parts):
    near = [over_fsdp(parts[1].astype(low), 1), over_fsdp(parts[3].astype(low), 1)]
    own = parts[0].astype(wide) + near[0].astype(wide)
    away = parts[2].astype(wide) + near[1].astype(wide)
    return own + over_fsdp(away.astype(low), 2).astype(wide)


def stack_kernel(index_ref, *refs):
    parts, out_ref = refs[:4], refs[4]
    for k in range(4):

        @pl.when(pl.program_id(1) == index_ref[0] ^ k)
        def _(k=k):
            out_ref[...] = parts[k][...]


def stack_rows(index, parts):
    height, width = parts[0].shape
    tile = math.gcd(width, 768) if width % 768 == 0 else math.gcd(width, 512)
    return pl.pallas_call(
        stack_kernel,
        grid_spec=pltpu.PrefetchScalarGridSpec(
            num_scalar_prefetch=1,
            grid=(width // tile, 4),
            in_specs=[pl.BlockSpec((height, tile), lambda j, i, index: (0, j))] * 4,
            out_specs=pl.BlockSpec((height, tile), lambda j, i, index: (i, j)),
        ),
        out_shape=jax.ShapeDtypeStruct((4 * height, width), parts[0].dtype),
        cost_estimate=pl.CostEstimate(
            flops=0, bytes_accessed=16 * height * width, transcendentals=0
        ),
        name="stack_rows",
    )(index.reshape(1), *parts)


def sort_rows(order_ref, load_ref, queries, keys, values):
    for slot in range(load_ref.shape[0] // BLK):
        block = order_ref[slot]
        piece = load_ref[slot * BLK : (slot + 1) * BLK, :]
        place = pl.ds(pl.multiple_of(block * BLK, BLK), BLK)
        half = pl.ds(pl.multiple_of((block % 2) * BLK, BLK), BLK)
        other = pl.ds(pl.multiple_of((block % 2) * BLK + 2 * BLK, BLK), BLK)
        queries[block // 2, half, :] = piece[:, :HD]
        queries[block // 2, other, :] = piece[:, HD : 2 * HD]
        keys[place, :] = piece[:, 2 * HD : 3 * HD]
        values[place, :] = piece[:, 3 * HD :]


def forward_kernel(order_ref, load_ref, out_ref, queries, keys, values, mixed):
    sort_rows(order_ref, load_ref, queries, keys, values)
    step = 2 * BLK
    query_at = lax.broadcasted_iota(jnp.int32, (2 * step, step), 0) % step
    key_at = lax.broadcasted_iota(jnp.int32, (2 * step, step), 1)
    allowed = key_at <= query_at
    for i in range(keys.shape[0] // step):
        reach = (i + 1) * step
        query = queries[i]
        ahead = contract_last(query, keys[i * step : reach, :]) * scale
        ahead = jnp.where(allowed, ahead, masked_score)
        top = jnp.max(ahead, axis=1, keepdims=True)
        if i:
            before = contract_last(query, keys[: i * step, :]) * scale
            top = jnp.maximum(top, jnp.max(before, axis=1, keepdims=True))
        soft = jnp.exp(ahead - top)
        total = jnp.sum(soft, axis=1, keepdims=True)
        result = product(soft.astype(low), values[i * step : reach, :])
        if i:
            soft = jnp.exp(before - top)
            total = total + jnp.sum(soft, axis=1, keepdims=True)
            result = result + product(soft.astype(low), values[: i * step, :])
        result = (result / total).astype(low)
        mixed[i * step : reach, :HD] = result[:step]
        mixed[i * step : reach, HD:] = result[step:]
    for slot in range(load_ref.shape[0] // BLK):
        place = pl.ds(pl.multiple_of(order_ref[slot] * BLK, BLK), BLK)
        out_ref[slot * BLK : (slot + 1) * BLK, :] = mixed[place, :]


def backward_kernel(
    order_ref, load_ref, grad_ref, out_ref, queries, keys, values, grads, key_sum, value_sum, sent
):
    sort_rows(order_ref, load_ref, queries, keys, values)
    step = 2 * BLK
    length = keys.shape[0]
    for slot in range(length // BLK):
        block = order_ref[slot]
        piece = grad_ref[slot * BLK : (slot + 1) * BLK, :]
        half = pl.ds(pl.multiple_of((block % 2) * BLK, BLK), BLK)
        other = pl.ds(pl.multiple_of((block % 2) * BLK + 2 * BLK, BLK), BLK)
        grads[block // 2, half, :] = piece[:, :HD]
        grads[block // 2, other, :] = piece[:, HD:]
    key_at = lax.broadcasted_iota(jnp.int32, (step, 2 * step), 0)
    query_at = lax.broadcasted_iota(jnp.int32, (step, 2 * step), 1) % step
    allowed = key_at <= query_at
    for i in range(length // step):
        query = queries[i]
        grad = grads[i]
        scores = []
        top = None
        for j in range(i + 1):
            score = contract_last(keys[j * step : (j + 1) * step, :], query) * scale
            if j == i:
                score = jnp.where(allowed, score, masked_score)
            high = jnp.max(score, axis=0, keepdims=True)
            top = high if top is None else jnp.maximum(top, high)
            scores.append(score)
        total = jnp.zeros_like(top)
        delta = jnp.zeros_like(top)
        softs = []
        slopes = []
        for j in range(i + 1):
            soft = jnp.exp(scores[j] - top)
            slope = contract_last(values[j * step : (j + 1) * step, :], grad)
            total = total + jnp.sum(soft, axis=0, keepdims=True)
            delta = delta + jnp.sum(soft * slope, axis=0, keepdims=True)
            softs.append(soft)
            slopes.append(slope)
        share = 1.0 / total
        delta = delta * share
        query_sum = jnp.zeros((2 * step, HD), wide)
        for j in range(i + 1):
            place = slice(j * step, (j + 1) * step)
            soft = softs[j] * share
            steep = (soft * (slopes[j] - delta)).astype(low)
            key_part = product(steep, query)
            value_part = product(soft.astype(low), grad)
            if j == i:
                key_sum[place, :] = key_part
                value_sum[place, :] = value_part
            else:
                key_sum[place, :] += key_part
                value_sum[place, :] += value_part
            query_sum = query_sum + contract_first(steep, keys[place, :])
        query_sum = (query_sum * scale).astype(low)
        sent[i * step : (i + 1) * step, :HD] = query_sum[:step]
        sent[i * step : (i + 1) * step, HD : 2 * HD] = query_sum[step:]
    sent[:, 2 * HD : 3 * HD] = (key_sum[...] * scale).astype(low)
    sent[:, 3 * HD :] = value_sum[...].astype(low)
    for slot in range(length // BLK):
        place = pl.ds(pl.multiple_of(order_ref[slot] * BLK, BLK), BLK)
        out_ref[slot * BLK : (slot + 1) * BLK, :] = sent[place, :]


def attention_call(kernel, order, arrays, width, scratch, products, name):
    length = arrays[0].shape[0]
    half = (length * length) // 2 * GROUP
    whole = pl.BlockSpec(memory_space=pltpu.VMEM)
    return pl.pallas_call(
        kernel,
        grid_spec=pltpu.PrefetchScalarGridSpec(
            num_scalar_prefetch=1,
            grid=(),
            in_specs=[whole] * len(arrays),
            out_specs=whole,
            scratch_shapes=scratch,
        ),
        out_shape=jax.ShapeDtypeStruct((length, width), low),
        compiler_params=pltpu.CompilerParams(vmem_limit_bytes=56 << 20),
        cost_estimate=pl.CostEstimate(
            flops=2 * products * half * 256, bytes_accessed=8 * length * width, transcendentals=half
        ),
        name=name,
    )(order, *arrays)


def attention_forward(order, load):
    length = load.shape[0]
    scratch = [
        pltpu.VMEM((length // (2 * BLK), 4 * BLK, HD), low),
        pltpu.VMEM((length, HD), low),
        pltpu.VMEM((length, HD), low),
        pltpu.VMEM((length, 2 * HD), low),
    ]
    return attention_call(forward_kernel, order, (load,), 2 * HD, scratch, 2, "attention_forward")


def attention_backward(order, load, grad):
    length = load.shape[0]
    scratch = [
        pltpu.VMEM((length // (2 * BLK), 4 * BLK, HD), low),
        pltpu.VMEM((length, HD), low),
        pltpu.VMEM((length, HD), low),
        pltpu.VMEM((length // (2 * BLK), 4 * BLK, HD), low),
        pltpu.VMEM((length, HD), wide),
        pltpu.VMEM((length, HD), wide),
        pltpu.VMEM((length, 4 * HD), low),
    ]
    return attention_call(
        backward_kernel, order, (load, grad), 4 * HD, scratch, 5, "attention_backward"
    )


def scores_of(query_rot, keys_all, own_places, all_places, start, block_size):
    key_block = lax.dynamic_slice_in_dim(keys_all, start, block_size, 0)
    key_places = lax.dynamic_slice_in_dim(all_places, start, block_size, 0)
    raw = (
        jnp.einsum("rkgd,skd->rkgs", query_rot, key_block, preferred_element_type=wide) * scale
    )
    allowed = key_places[None, None, None, :] <= own_places[:, None, None, None]
    return (jnp.where(allowed, raw, masked_score), key_block)


def rows_forward(query_rot, keys_all, values_all, own_places, all_places):
    row_count = query_rot.shape[0]
    key_total = keys_all.shape[0]
    block_size = math.gcd(key_total, 512)

    def step(block_index, carry):
        top_score, total, mixed = carry
        start = block_index * block_size
        scores, _ = scores_of(query_rot, keys_all, own_places, all_places, start, block_size)
        value_block = lax.dynamic_slice_in_dim(values_all, start, block_size, 0)
        new_top = jnp.maximum(top_score, jnp.max(scores, axis=-1))
        soft = jnp.exp(scores - new_top[..., None])
        shrink = jnp.exp(top_score - new_top)
        total = total * shrink + jnp.sum(soft, axis=-1)
        mixed = mixed * shrink[..., None] + jnp.einsum(
            "rkgs,skd->rkgd", soft.astype(low), value_block, preferred_element_type=wide
        )
        return (new_top, total, mixed)

    start_top = jnp.full((row_count, HK, GROUP), masked_score, wide)
    start_total = jnp.zeros((row_count, HK, GROUP), wide)
    start_mixed = jnp.zeros((row_count, HK, GROUP, HD), wide)
    top_score, total, mixed = lax.fori_loop(
        0, key_total // block_size, step, (start_top, start_total, start_mixed)
    )
    return (mixed / total[..., None], top_score + jnp.log(total))


def rows_backward(
    query_rot, keys_all, values_all, own_places, all_places, log_total, delta, grad_mixed
):
    row_count = query_rot.shape[0]
    key_total = keys_all.shape[0]
    block_size = math.gcd(key_total, 512)

    def step(block_index, carry):
        grad_query, grad_keys, grad_values = carry
        start = block_index * block_size
        scores, key_block = scores_of(
            query_rot, keys_all, own_places, all_places, start, block_size
        )
        value_block = lax.dynamic_slice_in_dim(values_all, start, block_size, 0)
        soft = jnp.exp(scores - log_total[..., None])
        grad_soft = jnp.einsum(
            "rkgd,skd->rkgs", grad_mixed, value_block, preferred_element_type=wide
        )
        steep = (soft * (grad_soft - delta[..., None])).astype(low)
        grad_query = grad_query + scale * jnp.einsum(
            "rkgs,skd->rkgd", steep, key_block, preferred_element_type=wide
        )
        key_part = scale * jnp.einsum(
            "rkgs,rkgd->skd", steep, query_rot, preferred_element_type=wide
        )
        value_part = jnp.einsum(
            "rkgs,rkgd->skd", soft.astype(low), grad_mixed, preferred_element_type=wide
        )
        grad_keys = lax.dynamic_update_slice_in_dim(
            grad_keys, key_part.reshape(block_size, HK * HD), start, 0
        )
        grad_values = lax.dynamic_update_slice_in_dim(
            grad_values, value_part.reshape(block_size, HK * HD), start, 0
        )
        return (grad_query, grad_keys, grad_values)

    start_query = jnp.zeros((row_count, HK, GROUP, HD), wide)
    start_keys = jnp.zeros((key_total, HK * HD), wide)
    return lax.fori_loop(
        0, key_total // block_size, step, (start_query, start_keys, start_keys)
    )


def add_low(first, *others):
    total = first.astype(wide)
    for other in others:
        total = total + other.astype(wide)
    return total.astype(low)


def reduce_ctx(grad, dim, size):
    here = lax.axis_index("ctx")
    if size != 8:
        return lax.psum_scatter(grad, "ctx", scatter_dimension=dim, tiled=True)
    cut = (rows, columns)[dim]
    side, level = here % 2, here // 2
    half = grad.shape[dim] // 2
    piece = grad.shape[dim] // 8
    kept = add_low(cut(grad, side, half), over_ctx(cut(grad, 1 - side, half), 1))
    got = [over_ctx(cut(kept, level ^ k, piece), 2 * k) for k in (1, 2, 3)]
    return add_low(cut(kept, level, piece), *got)


def spread_kernel(where_ref, *refs):
    parts, out_ref = refs[:8], refs[8]
    piece = parts[0].shape[0]
    for k in range(8):
        place = pl.multiple_of((where_ref[0] ^ k) * piece, piece)
        out_ref[pl.ds(place, piece), :] = parts[k][...].astype(wide)


def spread_columns_kernel(where_ref, *refs):
    parts, out_ref = refs[:8], refs[8]
    piece = parts[0].shape[2]
    for k in range(8):
        place = pl.multiple_of((where_ref[0] ^ k) * piece, piece)
        out_ref[:, pl.ds(place, piece)] = parts[k][0].astype(wide)


def gather_ctx(piece):
    near = [piece] + [over_ctx(piece, 2 * k) for k in (1, 2, 3)]
    return near + [over_ctx(part, 1) for part in near]


def place_code(here):
    return (here % 2) * 4 + here // 2


def finish_rows(piece, size):
    if size != 8:
        return lax.all_gather(piece, "ctx", axis=0, tiled=True).astype(wide)
    parts = gather_ctx(piece)
    height, width = piece.shape
    tile = 384
    return pl.pallas_call(
        spread_kernel,
        grid_spec=pltpu.PrefetchScalarGridSpec(
            num_scalar_prefetch=1,
            grid=(width // tile,),
            in_specs=[pl.BlockSpec((height, tile), lambda i, where: (0, i))] * 8,
            out_specs=pl.BlockSpec((8 * height, tile), lambda i, where: (0, i)),
        ),
        out_shape=jax.ShapeDtypeStruct((8 * height, width), wide),
        cost_estimate=pl.CostEstimate(
            flops=0, bytes_accessed=48 * height * width, transcendentals=0
        ),
        name="spread_rows",
    )(place_code(lax.axis_index("ctx")).reshape(1), *parts)


def finish_columns(piece, size):
    here, part = lax.axis_index("ctx"), lax.axis_index("fsdp")
    height, width = piece.shape[1:]
    if size != 8:
        whole = lax.all_gather(piece, "ctx", axis=2, tiled=True)
        return jnp.concatenate(
            [
                lax.dynamic_index_in_dim(whole, part ^ k, 0, keepdims=False)
                for k in range(4)
            ],
            axis=1,
        ).astype(wide)
    parts = gather_ctx(piece)
    return pl.pallas_call(
        spread_columns_kernel,
        grid_spec=pltpu.PrefetchScalarGridSpec(
            num_scalar_prefetch=1,
            grid=(4,),
            in_specs=[pl.BlockSpec((1, height, width), lambda i, where: (where[1] ^ i, 0, 0))] * 8,
            out_specs=pl.BlockSpec((height, 8 * width), lambda i, where: (0, i)),
        ),
        out_shape=jax.ShapeDtypeStruct((height, 32 * width), wide),
        cost_estimate=pl.CostEstimate(
            flops=0, bytes_accessed=192 * height * width, transcendentals=0
        ),
        name="spread_columns",
    )(jnp.stack([place_code(here), part]), *parts)


def split_weight_grad(left, right, size):
    part = lax.axis_index("fsdp")
    piece = reduce_ctx(contract_first(left, right).astype(low), 1, size)
    height = piece.shape[0] // 4
    got = [over_fsdp(rows(piece, part ^ k, height), k) for k in (1, 2, 3)]
    return finish_columns(jnp.stack([rows(piece, part, height)] + got), size)


def own_rows_grad(left, right, size):
    part = lax.axis_index("fsdp")
    width = left.shape[1] // 4

    def term(k):
        return contract_first(columns(left, part ^ k, width), right)

    summed = scatter_fsdp([term(0), term(1), term(2), term(3)]).astype(low)
    return finish_rows(reduce_ctx(summed, 0, size), size)


def body(
    size,
    hidden_in,
    out_grad,
    positions,
    attn_gain,
    w_query,
    w_key,
    w_value,
    w_out,
    ffn_gain,
    w_gate,
    w_up,
    w_down,
):
    part, here = lax.axis_index("fsdp"), lax.axis_index("ctx")
    gains = lax.all_gather(jnp.stack([attn_gain, ffn_gain]), "fsdp", axis=1, tiled=True)
    gain_one, gain_two = gains[0].astype(wide), gains[1].astype(wide)

    def gathered(weight):
        return stack_rows(part, gather_fsdp(weight))

    def dealt(weight):
        width = weight.shape[1] // 4
        got = [over_fsdp(columns(weight, part ^ k, width), k) for k in (1, 2, 3)]
        return stack_rows(part, [columns(weight, part, width)] + got)

    full_query, full_key, full_value = gathered(w_query), gathered(w_key), gathered(w_value)
    full_out = gathered(w_out)
    part_gate, part_up, part_down = dealt(w_gate), dealt(w_up), dealt(w_down)

    rows_in = hidden_in[0].astype(wide)
    row_count = rows_in.shape[0]
    all_places = positions[0]
    own_places = lax.dynamic_slice_in_dim(all_places, here * row_count, row_count, 0)
    cosine, sine = angles_of(own_places)
    inverse_one = lax.rsqrt(jnp.mean(rows_in * rows_in, axis=1, keepdims=True) + epsilon)
    normed_one = (rows_in * inverse_one * gain_one).astype(low)
    query = product(normed_one, full_query)
    keys = product(normed_one, full_key)
    values = product(normed_one, full_value).astype(low)
    query_rot = rotate(query.reshape(row_count, HQ, HD), cosine, sine).astype(low)
    keys_rot = rotate(keys.reshape(row_count, HK, HD), cosine, sine).astype(low)

    if size == HK:
        load = jnp.concatenate(
            [
                query_rot.reshape(row_count, HK, GROUP * HD),
                keys_rot,
                values.reshape(row_count, HK, HD),
            ],
            axis=-1,
        ).transpose(1, 0, 2)
        load = lax.all_to_all(load, "ctx", 0, 0, tiled=True).reshape(size * row_count, 4 * HD)
        order = all_places[:: BLK] // BLK
        mixed = attention_forward(order, load).reshape(size, row_count, GROUP * HD)
        mixed_low = lax.all_to_all(mixed, "ctx", 0, 0, tiled=True)
        mixed_low = mixed_low.transpose(1, 0, 2).reshape(row_count, HQ * HD)
    else:
        keys_all = lax.all_gather(keys_rot, "ctx", axis=0, tiled=True)
        values_all = lax.all_gather(
            values.reshape(row_count, HK, HD), "ctx", axis=0, tiled=True
        )
        query_rot = query_rot.reshape(row_count, HK, GROUP, HD)
        mixed_exact, log_total = rows_forward(
            query_rot, keys_all, values_all, own_places, all_places
        )
        mixed_low = mixed_exact.reshape(row_count, HQ * HD).astype(low)

    middle = rows_in + contract_last(mixed_low, full_out)
    inverse_two = lax.rsqrt(jnp.mean(middle * middle, axis=1, keepdims=True) + epsilon)
    normed_two = (middle * inverse_two * gain_two).astype(low)

    normed_all = jnp.concatenate(gather_fsdp(normed_two), axis=0)
    grad_all = jnp.concatenate(gather_fsdp(out_grad[0]), axis=0)

    def quarters(array):
        return [array[k * row_count : (k + 1) * row_count] for k in range(4)]

    gate = product(normed_all, part_gate)
    upward = product(normed_all, part_up)
    sigmoid_gate = jax.nn.sigmoid(gate)
    swish = gate * sigmoid_gate
    hidden = (swish * upward).astype(low)
    result = (middle + scatter_fsdp(quarters(contract_last(hidden, part_down)))).astype(low)
    grad_hidden = product(grad_all, part_down)
    grad_gate = (grad_hidden * upward * sigmoid_gate * (1.0 + gate * (1.0 - sigmoid_gate))).astype(
        low
    )
    grad_up = (grad_hidden * swish).astype(low)
    grad_normed_two = scatter_fsdp(
        quarters(contract_last(grad_gate, part_gate) + contract_last(grad_up, part_up))
    )
    grad_middle_norm, grad_gain_two = rms_back(middle, inverse_two, gain_two, grad_normed_two)
    grad_middle = out_grad[0].astype(wide) + grad_middle_norm
    grad_branch = grad_middle.astype(low)
    grad_mixed = product(grad_branch, full_out).astype(low)

    if size == HK:
        grad_mixed = grad_mixed.reshape(row_count, HK, GROUP * HD).transpose(1, 0, 2)
        grad_mixed = lax.all_to_all(grad_mixed, "ctx", 0, 0, tiled=True)
        grad_load = attention_backward(
            order, load, grad_mixed.reshape(size * row_count, GROUP * HD)
        ).reshape(size, row_count, 4 * HD)
        grad_load = lax.all_to_all(grad_load, "ctx", 0, 0, tiled=True)
        grad_load = grad_load.transpose(1, 0, 2).astype(wide)
        grad_query = grad_load[:, :, : GROUP * HD].reshape(row_count, HQ, HD)
        grad_keys = grad_load[:, :, GROUP * HD : (GROUP + 1) * HD]
        grad_values = grad_load[:, :, (GROUP + 1) * HD :].reshape(row_count, HK * HD)
    else:
        grad_mixed = grad_mixed.reshape(row_count, HK, GROUP, HD)
        delta = jnp.sum(grad_mixed.astype(wide) * mixed_exact, axis=-1)
        grad_query, grad_keys, grad_values = rows_backward(
            query_rot, keys_all, values_all, own_places, all_places, log_total, delta, grad_mixed
        )
        grad_query = grad_query.reshape(row_count, HQ, HD)
        grad_keys, grad_values = (
            lax.psum_scatter(whole.astype(low), "ctx", scatter_dimension=0, tiled=True).astype(
                wide
            )
            for whole in (grad_keys, grad_values)
        )
        grad_keys = grad_keys.reshape(row_count, HK, HD)
    grad_query_raw = rotate(grad_query, cosine, -sine).reshape(row_count, HQ * HD).astype(low)
    grad_keys_raw = rotate(grad_keys, cosine, -sine).reshape(row_count, HK * HD).astype(low)
    grad_values_low = grad_values.astype(low)
    grad_normed_one = (
        contract_last(grad_query_raw, full_query)
        + contract_last(grad_keys_raw, full_key)
        + contract_last(grad_values_low, full_value)
    )
    grad_rows_norm, grad_gain_one = rms_back(rows_in, inverse_one, gain_one, grad_normed_one)
    input_grad = (grad_middle + grad_rows_norm)[None]

    down_grad = split_weight_grad(grad_all, hidden, size)
    gate_grad = split_weight_grad(normed_all, grad_gate, size)
    up_grad = split_weight_grad(normed_all, grad_up, size)
    out_weight_grad = own_rows_grad(grad_branch, mixed_low, size)
    value_grad = own_rows_grad(normed_one, grad_values_low, size)
    key_grad = own_rows_grad(normed_one, grad_keys_raw, size)
    query_grad = own_rows_grad(normed_one, grad_query_raw, size)
    gain_grads = lax.psum(jnp.stack([grad_gain_one, grad_gain_two]), ("ctx", "fsdp"))
    gain_grads = columns(gain_grads, part, attn_gain.shape[0])
    return (
        result[None],
        input_grad,
        gain_grads[0],
        query_grad,
        key_grad,
        value_grad,
        out_weight_grad,
        gain_grads[1],
        gate_grad,
        up_grad,
        down_grad,
    )


def solution(mesh):
    matrix = P("fsdp", None)
    stream = P("fsdp", "ctx", None)
    return jax.shard_map(
        functools.partial(body, mesh.shape["ctx"]),
        mesh=mesh,
        in_specs=(stream, stream, matrix, P("fsdp"))
        + (matrix,) * 4
        + (P("fsdp"),)
        + (matrix,) * 3,
        out_specs=(stream, stream, P("fsdp")) + (matrix,) * 4 + (P("fsdp"),) + (matrix,) * 3,
        check_vma=False,
    )
```

time: 1720 us -> 1040 us (0.60)
  waiting for transfers between devices: 1310 us -> 419 us
  starting transfers between devices: 1.23 us -> 251 us
  matrix products: 226 us -> 79 us
  Pallas kernels: 0 us -> 103 us
  blocking collectives: 40.7 us -> 88.7 us
  local copies, waits for them, and re-layouts: 77.6 us -> 50.4 us
    reduce_scatter x8 -> x0, waiting for transfers between devices: 483 us -> none  [the longest x1 102 us: body(): lax.psum_scatter(contract_first(normed_two, grad_gate).astype(jnp.bfloat1...]
    ppermute x0 -> x131, waiting for transfers between devices: none -> 384 us  [swap(): return lax.ppermute(array, axis, [(i, i ^ bits) for i in range(size)])]
    all_gather x9 -> x0, waiting for transfers between devices: 369 us -> none  [the longest x1 74.2 us: body(): lax.all_gather(shards[7], 'fsdp', axis=0, tiled=True)]
    psum x1 -> x0, waiting for transfers between devices: 369 us -> none  [body(): lax.psum(down_part, 'ctx').astype(jnp.float32)]
    ppermute x0 -> x131, starting transfers between devices: none -> 231 us  [swap(): return lax.ppermute(array, axis, [(i, i ^ bits) for i in range(size)])]
    dot_general x35 -> x7, matrix products: 150 us -> 32.1 us  [product(): return jnp.dot(left, right, preferred_element_type=wide)]
    pallas_call x0 -> x16, Pallas kernels: none -> 103 us  [the longest x7 37.1 us: stack_rows(): pl.pallas_call(stack_kernel, grid_spec=pltpu.PrefetchScalarGridSpec(num_s...]
    unnamed x20 -> x0, waiting for transfers between devices: 83.4 us -> none
  transfers between devices with their start and end apart: 19 -> 135, of which waited for: 18 -> 33; matrix products, arithmetic and copies ran while one was open for 12% -> 10% of each run, Pallas kernels for 0% -> 9%
where the time goes in v1:
time: 1040 us; the launch traced here: 1030 us
  waiting for transfers between devices  419 us (40%)
  starting transfers between devices  251 us (24%)
  Pallas kernels  103 us (10%)
  blocking collectives  88.7 us (9%)
  matrix products  79 us (8%)
  local copies, waits for them, and re-layouts  50.4 us (5%)
  other arithmetic  34.5 us (3%)
    ppermute x131, waiting for transfers between devices, swap(): return lax.ppermute(array, axis, [(i, i ^ bits) for i in range(size)])  384 us
    ppermute x131, starting transfers between devices, swap(): return lax.ppermute(array, axis, [(i, i ^ bits) for i in range(size)])  231 us
    all_gather x1, blocking collectives, body(): lax.all_gather(jnp.stack([attn_gain, ffn_gain]), 'fsdp', axis=1, tiled=True)  49.4 us
    psum x1, blocking collectives, body(): lax.psum(jnp.stack([grad_gain_one, grad_gain_two]), ('ctx', 'fsdp'))  39.2 us
    pallas_call x7, Pallas kernels, stack_rows(): pl.pallas_call(stack_kernel, grid_spec=pltpu.PrefetchScalarGridSpec(num_s...  37.1 us
    pallas_call x2, Pallas kernels, attention_call(): pl.pallas_call(kernel, grid_spec=pltpu.PrefetchScalarGridSpec(num_scalar_...  36.4 us
    all_to_all x1, waiting for transfers between devices, body(): lax.all_to_all(load, 'ctx', 0, 0, tiled=True)  34.4 us
    dot_general x7, matrix products, product(): return jnp.dot(left, right, preferred_element_type=wide)  32.1 us
  transfers between devices with their start and end apart: 135, of which 33 were waited for; matrix products, arithmetic and copies ran while one was open for 10% of the time, Pallas kernels for 9%

profile of v1, /device:TPU:0, one launch (start us, length us, event | category | flops | bytes accessed | tf_op | source)
XLA Modules:
  0.0 1027.5 jit_solution(6674185370247341286)
XLA Ops:
  7.3 49.4 %all_gather.3 = bf16[2,1536]{1,0:T(2,128)(2,1)S(1)} all-gather(bf16[2,384]{1,0:T(2,128)(2,1)S(1)} %pad_maximum_fusion.11), channel_id=1, replica_groups=mesh['ctx'=8,'fsdp'=4] {'fsdp'}, dimensions={1}, use_global_device_ids=true | all-gather | bytes 7680 | tf_op jit(solution)/shard_map/all_gather | solution.py:491
  79.8 6.7 stack_rows.7
  86.5 6.6 copy.31
  93.1 3.9 fusion.31
  101.6 6.8 all-to-all-start
  111.4 34.4 %all-to-all-done = bf16[8,256,384]{2,1,0:T(8,128)(2,1)S(1)} async-done(((bf16[8,256,384]{2,1,0:T(8,128)(2,1)}), bf16[8,256,384]{2,1,0:T(8,128)(2,1)S(1)}, u32[]{:S(2)}, u32[]{:S(2)}) %all-to-all-start) | async-done | bytes 1572896 | tf_op jit(solution)/shard_map/all_to_all | solution.py:528
  146.9 12.3 %attention_forward.1 = bf16[2048,192]{1,0:T(8,128)(2,1)} custom-call(s32[16]{0:T(128)} %and_select_fusion.order_ref, bf16[2048,384]{1,0:T(8,128)(2,1)} %bitcast.164), custom_call_target="tpu_custom_call" | custom-call | flops 4294967296 | bytes 3145728 | tf_op jit(solution)/shard_map/attention_forward/pallas_call | solution.py:234
  161.5 3.8 all-to-all-start.1
  176.5 6.5 stack_rows.10
  183.6 6.7 collective-permute-done.22.refs_2_
  190.6 15.6 %collective-permute-done.23.refs_3_ = bf16[384,1024]{1,0:T(8,128)(2,1)} collective-permute-done((bf16[384,1024]{1,0:T(8,128)(2,1)}, bf16[384,1024]{1,0:T(8,128)(2,1)}, u32[]{:S(2)}, u32[]{:S(2)}) %collective-permute-start.23) | collective-permute-done | bytes 786464 | tf_op jit(solution)/shard_map/ppermute | solution.py:61
  207.0 3.9 multiply_reduce_fusion.2
  210.9 13.1 %collective-permute-done.28 = bf16[256,1536]{1,0:T(8,128)(2,1)} collective-permute-done((bf16[256,1536]{1,0:T(8,128)(2,1)}, bf16[256,1536]{1,0:T(8,128)(2,1)}, u32[]{:S(2)}, u32[]{:S(2)}) %collective-permute-start.28) | collective-permute-done | bytes 786464 | tf_op jit(solution)/shard_map/ppermute | solution.py:61
  226.6 14.3 %collective-permute-done.19.refs_2_ = bf16[384,1024]{1,0:T(8,128)(2,1)} collective-permute-done((bf16[384,1024]{1,0:T(8,128)(2,1)}, bf16[384,1024]{1,0:T(8,128)(2,1)}, u32[]{:S(2)}, u32[]{:S(2)}) %collective-permute-start.19) | collective-permute-done | bytes 786464 | tf_op jit(solution)/shard_map/ppermute | solution.py:61
  242.4 14.4 %collective-permute-done.20.refs_3_ = bf16[384,1024]{1,0:T(8,128)(2,1)} collective-permute-done((bf16[384,1024]{1,0:T(8,128)(2,1)}, bf16[384,1024]{1,0:T(8,128)(2,1)}, u32[]{:S(2)}, u32[]{:S(2)}) %collective-permute-start.20) | collective-permute-done | bytes 786464 | tf_op jit(solution)/shard_map/ppermute | solution.py:61
  257.6 5.5 stack_rows.13
  263.1 5.5 stack_rows.12
  268.7 5.9 collective-permute-done.16.refs_2_
  274.6 15.9 %collective-permute-done.17.refs_3_ = bf16[384,1024]{1,0:T(8,128)(2,1)} collective-permute-done((bf16[384,1024]{1,0:T(8,128)(2,1)}, bf16[384,1024]{1,0:T(8,128)(2,1)}, u32[]{:S(2)}, u32[]{:S(2)}) %collective-permute-start.17) | collective-permute-done | bytes 786464 | tf_op jit(solution)/shard_map/ppermute | solution.py:61
  290.5 5.7 stack_rows.11
  297.0 10.9 %collective-permute-done.13 = bf16[256,1536]{1,0:T(8,128)(2,1)} collective-permute-done((bf16[256,1536]{1,0:T(8,128)(2,1)}, bf16[256,1536]{1,0:T(8,128)(2,1)}, u32[]{:S(2)}, u32[]{:S(2)}) %collective-permute-start.13) | collective-permute-done | bytes 786464 | tf_op jit(solution)/shard_map/ppermute | solution.py:61
  307.9 6.3 fusion.28
  314.2 7.4 fusion.88
  321.6 9.9 multiply_convert_fusion.1
  340.4 5.1 fusion.94
  347.3 4.9 convolution_convert_fusion.2
  354.5 6.0 convolution_convert_fusion.1
  360.5 6.0 convolution_convert_fusion
  370.6 19.1 %collective-permute-done.89 = bf16[1536,512]{1,0:T(8,128)(2,1)S(1)} collective-permute-done((bf16[1536,512]{1,0:T(8,128)(2,1)S(1)}, bf16[1536,512]{1,0:T(8,128)(2,1)S(1)}, u32[]{:S(2)}, u32[]{:S(2)}) %collective-permute-start.89) | collective-permute-done | bytes 1572896 | tf_op jit(solution)/shard_map/ppermute | solution.py:61
  393.1 30.3 %collective-permute-done.103 = bf16[1536,512]{1,0:T(8,128)(2,1)S(1)} collective-permute-done((bf16[1536,512]{1,0:T(8,128)(2,1)S(1)}, bf16[1536,512]{1,0:T(8,128)(2,1)S(1)}, u32[]{:S(2)}, u32[]{:S(2)}) %collective-permute-start.103) | collective-permute-done | bytes 1572896 | tf_op jit(solution)/shard_map/ppermute | solution.py:61
  426.9 30.1 %collective-permute-done.117 = bf16[1536,512]{1,0:T(8,128)(2,1)S(1)} collective-permute-done((bf16[1536,512]{1,0:T(8,128)(2,1)S(1)}, bf16[1536,512]{1,0:T(8,128)(2,1)S(1)}, u32[]{:S(2)}, u32[]{:S(2)}) %collective-permute-start.117) | collective-permute-done | bytes 1572896 | tf_op jit(solution)/shard_map/ppermute | solution.py:61
  467.7 4.2 fusion.90
  475.3 4.9 all-to-all-start.2
  484.3 4.3 collective-permute-start.104
  488.6 32.1 %collective-permute-done.91 = bf16[1536,128]{1,0:T(8,128)(2,1)} collective-permute-done((bf16[1536,128]{1,0:T(8,128)(2,1)}, bf16[1536,128]{1,0:T(8,128)(2,1)}, u32[]{:S(2)}, u32[]{:S(2)}) %collective-permute-start.91) | collective-permute-done | bytes 393248 | tf_op jit(solution)/shard_map/ppermute | solution.py:61
  525.0 21.5 %collective-permute-start.118 = (bf16[1536,128]{1,0:T(8,128)(2,1)S(1)}, bf16[1536,128]{1,0:T(8,128)(2,1)S(1)}, u32[]{:S(2)}, u32[]{:S(2)}) collective-permute-start(bf16[1536,128]{1,0:T(8,128)(2,1)S(1)} %get-tuple-element.46), channel_id=1, source_target_pairs={{0,8},{4,12},{8,0},{12,4},{16,24},{20,28},{24,16},{28,20},{1,9},{5... | collective-permute-start | bytes 1179656 | tf_op jit(solution)/shard_map/ppermute | solution.py:61
  546.6 7.9 collective-permute-done.105
  557.8 20.9 %collective-permute-done.119 = bf16[1536,128]{1,0:T(8,128)(2,1)S(1)} collective-permute-done((bf16[1536,128]{1,0:T(8,128)(2,1)S(1)}, bf16[1536,128]{1,0:T(8,128)(2,1)S(1)}, u32[]{:S(2)}, u32[]{:S(2)}) %collective-permute-start.119) | collective-permute-done | bytes 393248 | tf_op jit(solution)/shard_map/ppermute | solution.py:61
  593.7 24.1 %attention_backward.1 = bf16[2048,384]{1,0:T(8,128)(2,1)} custom-call(s32[16]{0:T(128)} %and_select_fusion.order_ref, bf16[2048,384]{1,0:T(8,128)(2,1)} %bitcast.165, bf16[2048,192]{1,0:T(8,128)(2,1)} %bitcast.168), custom_call_target="tpu_custom_call" | custom-call | flops 10737418240 | bytes 6291456 | tf_op jit(solution)/shard_map/attention_backward/pallas_call | solution.py:234
  620.4 4.6 all-to-all-start.3
  634.2 27.0 %collective-permute-done.96.refs_1_ = bf16[4,384,128]{2,1,0:T(8,128)(2,1)S(1)} collective-permute-done((bf16[4,384,128]{2,1,0:T(8,128)(2,1)S(1)}, bf16[4,384,128]{2,1,0:T(8,128)(2,1)S(1)}, u32[]{:S(2)}, u32[]{:S(2)}) %collective-permute-start.96) | collective-permute-done | bytes 393248 | tf_op jit(solution)/shard_map/ppermute | solution.py:61
  664.9 24.0 %collective-permute-done.97.refs_2_ = bf16[4,384,128]{2,1,0:T(8,128)(2,1)S(1)} collective-permute-done((bf16[4,384,128]{2,1,0:T(8,128)(2,1)S(1)}, bf16[4,384,128]{2,1,0:T(8,128)(2,1)S(1)}, u32[]{:S(2)}, u32[]{:S(2)}) %collective-permute-start.97) | collective-permute-done | bytes 393248 | tf_op jit(solution)/shard_map/ppermute | solution.py:61
  693.9 23.8 %collective-permute-start.124 = (bf16[4,384,128]{2,1,0:T(8,128)(2,1)S(1)}, bf16[4,384,128]{2,1,0:T(8,128)(2,1)}, u32[]{:S(2)}, u32[]{:S(2)}) collective-permute-start(bf16[4,384,128]{2,1,0:T(8,128)(2,1)S(1)} %pad_maximum_fusion.9.refs_0_), channel_id=1, source_target_pairs={{0,8},{4,12},{8,0},{12,4},{16,24},{20,28},{24,16},{28,20},{1,9},{5... | collective-permute-start | bytes 1179656 | tf_op jit(solution)/shard_map/ppermute | solution.py:61
  717.7 4.7 collective-permute-done.111.refs_2_
  726.3 3.9 collective-permute-done.124.refs_1_
  731.7 24.6 %collective-permute-done.125.refs_2_ = bf16[4,384,128]{2,1,0:T(8,128)(2,1)} collective-permute-done((bf16[4,384,128]{2,1,0:T(8,128)(2,1)S(1)}, bf16[4,384,128]{2,1,0:T(8,128)(2,1)}, u32[]{:S(2)}, u32[]{:S(2)}) %collective-permute-start.125) | collective-permute-done | bytes 393248 | tf_op jit(solution)/shard_map/ppermute | solution.py:61
  763.3 7.8 collective-permute-start.80
  771.1 7.7 collective-permute-start.79
  779.5 5.9 collective-permute-done.114.refs_5_
  793.8 10.2 collective-permute-start.82
  803.9 9.2 collective-permute-start.83
  814.7 4.3 collective-permute-done.129.refs_6_
  823.8 6.1 spread_columns.3
  830.0 6.1 spread_columns.4
  836.1 6.1 spread_columns.5
  864.6 12.0 %collective-permute-done.49 = bf16[384,768]{1,0:T(8,128)(2,1)S(1)} collective-permute-done((bf16[384,768]{1,0:T(8,128)(2,1)S(1)}, bf16[384,768]{1,0:T(8,128)(2,1)S(1)}, u32[]{:S(2)}, u32[]{:S(2)}) %collective-permute-start.49) | collective-permute-done | bytes 589856 | tf_op jit(solution)/shard_map/ppermute | solution.py:61
  878.3 10.9 %collective-permute-done.63 = bf16[384,768]{1,0:T(8,128)(2,1)S(1)} collective-permute-done((bf16[384,768]{1,0:T(8,128)(2,1)S(1)}, bf16[384,768]{1,0:T(8,128)(2,1)S(1)}, u32[]{:S(2)}, u32[]{:S(2)}) %collective-permute-start.63) | collective-permute-done | bytes 589856 | tf_op jit(solution)/shard_map/ppermute | solution.py:61
  892.0 10.1 collective-permute-start.52
  902.6 11.4 %collective-permute-done.35 = bf16[384,1536]{1,0:T(8,128)(2,1)S(1)} collective-permute-done((bf16[384,1536]{1,0:T(8,128)(2,1)S(1)}, bf16[384,1536]{1,0:T(8,128)(2,1)S(1)}, u32[]{:S(2)}, u32[]{:S(2)}) %collective-permute-start.35) | collective-permute-done | bytes 1179680 | tf_op jit(solution)/shard_map/ppermute | solution.py:61
  917.1 10.1 collective-permute-start.66
  936.4 4.0 collective-permute-start.68
  947.8 4.3 collective-permute-done.69.refs_2_
  954.1 6.0 collective-permute-done.38
  977.8 39.2 %psum.7 = f32[2,1536]{1,0:T(2,128)S(1)} all-reduce(f32[2,1536]{1,0:T(2,128)S(1)} %pad_maximum_fusion.10), channel_id=1, replica_groups=mesh['ctx'=8,'fsdp'=4] {'ctx','fsdp'}, use_global_device_ids=true, to_apply=%region_6.7 | all-reduce | flops 3072 | bytes 24576 | tf_op jit(solution)/shard_map/psum | solution.py:616
  (544 shorter events, 248.0 us)
Async XLA Ops:
  0.6 60.1 %collective-permute-start.6 = (bf16[384,768]{1,0:T(8,128)(2,1)}, bf16[384,768]{1,0:T(8,128)(2,1)S(1)}, u32[]{:S(2)}, u32[]{:S(2)}) collective-permute-start(bf16[384,768]{1,0:T(8,128)(2,1)} %refs_0_.6), channel_id=1, source_target_pairs={{0,1},{1,0},{2,3},{3,2},{4,5},{5,4},{6,7},{7,6},{8,9},{9,8},{10,11... | collective-permute-start | bytes 1769480 | tf_op jit(solution)/shard_map/ppermute | solution.py:61
  1.2 57.0 %collective-permute-start.7 = (bf16[384,768]{1,0:T(8,128)(2,1)}, bf16[384,768]{1,0:T(8,128)(2,1)S(1)}, u32[]{:S(2)}, u32[]{:S(2)}) collective-permute-start(bf16[384,768]{1,0:T(8,128)(2,1)} %refs_0_.6), channel_id=1, source_target_pairs={{0,2},{1,3},{2,0},{3,1},{4,6},{5,7},{6,4},{7,5},{8,10},{9,11},{10,... | collective-permute-start | bytes 1769480 | tf_op jit(solution)/shard_map/ppermute | solution.py:61
  3.7 65.8 %collective-permute-start.3 = (bf16[384,768]{1,0:T(8,128)(2,1)}, bf16[384,768]{1,0:T(8,128)(2,1)S(1)}, u32[]{:S(2)}, u32[]{:S(2)}) collective-permute-start(bf16[384,768]{1,0:T(8,128)(2,1)} %refs_0_.5), channel_id=1, source_target_pairs={{0,1},{1,0},{2,3},{3,2},{4,5},{5,4},{6,7},{7,6},{8,9},{9,8},{10,11... | collective-permute-start | bytes 1769480 | tf_op jit(solution)/shard_map/ppermute | solution.py:61
  3.9 57.0 %collective-permute-start.4 = (bf16[384,768]{1,0:T(8,128)(2,1)}, bf16[384,768]{1,0:T(8,128)(2,1)S(1)}, u32[]{:S(2)}, u32[]{:S(2)}) collective-permute-start(bf16[384,768]{1,0:T(8,128)(2,1)} %refs_0_.5), channel_id=1, source_target_pairs={{0,2},{1,3},{2,0},{3,1},{4,6},{5,7},{6,4},{7,5},{8,10},{9,11},{10,... | collective-permute-start | bytes 1769480 | tf_op jit(solution)/shard_map/ppermute | solution.py:61
  4.2 57.1 %collective-permute-start.1 = (bf16[384,1536]{1,0:T(8,128)(2,1)}, bf16[384,1536]{1,0:T(8,128)(2,1)}, u32[]{:S(2)}, u32[]{:S(2)}) collective-permute-start(bf16[384,1536]{1,0:T(8,128)(2,1)} %refs_0_.4), channel_id=1, source_target_pairs={{0,2},{1,3},{2,0},{3,1},{4,6},{5,7},{6,4},{7,5},{8,10},{9,11},{10,... | collective-permute-start | bytes 3538952 | tf_op jit(solution)/shard_map/ppermute | solution.py:61
  101.6 44.2 %all-to-all-start = ((bf16[8,256,384]{2,1,0:T(8,128)(2,1)}), bf16[8,256,384]{2,1,0:T(8,128)(2,1)S(1)}, u32[]{:S(2)}, u32[]{:S(2)}) async-start(bf16[8,256,384]{2,1,0:T(8,128)(2,1)} %maximum_bitcast_fusion), calls=%async_computation | async-start | bytes 3145728 | tf_op jit(solution)/shard_map/all_to_all | solution.py:528
  108.4 57.0 %collective-permute-start.10 = (bf16[384,1536]{1,0:T(8,128)(2,1)S(1)}, bf16[384,1536]{1,0:T(8,128)(2,1)}, u32[]{:S(2)}, u32[]{:S(2)}) collective-permute-start(bf16[384,1536]{1,0:T(8,128)(2,1)S(1)} %copy-done.24), channel_id=1, source_target_pairs={{0,2},{1,3},{2,0},{3,1},{4,6},{5,7},{6,4},{7,5},{8,10},{9,11},{10,... | collective-permute-start | bytes 3538952 | tf_op jit(solution)/shard_map/ppermute | solution.py:61
  161.5 45.6 %all-to-all-start.1 = ((bf16[8,256,192]{1,2,0:T(8,128)(2,1)}), bf16[8,256,192]{1,2,0:T(8,128)(2,1)S(1)}, u32[]{:S(2)}, u32[]{:S(2)}) async-start(bf16[8,256,192]{1,2,0:T(8,128)(2,1)} %copy.38), calls=%async_computation.1 | async-start | bytes 1572864 | tf_op jit(solution)/shard_map/all_to_all | solution.py:531
  171.2 35.1 %collective-permute-start.23 = (bf16[384,1024]{1,0:T(8,128)(2,1)}, bf16[384,1024]{1,0:T(8,128)(2,1)}, u32[]{:S(2)}, u32[]{:S(2)}) collective-permute-start(bf16[384,1024]{1,0:T(8,128)(2,1)} %get-tuple-element.30), channel_id=1, source_target_pairs={{0,3},{1,2},{2,1},{3,0},{4,7},{5,6},{6,5},{7,4},{8,11},{9,10},{10,... | collective-permute-start | bytes 2359304 | tf_op jit(solution)/shard_map/ppermute | solution.py:61
  173.2 50.8 %collective-permute-start.28 = (bf16[256,1536]{1,0:T(8,128)(2,1)}, bf16[256,1536]{1,0:T(8,128)(2,1)}, u32[]{:S(2)}, u32[]{:S(2)}) collective-permute-start(bf16[256,1536]{1,0:T(8,128)(2,1)} %bitcast.18), channel_id=1, source_target_pairs={{0,2},{1,3},{2,0},{3,1},{4,6},{5,7},{6,4},{7,5},{8,10},{9,11},{10,... | collective-permute-start | bytes 2359304 | tf_op jit(solution)/shard_map/ppermute | solution.py:61
  174.7 50.8 %collective-permute-start.18 = (bf16[384,1024]{1,0:T(8,128)(2,1)}, bf16[384,1024]{1,0:T(8,128)(2,1)}, u32[]{:S(2)}, u32[]{:S(2)}) collective-permute-start(bf16[384,1024]{1,0:T(8,128)(2,1)} %get-tuple-element.39), channel_id=1, source_target_pairs={{0,1},{1,0},{2,3},{3,2},{4,5},{5,4},{6,7},{7,6},{8,9},{9,8},{10,11... | collective-permute-start | bytes 2359304 | tf_op jit(solution)/shard_map/ppermute | solution.py:61
  183.0 57.9 %collective-permute-start.19 = (bf16[384,1024]{1,0:T(8,128)(2,1)}, bf16[384,1024]{1,0:T(8,128)(2,1)}, u32[]{:S(2)}, u32[]{:S(2)}) collective-permute-start(bf16[384,1024]{1,0:T(8,128)(2,1)} %get-tuple-element.41), channel_id=1, source_target_pairs={{0,2},{1,3},{2,0},{3,1},{4,6},{5,7},{6,4},{7,5},{8,10},{9,11},{10,... | collective-permute-start | bytes 2359304 | tf_op jit(solution)/shard_map/ppermute | solution.py:61
  190.4 66.5 %collective-permute-start.20 = (bf16[384,1024]{1,0:T(8,128)(2,1)}, bf16[384,1024]{1,0:T(8,128)(2,1)}, u32[]{:S(2)}, u32[]{:S(2)}) collective-permute-start(bf16[384,1024]{1,0:T(8,128)(2,1)} %get-tuple-element.38), channel_id=1, source_target_pairs={{0,3},{1,2},{2,1},{3,0},{4,7},{5,6},{6,5},{7,4},{8,11},{9,10},{10,... | collective-permute-start | bytes 2359304 | tf_op jit(solution)/shard_map/ppermute | solution.py:61
  206.3 51.3 %collective-permute-start.15 = (bf16[384,1024]{1,0:T(8,128)(2,1)}, bf16[384,1024]{1,0:T(8,128)(2,1)}, u32[]{:S(2)}, u32[]{:S(2)}) collective-permute-start(bf16[384,1024]{1,0:T(8,128)(2,1)} %get-tuple-element.35), channel_id=1, source_target_pairs={{0,1},{1,0},{2,3},{3,2},{4,5},{5,4},{6,7},{7,6},{8,9},{9,8},{10,11... | collective-permute-start | bytes 2359304 | tf_op jit(solution)/shard_map/ppermute | solution.py:61
  224.1 50.6 %collective-permute-start.16 = (bf16[384,1024]{1,0:T(8,128)(2,1)}, bf16[384,1024]{1,0:T(8,128)(2,1)}, u32[]{:S(2)}, u32[]{:S(2)}) collective-permute-start(bf16[384,1024]{1,0:T(8,128)(2,1)} %get-tuple-element.37), channel_id=1, source_target_pairs={{0,2},{1,3},{2,0},{3,1},{4,6},{5,7},{6,4},{7,5},{8,10},{9,11},{10,... | collective-permute-start | bytes 2359304 | tf_op jit(solution)/shard_map/ppermute | solution.py:61
  225.6 65.0 %collective-permute-start.17 = (bf16[384,1024]{1,0:T(8,128)(2,1)}, bf16[384,1024]{1,0:T(8,128)(2,1)}, u32[]{:S(2)}, u32[]{:S(2)}) collective-permute-start(bf16[384,1024]{1,0:T(8,128)(2,1)} %get-tuple-element.34), channel_id=1, source_target_pairs={{0,3},{1,2},{2,1},{3,0},{4,7},{5,6},{6,5},{7,4},{8,11},{9,10},{10,... | collective-permute-start | bytes 2359304 | tf_op jit(solution)/shard_map/ppermute | solution.py:61
  240.9 67.0 %collective-permute-start.13 = (bf16[256,1536]{1,0:T(8,128)(2,1)}, bf16[256,1536]{1,0:T(8,128)(2,1)}, u32[]{:S(2)}, u32[]{:S(2)}) collective-permute-start(bf16[256,1536]{1,0:T(8,128)(2,1)} %multiply_convert_fusion.3), channel_id=1, source_target_pairs={{0,2},{1,3},{2,0},{3,1},{4,6},{5,7},{6,4},{7,5},{8,10},{9,11},{10,... | collective-permute-start | bytes 2359304 | tf_op jit(solution)/shard_map/ppermute | solution.py:61
  256.8 51.0 %collective-permute-start.27 = (bf16[256,1536]{1,0:T(8,128)(2,1)}, bf16[256,1536]{1,0:T(8,128)(2,1)}, u32[]{:S(2)}, u32[]{:S(2)}) collective-permute-start(bf16[256,1536]{1,0:T(8,128)(2,1)} %bitcast.18), channel_id=1, source_target_pairs={{0,1},{1,0},{2,3},{3,2},{4,5},{5,4},{6,7},{7,6},{8,9},{9,8},{10,11... | collective-permute-start | bytes 2359304 | tf_op jit(solution)/shard_map/ppermute | solution.py:61
  257.6 50.3 %collective-permute-start.29 = (bf16[256,1536]{1,0:T(8,128)(2,1)}, bf16[256,1536]{1,0:T(8,128)(2,1)}, u32[]{:S(2)}, u32[]{:S(2)}) collective-permute-start(bf16[256,1536]{1,0:T(8,128)(2,1)} %collective-permute-done.28), channel_id=1, source_target_pairs={{0,1},{1,0},{2,3},{3,2},{4,5},{5,4},{6,7},{7,6},{8,9},{9,8},{10,11... | collective-permute-start | bytes 2359304 | tf_op jit(solution)/shard_map/ppermute | solution.py:61
  339.1 123.3 %collective-permute-start.30 = (bf16[256,1536]{1,0:T(8,128)(2,1)S(1)}, bf16[256,1536]{1,0:T(8,128)(2,1)S(1)}, u32[]{:S(2)}, u32[]{:S(2)}) collective-permute-start(bf16[256,1536]{1,0:T(8,128)(2,1)S(1)} %get-tuple-element.26), channel_id=1, source_target_pairs={{0,1},{1,0},{2,3},{3,2},{4,5},{5,4},{6,7},{7,6},{8,9},{9,8},{10,11... | collective-permute-start | bytes 2359304 | tf_op jit(solution)/shard_map/ppermute | solution.py:61
  346.9 117.2 %collective-permute-start.24 = (bf16[256,1536]{1,0:T(8,128)(2,1)S(1)}, bf16[256,1536]{1,0:T(8,128)(2,1)S(1)}, u32[]{:S(2)}, u32[]{:S(2)}) collective-permute-start(bf16[256,1536]{1,0:T(8,128)(2,1)S(1)} %get-tuple-element.28), channel_id=1, source_target_pairs={{0,1},{1,0},{2,3},{3,2},{4,5},{5,4},{6,7},{7,6},{8,9},{9,8},{10,11... | collective-permute-start | bytes 2359304 | tf_op jit(solution)/shard_map/ppermute | solution.py:61
  352.4 37.4 %collective-permute-start.89 = (bf16[1536,512]{1,0:T(8,128)(2,1)S(1)}, bf16[1536,512]{1,0:T(8,128)(2,1)S(1)}, u32[]{:S(2)}, u32[]{:S(2)}) collective-permute-start(bf16[1536,512]{1,0:T(8,128)(2,1)S(1)} %constant_dynamic-slice_fusion.21), channel_id=1, source_target_pairs={{0,4},{4,0},{8,12},{12,8},{16,20},{20,16},{24,28},{28,24},{1,5},{5... | collective-permute-start | bytes 4718600 | tf_op jit(solution)/shard_map/ppermute | solution.py:61
  366.9 56.5 %collective-permute-start.103 = (bf16[1536,512]{1,0:T(8,128)(2,1)S(1)}, bf16[1536,512]{1,0:T(8,128)(2,1)S(1)}, u32[]{:S(2)}, u32[]{:S(2)}) collective-permute-start(bf16[1536,512]{1,0:T(8,128)(2,1)S(1)} %constant_dynamic-slice_fusion.14), channel_id=1, source_target_pairs={{0,4},{4,0},{8,12},{12,8},{16,20},{20,16},{24,28},{28,24},{1,5},{5... | collective-permute-start | bytes 4718600 | tf_op jit(solution)/shard_map/ppermute | solution.py:61
  368.3 88.7 %collective-permute-start.117 = (bf16[1536,512]{1,0:T(8,128)(2,1)S(1)}, bf16[1536,512]{1,0:T(8,128)(2,1)S(1)}, u32[]{:S(2)}, u32[]{:S(2)}) collective-permute-start(bf16[1536,512]{1,0:T(8,128)(2,1)S(1)} %constant_dynamic-slice_fusion.7), channel_id=1, source_target_pairs={{0,4},{4,0},{8,12},{12,8},{16,20},{20,16},{24,28},{28,24},{1,5},{5... | collective-permute-start | bytes 4718600 | tf_op jit(solution)/shard_map/ppermute | solution.py:61
  389.8 72.7 %collective-permute-start.32 = (bf16[256,1536]{1,0:T(8,128)(2,1)S(1)}, bf16[256,1536]{1,0:T(8,128)(2,1)S(1)}, u32[]{:S(2)}, u32[]{:S(2)}) collective-permute-start(bf16[256,1536]{1,0:T(8,128)(2,1)S(1)} %fusion.20), channel_id=1, source_target_pairs={{0,2},{1,3},{2,0},{3,1},{4,6},{5,7},{6,4},{7,5},{8,10},{9,11},{10,... | collective-permute-start | bytes 2359304 | tf_op jit(solution)/shard_map/ppermute | solution.py:61
  423.5 44.2 %collective-permute-start.26 = (bf16[256,1536]{1,0:T(8,128)(2,1)S(1)}, bf16[256,1536]{1,0:T(8,128)(2,1)S(1)}, u32[]{:S(2)}, u32[]{:S(2)}) collective-permute-start(bf16[256,1536]{1,0:T(8,128)(2,1)S(1)} %fusion.22), channel_id=1, source_target_pairs={{0,2},{1,3},{2,0},{3,1},{4,6},{5,7},{6,4},{7,5},{8,10},{9,11},{10,... | collective-permute-start | bytes 2359304 | tf_op jit(solution)/shard_map/ppermute | solution.py:61
  462.4 58.3 %collective-permute-start.91 = (bf16[1536,128]{1,0:T(8,128)(2,1)}, bf16[1536,128]{1,0:T(8,128)(2,1)}, u32[]{:S(2)}, u32[]{:S(2)}) collective-permute-start(bf16[1536,128]{1,0:T(8,128)(2,1)} %get-tuple-element.54), channel_id=1, source_target_pairs={{0,16},{4,20},{8,24},{12,28},{16,0},{20,4},{24,8},{28,12},{1,17},{... | collective-permute-start | bytes 1179656 | tf_op jit(solution)/shard_map/ppermute | solution.py:61
  462.4 61.0 %collective-permute-start.90 = (bf16[1536,128]{1,0:T(8,128)(2,1)}, bf16[1536,128]{1,0:T(8,128)(2,1)}, u32[]{:S(2)}, u32[]{:S(2)}) collective-permute-start(bf16[1536,128]{1,0:T(8,128)(2,1)} %get-tuple-element.52), channel_id=1, source_target_pairs={{0,8},{4,12},{8,0},{12,4},{16,24},{20,28},{24,16},{28,20},{1,9},{5... | collective-permute-start | bytes 1179656 | tf_op jit(solution)/shard_map/ppermute | solution.py:61
  464.1 60.9 %collective-permute-start.106 = (bf16[1536,128]{1,0:T(8,128)(2,1)}, bf16[1536,128]{1,0:T(8,128)(2,1)}, u32[]{:S(2)}, u32[]{:S(2)}) collective-permute-start(bf16[1536,128]{1,0:T(8,128)(2,1)} %get-tuple-element.50), channel_id=1, source_target_pairs={{0,24},{4,28},{8,16},{12,20},{16,8},{20,12},{24,0},{28,4},{1,25},{... | collective-permute-start | bytes 1179656 | tf_op jit(solution)/shard_map/ppermute | solution.py:61
  467.7 86.8 %collective-permute-start.105 = (bf16[1536,128]{1,0:T(8,128)(2,1)}, bf16[1536,128]{1,0:T(8,128)(2,1)}, u32[]{:S(2)}, u32[]{:S(2)}) collective-permute-start(bf16[1536,128]{1,0:T(8,128)(2,1)} %get-tuple-element.51), channel_id=1, source_target_pairs={{0,16},{4,20},{8,24},{12,28},{16,0},{20,4},{24,8},{28,12},{1,17},{... | collective-permute-start | bytes 1179656 | tf_op jit(solution)/shard_map/ppermute | solution.py:61
  475.3 117.1 %all-to-all-start.2 = ((bf16[8,256,192]{1,2,0:T(8,128)(2,1)}), bf16[8,256,192]{1,2,0:T(8,128)(2,1)S(1)}, u32[]{:S(2)}, u32[]{:S(2)}) async-start(bf16[8,256,192]{1,2,0:T(8,128)(2,1)} %bitcast.162), calls=%async_computation.2 | async-start | bytes 1572864 | tf_op jit(solution)/shard_map/all_to_all | solution.py:575
  484.3 70.2 %collective-permute-start.104 = (bf16[1536,128]{1,0:T(8,128)(2,1)S(1)}, bf16[1536,128]{1,0:T(8,128)(2,1)S(1)}, u32[]{:S(2)}, u32[]{:S(2)}) collective-permute-start(bf16[1536,128]{1,0:T(8,128)(2,1)S(1)} %copy-done.48), channel_id=1, source_target_pairs={{0,8},{4,12},{8,0},{12,4},{16,24},{20,28},{24,16},{28,20},{1,9},{5... | collective-permute-start | bytes 1179656 | tf_op jit(solution)/shard_map/ppermute | solution.py:61
  520.7 35.8 %collective-permute-start.120 = (bf16[1536,128]{1,0:T(8,128)(2,1)S(1)}, bf16[1536,128]{1,0:T(8,128)(2,1)S(1)}, u32[]{:S(2)}, u32[]{:S(2)}) collective-permute-start(bf16[1536,128]{1,0:T(8,128)(2,1)S(1)} %copy-done.47), channel_id=1, source_target_pairs={{0,24},{4,28},{8,16},{12,20},{16,8},{20,12},{24,0},{28,4},{1,25},{... | collective-permute-start | bytes 1179656 | tf_op jit(solution)/shard_map/ppermute | solution.py:61
  523.5 55.2 %collective-permute-start.119 = (bf16[1536,128]{1,0:T(8,128)(2,1)S(1)}, bf16[1536,128]{1,0:T(8,128)(2,1)S(1)}, u32[]{:S(2)}, u32[]{:S(2)}) collective-permute-start(bf16[1536,128]{1,0:T(8,128)(2,1)S(1)} %copy-done.46), channel_id=1, source_target_pairs={{0,16},{4,20},{8,24},{12,28},{16,0},{20,4},{24,8},{28,12},{1,17},{... | collective-permute-start | bytes 1179656 | tf_op jit(solution)/shard_map/ppermute | solution.py:61
  525.0 55.3 %collective-permute-start.118 = (bf16[1536,128]{1,0:T(8,128)(2,1)S(1)}, bf16[1536,128]{1,0:T(8,128)(2,1)S(1)}, u32[]{:S(2)}, u32[]{:S(2)}) collective-permute-start(bf16[1536,128]{1,0:T(8,128)(2,1)S(1)} %get-tuple-element.46), channel_id=1, source_target_pairs={{0,8},{4,12},{8,0},{12,4},{16,24},{20,28},{24,16},{28,20},{1,9},{5... | collective-permute-start | bytes 1179656 | tf_op jit(solution)/shard_map/ppermute | solution.py:61
  554.5 72.6 %collective-permute-start.75 = (bf16[384,1536]{1,0:T(8,128)(2,1)}, bf16[384,1536]{1,0:T(8,128)(2,1)}, u32[]{:S(2)}, u32[]{:S(2)}) collective-permute-start(bf16[384,1536]{1,0:T(8,128)(2,1)} %convolution_convert_fusion.4), channel_id=1, source_target_pairs={{0,1},{1,0},{2,3},{3,2},{4,5},{5,4},{6,7},{7,6},{8,9},{9,8},{10,11... | collective-permute-start | bytes 3538952 | tf_op jit(solution)/shard_map/ppermute | solution.py:61
  586.0 43.4 %collective-permute-start.77 = (bf16[384,1536]{1,0:T(8,128)(2,1)}, bf16[384,1536]{1,0:T(8,128)(2,1)}, u32[]{:S(2)}, u32[]{:S(2)}) collective-permute-start(bf16[384,1536]{1,0:T(8,128)(2,1)} %add_convert_fusion.4), channel_id=1, source_target_pairs={{0,2},{1,3},{2,0},{3,1},{4,6},{5,7},{6,4},{7,5},{8,10},{9,11},{10,... | collective-permute-start | bytes 3538952 | tf_op jit(solution)/shard_map/ppermute | solution.py:61
  586.7 38.2 %collective-permute-start.123 = (bf16[384,128]{1,0:T(8,128)(2,1)}, bf16[384,128]{1,0:T(8,128)(2,1)}, u32[]{:S(2)}, u32[]{:S(2)}) collective-permute-start(bf16[384,128]{1,0:T(8,128)(2,1)} %get-tuple-element.65), channel_id=1, source_target_pairs={{0,3},{1,2},{2,1},{3,0},{4,7},{5,6},{6,5},{7,4},{8,11},{9,10},{10,... | collective-permute-start | bytes 294920 | tf_op jit(solution)/shard_map/ppermute | solution.py:61
  589.6 42.0 %collective-permute-start.122 = (bf16[384,128]{1,0:T(8,128)(2,1)}, bf16[384,128]{1,0:T(8,128)(2,1)}, u32[]{:S(2)}, u32[]{:S(2)}) collective-permute-start(bf16[384,128]{1,0:T(8,128)(2,1)} %get-tuple-element.66), channel_id=1, source_target_pairs={{0,2},{1,3},{2,0},{3,1},{4,6},{5,7},{6,4},{7,5},{8,10},{9,11},{10,... | collective-permute-start | bytes 294920 | tf_op jit(solution)/shard_map/ppermute | solution.py:61
  591.6 42.0 %collective-permute-start.121 = (bf16[384,128]{1,0:T(8,128)(2,1)}, bf16[384,128]{1,0:T(8,128)(2,1)}, u32[]{:S(2)}, u32[]{:S(2)}) collective-permute-start(bf16[384,128]{1,0:T(8,128)(2,1)} %get-tuple-element.67), channel_id=1, source_target_pairs={{0,1},{1,0},{2,3},{3,2},{4,5},{5,4},{6,7},{7,6},{8,9},{9,8},{10,11... | collective-permute-start | bytes 294920 | tf_op jit(solution)/shard_map/ppermute | solution.py:61
  620.4 226.3 %all-to-all-start.3 = ((bf16[8,256,384]{1,2,0:T(8,128)(2,1)}), bf16[8,256,384]{1,2,0:T(8,128)(2,1)}, u32[]{:S(2)}, u32[]{:S(2)}) async-start(bf16[8,256,384]{1,2,0:T(8,128)(2,1)} %copy.41), calls=%async_computation.3 | async-start | bytes 3145728 | tf_op jit(solution)/shard_map/all_to_all | solution.py:579
  625.0 36.2 %collective-permute-start.96 = (bf16[4,384,128]{2,1,0:T(8,128)(2,1)S(1)}, bf16[4,384,128]{2,1,0:T(8,128)(2,1)S(1)}, u32[]{:S(2)}, u32[]{:S(2)}) collective-permute-start(bf16[4,384,128]{2,1,0:T(8,128)(2,1)S(1)} %pad_maximum_fusion.7.refs_0_), channel_id=1, source_target_pairs={{0,8},{4,12},{8,0},{12,4},{16,24},{20,28},{24,16},{28,20},{1,9},{5... | collective-permute-start | bytes 1179656 | tf_op jit(solution)/shard_map/ppermute | solution.py:61
  627.0 61.9 %collective-permute-start.97 = (bf16[4,384,128]{2,1,0:T(8,128)(2,1)S(1)}, bf16[4,384,128]{2,1,0:T(8,128)(2,1)S(1)}, u32[]{:S(2)}, u32[]{:S(2)}) collective-permute-start(bf16[4,384,128]{2,1,0:T(8,128)(2,1)S(1)} %pad_maximum_fusion.7.refs_0_), channel_id=1, source_target_pairs={{0,16},{4,20},{8,24},{12,28},{16,0},{20,4},{24,8},{28,12},{1,17},{... | collective-permute-start | bytes 1179656 | tf_op jit(solution)/shard_map/ppermute | solution.py:61
  629.4 61.2 %collective-permute-start.98 = (bf16[4,384,128]{2,1,0:T(8,128)(2,1)S(1)}, bf16[4,384,128]{2,1,0:T(8,128)(2,1)S(1)}, u32[]{:S(2)}, u32[]{:S(2)}) collective-permute-start(bf16[4,384,128]{2,1,0:T(8,128)(2,1)S(1)} %pad_maximum_fusion.7.refs_0_), channel_id=1, source_target_pairs={{0,24},{4,28},{8,16},{12,20},{16,8},{20,12},{24,0},{28,4},{1,25},{... | collective-permute-start | bytes 1179656 | tf_op jit(solution)/shard_map/ppermute | solution.py:61
  631.6 60.6 %collective-permute-start.99 = (bf16[4,384,128]{2,1,0:T(8,128)(2,1)S(1)}, bf16[4,384,128]{2,1,0:T(8,128)(2,1)S(1)}, u32[]{:S(2)}, u32[]{:S(2)}) collective-permute-start(bf16[4,384,128]{2,1,0:T(8,128)(2,1)S(1)} %pad_maximum_fusion.7.refs_0_), channel_id=1, source_target_pairs={{0,4},{4,0},{8,12},{12,8},{16,20},{20,16},{24,28},{28,24},{1,5},{5... | collective-permute-start | bytes 1179656 | tf_op jit(solution)/shard_map/ppermute | solution.py:61
  633.6 60.2 %collective-permute-start.110 = (bf16[4,384,128]{2,1,0:T(8,128)(2,1)}, bf16[4,384,128]{2,1,0:T(8,128)(2,1)S(1)}, u32[]{:S(2)}, u32[]{:S(2)}) collective-permute-start(bf16[4,384,128]{2,1,0:T(8,128)(2,1)} %pad_maximum_fusion.8.refs_0_), channel_id=1, source_target_pairs={{0,8},{4,12},{8,0},{12,4},{16,24},{20,28},{24,16},{28,20},{1,9},{5... | collective-permute-start | bytes 1179656 | tf_op jit(solution)/shard_map/ppermute | solution.py:61
  661.1 61.3 %collective-permute-start.111 = (bf16[4,384,128]{2,1,0:T(8,128)(2,1)}, bf16[4,384,128]{2,1,0:T(8,128)(2,1)S(1)}, u32[]{:S(2)}, u32[]{:S(2)}) collective-permute-start(bf16[4,384,128]{2,1,0:T(8,128)(2,1)} %pad_maximum_fusion.8.refs_0_), channel_id=1, source_target_pairs={{0,16},{4,20},{8,24},{12,28},{16,0},{20,4},{24,8},{28,12},{1,17},{... | collective-permute-start | bytes 1179656 | tf_op jit(solution)/shard_map/ppermute | solution.py:61
  689.0 33.4 %collective-permute-start.112 = (bf16[4,384,128]{2,1,0:T(8,128)(2,1)}, bf16[4,384,128]{2,1,0:T(8,128)(2,1)S(1)}, u32[]{:S(2)}, u32[]{:S(2)}) collective-permute-start(bf16[4,384,128]{2,1,0:T(8,128)(2,1)} %pad_maximum_fusion.8.refs_0_), channel_id=1, source_target_pairs={{0,24},{4,28},{8,16},{12,20},{16,8},{20,12},{24,0},{28,4},{1,25},{... | collective-permute-start | bytes 1179656 | tf_op jit(solution)/shard_map/ppermute | solution.py:61
  690.6 67.6 %collective-permute-start.78 = (bf16[192,1536]{1,0:T(8,128)(2,1)S(1)}, bf16[192,1536]{1,0:T(8,128)(2,1)S(1)}, u32[]{:S(2)}, u32[]{:S(2)}) collective-permute-start(bf16[192,1536]{1,0:T(8,128)(2,1)S(1)} %constant_dynamic-slice_fusion.25), channel_id=1, source_target_pairs={{0,4},{4,0},{8,12},{12,8},{16,20},{20,16},{24,28},{28,24},{1,5},{5... | collective-permute-start | bytes 1769480 | tf_op jit(solution)/shard_map/ppermute | solution.py:61
  692.2 33.4 %collective-permute-start.113 = (bf16[4,384,128]{2,1,0:T(8,128)(2,1)}, bf16[4,384,128]{2,1,0:T(8,128)(2,1)}, u32[]{:S(2)}, u32[]{:S(2)}) collective-permute-start(bf16[4,384,128]{2,1,0:T(8,128)(2,1)} %pad_maximum_fusion.8.refs_0_), channel_id=1, source_target_pairs={{0,4},{4,0},{8,12},{12,8},{16,20},{20,16},{24,28},{28,24},{1,5},{5... | collective-permute-start | bytes 1179656 | tf_op jit(solution)/shard_map/ppermute | solution.py:61
  693.9 36.3 %collective-permute-start.124 = (bf16[4,384,128]{2,1,0:T(8,128)(2,1)S(1)}, bf16[4,384,128]{2,1,0:T(8,128)(2,1)}, u32[]{:S(2)}, u32[]{:S(2)}) collective-permute-start(bf16[4,384,128]{2,1,0:T(8,128)(2,1)S(1)} %pad_maximum_fusion.9.refs_0_), channel_id=1, source_target_pairs={{0,8},{4,12},{8,0},{12,4},{16,24},{20,28},{24,16},{28,20},{1,9},{5... | collective-permute-start | bytes 1179656 | tf_op jit(solution)/shard_map/ppermute | solution.py:61
  722.4 33.8 %collective-permute-start.125 = (bf16[4,384,128]{2,1,0:T(8,128)(2,1)S(1)}, bf16[4,384,128]{2,1,0:T(8,128)(2,1)}, u32[]{:S(2)}, u32[]{:S(2)}) collective-permute-start(bf16[4,384,128]{2,1,0:T(8,128)(2,1)S(1)} %pad_maximum_fusion.9.refs_0_), channel_id=1, source_target_pairs={{0,16},{4,20},{8,24},{12,28},{16,0},{20,4},{24,8},{28,12},{1,17},{... | collective-permute-start | bytes 1179656 | tf_op jit(solution)/shard_map/ppermute | solution.py:61
  723.9 33.8 %collective-permute-start.126 = (bf16[4,384,128]{2,1,0:T(8,128)(2,1)S(1)}, bf16[4,384,128]{2,1,0:T(8,128)(2,1)}, u32[]{:S(2)}, u32[]{:S(2)}) collective-permute-start(bf16[4,384,128]{2,1,0:T(8,128)(2,1)S(1)} %pad_maximum_fusion.9.refs_0_), channel_id=1, source_target_pairs={{0,24},{4,28},{8,16},{12,20},{16,8},{20,12},{24,0},{28,4},{1,25},{... | collective-permute-start | bytes 1179656 | tf_op jit(solution)/shard_map/ppermute | solution.py:61
  725.6 36.1 %collective-permute-start.127 = (bf16[4,384,128]{2,1,0:T(8,128)(2,1)S(1)}, bf16[4,384,128]{2,1,0:T(8,128)(2,1)S(1)}, u32[]{:S(2)}, u32[]{:S(2)}) collective-permute-start(bf16[4,384,128]{2,1,0:T(8,128)(2,1)S(1)} %pad_maximum_fusion.9.refs_0_), channel_id=1, source_target_pairs={{0,4},{4,0},{8,12},{12,8},{16,20},{20,16},{24,28},{28,24},{1,5},{5... | collective-permute-start | bytes 1179656 | tf_op jit(solution)/shard_map/ppermute | solution.py:61
  730.2 33.1 %collective-permute-start.100 = (bf16[4,384,128]{2,1,0:T(8,128)(2,1)}, bf16[4,384,128]{2,1,0:T(8,128)(2,1)}, u32[]{:S(2)}, u32[]{:S(2)}) collective-permute-start(bf16[4,384,128]{2,1,0:T(8,128)(2,1)} %copy-done.33), channel_id=1, source_target_pairs={{0,4},{4,0},{8,12},{12,8},{16,20},{20,16},{24,28},{28,24},{1,5},{5... | collective-permute-start | bytes 1179656 | tf_op jit(solution)/shard_map/ppermute | solution.py:61
  788.9 47.1 %collective-permute-start.130 = (bf16[4,384,128]{2,1,0:T(8,128)(2,1)}, bf16[4,384,128]{2,1,0:T(8,128)(2,1)}, u32[]{:S(2)}, u32[]{:S(2)}) collective-permute-start(bf16[4,384,128]{2,1,0:T(8,128)(2,1)} %collective-permute-done.126.refs_3_), channel_id=1, source_target_pairs={{0,4},{4,0},{8,12},{12,8},{16,20},{20,16},{24,28},{28,24},{1,5},{5... | collective-permute-start | bytes 1179656 | tf_op jit(solution)/shard_map/ppermute | solution.py:61
  855.6 46.4 %collective-permute-start.33 = (bf16[384,1536]{1,0:T(8,128)(2,1)S(1)}, bf16[384,1536]{1,0:T(8,128)(2,1)S(1)}, u32[]{:S(2)}, u32[]{:S(2)}) collective-permute-start(bf16[384,1536]{1,0:T(8,128)(2,1)S(1)} %convolution_convert_fusion.6), channel_id=1, source_target_pairs={{0,1},{1,0},{2,3},{3,2},{4,5},{5,4},{6,7},{7,6},{8,9},{9,8},{10,11... | collective-permute-start | bytes 3538952 | tf_op jit(solution)/shard_map/ppermute | solution.py:61
  864.1 49.9 %collective-permute-start.35 = (bf16[384,1536]{1,0:T(8,128)(2,1)S(1)}, bf16[384,1536]{1,0:T(8,128)(2,1)S(1)}, u32[]{:S(2)}, u32[]{:S(2)}) collective-permute-start(bf16[384,1536]{1,0:T(8,128)(2,1)S(1)} %add_convert_fusion.6), channel_id=1, source_target_pairs={{0,2},{1,3},{2,0},{3,1},{4,6},{5,7},{6,4},{7,5},{8,10},{9,11},{10,... | collective-permute-start | bytes 3538952 | tf_op jit(solution)/shard_map/ppermute | solution.py:61
  892.0 35.2 %collective-permute-start.52 = (bf16[48,768]{1,0:T(8,128)(2,1)S(1)}, bf16[48,768]{1,0:T(8,128)(2,1)S(1)}, u32[]{:S(2)}, u32[]{:S(2)}) collective-permute-start(bf16[48,768]{1,0:T(8,128)(2,1)S(1)} %get-tuple-element.81), channel_id=1, source_target_pairs={{0,16},{4,20},{8,24},{12,28},{16,0},{20,4},{24,8},{28,12},{1,17},{... | collective-permute-start | bytes 221192 | tf_op jit(solution)/shard_map/ppermute | solution.py:61
  970.5 49.1 %collective-permute-start.74 = (bf16[48,768]{1,0:T(8,128)(2,1)S(1)}, bf16[48,768]{1,0:T(8,128)(2,1)S(1)}, u32[]{:S(2)}, u32[]{:S(2)}) collective-permute-start(bf16[48,768]{1,0:T(8,128)(2,1)S(1)} %collective-permute-done.70.refs_3_), channel_id=1, source_target_pairs={{0,4},{4,0},{8,12},{12,8},{16,20},{20,16},{24,28},{28,24},{1,5},{5... | collective-permute-start | bytes 221192 | tf_op jit(solution)/shard_map/ppermute | solution.py:61
  971.5 50.7 %collective-permute-start.43 = (bf16[48,1536]{1,0:T(8,128)(2,1)S(1)}, bf16[48,1536]{1,0:T(8,128)(2,1)S(1)}, u32[]{:S(2)}, u32[]{:S(2)}) collective-permute-start(bf16[48,1536]{1,0:T(8,128)(2,1)S(1)} %add_convert_fusion.23.refs_0_), channel_id=1, source_target_pairs={{0,4},{4,0},{8,12},{12,8},{16,20},{20,16},{24,28},{28,24},{1,5},{5... | collective-permute-start | bytes 442376 | tf_op jit(solution)/shard_map/ppermute | solution.py:61
  972.7 49.6 %collective-permute-start.44 = (bf16[48,1536]{1,0:T(8,128)(2,1)S(1)}, bf16[48,1536]{1,0:T(8,128)(2,1)S(1)}, u32[]{:S(2)}, u32[]{:S(2)}) collective-permute-start(bf16[48,1536]{1,0:T(8,128)(2,1)S(1)} %collective-permute-done.40.refs_1_), channel_id=1, source_target_pairs={{0,4},{4,0},{8,12},{12,8},{16,20},{20,16},{24,28},{28,24},{1,5},{5... | collective-permute-start | bytes 442376 | tf_op jit(solution)/shard_map/ppermute | solution.py:61
  975.7 46.6 %collective-permute-start.45 = (bf16[48,1536]{1,0:T(8,128)(2,1)S(1)}, bf16[48,1536]{1,0:T(8,128)(2,1)S(1)}, u32[]{:S(2)}, u32[]{:S(2)}) collective-permute-start(bf16[48,1536]{1,0:T(8,128)(2,1)S(1)} %collective-permute-done.41.refs_2_), channel_id=1, source_target_pairs={{0,4},{4,0},{8,12},{12,8},{16,20},{20,16},{24,28},{28,24},{1,5},{5... | collective-permute-start | bytes 442376 | tf_op jit(solution)/shard_map/ppermute | solution.py:61
  976.8 45.6 %collective-permute-start.46 = (bf16[48,1536]{1,0:T(8,128)(2,1)S(1)}, bf16[48,1536]{1,0:T(8,128)(2,1)S(1)}, u32[]{:S(2)}, u32[]{:S(2)}) collective-permute-start(bf16[48,1536]{1,0:T(8,128)(2,1)S(1)} %collective-permute-done.42.refs_3_), channel_id=1, source_target_pairs={{0,4},{4,0},{8,12},{12,8},{16,20},{20,16},{24,28},{28,24},{1,5},{5... | collective-permute-start | bytes 442376 | tf_op jit(solution)/shard_map/ppermute | solution.py:61
  (168 other events, 3066.0 us)

commit v2 on v1

v2 whole, which is shorter than its diff:
```python
import math

import jax
import jax.numpy as jnp
from jax import lax
from jax.experimental import pallas as pl
from jax.experimental.pallas import tpu as pltpu
from jax.sharding import PartitionSpec as P

HQ = 16
HK = 8
HD = 96
GROUP = HQ // HK
BLK = 128

epsilon = 1e-05
rope_base = 100000.0
masked_score = -1e30
scale = 1.0 / math.sqrt(HD)
low = jnp.bfloat16
wide = jnp.float32
brief = pl.CostEstimate(flops=0, bytes_accessed=0, transcendentals=0)
lasting = pl.CostEstimate(flops=10**11, bytes_accessed=0, transcendentals=0)


def angles_of(places):
    frequency = jnp.exp(jnp.arange(HD // 2, dtype=wide) * (-2.0 * math.log(rope_base) / HD))
    turned = places.astype(wide)[:, None] * frequency[None, :]
    return (jnp.cos(turned)[:, None, :], jnp.sin(turned)[:, None, :])


def product(left, right):
    return jnp.dot(left, right, preferred_element_type=wide)


def contract_last(left, right):
    return lax.dot_general(left, right, (((1,), (1,)), ((), ())), preferred_element_type=wide)


def contract_first(left, right):
    return lax.dot_general(left, right, (((0,), (0,)), ((), ())), preferred_element_type=wide)


def swap(array, axis, bits, size):
    return lax.ppermute(array, axis, [(i, i ^ bits) for i in range(size)])


def over_fsdp(array, bits):
    return swap(array, "fsdp", bits, 4)


def over_ctx(array, bits):
    return swap(array, "ctx", bits, lax.axis_size("ctx"))


def columns(array, index, width):
    return lax.dynamic_slice_in_dim(array, index * width, width, array.ndim - 1)


def rows(array, index, height):
    return lax.dynamic_slice_in_dim(array, index * height, height, 0)


def after(array, *others):
    return lax.optimization_barrier((array, *others))[0]


def add_low(first, *others):
    total = first.astype(wide)
    for other in others:
        total = total + other.astype(wide)
    return total.astype(low)


def gather_fsdp(array, *others):
    far = after(over_fsdp(array, 2), *others)
    pair = over_fsdp(jnp.concatenate([array, far], axis=0), 1)
    return jnp.concatenate([array, far, pair], axis=0)


def scatter_fsdp(terms, *others):
    half, height = terms.shape[0] // 2, terms.shape[0] // 4
    kept, got = terms[:half], over_fsdp(terms[half:], 1)
    passed = add_low(kept[height:], got[height:])
    away = after(over_fsdp(passed, 2), *others)
    total = kept[:height].astype(wide) + got[:height].astype(wide) + away.astype(wide)
    return total, passed


ALL, REST, MINE, OTHER = 0, 3, 4, 8
heads_plan = (
    (0, ALL),
    (1, ALL),
    (2, MINE + 1),
    (2, OTHER + 1),
    (2, REST),
    (3, MINE + 1),
    (3, OTHER + 1),
    (3, REST),
)
outward_plan = ((0, ALL), (1, ALL), (2, MINE + 2), (2, OTHER + 2), (3, MINE + 2), (3, OTHER + 2))
units_plan = ((0, ALL), (1, ALL), (2, MINE + 1), (2, OTHER + 1), (3, MINE + 2), (3, OTHER + 2))


def gather_thirds(own):
    side = lax.axis_index("ctx") % 2
    third = own.shape[1] // 3
    far = over_fsdp(columns(own, side, third), 2)
    rest = over_fsdp(after(own[:, 2 * third :], far), 2)
    near = over_fsdp(own, 1)
    other = over_ctx(far, 1)
    return (
        own,
        near,
        far,
        other,
        rest,
        over_fsdp(far, 1),
        over_fsdp(other, 1),
        over_fsdp(rest, 1),
    )


def gather_halves(own):
    far = over_fsdp(columns(own, lax.axis_index("ctx") // 2 % 2, own.shape[1] // 2), 2)
    near = over_fsdp(own, 1)
    other = over_ctx(far, 2)
    return (own, near, far, other, over_fsdp(far, 1), over_fsdp(other, 1))


def fill_weight(code_ref, plan, pieces, out):
    part = code_ref[0]
    for (k, which), piece in zip(plan, pieces):
        height, width = piece.shape
        across = pl.ds(pl.multiple_of((part ^ k) * height, height), height)
        if which == ALL:
            out[across, :] = piece[...]
        elif which == REST:
            out[across, 2 * width :] = piece[...]
        else:
            side = code_ref[which % MINE]
            place = 1 - side if which >= OTHER else side
            out[across, lanes(place, width)] = piece[...]


def whole_call(kernel, code, arrays, outs, scratch, flops, name):
    spec = pl.BlockSpec(memory_space=pltpu.VMEM)
    moved = sum(math.prod(a.shape) * a.dtype.itemsize for a in (*arrays, *outs))
    return pl.pallas_call(
        kernel,
        grid_spec=pltpu.PrefetchScalarGridSpec(
            num_scalar_prefetch=1,
            grid=(),
            in_specs=[spec] * len(arrays),
            out_specs=[spec] * len(outs),
            scratch_shapes=scratch,
        ),
        out_shape=outs,
        compiler_params=pltpu.CompilerParams(vmem_limit_bytes=56 << 20),
        cost_estimate=pl.CostEstimate(flops=flops, bytes_accessed=moved, transcendentals=0),
        name=name,
    )(code, *arrays)


def lanes(index, width):
    return pl.ds(pl.multiple_of(index * width, 128), width)


def gained(code_ref, gains, row, out):
    for k in range(4):
        out[:, lanes(code_ref[0] ^ k, gains[k].shape[1])] = gains[k][row : row + 1, :].astype(wide)


def turned(values, cosine, sine):
    half = values.shape[1] // 2
    return values * cosine + jnp.concatenate([values[:, half:], values[:, :half]], axis=1) * sine


def inverse_rms(values):
    return lax.rsqrt(jnp.mean(values * values, axis=1, keepdims=True) + epsilon)


def slot_of_head(head):
    if head < HQ:
        return head // GROUP, head % GROUP
    return (head - HQ) % HK, GROUP + (head - HQ) // HK


def heads_kernel(code_ref, rows_ref, cosine_ref, sine_ref, *refs):
    gains, pieces = refs[:4], refs[4:12]
    normed_ref, load_ref, gain, weight, total = refs[12:]
    gained(code_ref, gains, 0, gain)
    fill_weight(code_ref, heads_plan, pieces, weight)
    values = rows_ref[...].astype(wide)
    normed_ref[...] = (values * inverse_rms(values) * gain[...]).astype(low)
    total[...] = product(normed_ref[...], weight[...])
    cosine, sine = cosine_ref[...], sine_ref[...]
    for head in range(HQ + 2 * HK):
        part = total[:, head * HD : (head + 1) * HD]
        if head < HQ + HK:
            part = turned(part, cosine, sine)
        group, place = slot_of_head(head)
        load_ref[group, :, place * HD : (place + 1) * HD] = part.astype(low)


def heads_call(code, rows_in, cosine, sine, gains, pieces):
    count, width = rows_in.shape
    total = pieces[0].shape[1]
    outs = [
        jax.ShapeDtypeStruct((count, width), low),
        jax.ShapeDtypeStruct((HK, count, (GROUP + 2) * HD), low),
    ]
    scratch = [
        pltpu.VMEM((1, width), wide),
        pltpu.VMEM((width, total), low),
        pltpu.VMEM((count, total), wide),
    ]
    return whole_call(
        heads_kernel,
        code,
        (rows_in, cosine, sine, *gains, *pieces),
        outs,
        scratch,
        2 * count * width * total,
        "query_key_value",
    )


def middle_kernel(code_ref, rows_ref, mixed_ref, *refs):
    gains, pieces = refs[:4], refs[4:10]
    flat_ref, middle_ref, normed_ref, gain, weight = refs[10:]
    gained(code_ref, gains, 1, gain)
    fill_weight(code_ref, outward_plan, pieces, weight)
    span = mixed_ref.shape[2]
    for group in range(mixed_ref.shape[0]):
        flat_ref[:, group * span : (group + 1) * span] = mixed_ref[group]
    middle = contract_last(flat_ref[...], weight[...]) + rows_ref[...].astype(wide)
    middle_ref[...] = middle
    normed_ref[...] = (middle * inverse_rms(middle) * gain[...]).astype(low)


def middle_call(code, rows_in, mixed, gains, pieces):
    count, width = rows_in.shape
    outs = [
        jax.ShapeDtypeStruct((count, HQ * HD), low),
        jax.ShapeDtypeStruct((count, width), wide),
        jax.ShapeDtypeStruct((count, width), low),
    ]
    return whole_call(
        middle_kernel,
        code,
        (rows_in, mixed, *gains, *pieces),
        outs,
        [pltpu.VMEM((1, width), wide), pltpu.VMEM((width, HQ * HD), low)],
        2 * count * width * HQ * HD,
        "attention_output",
    )


def norm_back(values, gain, grad):
    inverse = inverse_rms(values)
    weighted = gain * grad
    inner = jnp.mean(values * weighted, axis=1, keepdims=True)
    back = inverse * weighted - values * inverse * inverse * inverse * inner
    return back, jnp.sum(grad * values * inverse, axis=0, keepdims=True)


def middle_back_kernel(code_ref, middle_ref, grad_ref, out_grad_ref, *refs):
    gains, pieces = refs[:4], refs[4:10]
    grad_middle_ref, branch_ref, sent_ref, gain_grad_ref, gain, weight = refs[10:]
    gained(code_ref, gains, 1, gain)
    fill_weight(code_ref, outward_plan, pieces, weight)
    back, gain_grad_ref[...] = norm_back(middle_ref[...], gain[...], grad_ref[...])
    grad_middle = out_grad_ref[...].astype(wide) + back
    grad_middle_ref[...] = grad_middle
    branch_ref[...] = grad_middle.astype(low)
    total = product(branch_ref[...], weight[...]).astype(low)
    span = sent_ref.shape[2]
    for group in range(sent_ref.shape[0]):
        sent_ref[group] = total[:, group * span : (group + 1) * span]


def middle_back_call(code, middle, grad, out_grad, gains, pieces):
    count, width = middle.shape
    outs = [
        jax.ShapeDtypeStruct((count, width), wide),
        jax.ShapeDtypeStruct((count, width), low),
        jax.ShapeDtypeStruct((HK, count, GROUP * HD), low),
        jax.ShapeDtypeStruct((1, width), wide),
    ]
    return whole_call(
        middle_back_kernel,
        code,
        (middle, grad, out_grad, *gains, *pieces),
        outs,
        [pltpu.VMEM((1, width), wide), pltpu.VMEM((width, HQ * HD), low)],
        2 * count * width * HQ * HD,
        "attention_output_back",
    )


def heads_back_kernel(
    code_ref, load_ref, rows_ref, grad_middle_ref, cosine_ref, sine_ref, *refs
):
    gains, pieces = refs[:4], refs[4:12]
    raw_ref, input_grad_ref, gain_grad_ref, gain, weight, raw = refs[12:]
    gained(code_ref, gains, 0, gain)
    fill_weight(code_ref, heads_plan, pieces, weight)
    cosine, sine = cosine_ref[...], sine_ref[...]
    for head in range(HQ + 2 * HK):
        group, place = slot_of_head(head)
        part = load_ref[group, :, place * HD : (place + 1) * HD]
        if head < HQ + HK:
            part = turned(part.astype(wide), cosine, -sine).astype(low)
        raw[:, head * HD : (head + 1) * HD] = part
    quarter = raw_ref.shape[3]
    for k in range(4):
        for i in range(2):
            first = (4 * i + k) * quarter
            raw_ref[i, k] = raw[:, first : first + quarter]
    grad = contract_last(raw[...], weight[...])
    back, gain_grad_ref[...] = norm_back(rows_ref[...].astype(wide), gain[...], grad)
    input_grad_ref[...] = grad_middle_ref[...] + back


def heads_back_call(code, load, rows_in, grad_middle, cosine, sine, gains, pieces):
    count, width = rows_in.shape
    total = pieces[0].shape[1]
    outs = [
        jax.ShapeDtypeStruct((2, 4, count, total // 8), low),
        jax.ShapeDtypeStruct((count, width), wide),
        jax.ShapeDtypeStruct((1, width), wide),
    ]
    return whole_call(
        heads_back_kernel,
        code,
        (load, rows_in, grad_middle, cosine, sine, *gains, *pieces),
        outs,
        [
            pltpu.VMEM((1, width), wide),
            pltpu.VMEM((width, total), low),
            pltpu.VMEM((count, total), low),
        ],
        2 * count * width * total,
        "query_key_value_back",
    )


def units_kernel(code_ref, normed_ref, grad_ref, *refs):
    pieces = refs[:6]
    out_ref, back_ref, hidden_ref, grad_gate_ref, grad_up_ref, weights = refs[6:]

    @pl.when(pl.program_id(0) == 0)
    def _():
        for i in range(3):
            fill_weight(code_ref, units_plan, [piece.at[i] for piece in pieces], weights.at[i])

    gate = product(normed_ref[...], weights[0])
    upward = product(normed_ref[...], weights[1])
    sigmoid_gate = jax.nn.sigmoid(gate)
    swish = gate * sigmoid_gate
    hidden = (swish * upward).astype(low)
    hidden_ref[...] = hidden
    grad_hidden = product(grad_ref[...], weights[2])
    grad_gate = (
        grad_hidden * upward * sigmoid_gate * (1.0 + gate * (1.0 - sigmoid_gate))
    ).astype(low)
    grad_up = (grad_hidden * swish).astype(low)
    grad_gate_ref[...] = grad_gate
    grad_up_ref[...] = grad_up
    back_ref[...] = (
        contract_last(grad_gate, weights[0]) + contract_last(grad_up, weights[1])
    ).astype(low)
    out_ref[...] = contract_last(hidden, weights[2]).astype(low)


def units_call(code, normed, grad, pieces):
    count, width = normed.shape
    units = pieces[0].shape[2]
    tile = 512
    wide_block = pl.BlockSpec((tile, width), lambda i, code: (i, 0))
    unit_block = pl.BlockSpec((tile, units), lambda i, code: (i, 0))
    return pl.pallas_call(
        units_kernel,
        grid_spec=pltpu.PrefetchScalarGridSpec(
            num_scalar_prefetch=1,
            grid=(count // tile,),
            in_specs=[wide_block, wide_block]
            + [pl.BlockSpec(memory_space=pltpu.VMEM)] * len(pieces),
            out_specs=[wide_block, wide_block, unit_block, unit_block, unit_block],
            scratch_shapes=[pltpu.VMEM((3, width, units), low)],
        ),
        out_shape=[jax.ShapeDtypeStruct((count, width), low)] * 2
        + [jax.ShapeDtypeStruct((count, units), low)] * 3,
        compiler_params=pltpu.CompilerParams(vmem_limit_bytes=60 << 20),
        cost_estimate=pl.CostEstimate(
            flops=12 * count * width * units,
            bytes_accessed=8 * count * width + 6 * width * units,
            transcendentals=count * units,
        ),
        name="feed_forward",
    )(code, normed, grad, *pieces)


def deal_weights(weights):
    part, here = lax.axis_index("fsdp"), lax.axis_index("ctx")
    width = weights[0].shape[1] // 4

    def taken(k):
        return jnp.stack([columns(weight, part ^ k, width) for weight in weights])

    def half(k, side):
        return jnp.stack(
            [columns(weight, (part ^ k) * 2 + side, width // 2) for weight in weights]
        )

    return taken(0), taken(1), half(2, here % 2), half(3, here // 2 % 2)


def slot_of(ref, slot):
    return ref.at[slot // 2, (slot % 2) * BLK : (slot % 2 + 1) * BLK, :]


def sort_rows(order_ref, load_ref, queries, keys, values):
    for slot in range(2 * load_ref.shape[0]):
        block = order_ref[slot]
        piece = slot_of(load_ref, slot)[...]
        place = pl.ds(pl.multiple_of(block * BLK, BLK), BLK)
        half = pl.ds(pl.multiple_of((block % 2) * BLK, BLK), BLK)
        other = pl.ds(pl.multiple_of((block % 2) * BLK + 2 * BLK, BLK), BLK)
        queries[block // 2, half, :] = piece[:, :HD]
        queries[block // 2, other, :] = piece[:, HD : 2 * HD]
        keys[place, :] = piece[:, 2 * HD : 3 * HD]
        values[place, :] = piece[:, 3 * HD :]


def forward_kernel(order_ref, load_ref, out_ref, queries, keys, values, mixed):
    sort_rows(order_ref, load_ref, queries, keys, values)
    step = 2 * BLK
    query_at = lax.broadcasted_iota(jnp.int32, (2 * step, step), 0) % step
    key_at = lax.broadcasted_iota(jnp.int32, (2 * step, step), 1)
    allowed = key_at <= query_at
    for i in range(keys.shape[0] // step):
        reach = (i + 1) * step
        query = queries[i]
        ahead = contract_last(query, keys[i * step : reach, :]) * scale
        ahead = jnp.where(allowed, ahead, masked_score)
        top = jnp.max(ahead, axis=1, keepdims=True)
        if i:
            before = contract_last(query, keys[: i * step, :]) * scale
            top = jnp.maximum(top, jnp.max(before, axis=1, keepdims=True))
        soft = jnp.exp(ahead - top)
        total = jnp.sum(soft, axis=1, keepdims=True)
        result = product(soft.astype(low), values[i * step : reach, :])
        if i:
            soft = jnp.exp(before - top)
            total = total + jnp.sum(soft, axis=1, keepdims=True)
            result = result + product(soft.astype(low), values[: i * step, :])
        result = (result / total).astype(low)
        mixed[i * step : reach, :HD] = result[:step]
        mixed[i * step : reach, HD:] = result[step:]
    for slot in range(2 * load_ref.shape[0]):
        place = pl.ds(pl.multiple_of(order_ref[slot] * BLK, BLK), BLK)
        slot_of(out_ref, slot)[...] = mixed[place, :]


def backward_kernel(
    order_ref, load_ref, grad_ref, out_ref, queries, keys, values, grads, key_sum, value_sum, sent
):
    sort_rows(order_ref, load_ref, queries, keys, values)
    step = 2 * BLK
    length = keys.shape[0]
    for slot in range(length // BLK):
        block = order_ref[slot]
        piece = slot_of(grad_ref, slot)[...]
        half = pl.ds(pl.multiple_of((block % 2) * BLK, BLK), BLK)
        other = pl.ds(pl.multiple_of((block % 2) * BLK + 2 * BLK, BLK), BLK)
        grads[block // 2, half, :] = piece[:, :HD]
        grads[block // 2, other, :] = piece[:, HD:]
    key_at = lax.broadcasted_iota(jnp.int32, (step, 2 * step), 0)
    query_at = lax.broadcasted_iota(jnp.int32, (step, 2 * step), 1) % step
    allowed = key_at <= query_at
    for i in range(length // step):
        query = queries[i]
        grad = grads[i]
        scores = []
        top = None
        for j in range(i + 1):
            score = contract_last(keys[j * step : (j + 1) * step, :], query) * scale
            if j == i:
                score = jnp.where(allowed, score, masked_score)
            high = jnp.max(score, axis=0, keepdims=True)
            top = high if top is None else jnp.maximum(top, high)
            scores.append(score)
        total = jnp.zeros_like(top)
        delta = jnp.zeros_like(top)
        softs = []
        slopes = []
        for j in range(i + 1):
            soft = jnp.exp(scores[j] - top)
            slope = contract_last(values[j * step : (j + 1) * step, :], grad)
            total = total + jnp.sum(soft, axis=0, keepdims=True)
            delta = delta + jnp.sum(soft * slope, axis=0, keepdims=True)
            softs.append(soft)
            slopes.append(slope)
        share = 1.0 / total
        delta = delta * share
        query_sum = jnp.zeros((2 * step, HD), wide)
        for j in range(i + 1):
            place = slice(j * step, (j + 1) * step)
            soft = softs[j] * share
            steep = (soft * (slopes[j] - delta)).astype(low)
            key_part = product(steep, query)
            value_part = product(soft.astype(low), grad)
            if j == i:
                key_sum[place, :] = key_part
                value_sum[place, :] = value_part
            else:
                key_sum[place, :] += key_part
                value_sum[place, :] += value_part
            query_sum = query_sum + contract_first(steep, keys[place, :])
        query_sum = (query_sum * scale).astype(low)
        sent[i * step : (i + 1) * step, :HD] = query_sum[:step]
        sent[i * step : (i + 1) * step, HD : 2 * HD] = query_sum[step:]
    sent[:, 2 * HD : 3 * HD] = (key_sum[...] * scale).astype(low)
    sent[:, 3 * HD :] = value_sum[...].astype(low)
    for slot in range(length // BLK):
        place = pl.ds(pl.multiple_of(order_ref[slot] * BLK, BLK), BLK)
        slot_of(out_ref, slot)[...] = sent[place, :]


def attention_call(kernel, order, arrays, width, scratch, products, name):
    devices, height = arrays[0].shape[:2]
    length = devices * height
    half = (length * length) // 2 * GROUP
    whole = pl.BlockSpec(memory_space=pltpu.VMEM)
    return pl.pallas_call(
        kernel,
        grid_spec=pltpu.PrefetchScalarGridSpec(
            num_scalar_prefetch=1,
            grid=(),
            in_specs=[whole] * len(arrays),
            out_specs=whole,
            scratch_shapes=scratch,
        ),
        out_shape=jax.ShapeDtypeStruct((devices, height, width), low),
        compiler_params=pltpu.CompilerParams(vmem_limit_bytes=56 << 20),
        cost_estimate=pl.CostEstimate(
            flops=2 * products * half * 256, bytes_accessed=8 * length * width, transcendentals=half
        ),
        name=name,
    )(order, *arrays)


def attention_forward(order, load):
    length = load.shape[0] * load.shape[1]
    scratch = [
        pltpu.VMEM((length // (2 * BLK), 4 * BLK, HD), low),
        pltpu.VMEM((length, HD), low),
        pltpu.VMEM((length, HD), low),
        pltpu.VMEM((length, 2 * HD), low),
    ]
    return attention_call(forward_kernel, order, (load,), 2 * HD, scratch, 2, "attention_forward")


def attention_backward(order, load, grad):
    length = load.shape[0] * load.shape[1]
    scratch = [
        pltpu.VMEM((length // (2 * BLK), 4 * BLK, HD), low),
        pltpu.VMEM((length, HD), low),
        pltpu.VMEM((length, HD), low),
        pltpu.VMEM((length // (2 * BLK), 4 * BLK, HD), low),
        pltpu.VMEM((length, HD), wide),
        pltpu.VMEM((length, HD), wide),
        pltpu.VMEM((length, 4 * HD), low),
    ]
    return attention_call(
        backward_kernel, order, (load, grad), 4 * HD, scratch, 5, "attention_backward"
    )


def scores_of(query_rot, keys_all, own_places, all_places, start, block_size):
    key_block = lax.dynamic_slice_in_dim(keys_all, start, block_size, 0)
    key_places = lax.dynamic_slice_in_dim(all_places, start, block_size, 0)
    raw = (
        jnp.einsum("rkgd,skd->rkgs", query_rot, key_block, preferred_element_type=wide) * scale
    )
    allowed = key_places[None, None, None, :] <= own_places[:, None, None, None]
    return (jnp.where(allowed, raw, masked_score), key_block)


def rows_forward(query_rot, keys_all, values_all, own_places, all_places):
    row_count = query_rot.shape[0]
    key_total = keys_all.shape[0]
    block_size = math.gcd(key_total, 512)

    def step(block_index, carry):
        top_score, total, mixed = carry
        start = block_index * block_size
        scores, _ = scores_of(query_rot, keys_all, own_places, all_places, start, block_size)
        value_block = lax.dynamic_slice_in_dim(values_all, start, block_size, 0)
        new_top = jnp.maximum(top_score, jnp.max(scores, axis=-1))
        soft = jnp.exp(scores - new_top[..., None])
        shrink = jnp.exp(top_score - new_top)
        total = total * shrink + jnp.sum(soft, axis=-1)
        mixed = mixed * shrink[..., None] + jnp.einsum(
            "rkgs,skd->rkgd", soft.astype(low), value_block, preferred_element_type=wide
        )
        return (new_top, total, mixed)

    start_top = jnp.full((row_count, HK, GROUP), masked_score, wide)
    start_total = jnp.zeros((row_count, HK, GROUP), wide)
    start_mixed = jnp.zeros((row_count, HK, GROUP, HD), wide)
    top_score, total, mixed = lax.fori_loop(
        0, key_total // block_size, step, (start_top, start_total, start_mixed)
    )
    return (mixed / total[..., None], top_score + jnp.log(total))


def rows_backward(
    query_rot, keys_all, values_all, own_places, all_places, log_total, delta, grad_mixed
):
    row_count = query_rot.shape[0]
    key_total = keys_all.shape[0]
    block_size = math.gcd(key_total, 512)

    def step(block_index, carry):
        grad_query, grad_keys, grad_values = carry
        start = block_index * block_size
        scores, key_block = scores_of(
            query_rot, keys_all, own_places, all_places, start, block_size
        )
        value_block = lax.dynamic_slice_in_dim(values_all, start, block_size, 0)
        soft = jnp.exp(scores - log_total[..., None])
        grad_soft = jnp.einsum(
            "rkgd,skd->rkgs", grad_mixed, value_block, preferred_element_type=wide
        )
        steep = (soft * (grad_soft - delta[..., None])).astype(low)
        grad_query = grad_query + scale * jnp.einsum(
            "rkgs,skd->rkgd", steep, key_block, preferred_element_type=wide
        )
        key_part = scale * jnp.einsum(
            "rkgs,rkgd->skd", steep, query_rot, preferred_element_type=wide
        )
        value_part = jnp.einsum(
            "rkgs,rkgd->skd", soft.astype(low), grad_mixed, preferred_element_type=wide
        )
        grad_keys = lax.dynamic_update_slice_in_dim(
            grad_keys, key_part.reshape(block_size, HK * HD), start, 0
        )
        grad_values = lax.dynamic_update_slice_in_dim(
            grad_values, value_part.reshape(block_size, HK * HD), start, 0
        )
        return (grad_query, grad_keys, grad_values)

    start_query = jnp.zeros((row_count, HK, GROUP, HD), wide)
    start_keys = jnp.zeros((key_total, HK * HD), wide)
    return lax.fori_loop(
        0, key_total // block_size, step, (start_query, start_keys, start_keys)
    )


def exchange_levels(cut):
    return [over_ctx(cut(k), 2 * k) for k in (1, 2, 3)]


def reduce_ctx(grad, dim, *others):
    here, size = lax.axis_index("ctx"), lax.axis_size("ctx")
    if size != 8:
        return lax.psum_scatter(grad, "ctx", scatter_dimension=dim, tiled=True)

    def cut(array, index, width):
        return lax.dynamic_slice_in_dim(array, index * width, width, dim)

    first, second = (others[:1], others[1:]) if others else ((), ())
    side, level = here % 2, here // 2
    half, piece = grad.shape[dim] // 2, grad.shape[dim] // 8
    got = after(over_ctx(cut(grad, 1 - side, half), 1), *first)
    kept = add_low(cut(grad, side, half), got)
    got = exchange_levels(lambda k: cut(kept, level ^ k, piece))
    got = [after(array, *second) for array in got]
    return add_low(cut(kept, level, piece), *got)


def place_code():
    here = lax.axis_index("ctx")
    return jnp.stack([(here % 2) * 4 + here // 2, lax.axis_index("fsdp")]).astype(jnp.int32)


def deal_fsdp(cut, *others):
    got = [over_fsdp(cut(k), k) for k in (1, 2, 3)]
    return jnp.stack([cut(0)] + [after(array, *others) for array in got])


def spread_rows_kernel(where_ref, *refs):
    parts, outs = refs[:5], refs[5:]
    piece = parts[0].shape[1]
    for i, out_ref in enumerate(outs):

        @pl.when(pl.program_id(0) // (4 // len(outs)) == i)
        def _(out_ref=out_ref):
            for k in range(8):
                part = parts[k][0] if k < 4 else parts[4][k - 4, 0]
                place = pl.multiple_of((where_ref[0] ^ k) * piece, piece)
                out_ref[pl.ds(place, piece), :] = part.astype(wide)


def spread_rows_call(near, far, count):
    _, height, width = near[0].shape
    each = 4 // count

    def place_of(number):
        return lambda i, where: (0, jnp.clip(i - number * each, 0, each - 1))

    return pl.pallas_call(
        spread_rows_kernel,
        grid_spec=pltpu.PrefetchScalarGridSpec(
            num_scalar_prefetch=1,
            grid=(4,),
            in_specs=[pl.BlockSpec((1, height, width), lambda i, where: (where[1] ^ i, 0, 0))] * 4
            + [pl.BlockSpec((4, 1, height, width), lambda i, where: (0, where[1] ^ i, 0, 0))],
            out_specs=[pl.BlockSpec((8 * height, width), place_of(k)) for k in range(count)],
        ),
        out_shape=[jax.ShapeDtypeStruct((8 * height, each * width), wide)] * count,
        cost_estimate=brief,
        name="spread_rows",
    )(place_code(), *near, far)


def dealt_grads(left, right, count, *others):
    size = lax.axis_size("ctx")
    grad = contract_first(left, right).astype(low).reshape(4, left.shape[1] // 4, right.shape[1])
    part = lax.axis_index("fsdp")
    piece = reduce_ctx(grad, 1, *others[:2])
    _, height, width = piece.shape
    mine = deal_fsdp(
        lambda k: lax.dynamic_index_in_dim(piece, part ^ k, 0, keepdims=False), *others[2:3]
    )
    if size != 8:
        whole = lax.all_gather(mine, "ctx", axis=1, tiled=True).astype(wide)
        blocks = [lax.dynamic_index_in_dim(whole, part ^ k, 0, keepdims=False) for k in range(4)]
        each = 4 // count
        whole = [jnp.concatenate(blocks[i * each : (i + 1) * each], axis=1) for i in range(count)]
        return [*whole, grad, piece, piece]
    near = [mine] + [after(array, *others[3:4]) for array in exchange_levels(lambda k: mine)]
    far = after(over_ctx(jnp.stack(near), 1), *others[4:5])
    return [*spread_rows_call(near, far, count), grad, piece, near[-1]]


ring = (0, 2, 4, 6, 7, 5, 3, 1)


def turn_ring(array, step):
    count = len(ring)
    return lax.ppermute(
        array, "ctx", [(ring[i], ring[(i + step) % count]) for i in range(count)]
    )


def deal_kernel(code_ref, *refs):
    count = len(ring)
    outs = refs[2 * count :]
    for lower in range(2):
        for step in range(count):
            part = refs[lower * count + step]
            height = part.shape[1]
            width = part.shape[2] // len(outs)
            place = pl.multiple_of(code_ref[1 + lower * count + step] * width, width)
            for i, out_ref in enumerate(outs):
                out_ref[lower * height : (lower + 1) * height, pl.ds(place, width)] = part[
                    0, :, i * width : (i + 1) * width
                ].astype(wide)


def gather_ring(mine, count):
    here, size, part = lax.axis_index("ctx"), lax.axis_size("ctx"), lax.axis_index("fsdp")
    _, height, span = mine.shape
    width = span // count * size
    if size != 8:
        whole = lax.all_gather(mine, "ctx", axis=0)
        whole = jnp.stack(
            [lax.dynamic_index_in_dim(whole, part ^ k, 1, keepdims=False) for k in range(4)]
        ).reshape(4, size, height, count, span // count)
        whole = whole.transpose(3, 2, 0, 1, 4).reshape(count, height, 4 * width)
        return tuple(whole[i].astype(wide) for i in range(count))
    upper, lower = [mine[:, : height // 2]], [mine[:, height // 2 :]]
    for _ in range(size - 1):
        upper.append(turn_ring(upper[-1], 1))
        lower.append(turn_ring(lower[-1], -1))
    order = jnp.asarray(ring, jnp.int32)
    turn = jnp.argmax(order == here).astype(jnp.int32)
    steps = jnp.arange(size, dtype=jnp.int32)
    code = jnp.concatenate(
        [part.reshape(1), order[(turn - steps) % size], order[(turn + steps) % size]]
    ).astype(jnp.int32)
    half = (1, height // 2, span)
    return pl.pallas_call(
        deal_kernel,
        grid_spec=pltpu.PrefetchScalarGridSpec(
            num_scalar_prefetch=1,
            grid=(4,),
            in_specs=[pl.BlockSpec(half, lambda i, code: (code[0] ^ i, 0, 0))] * (2 * size),
            out_specs=[pl.BlockSpec((height, width), lambda i, code: (0, i))] * count,
        ),
        out_shape=[jax.ShapeDtypeStruct((height, 4 * width), wide)] * count,
        compiler_params=pltpu.CompilerParams(vmem_limit_bytes=56 << 20),
        cost_estimate=brief,
        name="deal_columns",
    )(code, *upper, *lower)


def deal_rows(piece, *others):
    part = lax.axis_index("fsdp")
    return deal_fsdp(lambda k: rows(piece, part ^ k, piece.shape[0] // 4), *others)


def unit_grads_kernel(normed_ref, grad_ref, gate_ref, up_ref, hidden_ref, out_ref, flipped):
    @pl.when(pl.program_id(0) == 0)
    def _():
        flipped[0] = normed_ref[...].T
        flipped[1] = grad_ref[...].T

    piece = hidden_ref.shape[1]
    right = jnp.concatenate([gate_ref[...], up_ref[...]], axis=1)
    out_ref[:, : 2 * piece] = product(flipped[0], right).astype(low)
    out_ref[:, 2 * piece :] = product(flipped[1], hidden_ref[...]).astype(low)


def unit_grads(normed, grad, grad_gate, grad_up, hidden):
    size = lax.axis_size("ctx")
    count, depth = normed.shape
    piece = hidden.shape[1] // size
    rights = (grad_gate, grad_up, hidden)
    if piece % 128:
        cut = [
            contract_first(left, right).astype(low).reshape(depth, size, piece)
            for left, right in zip((normed, normed, grad), rights)
        ]
        return jnp.concatenate(cut, axis=2).transpose(1, 0, 2).reshape(size * depth, 3 * piece)
    whole = pl.BlockSpec(memory_space=pltpu.VMEM)
    return pl.pallas_call(
        unit_grads_kernel,
        grid=(size,),
        in_specs=[whole, whole] + [pl.BlockSpec((count, piece), lambda i: (0, i))] * 3,
        out_specs=pl.BlockSpec((depth, 3 * piece), lambda i: (i, 0)),
        scratch_shapes=[pltpu.VMEM((2, depth, count), low)],
        out_shape=jax.ShapeDtypeStruct((size * depth, 3 * piece), low),
        compiler_params=pltpu.CompilerParams(vmem_limit_bytes=40 << 20),
        cost_estimate=lasting,
        name="unit_grads",
    )(normed, grad, *rights)


def sum_gains(array, *others):
    part, size = lax.axis_index("fsdp"), lax.axis_size("ctx")
    width = array.shape[1] // 4
    array = jnp.sum(deal_fsdp(lambda k: columns(array, part ^ k, width)), axis=0)
    array = array + after(over_ctx(array, 1), others[0])
    if size == 8:
        return array + sum(after(got, others[1]) for got in exchange_levels(lambda k: array))
    bits = 2
    while bits < size:
        array = array + over_ctx(array, bits)
        bits *= 2
    return array


def body(
    hidden_in,
    out_grad,
    positions,
    attn_gain,
    w_query,
    w_key,
    w_value,
    w_out,
    ffn_gain,
    w_gate,
    w_up,
    w_down,
):
    part, here, size = lax.axis_index("fsdp"), lax.axis_index("ctx"), lax.axis_size("ctx")
    code = jnp.stack([part, here % 2, here // 2 % 2]).astype(jnp.int32)
    own_gains = jnp.stack([attn_gain, ffn_gain])
    gains = [own_gains] + [over_fsdp(own_gains, k) for k in (1, 2, 3)]
    rows_in, grad_down = hidden_in[0], out_grad[0]
    row_count = rows_in.shape[0]
    all_places = positions[0]
    own_places = lax.dynamic_slice_in_dim(all_places, here * row_count, row_count, 0)
    cosine, sine = angles_of(own_places)
    cosine = jnp.concatenate([cosine[:, 0], cosine[:, 0]], axis=1)
    sine = jnp.concatenate([-sine[:, 0], sine[:, 0]], axis=1)

    heads = gather_thirds(jnp.concatenate([w_query, w_key, w_value], axis=1))
    normed_one, load = heads_call(code, rows_in, cosine, sine, gains, heads)
    outward = gather_halves(w_out)
    own, near, far, both = deal_weights((w_gate, w_up, w_down))
    load, near, far, both, _ = lax.optimization_barrier((load, near, far, both, outward[2]))
    far, both = over_fsdp(far, 2), over_fsdp(both, 3)
    near = over_fsdp(near, 1)
    far_other, both_other = over_ctx(far, 1), over_ctx(both, 2)
    grad_all = gather_fsdp(grad_down)

    if size == HK:
        load = lax.all_to_all(load, "ctx", 0, 0, tiled=True)
        order = all_places[::BLK] // BLK
        mixed = attention_forward(order, load)
        mixed = lax.all_to_all(after(mixed, far, outward[3]), "ctx", 0, 0, tiled=True)
    else:
        query_rot = load[:, :, : GROUP * HD].transpose(1, 0, 2)
        query_rot = query_rot.reshape(row_count, HK, GROUP, HD)
        keys_values = load[:, :, GROUP * HD :].transpose(1, 0, 2)
        keys_values = lax.all_gather(keys_values, "ctx", axis=0, tiled=True)
        keys_all, values_all = keys_values[:, :, :HD], keys_values[:, :, HD:]
        mixed_exact, log_total = rows_forward(
            query_rot, keys_all, values_all, own_places, all_places
        )
        mixed = mixed_exact.reshape(row_count, HK, GROUP * HD).transpose(1, 0, 2).astype(low)

    dealt = (own, near, far, far_other, both, both_other)
    mixed_low, middle, normed_two = middle_call(
        code, rows_in, after(mixed, both, far_other, grad_all), gains, outward
    )
    normed_all = gather_fsdp(normed_two, both_other)
    out_terms, back_terms, hidden, grad_gate, grad_up = units_call(
        code, normed_all, grad_all, dealt
    )
    grad_normed_two, passed = scatter_fsdp(back_terms)
    unit_terms = unit_grads(normed_all, grad_all, after(grad_gate, passed), grad_up, hidden)
    grad_normed_two, unit_terms = lax.optimization_barrier((grad_normed_two, unit_terms))
    grad_middle, grad_branch, grad_mixed, grad_gain_two = middle_back_call(
        code, middle, grad_normed_two, grad_down, gains, outward
    )
    unit_sums = lax.psum_scatter(unit_terms, "ctx", scatter_dimension=0, tiled=True)

    if size == HK:
        grad_mixed = lax.all_to_all(grad_mixed, "ctx", 0, 0, tiled=True)
        grad_load = attention_backward(order, load, grad_mixed)
        mid = grad_load
        grad_load = lax.all_to_all(grad_load, "ctx", 0, 0, tiled=True)
    else:
        grad_mixed = grad_mixed.transpose(1, 0, 2).reshape(row_count, HK, GROUP, HD)
        delta = jnp.sum(grad_mixed.astype(wide) * mixed_exact, axis=-1)
        grad_query, grad_keys, grad_values = rows_backward(
            query_rot, keys_all, values_all, own_places, all_places, log_total, delta, grad_mixed
        )
        grad_keys, grad_values = (
            lax.psum_scatter(whole.astype(low), "ctx", scatter_dimension=0, tiled=True)
            for whole in (grad_keys, grad_values)
        )
        grad_load = jnp.concatenate(
            [
                grad_query.reshape(row_count, HK, GROUP * HD).astype(low),
                grad_keys.reshape(row_count, HK, HD),
                grad_values.reshape(row_count, HK, HD),
            ],
            axis=2,
        ).transpose(1, 0, 2)
        mid = grad_load

    grad_raw, input_grad, grad_gain_one = heads_back_call(
        code, grad_load, rows_in, grad_middle, cosine, sine, gains, heads
    )
    early, late = grad_branch, input_grad
    result, _ = scatter_fsdp(after(out_terms, grad_normed_two), mid)
    result = (middle + result).astype(low)
    quarter = HQ * HD // 4
    turn = (0, 2, 1, 3)

    def own_columns(cut, *others):
        dealt = deal_fsdp(cut, *others)
        return jnp.concatenate([dealt[k] for k in turn], axis=0)

    branch_all = gather_fsdp(grad_branch, mid)
    mixed_part = own_columns(lambda k: columns(mixed_low, part ^ k, quarter), mid)
    normed_one_all = gather_fsdp(after(normed_one, early), mid)
    out_weight_grad, *_ = dealt_grads(branch_all, mixed_part, 1, mid, late, late, late, late)

    def raw_part(i):
        return own_columns(
            lambda k: lax.dynamic_index_in_dim(grad_raw[i], part ^ k, 0, keepdims=False)
        )

    query_grad, first_terms, summed, last = dealt_grads(normed_one_all, raw_part(0), 1)
    key_grad, value_grad, second_terms, *_ = dealt_grads(normed_one_all, raw_part(1), 2)
    unit_sums = after(unit_sums, first_terms, second_terms)
    gate_grad, up_grad, down_grad = gather_ring(deal_rows(unit_sums), 3)
    gain_grads = sum_gains(
        jnp.concatenate([grad_gain_one, grad_gain_two], axis=0), summed, last
    )
    return (
        result[None],
        input_grad[None],
        gain_grads[0],
        query_grad,
        key_grad,
        value_grad,
        out_weight_grad,
        gain_grads[1],
        gate_grad,
        up_grad,
        down_grad,
    )


def solution(mesh):
    matrix = P("fsdp", None)
    stream = P("fsdp", "ctx", None)
    return jax.shard_map(
        body,
        mesh=mesh,
        in_specs=(stream, stream, matrix, P("fsdp"))
        + (matrix,) * 4
        + (P("fsdp"),)
        + (matrix,) * 3,
        out_specs=(stream, stream, P("fsdp")) + (matrix,) * 4 + (P("fsdp"),) + (matrix,) * 3,
        check_vma=False,
    )
```

time: 1040 us -> 746 us (0.72)
  starting transfers between devices: 251 us -> 125 us
  blocking collectives: 88.7 us -> 0 us
  matrix products: 79 us -> 8.62 us
  waiting for transfers between devices: 419 us -> 353 us
  Pallas kernels: 103 us -> 149 us
  between operations: 2.53 us -> 15.3 us
    ppermute x131 -> x84, starting transfers between devices: 231 us -> 89 us  [swap(): return lax.ppermute(array, axis, [(i, i ^ bits) for i in range(size)])]
    ppermute x131 -> x84, waiting for transfers between devices: 384 us -> 245 us  [swap(): return lax.ppermute(array, axis, [(i, i ^ bits) for i in range(size)])]
    dot_general x14 -> x0, matrix products: 51.5 us -> none  [the longest x7 32.1 us: product(): return jnp.dot(left, right, preferred_element_type=wide)]
    all_gather x1 -> x0, blocking collectives: 49.4 us -> none  [body(): lax.all_gather(jnp.stack([attn_gain, ffn_gain]), 'fsdp', axis=1, tiled=True)]
    pallas_call x14 -> x10, Pallas kernels: 66.5 us -> 112 us  [the longest x4 39.4 us: whole_call(): pl.pallas_call(kernel, grid_spec=pltpu.PrefetchScalarGridSpec(num_scalar_...]
    all_to_all x1, waiting for transfers between devices: 0.01 us -> 39.3 us  [body(): grad_mixed = lax.all_to_all(grad_mixed, 'ctx', 0, 0, tiled=True)]
    psum x1 -> x0, blocking collectives: 39.2 us -> none  [body(): lax.psum(jnp.stack([grad_gain_one, grad_gain_two]), ('ctx', 'fsdp'))]
    reduce_scatter x0 -> x1, waiting for transfers between devices: none -> 32.9 us  [body(): lax.psum_scatter(unit_terms, 'ctx', scatter_dimension=0, tiled=True)]
  transfers between devices with their start and end apart: 135 -> 103, of which waited for: 33 -> 41; matrix products, arithmetic and copies ran while one was open for 10% -> 10% of each run, Pallas kernels for 9% -> 15%
where the time goes in v2:
time: 746 us; the launch traced here: 738 us
  waiting for transfers between devices  353 us (47%)
  Pallas kernels  149 us (20%)
  starting transfers between devices  125 us (17%)
  local copies, waits for them, and re-layouts  45 us (6%)
  other arithmetic  42.8 us (6%)
  between operations  15.3 us (2%)
  matrix products  8.62 us (1%)
    ppermute x84, waiting for transfers between devices, swap(): return lax.ppermute(array, axis, [(i, i ^ bits) for i in range(size)])  245 us
    ppermute x84, starting transfers between devices, swap(): return lax.ppermute(array, axis, [(i, i ^ bits) for i in range(size)])  89 us
    pallas_call x4, Pallas kernels, whole_call(): pl.pallas_call(kernel, grid_spec=pltpu.PrefetchScalarGridSpec(num_scalar_...  39.4 us
    all_to_all x1, waiting for transfers between devices, body(): grad_mixed = lax.all_to_all(grad_mixed, 'ctx', 0, 0, tiled=True)  39.3 us
    pallas_call x2, Pallas kernels, attention_call(): pl.pallas_call(kernel, grid_spec=pltpu.PrefetchScalarGridSpec(num_scalar_...  36.4 us
    reduce_scatter x1, waiting for transfers between devices, body(): lax.psum_scatter(unit_terms, 'ctx', scatter_dimension=0, tiled=True)  32.9 us
    pallas_call x1, Pallas kernels, units_call(): pl.pallas_call(units_kernel, grid_spec=pltpu.PrefetchScalarGridSpec(num_s...  28.1 us
    pallas_call x1, Pallas kernels, unit_grads(): pl.pallas_call(unit_grads_kernel, grid=(size,), in_specs=[whole, whole] +...  19.2 us
  transfers between devices with their start and end apart: 103, of which 41 were waited for; matrix products, arithmetic and copies ran while one was open for 10% of the time, Pallas kernels for 15%

profile of v2, /device:TPU:0, one launch (start us, length us, event | category | flops | bytes accessed | tf_op | source)
XLA Modules:
  0.0 738.4 jit_solution(5413583917930056232)
XLA Ops:
  10.0 2.9 collective-permute-start.4
  15.5 15.3 %collective-permute-done.4.refs_6_ = bf16[384,1024]{1,0:T(8,128)(2,1)} collective-permute-done((bf16[384,1024]{1,0:T(8,128)(2,1)}, bf16[384,1024]{1,0:T(8,128)(2,1)}, u32[]{:S(2)}, u32[]{:S(2)}) %collective-permute-start.4) | collective-permute-done | bytes 786464 | tf_op jit(solution)/shard_map/ppermute | solution.py:45
  39.4 11.6 %collective-permute-done.5.refs_7_ = bf16[384,1024]{1,0:T(8,128)(2,1)} collective-permute-done((bf16[384,1024]{1,0:T(8,128)(2,1)}, bf16[384,1024]{1,0:T(8,128)(2,1)}, u32[]{:S(2)}, u32[]{:S(2)}) %collective-permute-start.5) | collective-permute-done | bytes 786464 | tf_op jit(solution)/shard_map/ppermute | solution.py:45
  56.9 2.4 collective-permute-done.2.refs_3_
  60.0 3.4 dynamic-slice_bitcast_fusion
  65.1 11.5 %query_key_value.1 = (bf16[256,1536]{1,0:T(8,128)(2,1)}, bf16[8,256,384]{2,1,0:T(8,128)(2,1)}) custom-call(s32[3]{0:T(128)} %pad_add_fusion.code_ref, bf16[256,1536]{1,0:T(8,128)(2,1)} %bitcast.111, f32[256,96]{1,0:T(8,128)} %get-tuple-element.196.cosine_ref, f32[256,96]{1,0:T(8,128)} %get-tuple-element.197.sine_ref, bf16[2,384]{1,0:T(2,128)(2,1)} %copy-done.50, ...), custom_call_target="tpu_custom_call" | custom-call | flops 2415919104 | bytes 12785664 | tf_op jit(solution)/shard_map/query_key_value/pallas_call | solution.py:149
  77.4 6.1 all-to-all-start
  85.7 18.4 %collective-permute-done.15 = bf16[256,1536]{1,0:T(8,128)(2,1)S(1)} collective-permute-done((bf16[256,1536]{1,0:T(8,128)(2,1)S(1)}, bf16[256,1536]{1,0:T(8,128)(2,1)S(1)}, u32[]{:S(2)}, u32[]{:S(2)}) %collective-permute-start.15) | collective-permute-done | bytes 786464 | tf_op jit(solution)/shard_map/ppermute | solution.py:45
  110.3 10.4 %all-to-all-done.load_ref = bf16[8,256,384]{2,1,0:T(8,128)(2,1)} async-done(((bf16[8,256,384]{2,1,0:T(8,128)(2,1)}), bf16[8,256,384]{2,1,0:T(8,128)(2,1)}, u32[]{:S(2)}, u32[]{:S(2)}) %all-to-all-start) | async-done | bytes 1572896 | tf_op jit(solution)/shard_map/all_to_all | solution.py:905
  120.7 12.3 %attention_forward.1 = bf16[8,256,192]{2,1,0:T(8,128)(2,1)} custom-call(s32[16]{0:T(128)} %and_select_fusion.2.order_ref, bf16[8,256,384]{2,1,0:T(8,128)(2,1)} %all-to-all-done.load_ref), custom_call_target="tpu_custom_call" | custom-call | flops 4294967296 | bytes 3145728 | tf_op jit(solution)/shard_map/attention_forward/pallas_call | solution.py:537
  133.0 2.4 copy.24
  135.4 4.2 all-to-all-start.1
  142.6 9.3 %collective-permute-done.13.refs_4_ = bf16[3,384,512]{2,1,0:T(8,128)(2,1)} collective-permute-done((bf16[3,384,512]{2,1,0:T(8,128)(2,1)}, bf16[3,384,512]{2,1,0:T(8,128)(2,1)}, u32[]{:S(2)}, u32[]{:S(2)}) %collective-permute-start.13) | collective-permute-done | bytes 1179680 | tf_op jit(solution)/shard_map/ppermute | solution.py:45
  153.3 3.5 pad_maximum_fusion.grad_ref
  156.7 18.6 %collective-permute-done.14.refs_3_ = bf16[3,384,512]{2,1,0:T(8,128)(2,1)} collective-permute-done((bf16[3,384,512]{2,1,0:T(8,128)(2,1)}, bf16[3,384,512]{2,1,0:T(8,128)(2,1)}, u32[]{:S(2)}, u32[]{:S(2)}) %collective-permute-start.14) | collective-permute-done | bytes 1179680 | tf_op jit(solution)/shard_map/ppermute | solution.py:45
  178.6 6.8 attention_output.1
  185.8 17.7 %collective-permute-done.20 = bf16[256,1536]{1,0:T(8,128)(2,1)S(1)} collective-permute-done((bf16[256,1536]{1,0:T(8,128)(2,1)}, bf16[256,1536]{1,0:T(8,128)(2,1)S(1)}, u32[]{:S(2)}, u32[]{:S(2)}) %collective-permute-start.20) | collective-permute-done | bytes 786464 | tf_op jit(solution)/shard_map/ppermute | solution.py:45
  210.0 28.1 %feed_forward.1 = (bf16[1024,1536]{1,0:T(8,128)(2,1)}, bf16[1024,1536]{1,0:T(8,128)(2,1)}, bf16[1024,1024]{1,0:T(8,128)(2,1)}, bf16[1024,1024]{1,0:T(8,128)(2,1)}, bf16[1024,1024]{1,0:T(8,128)(2,1)}) custom-call(s32[3]{0:T(128)} %pad_add_fusion.code_ref, bf16[1024,1536]{1,0:T(8,128)(2,1)} %copy-done.1, bf16[1024,1536]{1,0:T(8,128)(2,1)} %pad_maximum_fusion.grad_ref, ...), custom_call_target="tpu_custom_call" | custom-call | flops 19327352832 | bytes 22020096 | tf_op jit(solution)/shard_map/feed_forward/pallas_call | solution.py:383
  240.0 3.3 collective-permute-done.24
  250.0 19.2 %unit_grads.1 = bf16[12288,384]{1,0:T(8,128)(2,1)} custom-call(bf16[1024,1536]{1,0:T(8,128)(2,1)S(1)} %copy-done.2, bf16[1024,1536]{1,0:T(8,128)(2,1)S(1)} %copy-done, bf16[1024,1024]{1,0:T(8,128)(2,1)S(1)} %copy-done.4, bf16[1024,1024]{1,0:T(8,128)(2,1)S(1)} %copy-done.5, bf16[1024,1024]{1,0:T(8,128)(2,1)S(1)} %copy-done.3), custom_call_target="tpu_custom_call" | custom-call | flops 99999997952 | tf_op jit(solution)/shard_map/unit_grads/pallas_call | solution.py:841
  269.2 2.6 convert_add_fusion.grad_ref
  271.9 7.8 %attention_output_back.1 = (f32[256,1536]{1,0:T(8,128)}, bf16[256,1536]{1,0:T(8,128)(2,1)}, bf16[8,256,192]{2,1,0:T(8,128)(2,1)}, f32[1,1536]{1,0:T(1,128)}) custom-call(s32[3]{0:T(128)} %pad_add_fusion.code_ref, f32[256,1536]{1,0:T(8,128)} %get-tuple-element.76.middle_ref, f32[256,1536]{1,0:T(8,128)} %convert_add_fusion.grad_ref, ...), custom_call_target="tpu_custom_call" | custom-call | flops 1207959552 | bytes 11808768 | tf_op jit(solution)/shard_map/attention_output_back/pallas_call | solution.py:149
  279.7 2.3 copy.26
  282.0 6.0 all-to-all-start.2
  289.8 39.3 %all-to-all-done.2 = bf16[8,256,192]{1,2,0:T(8,128)(2,1)S(1)} async-done(((bf16[8,256,192]{1,2,0:T(8,128)(2,1)}), bf16[8,256,192]{1,2,0:T(8,128)(2,1)S(1)}, u32[]{:S(2)}, u32[]{:S(2)}) %all-to-all-start.2) | async-done | bytes 786464 | tf_op jit(solution)/shard_map/all_to_all | solution.py:937
  330.4 24.0 %attention_backward.1 = bf16[8,256,384]{2,1,0:T(8,128)(2,1)} custom-call(s32[16]{0:T(128)} %and_select_fusion.2.order_ref, bf16[8,256,384]{2,1,0:T(8,128)(2,1)} %all-to-all-done.load_ref, bf16[8,256,192]{2,1,0:T(8,128)(2,1)} %copy.27.grad_ref), custom_call_target="tpu_custom_call" | custom-call | flops 10737418240 | bytes 6291456 | tf_op jit(solution)/shard_map/attention_backward/pallas_call | solution.py:537
  354.5 3.7 all-to-all-start.3
  358.2 2.8 pad_maximum_fusion.6
  367.2 14.2 %collective-permute-done.32 = bf16[256,1536]{1,0:T(8,128)(2,1)S(1)} collective-permute-done((bf16[256,1536]{1,0:T(8,128)(2,1)S(1)}, bf16[256,1536]{1,0:T(8,128)(2,1)S(1)}, u32[]{:S(2)}, u32[]{:S(2)}) %collective-permute-start.32) | collective-permute-done | bytes 786464 | tf_op jit(solution)/shard_map/ppermute | solution.py:45
  385.4 4.1 collective-permute-done.67
  389.5 3.7 fusion.6
  396.1 14.2 %all-to-all-done.3.load_ref = bf16[8,256,384]{2,1,0:T(8,128)(2,1)S(1)} async-done(((bf16[8,256,384]{2,1,0:T(8,128)(2,1)}), bf16[8,256,384]{2,1,0:T(8,128)(2,1)S(1)}, u32[]{:S(2)}, u32[]{:S(2)}) %all-to-all-start.3) | async-done | bytes 1572896 | tf_op jit(solution)/shard_map/all_to_all | solution.py:940
  411.5 13.3 %query_key_value_back.1 = (bf16[2,4,256,384]{3,2,1,0:T(8,128)(2,1)}, f32[256,1536]{1,0:T(8,128)}, f32[1,1536]{1,0:T(1,128)}) custom-call(s32[3]{0:T(128)} %pad_add_fusion.code_ref, bf16[8,256,384]{2,1,0:T(8,128)(2,1)} %copy-done.11, bf16[256,1536]{1,0:T(8,128)(2,1)} %bitcast.113, f32[256,1536]{1,0:T(8,128)} %get-tuple-element.90.grad_middle_ref, ...), custom_call_target="tpu_custom_call" | custom-call | flops 2415919104 | bytes 16723968 | tf_op jit(solution)/shard_map/query_key_value_back/pallas_call | solution.py:149
  430.6 2.9 collective-permute-done.36
  438.4 3.5 collective-permute-done.53
  442.0 4.6 collective-permute-done.51
  446.5 2.9 convolution_convert_fusion.1
  451.5 32.9 %reduce-scatter.2.cloned.1.call-done = bf16[1536,384]{1,0:T(8,128)(2,1)} async-done(((bf16[12288,384]{1,0:T(8,128)(2,1)}), bf16[1536,384]{1,0:T(8,128)(2,1)}) %reduce-scatter.2.cloned.1.call-update) | async-done | bytes 1179664 | tf_op jit(solution)/shard_map/reduce_scatter | solution.py:934
  489.4 5.8 collective-permute-done.83
  496.8 4.8 collective-permute-done.82
  508.6 9.3 %collective-permute-done.37 = bf16[4,192,384]{2,1,0:T(8,128)(2,1)S(1)} collective-permute-done((bf16[4,192,384]{2,1,0:T(8,128)(2,1)S(1)}, bf16[4,192,384]{2,1,0:T(8,128)(2,1)S(1)}, u32[]{:S(2)}, u32[]{:S(2)}) %collective-permute-start.37) | collective-permute-done | bytes 589856 | tf_op jit(solution)/shard_map/ppermute | solution.py:45
  520.7 9.9 %collective-permute-done.84.refs_1_ = bf16[4,192,384]{2,1,0:T(8,128)(2,1)S(1)} collective-permute-done((bf16[4,192,384]{2,1,0:T(8,128)(2,1)S(1)}, bf16[4,192,384]{2,1,0:T(8,128)(2,1)S(1)}, u32[]{:S(2)}, u32[]{:S(2)}) %collective-permute-start.84) | collective-permute-done | bytes 589856 | tf_op jit(solution)/shard_map/ppermute | solution.py:755
  534.1 2.3 collective-permute-start.40
  536.6 6.7 collective-permute-done.54
  543.3 8.9 %collective-permute-done.40 = bf16[4,48,384]{2,1,0:T(8,128)(2,1)S(1)} collective-permute-done((bf16[4,48,384]{2,1,0:T(8,128)(2,1)S(1)}, bf16[4,48,384]{2,1,0:T(8,128)(2,1)S(1)}, u32[]{:S(2)}, u32[]{:S(2)}) %collective-permute-start.40) | collective-permute-done | bytes 147488 | tf_op jit(solution)/shard_map/ppermute | solution.py:45
  552.2 3.3 collective-permute-start.38
  557.8 2.2 collective-permute-done.38
  567.2 14.4 %collective-permute-done.77.refs_1_ = bf16[4,48,384]{2,1,0:T(8,128)(2,1)S(1)} collective-permute-done((bf16[4,48,384]{2,1,0:T(8,128)(2,1)S(1)}, bf16[4,48,384]{2,1,0:T(8,128)(2,1)S(1)}, u32[]{:S(2)}, u32[]{:S(2)}) %collective-permute-start.77) | collective-permute-done | bytes 147488 | tf_op jit(solution)/shard_map/ppermute | solution.py:45
  583.8 2.2 add_convert_fusion.1
  588.8 18.3 %collective-permute-done.43 = bf16[48,384]{1,0:T(8,128)(2,1)S(1)} collective-permute-done((bf16[48,384]{1,0:T(8,128)(2,1)}, bf16[48,384]{1,0:T(8,128)(2,1)S(1)}, u32[]{:S(2)}, u32[]{:S(2)}) %collective-permute-start.43) | collective-permute-done | bytes 36896 | tf_op jit(solution)/shard_map/ppermute | solution.py:45
  608.6 3.0 collective-permute-start.79
  614.8 6.3 collective-permute-done.78.refs_2_
  628.5 2.6 collective-permute-start.48
  631.8 2.9 collective-permute-start.49
  635.5 11.6 %collective-permute-start.61 = (bf16[4,48,384]{2,1,0:T(8,128)(2,1)}, bf16[4,48,384]{2,1,0:T(8,128)(2,1)}, u32[]{:S(2)}, u32[]{:S(2)}) collective-permute-start(bf16[4,48,384]{2,1,0:T(8,128)(2,1)} %get-tuple-element.177.refs_0_), channel_id=1, source_target_pairs={{0,8},{4,12},{8,0},{12,4},{16,24},{20,28},{24,16},{28,20},{1,9},{5... | collective-permute-start | bytes 442376 | tf_op jit(solution)/shard_map/ppermute | solution.py:45
  656.6 18.5 %collective-permute-done.62.refs_2_ = bf16[4,48,384]{2,1,0:T(8,128)(2,1)} collective-permute-done((bf16[4,48,384]{2,1,0:T(8,128)(2,1)}, bf16[4,48,384]{2,1,0:T(8,128)(2,1)}, u32[]{:S(2)}, u32[]{:S(2)}) %collective-permute-start.62) | collective-permute-done | bytes 147488 | tf_op jit(solution)/shard_map/ppermute | solution.py:45
  681.2 2.2 collective-permute-start.46
  687.5 2.4 fusion.9
  690.0 4.5 spread_rows.5
  695.0 5.0 collective-permute-done.50.refs_4_
  700.0 4.5 spread_rows.3
  704.5 8.2 %collective-permute-done.64.refs_4_ = bf16[4,4,48,384]{3,2,1,0:T(8,128)(2,1)} collective-permute-done((bf16[4,4,48,384]{3,2,1,0:T(8,128)(2,1)}, bf16[4,4,48,384]{3,2,1,0:T(8,128)(2,1)}, u32[]{:S(2)}, u32[]{:S(2)}) %collective-permute-start.64) | collective-permute-done | bytes 589856 | tf_op jit(solution)/shard_map/ppermute | solution.py:45
  712.7 4.7 spread_rows.4
  719.1 12.2 %deal_columns.1 = (f32[384,4096]{1,0:T(8,128)}, f32[384,4096]{1,0:T(8,128)}, f32[384,4096]{1,0:T(8,128)}) custom-call(s32[17]{0:T(128)} %pad_add_fusion.2.code_ref, bf16[4,192,384]{2,1,0:T(8,128)(2,1)} %copy-done.22, bf16[4,192,384]{2,1,0:T(8,128)(2,1)} %copy-done.37, bf16[4,192,384]{2,1,0:T(8,128)(2,1)} %copy-done.39, ...), custom_call_target="tpu_custom_call" | custom-call | tf_op jit(solution)/shard_map/deal_columns/pallas_call | solution.py:797
  (368 shorter events, 154.0 us)
Async XLA Ops:
  10.0 20.8 %collective-permute-start.4 = (bf16[384,1024]{1,0:T(8,128)(2,1)}, bf16[384,1024]{1,0:T(8,128)(2,1)}, u32[]{:S(2)}, u32[]{:S(2)}) collective-permute-start(bf16[384,1024]{1,0:T(8,128)(2,1)} %constant_dynamic-slice_fusion.31), channel_id=1, source_target_pairs={{0,2},{1,3},{2,0},{3,1},{4,6},{5,7},{6,4},{7,5},{8,10},{9,11},{10,... | collective-permute-start | bytes 2359304 | tf_op jit(solution)/shard_map/ppermute | solution.py:45
  12.9 52.1 %collective-permute-start.3 = (bf16[384,3072]{1,0:T(8,128)(2,1)S(1)}, bf16[384,3072]{1,0:T(8,128)(2,1)}, u32[]{:S(2)}, u32[]{:S(2)}) collective-permute-start(bf16[384,3072]{1,0:T(8,128)(2,1)S(1)} %constant_dynamic-update-slice_fusion.refs_4_), channel_id=1, source_target_pairs={{0,1},{1,0},{2,3},{3,2},{4,5},{5,4},{6,7},{7,6},{8,9},{9,8},{10,11... | collective-permute-start | bytes 7077896 | tf_op jit(solution)/shard_map/ppermute | solution.py:45
  13.0 39.7 %collective-permute-start = (bf16[2,384]{1,0:T(2,128)(2,1)S(1)}, bf16[2,384]{1,0:T(2,128)(2,1)S(1)}, u32[]{:S(2)}, u32[]{:S(2)}) collective-permute-start(bf16[2,384]{1,0:T(2,128)(2,1)S(1)} %pad_maximum_fusion.19.refs_0_), channel_id=1, source_target_pairs={{0,1},{1,0},{2,3},{3,2},{4,5},{5,4},{6,7},{7,6},{8,9},{9,8},{10,11... | collective-permute-start | bytes 4616 | tf_op jit(solution)/shard_map/ppermute | solution.py:45
  30.8 20.2 %collective-permute-start.6 = (bf16[384,1024]{1,0:T(8,128)(2,1)S(1)}, bf16[384,1024]{1,0:T(8,128)(2,1)}, u32[]{:S(2)}, u32[]{:S(2)}) collective-permute-start(bf16[384,1024]{1,0:T(8,128)(2,1)S(1)} %pad_maximum_fusion.10), channel_id=1, source_target_pairs={{0,2},{1,3},{2,0},{3,1},{4,6},{5,7},{6,4},{7,5},{8,10},{9,11},{10,... | collective-permute-start | bytes 2359304 | tf_op jit(solution)/shard_map/ppermute | solution.py:45
  32.5 18.4 %collective-permute-start.5 = (bf16[384,1024]{1,0:T(8,128)(2,1)}, bf16[384,1024]{1,0:T(8,128)(2,1)}, u32[]{:S(2)}, u32[]{:S(2)}) collective-permute-start(bf16[384,1024]{1,0:T(8,128)(2,1)} %collective-permute-done.4.refs_6_), channel_id=1, source_target_pairs={{0,4},{4,0},{8,12},{12,8},{16,20},{20,16},{24,28},{28,24},{1,5},{5... | collective-permute-start | bytes 2359304 | tf_op jit(solution)/shard_map/ppermute | solution.py:45
  39.4 25.6 %collective-permute-start.7 = (bf16[384,1024]{1,0:T(8,128)(2,1)}, bf16[384,1024]{1,0:T(8,128)(2,1)}, u32[]{:S(2)}, u32[]{:S(2)}) collective-permute-start(bf16[384,1024]{1,0:T(8,128)(2,1)} %collective-permute-done.4.refs_6_), channel_id=1, source_target_pairs={{0,1},{1,0},{2,3},{3,2},{4,5},{5,4},{6,7},{7,6},{8,9},{9,8},{10,11... | collective-permute-start | bytes 2359304 | tf_op jit(solution)/shard_map/ppermute | solution.py:45
  59.4 17.2 %collective-permute-start.10 = (bf16[384,768]{1,0:T(8,128)(2,1)S(1)}, bf16[384,768]{1,0:T(8,128)(2,1)S(1)}, u32[]{:S(2)}, u32[]{:S(2)}) collective-permute-start(bf16[384,768]{1,0:T(8,128)(2,1)S(1)} %constant_dynamic-slice_fusion.30), channel_id=1, source_target_pairs={{0,2},{1,3},{2,0},{3,1},{4,6},{5,7},{6,4},{7,5},{8,10},{9,11},{10,... | collective-permute-start | bytes 1769480 | tf_op jit(solution)/shard_map/ppermute | solution.py:45
  77.4 43.3 %all-to-all-start = ((bf16[8,256,384]{2,1,0:T(8,128)(2,1)}), bf16[8,256,384]{2,1,0:T(8,128)(2,1)}, u32[]{:S(2)}, u32[]{:S(2)}) async-start(bf16[8,256,384]{2,1,0:T(8,128)(2,1)} %get-tuple-element.71), calls=%async_computation | async-start | bytes 3145728 | tf_op jit(solution)/shard_map/all_to_all | solution.py:905
  83.6 20.5 %collective-permute-start.15 = (bf16[256,1536]{1,0:T(8,128)(2,1)S(1)}, bf16[256,1536]{1,0:T(8,128)(2,1)S(1)}, u32[]{:S(2)}, u32[]{:S(2)}) collective-permute-start(bf16[256,1536]{1,0:T(8,128)(2,1)S(1)} %bitcast.108), channel_id=1, source_target_pairs={{0,2},{1,3},{2,0},{3,1},{4,6},{5,7},{6,4},{7,5},{8,10},{9,11},{10,... | collective-permute-start | bytes 2359304 | tf_op jit(solution)/shard_map/ppermute | solution.py:45
  85.1 47.9 %collective-permute-start.11 = (bf16[3,384,512]{2,1,0:T(8,128)(2,1)}, bf16[3,384,512]{2,1,0:T(8,128)(2,1)}, u32[]{:S(2)}, u32[]{:S(2)}) collective-permute-start(bf16[3,384,512]{2,1,0:T(8,128)(2,1)} %pad_maximum_fusion.7), channel_id=1, source_target_pairs={{0,2},{1,3},{2,0},{3,1},{4,6},{5,7},{6,4},{7,5},{8,10},{9,11},{10,... | collective-permute-start | bytes 3538952 | tf_op jit(solution)/shard_map/ppermute | solution.py:45
  105.5 37.1 %collective-permute-start.16 = (bf16[512,1536]{1,0:T(8,128)(2,1)}, bf16[512,1536]{1,0:T(8,128)(2,1)}, u32[]{:S(2)}, u32[]{:S(2)}) collective-permute-start(bf16[512,1536]{1,0:T(8,128)(2,1)} %pad_maximum_fusion.3), channel_id=1, source_target_pairs={{0,1},{1,0},{2,3},{3,2},{4,5},{5,4},{6,7},{7,6},{8,9},{9,8},{10,11... | collective-permute-start | bytes 4718600 | tf_op jit(solution)/shard_map/ppermute | solution.py:45
  106.3 26.7 %collective-permute-start.12 = (bf16[384,768]{1,0:T(8,128)(2,1)S(1)}, bf16[384,768]{1,0:T(8,128)(2,1)S(1)}, u32[]{:S(2)}, u32[]{:S(2)}) collective-permute-start(bf16[384,768]{1,0:T(8,128)(2,1)S(1)} %copy-done.24), channel_id=1, source_target_pairs={{0,8},{4,12},{8,0},{12,4},{16,24},{20,28},{24,16},{28,20},{1,9},{5... | collective-permute-start | bytes 1769480 | tf_op jit(solution)/shard_map/ppermute | solution.py:45
  109.0 42.9 %collective-permute-start.13 = (bf16[3,384,512]{2,1,0:T(8,128)(2,1)}, bf16[3,384,512]{2,1,0:T(8,128)(2,1)}, u32[]{:S(2)}, u32[]{:S(2)}) collective-permute-start(bf16[3,384,512]{2,1,0:T(8,128)(2,1)} %pad_maximum_fusion.8), channel_id=1, source_target_pairs={{0,3},{1,2},{2,1},{3,0},{4,7},{5,6},{6,5},{7,4},{8,11},{9,10},{10,... | collective-permute-start | bytes 3538952 | tf_op jit(solution)/shard_map/ppermute | solution.py:45
  135.4 39.9 %all-to-all-start.1 = ((bf16[8,256,192]{1,2,0:T(8,128)(2,1)}), bf16[8,256,192]{1,2,0:T(8,128)(2,1)}, u32[]{:S(2)}, u32[]{:S(2)}) async-start(bf16[8,256,192]{1,2,0:T(8,128)(2,1)} %copy.24), calls=%async_computation.1 | async-start | bytes 1572864 | tf_op jit(solution)/shard_map/all_to_all | solution.py:908
  139.7 344.7 %reduce-scatter.2.cloned.1.call-start = ((), (), s32[]{:S(2)}) async-start(), calls=%async_computation.5 | async-start | bytes 10616832 | tf_op jit(solution)/shard_map/reduce_scatter | solution.py:934
  140.1 35.3 %collective-permute-start.14 = (bf16[3,384,512]{2,1,0:T(8,128)(2,1)}, bf16[3,384,512]{2,1,0:T(8,128)(2,1)}, u32[]{:S(2)}, u32[]{:S(2)}) collective-permute-start(bf16[3,384,512]{2,1,0:T(8,128)(2,1)} %collective-permute-done.11.refs_2_), channel_id=1, source_target_pairs={{0,4},{4,0},{8,12},{12,8},{16,20},{20,16},{24,28},{28,24},{1,5},{5... | collective-permute-start | bytes 3538952 | tf_op jit(solution)/shard_map/ppermute | solution.py:45
  142.0 35.6 %collective-permute-start.17 = (bf16[384,1536]{1,0:T(8,128)(2,1)S(1)}, bf16[384,1536]{1,0:T(8,128)(2,1)S(1)}, u32[]{:S(2)}, u32[]{:S(2)}) collective-permute-start(bf16[384,1536]{1,0:T(8,128)(2,1)S(1)} %copy-done.8), channel_id=1, source_target_pairs={{0,1},{1,0},{2,3},{3,2},{4,5},{5,4},{6,7},{7,6},{8,9},{9,8},{10,11... | collective-permute-start | bytes 3538952 | tf_op jit(solution)/shard_map/ppermute | solution.py:45
  142.0 35.6 %collective-permute-start.18 = (bf16[384,768]{1,0:T(8,128)(2,1)}, bf16[384,768]{1,0:T(8,128)(2,1)}, u32[]{:S(2)}, u32[]{:S(2)}) collective-permute-start(bf16[384,768]{1,0:T(8,128)(2,1)} %copy-done.23), channel_id=1, source_target_pairs={{0,1},{1,0},{2,3},{3,2},{4,5},{5,4},{6,7},{7,6},{8,9},{9,8},{10,11... | collective-permute-start | bytes 1769480 | tf_op jit(solution)/shard_map/ppermute | solution.py:45
  142.5 35.1 %collective-permute-start.19 = (bf16[384,768]{1,0:T(8,128)(2,1)}, bf16[384,768]{1,0:T(8,128)(2,1)}, u32[]{:S(2)}, u32[]{:S(2)}) collective-permute-start(bf16[384,768]{1,0:T(8,128)(2,1)} %copy-done.25), channel_id=1, source_target_pairs={{0,1},{1,0},{2,3},{3,2},{4,5},{5,4},{6,7},{7,6},{8,9},{9,8},{10,11... | collective-permute-start | bytes 1769480 | tf_op jit(solution)/shard_map/ppermute | solution.py:45
  151.8 34.0 %collective-permute-start.21 = (bf16[3,384,512]{2,1,0:T(8,128)(2,1)}, bf16[3,384,512]{2,1,0:T(8,128)(2,1)}, u32[]{:S(2)}, u32[]{:S(2)}) collective-permute-start(bf16[3,384,512]{2,1,0:T(8,128)(2,1)} %collective-permute-done.13.refs_4_), channel_id=1, source_target_pairs={{0,8},{4,12},{8,0},{12,4},{16,24},{20,28},{24,16},{28,20},{1,9},{5... | collective-permute-start | bytes 3538952 | tf_op jit(solution)/shard_map/ppermute | solution.py:45
  185.5 18.0 %collective-permute-start.20 = (bf16[256,1536]{1,0:T(8,128)(2,1)}, bf16[256,1536]{1,0:T(8,128)(2,1)S(1)}, u32[]{:S(2)}, u32[]{:S(2)}) collective-permute-start(bf16[256,1536]{1,0:T(8,128)(2,1)} %get-tuple-element.77), channel_id=1, source_target_pairs={{0,2},{1,3},{2,0},{3,1},{4,6},{5,7},{6,4},{7,5},{8,10},{9,11},{10,... | collective-permute-start | bytes 2359304 | tf_op jit(solution)/shard_map/ppermute | solution.py:45
  185.8 22.6 %collective-permute-start.23 = (bf16[3,384,1024]{2,1,0:T(8,128)(2,1)S(1)}, bf16[3,384,1024]{2,1,0:T(8,128)(2,1)}, u32[]{:S(2)}, u32[]{:S(2)}) collective-permute-start(bf16[3,384,1024]{2,1,0:T(8,128)(2,1)S(1)} %copy-done.26), channel_id=1, source_target_pairs={{0,1},{1,0},{2,3},{3,2},{4,5},{5,4},{6,7},{7,6},{8,9},{9,8},{10,11... | collective-permute-start | bytes 7077896 | tf_op jit(solution)/shard_map/ppermute | solution.py:45
  244.6 24.6 %collective-permute-start.25 = (bf16[256,1536]{1,0:T(8,128)(2,1)S(1)}, bf16[256,1536]{1,0:T(8,128)(2,1)S(1)}, u32[]{:S(2)}, u32[]{:S(2)}) collective-permute-start(bf16[256,1536]{1,0:T(8,128)(2,1)S(1)} %add_convert_fusion.2), channel_id=1, source_target_pairs={{0,2},{1,3},{2,0},{3,1},{4,6},{5,7},{6,4},{7,5},{8,10},{9,11},{10,... | collective-permute-start | bytes 2359304 | tf_op jit(solution)/shard_map/ppermute | solution.py:45
  282.0 47.2 %all-to-all-start.2 = ((bf16[8,256,192]{1,2,0:T(8,128)(2,1)}), bf16[8,256,192]{1,2,0:T(8,128)(2,1)S(1)}, u32[]{:S(2)}, u32[]{:S(2)}) async-start(bf16[8,256,192]{1,2,0:T(8,128)(2,1)} %copy.26), calls=%async_computation.2 | async-start | bytes 1572864 | tf_op jit(solution)/shard_map/all_to_all | solution.py:937
  288.0 70.2 %collective-permute-start.65 = (bf16[256,1536]{1,0:T(8,128)(2,1)}, bf16[256,1536]{1,0:T(8,128)(2,1)}, u32[]{:S(2)}, u32[]{:S(2)}) collective-permute-start(bf16[256,1536]{1,0:T(8,128)(2,1)} %get-tuple-element.95), channel_id=1, source_target_pairs={{0,2},{1,3},{2,0},{3,1},{4,6},{5,7},{6,4},{7,5},{8,10},{9,11},{10,... | collective-permute-start | bytes 2359304 | tf_op jit(solution)/shard_map/ppermute | solution.py:45
  354.5 55.9 %all-to-all-start.3 = ((bf16[8,256,384]{2,1,0:T(8,128)(2,1)}), bf16[8,256,384]{2,1,0:T(8,128)(2,1)S(1)}, u32[]{:S(2)}, u32[]{:S(2)}) async-start(bf16[8,256,384]{2,1,0:T(8,128)(2,1)} %attention_backward.1), calls=%async_computation.3 | async-start | bytes 3145728 | tf_op jit(solution)/shard_map/all_to_all | solution.py:940
  361.0 28.5 %collective-permute-start.66 = (bf16[512,1536]{1,0:T(8,128)(2,1)}, bf16[512,1536]{1,0:T(8,128)(2,1)}, u32[]{:S(2)}, u32[]{:S(2)}) collective-permute-start(bf16[512,1536]{1,0:T(8,128)(2,1)} %pad_maximum_fusion.6), channel_id=1, source_target_pairs={{0,1},{1,0},{2,3},{3,2},{4,5},{5,4},{6,7},{7,6},{8,9},{9,8},{10,11... | collective-permute-start | bytes 4718600 | tf_op jit(solution)/shard_map/ppermute | solution.py:45
  361.0 20.4 %collective-permute-start.32 = (bf16[256,1536]{1,0:T(8,128)(2,1)S(1)}, bf16[256,1536]{1,0:T(8,128)(2,1)S(1)}, u32[]{:S(2)}, u32[]{:S(2)}) collective-permute-start(bf16[256,1536]{1,0:T(8,128)(2,1)S(1)} %copy-done.17), channel_id=1, source_target_pairs={{0,2},{1,3},{2,0},{3,1},{4,6},{5,7},{6,4},{7,5},{8,10},{9,11},{10,... | collective-permute-start | bytes 2359304 | tf_op jit(solution)/shard_map/ppermute | solution.py:45
  365.0 20.4 %collective-permute-start.69 = (bf16[256,384]{1,0:T(8,128)(2,1)S(1)}, bf16[256,384]{1,0:T(8,128)(2,1)S(1)}, u32[]{:S(2)}, u32[]{:S(2)}) collective-permute-start(bf16[256,384]{1,0:T(8,128)(2,1)S(1)} %get-tuple-element.150), channel_id=1, source_target_pairs={{0,3},{1,2},{2,1},{3,0},{4,7},{5,6},{6,5},{7,4},{8,11},{9,10},{10,... | collective-permute-start | bytes 589832 | tf_op jit(solution)/shard_map/ppermute | solution.py:45
  365.2 20.2 %collective-permute-start.68 = (bf16[256,384]{1,0:T(8,128)(2,1)S(1)}, bf16[256,384]{1,0:T(8,128)(2,1)S(1)}, u32[]{:S(2)}, u32[]{:S(2)}) collective-permute-start(bf16[256,384]{1,0:T(8,128)(2,1)S(1)} %get-tuple-element.151), channel_id=1, source_target_pairs={{0,1},{1,0},{2,3},{3,2},{4,5},{5,4},{6,7},{7,6},{8,9},{9,8},{10,11... | collective-permute-start | bytes 589832 | tf_op jit(solution)/shard_map/ppermute | solution.py:45
  365.4 24.1 %collective-permute-start.67 = (bf16[256,384]{1,0:T(8,128)(2,1)S(1)}, bf16[256,384]{1,0:T(8,128)(2,1)S(1)}, u32[]{:S(2)}, u32[]{:S(2)}) collective-permute-start(bf16[256,384]{1,0:T(8,128)(2,1)S(1)} %get-tuple-element.152), channel_id=1, source_target_pairs={{0,2},{1,3},{2,0},{3,1},{4,6},{5,7},{6,4},{7,5},{8,10},{9,11},{10,... | collective-permute-start | bytes 589832 | tf_op jit(solution)/shard_map/ppermute | solution.py:45
  382.7 46.3 %collective-permute-start.33 = (bf16[512,1536]{1,0:T(8,128)(2,1)}, bf16[512,1536]{1,0:T(8,128)(2,1)}, u32[]{:S(2)}, u32[]{:S(2)}) collective-permute-start(bf16[512,1536]{1,0:T(8,128)(2,1)} %pad_maximum_fusion.5), channel_id=1, source_target_pairs={{0,1},{1,0},{2,3},{3,2},{4,5},{5,4},{6,7},{7,6},{8,9},{9,8},{10,11... | collective-permute-start | bytes 4718600 | tf_op jit(solution)/shard_map/ppermute | solution.py:45
  394.2 35.9 %collective-permute-start.70 = (bf16[4,192,384]{2,1,0:T(8,128)(2,1)S(1)}, bf16[4,192,384]{2,1,0:T(8,128)(2,1)S(1)}, u32[]{:S(2)}, u32[]{:S(2)}) collective-permute-start(bf16[4,192,384]{2,1,0:T(8,128)(2,1)S(1)} %constant_dynamic-slice_fusion.11), channel_id=1, source_target_pairs={{0,4},{4,0},{8,12},{12,8},{16,20},{20,16},{24,28},{28,24},{1,5},{5... | collective-permute-start | bytes 1769480 | tf_op jit(solution)/shard_map/ppermute | solution.py:45
  436.6 125.0 %collective-permute-start.26 = (bf16[512,1536]{1,0:T(8,128)(2,1)}, bf16[512,1536]{1,0:T(8,128)(2,1)S(1)}, u32[]{:S(2)}, u32[]{:S(2)}) collective-permute-start(bf16[512,1536]{1,0:T(8,128)(2,1)} %slice.75), channel_id=1, source_target_pairs={{0,1},{1,0},{2,3},{3,2},{4,5},{5,4},{6,7},{7,6},{8,9},{9,8},{10,11... | collective-permute-start | bytes 4718600 | tf_op jit(solution)/shard_map/ppermute | solution.py:45
  503.6 27.0 %collective-permute-start.84 = (bf16[4,192,384]{2,1,0:T(8,128)(2,1)S(1)}, bf16[4,192,384]{2,1,0:T(8,128)(2,1)S(1)}, u32[]{:S(2)}, u32[]{:S(2)}) collective-permute-start(bf16[4,192,384]{2,1,0:T(8,128)(2,1)S(1)} %get-tuple-element.144.refs_0_), channel_id=1, source_target_pairs={{0,8},{8,16},{16,24},{24,28},{28,20},{20,12},{12,4},{4,0},{1,9},{9... | collective-permute-start | bytes 1769480 | tf_op jit(solution)/shard_map/ppermute | solution.py:755
  505.5 25.1 %collective-permute-start.91 = (bf16[4,192,384]{2,1,0:T(8,128)(2,1)S(1)}, bf16[4,192,384]{2,1,0:T(8,128)(2,1)S(1)}, u32[]{:S(2)}, u32[]{:S(2)}) collective-permute-start(bf16[4,192,384]{2,1,0:T(8,128)(2,1)S(1)} %get-tuple-element.143.refs_8_), channel_id=1, source_target_pairs={{0,4},{8,0},{16,8},{24,16},{28,24},{20,28},{12,20},{4,12},{1,5},{9... | collective-permute-start | bytes 1769480 | tf_op jit(solution)/shard_map/ppermute | solution.py:755
  519.3 24.0 %collective-permute-start.54 = (bf16[4,192,384]{2,1,0:T(8,128)(2,1)S(1)}, bf16[4,192,384]{2,1,0:T(8,128)(2,1)S(1)}, u32[]{:S(2)}, u32[]{:S(2)}) collective-permute-start(bf16[4,192,384]{2,1,0:T(8,128)(2,1)S(1)} %constant_dynamic-slice_fusion.20), channel_id=1, source_target_pairs={{0,4},{4,0},{8,12},{12,8},{16,20},{20,16},{24,28},{28,24},{1,5},{5... | collective-permute-start | bytes 1769480 | tf_op jit(solution)/shard_map/ppermute | solution.py:45
  530.6 24.8 %collective-permute-start.85 = (bf16[4,192,384]{2,1,0:T(8,128)(2,1)S(1)}, bf16[4,192,384]{2,1,0:T(8,128)(2,1)S(1)}, u32[]{:S(2)}, u32[]{:S(2)}) collective-permute-start(bf16[4,192,384]{2,1,0:T(8,128)(2,1)S(1)} %collective-permute-done.84.refs_1_), channel_id=1, source_target_pairs={{0,8},{8,16},{16,24},{24,28},{28,20},{20,12},{12,4},{4,0},{1,9},{9... | collective-permute-start | bytes 1769480 | tf_op jit(solution)/shard_map/ppermute | solution.py:755
  530.6 24.9 %collective-permute-start.92 = (bf16[4,192,384]{2,1,0:T(8,128)(2,1)S(1)}, bf16[4,192,384]{2,1,0:T(8,128)(2,1)S(1)}, u32[]{:S(2)}, u32[]{:S(2)}) collective-permute-start(bf16[4,192,384]{2,1,0:T(8,128)(2,1)S(1)} %collective-permute-done.91.refs_9_), channel_id=1, source_target_pairs={{0,4},{8,0},{16,8},{24,16},{28,24},{20,28},{12,20},{4,12},{1,5},{9... | collective-permute-start | bytes 1769480 | tf_op jit(solution)/shard_map/ppermute | solution.py:755
  534.1 18.0 %collective-permute-start.40 = (bf16[4,48,384]{2,1,0:T(8,128)(2,1)S(1)}, bf16[4,48,384]{2,1,0:T(8,128)(2,1)S(1)}, u32[]{:S(2)}, u32[]{:S(2)}) collective-permute-start(bf16[4,48,384]{2,1,0:T(8,128)(2,1)S(1)} %get-tuple-element.168), channel_id=1, source_target_pairs={{0,24},{4,28},{8,16},{12,20},{16,8},{20,12},{24,0},{28,4},{1,25},{... | collective-permute-start | bytes 442376 | tf_op jit(solution)/shard_map/ppermute | solution.py:45
  555.4 26.3 %collective-permute-start.86 = (bf16[4,192,384]{2,1,0:T(8,128)(2,1)S(1)}, bf16[4,192,384]{2,1,0:T(8,128)(2,1)}, u32[]{:S(2)}, u32[]{:S(2)}) collective-permute-start(bf16[4,192,384]{2,1,0:T(8,128)(2,1)S(1)} %collective-permute-done.85.refs_2_), channel_id=1, source_target_pairs={{0,8},{8,16},{16,24},{24,28},{28,20},{20,12},{12,4},{4,0},{1,9},{9... | collective-permute-start | bytes 1769480 | tf_op jit(solution)/shard_map/ppermute | solution.py:755
  555.5 28.2 %collective-permute-start.93 = (bf16[4,192,384]{2,1,0:T(8,128)(2,1)S(1)}, bf16[4,192,384]{2,1,0:T(8,128)(2,1)}, u32[]{:S(2)}, u32[]{:S(2)}) collective-permute-start(bf16[4,192,384]{2,1,0:T(8,128)(2,1)S(1)} %collective-permute-done.92.refs_10_), channel_id=1, source_target_pairs={{0,4},{8,0},{16,8},{24,16},{28,24},{20,28},{12,20},{4,12},{1,5},{9... | collective-permute-start | bytes 1769480 | tf_op jit(solution)/shard_map/ppermute | solution.py:755
  561.6 20.0 %collective-permute-start.77 = (bf16[4,48,384]{2,1,0:T(8,128)(2,1)S(1)}, bf16[4,48,384]{2,1,0:T(8,128)(2,1)S(1)}, u32[]{:S(2)}, u32[]{:S(2)}) collective-permute-start(bf16[4,48,384]{2,1,0:T(8,128)(2,1)S(1)} %get-tuple-element.171.refs_0_), channel_id=1, source_target_pairs={{0,8},{4,12},{8,0},{12,4},{16,24},{20,28},{24,16},{28,20},{1,9},{5... | collective-permute-start | bytes 442376 | tf_op jit(solution)/shard_map/ppermute | solution.py:45
  563.8 17.8 %collective-permute-start.57 = (bf16[4,48,384]{2,1,0:T(8,128)(2,1)S(1)}, bf16[4,48,384]{2,1,0:T(8,128)(2,1)S(1)}, u32[]{:S(2)}, u32[]{:S(2)}) collective-permute-start(bf16[4,48,384]{2,1,0:T(8,128)(2,1)S(1)} %get-tuple-element.165), channel_id=1, source_target_pairs={{0,24},{4,28},{8,16},{12,20},{16,8},{20,12},{24,0},{28,4},{1,25},{... | collective-permute-start | bytes 442376 | tf_op jit(solution)/shard_map/ppermute | solution.py:45
  565.7 20.4 %collective-permute-start.56 = (bf16[4,48,384]{2,1,0:T(8,128)(2,1)S(1)}, bf16[4,48,384]{2,1,0:T(8,128)(2,1)}, u32[]{:S(2)}, u32[]{:S(2)}) collective-permute-start(bf16[4,48,384]{2,1,0:T(8,128)(2,1)S(1)} %get-tuple-element.166), channel_id=1, source_target_pairs={{0,16},{4,20},{8,24},{12,28},{16,0},{20,4},{24,8},{28,12},{1,17},{... | collective-permute-start | bytes 442376 | tf_op jit(solution)/shard_map/ppermute | solution.py:45
  581.7 31.0 %collective-permute-start.87 = (bf16[4,192,384]{2,1,0:T(8,128)(2,1)}, bf16[4,192,384]{2,1,0:T(8,128)(2,1)}, u32[]{:S(2)}, u32[]{:S(2)}) collective-permute-start(bf16[4,192,384]{2,1,0:T(8,128)(2,1)} %collective-permute-done.86.refs_3_), channel_id=1, source_target_pairs={{0,8},{8,16},{16,24},{24,28},{28,20},{20,12},{12,4},{4,0},{1,9},{9... | collective-permute-start | bytes 1769480 | tf_op jit(solution)/shard_map/ppermute | solution.py:755
  583.7 29.1 %collective-permute-start.94 = (bf16[4,192,384]{2,1,0:T(8,128)(2,1)}, bf16[4,192,384]{2,1,0:T(8,128)(2,1)}, u32[]{:S(2)}, u32[]{:S(2)}) collective-permute-start(bf16[4,192,384]{2,1,0:T(8,128)(2,1)} %collective-permute-done.93.refs_11_), channel_id=1, source_target_pairs={{0,4},{8,0},{16,8},{24,16},{28,24},{20,28},{12,20},{4,12},{1,5},{9... | collective-permute-start | bytes 1769480 | tf_op jit(solution)/shard_map/ppermute | solution.py:755
  586.0 42.5 %collective-permute-start.27 = (bf16[256,1536]{1,0:T(8,128)(2,1)}, bf16[256,1536]{1,0:T(8,128)(2,1)S(1)}, u32[]{:S(2)}, u32[]{:S(2)}) collective-permute-start(bf16[256,1536]{1,0:T(8,128)(2,1)} %add_convert_fusion.1), channel_id=1, source_target_pairs={{0,2},{1,3},{2,0},{3,1},{4,6},{5,7},{6,4},{7,5},{8,10},{9,11},{10,... | collective-permute-start | bytes 2359304 | tf_op jit(solution)/shard_map/ppermute | solution.py:45
  587.7 19.5 %collective-permute-start.43 = (bf16[48,384]{1,0:T(8,128)(2,1)}, bf16[48,384]{1,0:T(8,128)(2,1)S(1)}, u32[]{:S(2)}, u32[]{:S(2)}) collective-permute-start(bf16[48,384]{1,0:T(8,128)(2,1)} %get-tuple-element.186), channel_id=1, source_target_pairs={{0,2},{1,3},{2,0},{3,1},{4,6},{5,7},{6,4},{7,5},{8,10},{9,11},{10,... | collective-permute-start | bytes 110600 | tf_op jit(solution)/shard_map/ppermute | solution.py:45
  588.5 20.2 %collective-permute-start.42 = (bf16[48,384]{1,0:T(8,128)(2,1)S(1)}, bf16[48,384]{1,0:T(8,128)(2,1)}, u32[]{:S(2)}, u32[]{:S(2)}) collective-permute-start(bf16[48,384]{1,0:T(8,128)(2,1)S(1)} %get-tuple-element.187), channel_id=1, source_target_pairs={{0,1},{1,0},{2,3},{3,2},{4,5},{5,4},{6,7},{7,6},{8,9},{9,8},{10,11... | collective-permute-start | bytes 110600 | tf_op jit(solution)/shard_map/ppermute | solution.py:45
  612.7 36.8 %collective-permute-start.88 = (bf16[4,192,384]{2,1,0:T(8,128)(2,1)}, bf16[4,192,384]{2,1,0:T(8,128)(2,1)}, u32[]{:S(2)}, u32[]{:S(2)}) collective-permute-start(bf16[4,192,384]{2,1,0:T(8,128)(2,1)} %collective-permute-done.87.refs_4_), channel_id=1, source_target_pairs={{0,8},{8,16},{16,24},{24,28},{28,20},{20,12},{12,4},{4,0},{1,9},{9... | collective-permute-start | bytes 1769480 | tf_op jit(solution)/shard_map/ppermute | solution.py:755
  612.8 36.7 %collective-permute-start.95 = (bf16[4,192,384]{2,1,0:T(8,128)(2,1)}, bf16[4,192,384]{2,1,0:T(8,128)(2,1)}, u32[]{:S(2)}, u32[]{:S(2)}) collective-permute-start(bf16[4,192,384]{2,1,0:T(8,128)(2,1)} %collective-permute-done.94.refs_12_), channel_id=1, source_target_pairs={{0,4},{8,0},{16,8},{24,16},{28,24},{20,28},{12,20},{4,12},{1,5},{9... | collective-permute-start | bytes 1769480 | tf_op jit(solution)/shard_map/ppermute | solution.py:755
  628.5 20.4 %collective-permute-start.48 = (bf16[4,48,384]{2,1,0:T(8,128)(2,1)S(1)}, bf16[4,48,384]{2,1,0:T(8,128)(2,1)S(1)}, u32[]{:S(2)}, u32[]{:S(2)}) collective-permute-start(bf16[4,48,384]{2,1,0:T(8,128)(2,1)S(1)} %get-tuple-element.183.refs_0_), channel_id=1, source_target_pairs={{0,8},{4,12},{8,0},{12,4},{16,24},{20,28},{24,16},{28,20},{1,9},{5... | collective-permute-start | bytes 442376 | tf_op jit(solution)/shard_map/ppermute | solution.py:45
  631.8 19.8 %collective-permute-start.49 = (bf16[4,48,384]{2,1,0:T(8,128)(2,1)S(1)}, bf16[4,48,384]{2,1,0:T(8,128)(2,1)}, u32[]{:S(2)}, u32[]{:S(2)}) collective-permute-start(bf16[4,48,384]{2,1,0:T(8,128)(2,1)S(1)} %get-tuple-element.183.refs_0_), channel_id=1, source_target_pairs={{0,16},{4,20},{8,24},{12,28},{16,0},{20,4},{24,8},{28,12},{1,17},{... | collective-permute-start | bytes 442376 | tf_op jit(solution)/shard_map/ppermute | solution.py:45
  635.5 16.6 %collective-permute-start.61 = (bf16[4,48,384]{2,1,0:T(8,128)(2,1)}, bf16[4,48,384]{2,1,0:T(8,128)(2,1)}, u32[]{:S(2)}, u32[]{:S(2)}) collective-permute-start(bf16[4,48,384]{2,1,0:T(8,128)(2,1)} %get-tuple-element.177.refs_0_), channel_id=1, source_target_pairs={{0,8},{4,12},{8,0},{12,4},{16,24},{20,28},{24,16},{28,20},{1,9},{5... | collective-permute-start | bytes 442376 | tf_op jit(solution)/shard_map/ppermute | solution.py:45
  648.9 32.3 %collective-permute-start.80 = (bf16[4,4,48,384]{3,2,1,0:T(8,128)(2,1)}, bf16[4,4,48,384]{3,2,1,0:T(8,128)(2,1)}, u32[]{:S(2)}, u32[]{:S(2)}) collective-permute-start(bf16[4,4,48,384]{3,2,1,0:T(8,128)(2,1)} %pad_maximum_fusion.13), channel_id=1, source_target_pairs={{0,4},{4,0},{8,12},{12,8},{16,20},{20,16},{24,28},{28,24},{1,5},{5... | collective-permute-start | bytes 1769480 | tf_op jit(solution)/shard_map/ppermute | solution.py:45
  649.5 35.9 %collective-permute-start.89 = (bf16[4,192,384]{2,1,0:T(8,128)(2,1)}, bf16[4,192,384]{2,1,0:T(8,128)(2,1)}, u32[]{:S(2)}, u32[]{:S(2)}) collective-permute-start(bf16[4,192,384]{2,1,0:T(8,128)(2,1)} %collective-permute-done.88.refs_5_), channel_id=1, source_target_pairs={{0,8},{8,16},{16,24},{24,28},{28,20},{20,12},{12,4},{4,0},{1,9},{9... | collective-permute-start | bytes 1769480 | tf_op jit(solution)/shard_map/ppermute | solution.py:755
  649.6 35.9 %collective-permute-start.96 = (bf16[4,192,384]{2,1,0:T(8,128)(2,1)}, bf16[4,192,384]{2,1,0:T(8,128)(2,1)}, u32[]{:S(2)}, u32[]{:S(2)}) collective-permute-start(bf16[4,192,384]{2,1,0:T(8,128)(2,1)} %collective-permute-done.95.refs_13_), channel_id=1, source_target_pairs={{0,4},{8,0},{16,8},{24,16},{28,24},{20,28},{12,20},{4,12},{1,5},{9... | collective-permute-start | bytes 1769480 | tf_op jit(solution)/shard_map/ppermute | solution.py:755
  651.6 23.5 %collective-permute-start.62 = (bf16[4,48,384]{2,1,0:T(8,128)(2,1)}, bf16[4,48,384]{2,1,0:T(8,128)(2,1)}, u32[]{:S(2)}, u32[]{:S(2)}) collective-permute-start(bf16[4,48,384]{2,1,0:T(8,128)(2,1)} %get-tuple-element.177.refs_0_), channel_id=1, source_target_pairs={{0,16},{4,20},{8,24},{12,28},{16,0},{20,4},{24,8},{28,12},{1,17},{... | collective-permute-start | bytes 442376 | tf_op jit(solution)/shard_map/ppermute | solution.py:45
  652.1 24.2 %collective-permute-start.63 = (bf16[4,48,384]{2,1,0:T(8,128)(2,1)}, bf16[4,48,384]{2,1,0:T(8,128)(2,1)}, u32[]{:S(2)}, u32[]{:S(2)}) collective-permute-start(bf16[4,48,384]{2,1,0:T(8,128)(2,1)} %get-tuple-element.177.refs_0_), channel_id=1, source_target_pairs={{0,24},{4,28},{8,16},{12,20},{16,8},{20,12},{24,0},{28,4},{1,25},{... | collective-permute-start | bytes 442376 | tf_op jit(solution)/shard_map/ppermute | solution.py:45
  683.5 16.6 %collective-permute-start.50 = (bf16[4,4,48,384]{3,2,1,0:T(8,128)(2,1)}, bf16[4,4,48,384]{3,2,1,0:T(8,128)(2,1)}, u32[]{:S(2)}, u32[]{:S(2)}) collective-permute-start(bf16[4,4,48,384]{3,2,1,0:T(8,128)(2,1)} %pad_maximum_fusion.11), channel_id=1, source_target_pairs={{0,4},{4,0},{8,12},{12,8},{16,20},{20,16},{24,28},{28,24},{1,5},{5... | collective-permute-start | bytes 1769480 | tf_op jit(solution)/shard_map/ppermute | solution.py:45
  683.7 28.9 %collective-permute-start.64 = (bf16[4,4,48,384]{3,2,1,0:T(8,128)(2,1)}, bf16[4,4,48,384]{3,2,1,0:T(8,128)(2,1)}, u32[]{:S(2)}, u32[]{:S(2)}) collective-permute-start(bf16[4,4,48,384]{3,2,1,0:T(8,128)(2,1)} %pad_maximum_fusion.12), channel_id=1, source_target_pairs={{0,4},{4,0},{8,12},{12,8},{16,20},{20,16},{24,28},{28,24},{1,5},{5... | collective-permute-start | bytes 1769480 | tf_op jit(solution)/shard_map/ppermute | solution.py:45
  685.5 33.6 %collective-permute-start.90 = (bf16[4,192,384]{2,1,0:T(8,128)(2,1)}, bf16[4,192,384]{2,1,0:T(8,128)(2,1)}, u32[]{:S(2)}, u32[]{:S(2)}) collective-permute-start(bf16[4,192,384]{2,1,0:T(8,128)(2,1)} %collective-permute-done.89.refs_6_), channel_id=1, source_target_pairs={{0,8},{8,16},{16,24},{24,28},{28,20},{20,12},{12,4},{4,0},{1,9},{9... | collective-permute-start | bytes 1769480 | tf_op jit(solution)/shard_map/ppermute | solution.py:755
  685.5 33.6 %collective-permute-start.97 = (bf16[4,192,384]{2,1,0:T(8,128)(2,1)}, bf16[4,192,384]{2,1,0:T(8,128)(2,1)}, u32[]{:S(2)}, u32[]{:S(2)}) collective-permute-start(bf16[4,192,384]{2,1,0:T(8,128)(2,1)} %collective-permute-done.96.refs_14_), channel_id=1, source_target_pairs={{0,4},{8,0},{16,8},{24,16},{28,24},{20,28},{12,20},{4,12},{1,5},{9... | collective-permute-start | bytes 1769480 | tf_op jit(solution)/shard_map/ppermute | solution.py:755
  (101 other events, 1244.6 us)
Sparse Core Ops, SparseCore 0:
  272.0 212.3 reduce-scatter.1

commit v3 on v2

--- a/solution.py
+++ b/solution.py
@@ -59,6 +59,10 @@
 
 def rows(array, index, height):
     return lax.dynamic_slice_in_dim(array, index * height, height, 0)
+
+
+def together(*arrays):
+    return lax.optimization_barrier(arrays)
 
 
 def after(array, *others):
@@ -102,10 +106,10 @@
 units_plan = ((0, ALL), (1, ALL), (2, MINE + 1), (2, OTHER + 1), (3, MINE + 2), (3, OTHER + 2))
 
 
-def gather_thirds(own):
+def gather_thirds(own, *others):
     side = lax.axis_index("ctx") % 2
     third = own.shape[1] // 3
-    far = over_fsdp(columns(own, side, third), 2)
+    far = after(over_fsdp(columns(own, side, third), 2), *others)
     rest = over_fsdp(after(own[:, 2 * third :], far), 2)
     near = over_fsdp(own, 1)
     other = over_ctx(far, 1)
@@ -313,11 +317,11 @@
         if head < HQ + HK:
             part = turned(part.astype(wide), cosine, -sine).astype(low)
         raw[:, head * HD : (head + 1) * HD] = part
-    quarter = raw_ref.shape[3]
+    quarter = raw_ref.shape[2] // 2
     for k in range(4):
         for i in range(2):
             first = (4 * i + k) * quarter
-            raw_ref[i, k] = raw[:, first : first + quarter]
+            raw_ref[k, :, i * quarter : (i + 1) * quarter] = raw[:, first : first + quarter]
     grad = contract_last(raw[...], weight[...])
     back, gain_grad_ref[...] = norm_back(rows_ref[...].astype(wide), gain[...], grad)
     input_grad_ref[...] = grad_middle_ref[...] + back
@@ -327,7 +331,7 @@
     count, width = rows_in.shape
     total = pieces[0].shape[1]
     outs = [
-        jax.ShapeDtypeStruct((2, 4, count, total // 8), low),
+        jax.ShapeDtypeStruct((4, count, total // 4), low),
         jax.ShapeDtypeStruct((count, width), wide),
         jax.ShapeDtypeStruct((1, width), wide),
     ]
@@ -664,87 +668,23 @@
     return [over_ctx(cut(k), 2 * k) for k in (1, 2, 3)]
 
 
-def reduce_ctx(grad, dim, *others):
-    here, size = lax.axis_index("ctx"), lax.axis_size("ctx")
-    if size != 8:
-        return lax.psum_scatter(grad, "ctx", scatter_dimension=dim, tiled=True)
-
-    def cut(array, index, width):
-        return lax.dynamic_slice_in_dim(array, index * width, width, dim)
-
-    first, second = (others[:1], others[1:]) if others else ((), ())
-    side, level = here % 2, here // 2
-    half, piece = grad.shape[dim] // 2, grad.shape[dim] // 8
-    got = after(over_ctx(cut(grad, 1 - side, half), 1), *first)
-    kept = add_low(cut(grad, side, half), got)
-    got = exchange_levels(lambda k: cut(kept, level ^ k, piece))
-    got = [after(array, *second) for array in got]
-    return add_low(cut(kept, level, piece), *got)
-
-
-def place_code():
-    here = lax.axis_index("ctx")
-    return jnp.stack([(here % 2) * 4 + here // 2, lax.axis_index("fsdp")]).astype(jnp.int32)
-
-
 def deal_fsdp(cut, *others):
     got = [over_fsdp(cut(k), k) for k in (1, 2, 3)]
     return jnp.stack([cut(0)] + [after(array, *others) for array in got])
 
 
-def spread_rows_kernel(where_ref, *refs):
-    parts, outs = refs[:5], refs[5:]
-    piece = parts[0].shape[1]
-    for i, out_ref in enumerate(outs):
-
-        @pl.when(pl.program_id(0) // (4 // len(outs)) == i)
-        def _(out_ref=out_ref):
-            for k in range(8):
-                part = parts[k][0] if k < 4 else parts[4][k - 4, 0]
-                place = pl.multiple_of((where_ref[0] ^ k) * piece, piece)
-                out_ref[pl.ds(place, piece), :] = part.astype(wide)
-
-
-def spread_rows_call(near, far, count):
-    _, height, width = near[0].shape
-    each = 4 // count
-
-    def place_of(number):
-        return lambda i, where: (0, jnp.clip(i - number * each, 0, each - 1))
-
-    return pl.pallas_call(
-        spread_rows_kernel,
-        grid_spec=pltpu.PrefetchScalarGridSpec(
-            num_scalar_prefetch=1,
-            grid=(4,),
-            in_specs=[pl.BlockSpec((1, height, width), lambda i, where: (where[1] ^ i, 0, 0))] * 4
-            + [pl.BlockSpec((4, 1, height, width), lambda i, where: (0, where[1] ^ i, 0, 0))],
-            out_specs=[pl.BlockSpec((8 * height, width), place_of(k)) for k in range(count)],
-        ),
-        out_shape=[jax.ShapeDtypeStruct((8 * height, each * width), wide)] * count,
-        cost_estimate=brief,
-        name="spread_rows",
-    )(place_code(), *near, far)
-
-
-def dealt_grads(left, right, count, *others):
-    size = lax.axis_size("ctx")
-    grad = contract_first(left, right).astype(low).reshape(4, left.shape[1] // 4, right.shape[1])
-    part = lax.axis_index("fsdp")
-    piece = reduce_ctx(grad, 1, *others[:2])
-    _, height, width = piece.shape
-    mine = deal_fsdp(
-        lambda k: lax.dynamic_index_in_dim(piece, part ^ k, 0, keepdims=False), *others[2:3]
-    )
-    if size != 8:
-        whole = lax.all_gather(mine, "ctx", axis=1, tiled=True).astype(wide)
-        blocks = [lax.dynamic_index_in_dim(whole, part ^ k, 0, keepdims=False) for k in range(4)]
-        each = 4 // count
-        whole = [jnp.concatenate(blocks[i * each : (i + 1) * each], axis=1) for i in range(count)]
-        return [*whole, grad, piece, piece]
-    near = [mine] + [after(array, *others[3:4]) for array in exchange_levels(lambda k: mine)]
-    far = after(over_ctx(jnp.stack(near), 1), *others[4:5])
-    return [*spread_rows_call(near, far, count), grad, piece, near[-1]]
+def terms_of(left, right):
+    return contract_first(left, right).astype(low).reshape(4, left.shape[1] // 4, right.shape[1])
+
+
+def side_of(terms, other):
+    side, half = lax.axis_index("ctx") % 2, terms.shape[1] // 2
+    return lax.dynamic_slice_in_dim(terms, (side ^ other) * half, half, 1)
+
+
+def level_of(terms, k):
+    level, quarter = lax.axis_index("ctx") // 2, terms.shape[1] // 4
+    return lax.dynamic_slice_in_dim(terms, (level ^ k) * quarter, quarter, 1)
 
 
 ring = (0, 2, 4, 6, 7, 5, 3, 1)
@@ -757,33 +697,65 @@
     )
 
 
+def gather_plain(units, sums):
+    size, part = lax.axis_size("ctx"), lax.axis_index("fsdp")
+    _, height, span = units.shape
+    units = lax.all_gather(units, "ctx", axis=0)
+    units = jnp.stack(
+        [lax.dynamic_index_in_dim(units, part ^ k, 1, keepdims=False) for k in range(4)]
+    ).reshape(4, size, height, 3, span // 3)
+    units = units.transpose(3, 2, 0, 1, 4).reshape(3, height, -1).astype(wide)
+    sums = lax.all_gather(sums, "ctx", axis=1, tiled=True)
+    sums = [lax.dynamic_index_in_dim(sums, part ^ k, 0, keepdims=False) for k in range(4)]
+    sums = jnp.stack(sums, axis=1).astype(wide)
+    sums = sums.reshape(height, 4, 3, -1).transpose(2, 0, 1, 3).reshape(3, height, -1)
+    half = sums.shape[2] // 2
+    return (*units, sums[0], sums[1], sums[2, :, :half], sums[2, :, half:])
+
+
+UPPER = 176
+
+
 def deal_kernel(code_ref, *refs):
     count = len(ring)
     outs = refs[2 * count :]
+    units, (out_ref, query_ref, key_ref, value_ref) = outs[:3], outs[3:]
+    quarter = pl.program_id(0)
     for lower in range(2):
         for step in range(count):
             part = refs[lower * count + step]
-            height = part.shape[1]
-            width = part.shape[2] // len(outs)
-            place = pl.multiple_of(code_ref[1 + lower * count + step] * width, width)
-            for i, out_ref in enumerate(outs):
-                out_ref[lower * height : (lower + 1) * height, pl.ds(place, width)] = part[
-                    0, :, i * width : (i + 1) * width
-                ].astype(wide)
-
-
-def gather_ring(mine, count):
+            place = code_ref[1 + lower * count + step]
+            piece = part.shape[2] // 3
+            height = out_ref.shape[0] // count
+            first = (2 - lower) * height
+            here = slice(UPPER, None) if lower else slice(0, UPPER)
+            across = pl.ds(pl.multiple_of(place * piece, piece), piece)
+            for i, unit_ref in enumerate(units):
+                unit_ref[here, across] = part[0, first:, i * piece : (i + 1) * piece].astype(wide)
+            rows_at = pl.multiple_of(((place % 2) * 4 + place // 2) * height, height)
+            down = pl.ds(rows_at, height)
+            if not lower:
+                out_ref[down, :] = part[0, :height].astype(wide)
+                query_ref[down, :] = part[0, height:first].astype(wide)
+                continue
+
+            @pl.when(quarter < 2)
+            def _(part=part, down=down):
+                key_ref[down, :] = part[0, :height].astype(wide)
+
+            @pl.when(quarter >= 2)
+            def _(part=part, down=down):
+                value_ref[down, :] = part[0, :height].astype(wide)
+
+
+def gather_all(units, sums):
     here, size, part = lax.axis_index("ctx"), lax.axis_size("ctx"), lax.axis_index("fsdp")
-    _, height, span = mine.shape
-    width = span // count * size
     if size != 8:
-        whole = lax.all_gather(mine, "ctx", axis=0)
-        whole = jnp.stack(
-            [lax.dynamic_index_in_dim(whole, part ^ k, 1, keepdims=False) for k in range(4)]
-        ).reshape(4, size, height, count, span // count)
-        whole = whole.transpose(3, 2, 0, 1, 4).reshape(count, height, 4 * width)
-        return tuple(whole[i].astype(wide) for i in range(count))
-    upper, lower = [mine[:, : height // 2]], [mine[:, height // 2 :]]
+        return gather_plain(units, sums)
+    width = sums.shape[2] // 3
+    thirds = [sums[:, :, i * width : (i + 1) * width] for i in range(3)]
+    upper = [jnp.concatenate([thirds[0], thirds[1], units[:, :UPPER]], axis=1)]
+    lower = [jnp.concatenate([thirds[2], units[:, UPPER:]], axis=1)]
     for _ in range(size - 1):
         upper.append(turn_ring(upper[-1], 1))
         lower.append(turn_ring(lower[-1], -1))
@@ -793,19 +765,33 @@
     code = jnp.concatenate(
         [part.reshape(1), order[(turn - steps) % size], order[(turn + steps) % size]]
     ).astype(jnp.int32)
-    half = (1, height // 2, span)
+    height, across = units.shape[1], units.shape[2] // 3 * size
+
+    def incoming(array):
+        return pl.BlockSpec((1,) + array.shape[1:], lambda i, code: (code[0] ^ i, 0, 0))
+
+    def outgoing(count, index):
+        return pl.BlockSpec((height, count), lambda i, code: (0, index(i)))
+
     return pl.pallas_call(
         deal_kernel,
         grid_spec=pltpu.PrefetchScalarGridSpec(
             num_scalar_prefetch=1,
             grid=(4,),
-            in_specs=[pl.BlockSpec(half, lambda i, code: (code[0] ^ i, 0, 0))] * (2 * size),
-            out_specs=[pl.BlockSpec((height, width), lambda i, code: (0, i))] * count,
+            in_specs=[incoming(array) for array in (*upper, *lower)],
+            out_specs=[outgoing(across, lambda i: i)] * 3
+            + [outgoing(width, lambda i: i)] * 2
+            + [
+                outgoing(width, lambda i: jnp.minimum(i, 1)),
+                outgoing(width, lambda i: jnp.maximum(i - 2, 0)),
+            ],
         ),
-        out_shape=[jax.ShapeDtypeStruct((height, 4 * width), wide)] * count,
+        out_shape=[jax.ShapeDtypeStruct((height, 4 * across), wide)] * 3
+        + [jax.ShapeDtypeStruct((height, 4 * width), wide)] * 2
+        + [jax.ShapeDtypeStruct((height, 2 * width), wide)] * 2,
         compiler_params=pltpu.CompilerParams(vmem_limit_bytes=56 << 20),
         cost_estimate=brief,
-        name="deal_columns",
+        name="deal_gradients",
     )(code, *upper, *lower)
 
 
@@ -855,9 +841,9 @@
     part, size = lax.axis_index("fsdp"), lax.axis_size("ctx")
     width = array.shape[1] // 4
     array = jnp.sum(deal_fsdp(lambda k: columns(array, part ^ k, width)), axis=0)
-    array = array + after(over_ctx(array, 1), others[0])
+    array = array + after(over_ctx(array, 1), *others[0])
     if size == 8:
-        return array + sum(after(got, others[1]) for got in exchange_levels(lambda k: array))
+        return array + sum(after(got, *others[1]) for got in exchange_levels(lambda k: array))
     bits = 2
     while bits < size:
         array = array + over_ctx(array, bits)
@@ -891,21 +877,21 @@
     cosine = jnp.concatenate([cosine[:, 0], cosine[:, 0]], axis=1)
     sine = jnp.concatenate([-sine[:, 0], sine[:, 0]], axis=1)
 
-    heads = gather_thirds(jnp.concatenate([w_query, w_key, w_value], axis=1))
+    own, near, far, both = deal_weights((w_gate, w_up, w_down))
+    heads = gather_thirds(jnp.concatenate([w_query, w_key, w_value], axis=1), near, far, both)
     normed_one, load = heads_call(code, rows_in, cosine, sine, gains, heads)
     outward = gather_halves(w_out)
-    own, near, far, both = deal_weights((w_gate, w_up, w_down))
     load, near, far, both, _ = lax.optimization_barrier((load, near, far, both, outward[2]))
     far, both = over_fsdp(far, 2), over_fsdp(both, 3)
     near = over_fsdp(near, 1)
     far_other, both_other = over_ctx(far, 1), over_ctx(both, 2)
-    grad_all = gather_fsdp(grad_down)
 
     if size == HK:
         load = lax.all_to_all(load, "ctx", 0, 0, tiled=True)
         order = all_places[::BLK] // BLK
-        mixed = attention_forward(order, load)
-        mixed = lax.all_to_all(after(mixed, far, outward[3]), "ctx", 0, 0, tiled=True)
+        mixed = attention_forward(order, after(load, far))
+        grad_all = gather_fsdp(grad_down, mixed)
+        mixed = lax.all_to_all(after(mixed, far_other, outward[3]), "ctx", 0, 0, tiled=True)
     else:
         query_rot = load[:, :, : GROUP * HD].transpose(1, 0, 2)
         query_rot = query_rot.reshape(row_count, HK, GROUP, HD)
@@ -916,10 +902,11 @@
             query_rot, keys_all, values_all, own_places, all_places
         )
         mixed = mixed_exact.reshape(row_count, HK, GROUP * HD).transpose(1, 0, 2).astype(low)
+        grad_all = gather_fsdp(grad_down)
 
     dealt = (own, near, far, far_other, both, both_other)
     mixed_low, middle, normed_two = middle_call(
-        code, rows_in, after(mixed, both, far_other, grad_all), gains, outward
+        code, rows_in, after(mixed, both, grad_all), gains, outward
     )
     normed_all = gather_fsdp(normed_two, both_other)
     out_terms, back_terms, hidden, grad_gate, grad_up = units_call(
@@ -958,12 +945,6 @@
         ).transpose(1, 0, 2)
         mid = grad_load
 
-    grad_raw, input_grad, grad_gain_one = heads_back_call(
-        code, grad_load, rows_in, grad_middle, cosine, sine, gains, heads
-    )
-    early, late = grad_branch, input_grad
-    result, _ = scatter_fsdp(after(out_terms, grad_normed_two), mid)
-    result = (middle + result).astype(low)
     quarter = HQ * HD // 4
     turn = (0, 2, 1, 3)
 
@@ -973,20 +954,48 @@
 
     branch_all = gather_fsdp(grad_branch, mid)
     mixed_part = own_columns(lambda k: columns(mixed_low, part ^ k, quarter), mid)
-    normed_one_all = gather_fsdp(after(normed_one, early), mid)
-    out_weight_grad, *_ = dealt_grads(branch_all, mixed_part, 1, mid, late, late, late, late)
-
-    def raw_part(i):
-        return own_columns(
-            lambda k: lax.dynamic_index_in_dim(grad_raw[i], part ^ k, 0, keepdims=False)
-        )
-
-    query_grad, first_terms, summed, last = dealt_grads(normed_one_all, raw_part(0), 1)
-    key_grad, value_grad, second_terms, *_ = dealt_grads(normed_one_all, raw_part(1), 2)
-    unit_sums = after(unit_sums, first_terms, second_terms)
-    gate_grad, up_grad, down_grad = gather_ring(deal_rows(unit_sums), 3)
+    normed_one_all = gather_fsdp(after(normed_one, grad_branch), mid)
+    branch_terms = terms_of(branch_all, mixed_part)
+    if size == HK:
+        out_got = over_ctx(side_of(branch_terms, 1), 1)
+    grad_raw, input_grad, grad_gain_one = heads_back_call(
+        code, grad_load, rows_in, grad_middle, cosine, sine, gains, heads
+    )
+    result, _ = scatter_fsdp(after(out_terms, grad_normed_two), mid)
+    result = (middle + result).astype(low)
+    raw_part = own_columns(
+        lambda k: lax.dynamic_index_in_dim(grad_raw, part ^ k, 0, keepdims=False)
+    )
+    gain_terms = jnp.concatenate([grad_gain_one, grad_gain_two], axis=0)
+    if size == HK:
+        raw_part, out_got = together(raw_part, out_got)
+        out_kept = add_low(side_of(branch_terms, 0), out_got)
+        raw_terms = terms_of(normed_one_all, raw_part)
+        raw_got = over_ctx(side_of(raw_terms, 1), 1)
+        out_got = exchange_levels(lambda k: level_of(out_kept, k))
+        raw_got, out_got = together(raw_got, out_got)
+        raw_kept = add_low(side_of(raw_terms, 0), raw_got)
+        out_sums = add_low(level_of(out_kept, 0), *out_got)
+        raw_kept, unit_sums = together(raw_kept, unit_sums)
+        raw_got = exchange_levels(lambda k: level_of(raw_kept, k))
+        unit_mine = deal_rows(unit_sums)
+        raw_got, unit_mine = together(raw_got, unit_mine)
+        raw_sums = add_low(level_of(raw_kept, 0), *raw_got)
+    else:
+        raw_terms = terms_of(normed_one_all, raw_part)
+        out_sums, raw_sums = (
+            lax.psum_scatter(terms, "ctx", scatter_dimension=1, tiled=True)
+            for terms in (branch_terms, raw_terms)
+        )
+        raw_kept = raw_terms
+        unit_mine = deal_rows(unit_sums)
+    sums = jnp.concatenate([out_sums, raw_sums], axis=2)
+    sums = deal_fsdp(lambda k: lax.dynamic_index_in_dim(sums, part ^ k, 0, keepdims=False))
     gain_grads = sum_gains(
-        jnp.concatenate([grad_gain_one, grad_gain_two], axis=0), summed, last
+        gain_terms, (raw_kept,), (sums,)
+    )
+    gate_grad, up_grad, down_grad, out_weight_grad, query_grad, key_grad, value_grad = gather_all(
+        unit_mine, sums
     )
     return (
         result[None],

time: 746 us -> 691 us (0.926)
  starting transfers between devices: 125 us -> 88.8 us
  Pallas kernels: 149 us -> 138 us
  other arithmetic: 42.8 us -> 35 us
    ppermute x14, waiting for transfers between devices: 11.7 us -> 93.7 us  [turn_ring(): lax.ppermute(array, 'ctx', [(ring[i], ring[(i + step) % count]) for i in...]
    ppermute x84 -> x59, waiting for transfers between devices: 245 us -> 190 us  [swap(): return lax.ppermute(array, axis, [(i, i ^ bits) for i in range(size)])]
    ppermute x84 -> x59, starting transfers between devices: 89 us -> 49.5 us  [swap(): return lax.ppermute(array, axis, [(i, i ^ bits) for i in range(size)])]
    reduce_scatter x1, waiting for transfers between devices: 32.9 us -> 13.4 us  [body(): lax.psum_scatter(unit_terms, 'ctx', scatter_dimension=0, tiled=True)]
    pallas_call x4 -> x1, Pallas kernels: 25.7 us -> 15.3 us  [gather_all(): pl.pallas_call(deal_kernel, grid_spec=pltpu.PrefetchScalarGridSpec(num_sc...]
    another operation x8 -> x1, other arithmetic: 8.7 us -> 0.65 us  [gather_all(): turn = jnp.argmax(order == here).astype(jnp.int32)]
    unnamed x130 -> x126, local copies, waits for them, and re-layouts: 15.1 us -> 17.6 us
  transfers between devices with their start and end apart: 103 -> 78, of which waited for: 41 -> 40; matrix products, arithmetic and copies ran while one was open for 10% -> 9% of each run, Pallas kernels for 15% -> 14%
where the time goes in v3:
time: 691 us; the launch traced here: 683 us
  waiting for transfers between devices  355 us (51%)
  Pallas kernels  138 us (20%)
  starting transfers between devices  88.8 us (13%)
  local copies, waits for them, and re-layouts  42.3 us (6%)
  other arithmetic  35 us (5%)
  between operations  15.2 us (2%)
  matrix products  8.1 us (1%)
    ppermute x59, waiting for transfers between devices, swap(): return lax.ppermute(array, axis, [(i, i ^ bits) for i in range(size)])  190 us
    ppermute x14, waiting for transfers between devices, turn_ring(): lax.ppermute(array, 'ctx', [(ring[i], ring[(i + step) % count]) for i in...  93.7 us
    ppermute x59, starting transfers between devices, swap(): return lax.ppermute(array, axis, [(i, i ^ bits) for i in range(size)])  49.5 us
    all_to_all x1, waiting for transfers between devices, body(): grad_mixed = lax.all_to_all(grad_mixed, 'ctx', 0, 0, tiled=True)  39.6 us
    pallas_call x4, Pallas kernels, whole_call(): pl.pallas_call(kernel, grid_spec=pltpu.PrefetchScalarGridSpec(num_scalar_...  39.5 us
    pallas_call x2, Pallas kernels, attention_call(): pl.pallas_call(kernel, grid_spec=pltpu.PrefetchScalarGridSpec(num_scalar_...  36.4 us
    pallas_call x1, Pallas kernels, units_call(): pl.pallas_call(units_kernel, grid_spec=pltpu.PrefetchScalarGridSpec(num_s...  28 us
    pallas_call x1, Pallas kernels, unit_grads(): pl.pallas_call(unit_grads_kernel, grid=(size,), in_specs=[whole, whole] +...  19.2 us
  transfers between devices with their start and end apart: 78, of which 40 were waited for; matrix products, arithmetic and copies ran while one was open for 9% of the time, Pallas kernels for 14%

profile of v3, /device:TPU:0, one launch (start us, length us, event | category | flops | bytes accessed | tf_op | source)
XLA Modules:
  0.0 682.9 jit_solution(358648092763919222)
XLA Ops:
  10.5 2.5 collective-permute-start.4
  25.0 6.4 collective-permute-done.4.refs_6_
  35.3 15.7 %collective-permute-done.5.refs_7_ = bf16[384,1024]{1,0:T(8,128)(2,1)} collective-permute-done((bf16[384,1024]{1,0:T(8,128)(2,1)}, bf16[384,1024]{1,0:T(8,128)(2,1)}, u32[]{:S(2)}, u32[]{:S(2)}) %collective-permute-start.5) | collective-permute-done | bytes 786464 | tf_op jit(solution)/shard_map/ppermute | solution.py:45
  57.1 2.5 collective-permute-done.2.refs_3_
  63.2 11.5 %query_key_value.1 = (bf16[256,1536]{1,0:T(8,128)(2,1)}, bf16[8,256,384]{2,1,0:T(8,128)(2,1)}) custom-call(s32[3]{0:T(128)} %pad_add_fusion.code_ref, bf16[256,1536]{1,0:T(8,128)(2,1)} %bitcast.67, f32[256,96]{1,0:T(8,128)} %get-tuple-element.184.cosine_ref, f32[256,96]{1,0:T(8,128)} %get-tuple-element.185.sine_ref, bf16[2,384]{1,0:T(2,128)(2,1)} %copy-done.53, ...), custom_call_target="tpu_custom_call" | custom-call | flops 2415919104 | bytes 12785664 | tf_op jit(solution)/shard_map/query_key_value/pallas_call | solution.py:153
  76.0 5.5 all-to-all-start
  84.9 2.0 collective-permute-start.13
  87.0 23.8 %collective-permute-done.11.refs_2_ = bf16[3,384,512]{2,1,0:T(8,128)(2,1)} collective-permute-done((bf16[3,384,512]{2,1,0:T(8,128)(2,1)}, bf16[3,384,512]{2,1,0:T(8,128)(2,1)}, u32[]{:S(2)}, u32[]{:S(2)}) %collective-permute-start.11) | collective-permute-done | bytes 1179680 | tf_op jit(solution)/shard_map/ppermute | solution.py:45
  110.8 2.0 collective-permute-start.12
  112.8 5.3 all-to-all-done.load_ref
  118.1 12.3 %attention_forward.1 = bf16[8,256,192]{2,1,0:T(8,128)(2,1)} custom-call(s32[16]{0:T(128)} %and_select_fusion.2.order_ref, bf16[8,256,384]{2,1,0:T(8,128)(2,1)} %all-to-all-done.load_ref), custom_call_target="tpu_custom_call" | custom-call | flops 4294967296 | bytes 3145728 | tf_op jit(solution)/shard_map/attention_forward/pallas_call | solution.py:541
  132.5 3.9 collective-permute-done.12.refs_3_
  136.4 2.2 copy.24
  138.6 6.1 all-to-all-start.1
  145.8 13.9 %collective-permute-done.14.refs_4_ = bf16[3,384,512]{2,1,0:T(8,128)(2,1)} collective-permute-done((bf16[3,384,512]{2,1,0:T(8,128)(2,1)}, bf16[3,384,512]{2,1,0:T(8,128)(2,1)}, u32[]{:S(2)}, u32[]{:S(2)}) %collective-permute-start.14) | collective-permute-done | bytes 1179680 | tf_op jit(solution)/shard_map/ppermute | solution.py:45
  159.7 3.5 pad_maximum_fusion.grad_ref
  163.2 2.2 copy.25.mixed_ref
  166.4 6.8 attention_output.1
  174.2 14.2 %collective-permute-done.21.refs_5_ = bf16[3,384,512]{2,1,0:T(8,128)(2,1)} collective-permute-done((bf16[3,384,512]{2,1,0:T(8,128)(2,1)}, bf16[3,384,512]{2,1,0:T(8,128)(2,1)}, u32[]{:S(2)}, u32[]{:S(2)}) %collective-permute-start.21) | collective-permute-done | bytes 1179680 | tf_op jit(solution)/shard_map/ppermute | solution.py:45
  188.4 5.1 collective-permute-done.20
  200.0 28.0 %feed_forward.1 = (bf16[1024,1536]{1,0:T(8,128)(2,1)}, bf16[1024,1536]{1,0:T(8,128)(2,1)}, bf16[1024,1024]{1,0:T(8,128)(2,1)}, bf16[1024,1024]{1,0:T(8,128)(2,1)}, bf16[1024,1024]{1,0:T(8,128)(2,1)}) custom-call(s32[3]{0:T(128)} %pad_add_fusion.code_ref, bf16[1024,1536]{1,0:T(8,128)(2,1)} %copy-done.1, bf16[1024,1536]{1,0:T(8,128)(2,1)} %pad_maximum_fusion.grad_ref, ...), custom_call_target="tpu_custom_call" | custom-call | flops 19327352832 | bytes 22020096 | tf_op jit(solution)/shard_map/feed_forward/pallas_call | solution.py:387
  229.8 3.3 collective-permute-done.24
  240.2 19.2 %unit_grads.1 = bf16[12288,384]{1,0:T(8,128)(2,1)} custom-call(bf16[1024,1536]{1,0:T(8,128)(2,1)S(1)} %copy-done.2, bf16[1024,1536]{1,0:T(8,128)(2,1)S(1)} %copy-done, bf16[1024,1024]{1,0:T(8,128)(2,1)S(1)} %copy-done.4, bf16[1024,1024]{1,0:T(8,128)(2,1)S(1)} %copy-done.5, bf16[1024,1024]{1,0:T(8,128)(2,1)S(1)} %copy-done.3), custom_call_target="tpu_custom_call" | custom-call | flops 99999997952 | tf_op jit(solution)/shard_map/unit_grads/pallas_call | solution.py:827
  259.4 2.6 convert_add_fusion.grad_ref
  262.0 7.8 %attention_output_back.1 = (f32[256,1536]{1,0:T(8,128)}, bf16[256,1536]{1,0:T(8,128)(2,1)}, bf16[8,256,192]{2,1,0:T(8,128)(2,1)}, f32[1,1536]{1,0:T(1,128)}) custom-call(s32[3]{0:T(128)} %pad_add_fusion.code_ref, f32[256,1536]{1,0:T(8,128)} %get-tuple-element.84.middle_ref, f32[256,1536]{1,0:T(8,128)} %convert_add_fusion.grad_ref, ...), custom_call_target="tpu_custom_call" | custom-call | flops 1207959552 | bytes 11808768 | tf_op jit(solution)/shard_map/attention_output_back/pallas_call | solution.py:153
  269.8 2.2 copy.26
  272.0 4.3 all-to-all-start.2
  277.8 39.6 %all-to-all-done.2 = bf16[8,256,192]{1,2,0:T(8,128)(2,1)S(1)} async-done(((bf16[8,256,192]{1,2,0:T(8,128)(2,1)}), bf16[8,256,192]{1,2,0:T(8,128)(2,1)S(1)}, u32[]{:S(2)}, u32[]{:S(2)}) %all-to-all-start.2) | async-done | bytes 786464 | tf_op jit(solution)/shard_map/all_to_all | solution.py:924
  318.6 24.1 %attention_backward.1 = bf16[8,256,384]{2,1,0:T(8,128)(2,1)} custom-call(s32[16]{0:T(128)} %and_select_fusion.2.order_ref, bf16[8,256,384]{2,1,0:T(8,128)(2,1)} %all-to-all-done.load_ref, bf16[8,256,192]{2,1,0:T(8,128)(2,1)} %copy.27.grad_ref), custom_call_target="tpu_custom_call" | custom-call | flops 10737418240 | bytes 6291456 | tf_op jit(solution)/shard_map/attention_backward/pallas_call | solution.py:541
  342.7 4.1 all-to-all-start.3
  346.8 2.8 pad_maximum_fusion.7
  353.9 16.1 %collective-permute-done.32 = bf16[256,1536]{1,0:T(8,128)(2,1)} collective-permute-done((bf16[256,1536]{1,0:T(8,128)(2,1)S(1)}, bf16[256,1536]{1,0:T(8,128)(2,1)}, u32[]{:S(2)}, u32[]{:S(2)}) %collective-permute-start.32) | collective-permute-done | bytes 786464 | tf_op jit(solution)/shard_map/ppermute | solution.py:45
  373.4 4.6 collective-permute-done.39
  378.0 3.8 fusion.11
  383.1 2.0 collective-permute-start.42
  385.1 13.3 %all-to-all-done.3.load_ref = bf16[8,256,384]{2,1,0:T(8,128)(2,1)S(1)} async-done(((bf16[8,256,384]{2,1,0:T(8,128)(2,1)}), bf16[8,256,384]{2,1,0:T(8,128)(2,1)S(1)}, u32[]{:S(2)}, u32[]{:S(2)}) %all-to-all-start.3) | async-done | bytes 1572896 | tf_op jit(solution)/shard_map/all_to_all | solution.py:927
  399.5 13.3 %query_key_value_back.1 = (bf16[4,256,768]{2,1,0:T(8,128)(2,1)}, f32[256,1536]{1,0:T(8,128)}, f32[1,1536]{1,0:T(1,128)}) custom-call(s32[3]{0:T(128)} %pad_add_fusion.code_ref, bf16[8,256,384]{2,1,0:T(8,128)(2,1)} %copy-done.11, bf16[256,1536]{1,0:T(8,128)(2,1)} %bitcast.69, f32[256,1536]{1,0:T(8,128)} %get-tuple-element.98.grad_middle_ref, ...), custom_call_target="tpu_custom_call" | custom-call | flops 2415919104 | bytes 16723968 | tf_op jit(solution)/shard_map/query_key_value_back/pallas_call | solution.py:153
  416.6 9.0 %collective-permute-done.36 = bf16[256,768]{1,0:T(8,128)(2,1)S(1)} collective-permute-done((bf16[256,768]{1,0:T(8,128)(2,1)S(1)}, bf16[256,768]{1,0:T(8,128)(2,1)S(1)}, u32[]{:S(2)}, u32[]{:S(2)}) %collective-permute-start.36) | collective-permute-done | bytes 393248 | tf_op jit(solution)/shard_map/ppermute | solution.py:45
  425.5 8.7 %collective-permute-done.34 = bf16[256,768]{1,0:T(8,128)(2,1)S(1)} collective-permute-done((bf16[256,768]{1,0:T(8,128)(2,1)S(1)}, bf16[256,768]{1,0:T(8,128)(2,1)S(1)}, u32[]{:S(2)}, u32[]{:S(2)}) %collective-permute-start.34) | collective-permute-done | bytes 393248 | tf_op jit(solution)/shard_map/ppermute | solution.py:45
  435.4 4.3 convolution_convert_fusion
  443.1 2.0 collective-permute-start.45
  445.1 2.3 collective-permute-start.46
  447.4 11.3 %collective-permute-done.44 = bf16[4,48,384]{2,1,0:T(8,128)(2,1)S(1)} collective-permute-done((bf16[4,48,384]{2,1,0:T(8,128)(2,1)S(1)}, bf16[4,48,384]{2,1,0:T(8,128)(2,1)S(1)}, u32[]{:S(2)}, u32[]{:S(2)}) %collective-permute-start.44) | collective-permute-done | bytes 147488 | tf_op jit(solution)/shard_map/ppermute | solution.py:45
  458.7 6.3 collective-permute-done.45
  466.4 4.1 collective-permute-done.43
  472.1 13.4 %reduce-scatter.2.cloned.1.call-done = bf16[1536,384]{1,0:T(8,128)(2,1)} async-done(((bf16[12288,384]{1,0:T(8,128)(2,1)}), bf16[1536,384]{1,0:T(8,128)(2,1)}) %reduce-scatter.2.cloned.1.call-update) | async-done | bytes 1179664 | tf_op jit(solution)/shard_map/reduce_scatter | solution.py:921
  490.6 5.5 collective-permute-done.53
  498.1 4.4 collective-permute-done.52
  503.1 9.3 %collective-permute-done.49 = bf16[4,48,768]{2,1,0:T(8,128)(2,1)S(1)} collective-permute-done((bf16[4,48,768]{2,1,0:T(8,128)(2,1)S(1)}, bf16[4,48,768]{2,1,0:T(8,128)(2,1)S(1)}, u32[]{:S(2)}, u32[]{:S(2)}) %collective-permute-start.49) | collective-permute-done | bytes 294944 | tf_op jit(solution)/shard_map/ppermute | solution.py:45
  514.5 3.4 collective-permute-done.56
  518.0 2.4 collective-permute-done.55
  520.6 6.2 collective-permute-start.59
  527.0 18.0 %collective-permute-done.59.refs_1_ = bf16[4,272,384]{2,1,0:T(8,128)(2,1)S(1)} collective-permute-done((bf16[4,272,384]{2,1,0:T(8,128)(2,1)S(1)}, bf16[4,272,384]{2,1,0:T(8,128)(2,1)S(1)}, u32[]{:S(2)}, u32[]{:S(2)}) %collective-permute-start.59) | collective-permute-done | bytes 835616 | tf_op jit(solution)/shard_map/ppermute | solution.py:695
  545.0 2.5 collective-permute-start.60
  547.5 18.1 %collective-permute-done.60.refs_2_ = bf16[4,272,384]{2,1,0:T(8,128)(2,1)S(1)} collective-permute-done((bf16[4,272,384]{2,1,0:T(8,128)(2,1)S(1)}, bf16[4,272,384]{2,1,0:T(8,128)(2,1)S(1)}, u32[]{:S(2)}, u32[]{:S(2)}) %collective-permute-start.60) | collective-permute-done | bytes 835616 | tf_op jit(solution)/shard_map/ppermute | solution.py:695
  568.2 16.8 %collective-permute-done.61.refs_3_ = bf16[4,272,384]{2,1,0:T(8,128)(2,1)S(1)} collective-permute-done((bf16[4,272,384]{2,1,0:T(8,128)(2,1)S(1)}, bf16[4,272,384]{2,1,0:T(8,128)(2,1)S(1)}, u32[]{:S(2)}, u32[]{:S(2)}) %collective-permute-start.61) | collective-permute-done | bytes 835616 | tf_op jit(solution)/shard_map/ppermute | solution.py:695
  587.1 16.7 %collective-permute-done.62.refs_4_ = bf16[4,272,384]{2,1,0:T(8,128)(2,1)S(1)} collective-permute-done((bf16[4,272,384]{2,1,0:T(8,128)(2,1)S(1)}, bf16[4,272,384]{2,1,0:T(8,128)(2,1)S(1)}, u32[]{:S(2)}, u32[]{:S(2)}) %collective-permute-start.62) | collective-permute-done | bytes 835616 | tf_op jit(solution)/shard_map/ppermute | solution.py:695
  608.2 14.2 %collective-permute-done.63.refs_5_ = bf16[4,272,384]{2,1,0:T(8,128)(2,1)S(1)} collective-permute-done((bf16[4,272,384]{2,1,0:T(8,128)(2,1)S(1)}, bf16[4,272,384]{2,1,0:T(8,128)(2,1)S(1)}, u32[]{:S(2)}, u32[]{:S(2)}) %collective-permute-start.63) | collective-permute-done | bytes 835616 | tf_op jit(solution)/shard_map/ppermute | solution.py:695
  627.0 2.0 collective-permute-done.30
  632.4 7.1 %collective-permute-done.31 = f32[2,384]{1,0:T(2,128)S(1)} collective-permute-done((f32[2,384]{1,0:T(2,128)S(1)}, f32[2,384]{1,0:T(2,128)S(1)}, u32[]{:S(2)}, u32[]{:S(2)}) %collective-permute-start.31) | collective-permute-done | bytes 3104 | tf_op jit(solution)/shard_map/ppermute | solution.py:45
  639.6 4.4 collective-permute-start.57
  646.0 3.0 fusion.14
  649.6 8.9 %collective-permute-done.72.refs_15_ = bf16[4,256,384]{2,1,0:T(8,128)(2,1)S(1)} collective-permute-done((bf16[4,256,384]{2,1,0:T(8,128)(2,1)}, bf16[4,256,384]{2,1,0:T(8,128)(2,1)S(1)}, u32[]{:S(2)}, u32[]{:S(2)}) %collective-permute-start.72) | collective-permute-done | bytes 786464 | tf_op jit(solution)/shard_map/ppermute | solution.py:695
  660.5 15.3 %deal_gradients.1 = (f32[384,4096]{1,0:T(8,128)}, f32[384,4096]{1,0:T(8,128)}, f32[384,4096]{1,0:T(8,128)}, f32[384,1536]{1,0:T(8,128)}, f32[384,1536]{1,0:T(8,1...) custom-call(s32[17]{0:T(128)} %pad_add_fusion.1.code_ref, bf16[4,272,384]{2,1,0:T(8,128)(2,1)} %copy-done.14, ...), custom_call_target="tpu_custom_call" | custom-call | tf_op jit(solution)/shard_map/deal_gradients/pallas_call | solution.py:776
  (302 shorter events, 109.8 us)
Async XLA Ops:
  8.9 54.2 %collective-permute-start.3 = (bf16[384,3072]{1,0:T(8,128)(2,1)S(1)}, bf16[384,3072]{1,0:T(8,128)(2,1)}, u32[]{:S(2)}, u32[]{:S(2)}) collective-permute-start(bf16[384,3072]{1,0:T(8,128)(2,1)S(1)} %constant_dynamic-update-slice_fusion.refs_4_), channel_id=1, source_target_pairs={{0,1},{1,0},{2,3},{3,2},{4,5},{5,4},{6,7},{7,6},{8,9},{9,8},{10,11... | collective-permute-start | bytes 7077896 | tf_op jit(solution)/shard_map/ppermute | solution.py:45
  10.5 20.8 %collective-permute-start.4 = (bf16[384,1024]{1,0:T(8,128)(2,1)}, bf16[384,1024]{1,0:T(8,128)(2,1)}, u32[]{:S(2)}, u32[]{:S(2)}) collective-permute-start(bf16[384,1024]{1,0:T(8,128)(2,1)} %constant_dynamic-slice_fusion.24), channel_id=1, source_target_pairs={{0,2},{1,3},{2,0},{3,1},{4,6},{5,7},{6,4},{7,5},{8,10},{9,11},{10,... | collective-permute-start | bytes 2359304 | tf_op jit(solution)/shard_map/ppermute | solution.py:45
  31.4 19.6 %collective-permute-start.5 = (bf16[384,1024]{1,0:T(8,128)(2,1)}, bf16[384,1024]{1,0:T(8,128)(2,1)}, u32[]{:S(2)}, u32[]{:S(2)}) collective-permute-start(bf16[384,1024]{1,0:T(8,128)(2,1)} %collective-permute-done.4.refs_6_), channel_id=1, source_target_pairs={{0,4},{4,0},{8,12},{12,8},{16,20},{20,16},{24,28},{28,24},{1,5},{5... | collective-permute-start | bytes 2359304 | tf_op jit(solution)/shard_map/ppermute | solution.py:45
  33.1 19.0 %collective-permute-start.6 = (bf16[384,1024]{1,0:T(8,128)(2,1)}, bf16[384,1024]{1,0:T(8,128)(2,1)}, u32[]{:S(2)}, u32[]{:S(2)}) collective-permute-start(bf16[384,1024]{1,0:T(8,128)(2,1)} %pad_maximum_fusion.12), channel_id=1, source_target_pairs={{0,2},{1,3},{2,0},{3,1},{4,6},{5,7},{6,4},{7,5},{8,10},{9,11},{10,... | collective-permute-start | bytes 2359304 | tf_op jit(solution)/shard_map/ppermute | solution.py:45
  34.7 18.3 %collective-permute-start = (bf16[2,384]{1,0:T(2,128)(2,1)S(1)}, bf16[2,384]{1,0:T(2,128)(2,1)S(1)}, u32[]{:S(2)}, u32[]{:S(2)}) collective-permute-start(bf16[2,384]{1,0:T(2,128)(2,1)S(1)} %pad_maximum_fusion.17.refs_0_), channel_id=1, source_target_pairs={{0,1},{1,0},{2,3},{3,2},{4,5},{5,4},{6,7},{7,6},{8,9},{9,8},{10,11... | collective-permute-start | bytes 4616 | tf_op jit(solution)/shard_map/ppermute | solution.py:45
  34.8 28.4 %collective-permute-start.7 = (bf16[384,1024]{1,0:T(8,128)(2,1)}, bf16[384,1024]{1,0:T(8,128)(2,1)}, u32[]{:S(2)}, u32[]{:S(2)}) collective-permute-start(bf16[384,1024]{1,0:T(8,128)(2,1)} %collective-permute-done.4.refs_6_), channel_id=1, source_target_pairs={{0,1},{1,0},{2,3},{3,2},{4,5},{5,4},{6,7},{7,6},{8,9},{9,8},{10,11... | collective-permute-start | bytes 2359304 | tf_op jit(solution)/shard_map/ppermute | solution.py:45
  51.0 12.2 %collective-permute-start.8 = (bf16[384,1024]{1,0:T(8,128)(2,1)}, bf16[384,1024]{1,0:T(8,128)(2,1)}, u32[]{:S(2)}, u32[]{:S(2)}) collective-permute-start(bf16[384,1024]{1,0:T(8,128)(2,1)} %collective-permute-done.5.refs_7_), channel_id=1, source_target_pairs={{0,1},{1,0},{2,3},{3,2},{4,5},{5,4},{6,7},{7,6},{8,9},{9,8},{10,11... | collective-permute-start | bytes 2359304 | tf_op jit(solution)/shard_map/ppermute | solution.py:45
  52.1 11.0 %collective-permute-start.9 = (bf16[384,1024]{1,0:T(8,128)(2,1)}, bf16[384,1024]{1,0:T(8,128)(2,1)}, u32[]{:S(2)}, u32[]{:S(2)}) collective-permute-start(bf16[384,1024]{1,0:T(8,128)(2,1)} %collective-permute-done.6.refs_8_), channel_id=1, source_target_pairs={{0,1},{1,0},{2,3},{3,2},{4,5},{5,4},{6,7},{7,6},{8,9},{9,8},{10,11... | collective-permute-start | bytes 2359304 | tf_op jit(solution)/shard_map/ppermute | solution.py:45
  59.6 15.6 %collective-permute-start.10 = (bf16[384,768]{1,0:T(8,128)(2,1)}, bf16[384,768]{1,0:T(8,128)(2,1)S(1)}, u32[]{:S(2)}, u32[]{:S(2)}) collective-permute-start(bf16[384,768]{1,0:T(8,128)(2,1)} %constant_dynamic-slice_fusion.23), channel_id=1, source_target_pairs={{0,2},{1,3},{2,0},{3,1},{4,6},{5,7},{6,4},{7,5},{8,10},{9,11},{10,... | collective-permute-start | bytes 1769480 | tf_op jit(solution)/shard_map/ppermute | solution.py:45
  76.0 42.1 %all-to-all-start = ((bf16[8,256,384]{2,1,0:T(8,128)(2,1)}), bf16[8,256,384]{2,1,0:T(8,128)(2,1)}, u32[]{:S(2)}, u32[]{:S(2)}) async-start(bf16[8,256,384]{2,1,0:T(8,128)(2,1)} %get-tuple-element.77), calls=%async_computation | async-start | bytes 3145728 | tf_op jit(solution)/shard_map/all_to_all | solution.py:890
  81.5 29.3 %collective-permute-start.11 = (bf16[3,384,512]{2,1,0:T(8,128)(2,1)}, bf16[3,384,512]{2,1,0:T(8,128)(2,1)}, u32[]{:S(2)}, u32[]{:S(2)}) collective-permute-start(bf16[3,384,512]{2,1,0:T(8,128)(2,1)} %pad_maximum_fusion.8), channel_id=1, source_target_pairs={{0,2},{1,3},{2,0},{3,1},{4,6},{5,7},{6,4},{7,5},{8,10},{9,11},{10,... | collective-permute-start | bytes 3538952 | tf_op jit(solution)/shard_map/ppermute | solution.py:45
  82.0 48.3 %collective-permute-start.15 = (bf16[256,1536]{1,0:T(8,128)(2,1)S(1)}, bf16[256,1536]{1,0:T(8,128)(2,1)S(1)}, u32[]{:S(2)}, u32[]{:S(2)}) collective-permute-start(bf16[256,1536]{1,0:T(8,128)(2,1)S(1)} %bitcast.64), channel_id=1, source_target_pairs={{0,2},{1,3},{2,0},{3,1},{4,6},{5,7},{6,4},{7,5},{8,10},{9,11},{10,... | collective-permute-start | bytes 2359304 | tf_op jit(solution)/shard_map/ppermute | solution.py:45
  84.9 47.6 %collective-permute-start.13 = (bf16[384,768]{1,0:T(8,128)(2,1)S(1)}, bf16[384,768]{1,0:T(8,128)(2,1)}, u32[]{:S(2)}, u32[]{:S(2)}) collective-permute-start(bf16[384,768]{1,0:T(8,128)(2,1)S(1)} %copy-done.23), channel_id=1, source_target_pairs={{0,8},{4,12},{8,0},{12,4},{16,24},{20,28},{24,16},{28,20},{1,9},{5... | collective-permute-start | bytes 1769480 | tf_op jit(solution)/shard_map/ppermute | solution.py:45
  110.8 25.7 %collective-permute-start.12 = (bf16[3,384,512]{2,1,0:T(8,128)(2,1)}, bf16[3,384,512]{2,1,0:T(8,128)(2,1)}, u32[]{:S(2)}, u32[]{:S(2)}) collective-permute-start(bf16[3,384,512]{2,1,0:T(8,128)(2,1)} %collective-permute-done.11.refs_2_), channel_id=1, source_target_pairs={{0,4},{4,0},{8,12},{12,8},{16,20},{20,16},{24,28},{28,24},{1,5},{5... | collective-permute-start | bytes 3538952 | tf_op jit(solution)/shard_map/ppermute | solution.py:45
  131.8 27.9 %collective-permute-start.16 = (bf16[512,1536]{1,0:T(8,128)(2,1)}, bf16[512,1536]{1,0:T(8,128)(2,1)}, u32[]{:S(2)}, u32[]{:S(2)}) collective-permute-start(bf16[512,1536]{1,0:T(8,128)(2,1)} %pad_maximum_fusion.3), channel_id=1, source_target_pairs={{0,1},{1,0},{2,3},{3,2},{4,5},{5,4},{6,7},{7,6},{8,9},{9,8},{10,11... | collective-permute-start | bytes 4718600 | tf_op jit(solution)/shard_map/ppermute | solution.py:45
  131.8 27.9 %collective-permute-start.14 = (bf16[3,384,512]{2,1,0:T(8,128)(2,1)}, bf16[3,384,512]{2,1,0:T(8,128)(2,1)}, u32[]{:S(2)}, u32[]{:S(2)}) collective-permute-start(bf16[3,384,512]{2,1,0:T(8,128)(2,1)} %pad_maximum_fusion.9), channel_id=1, source_target_pairs={{0,3},{1,2},{2,1},{3,0},{4,7},{5,6},{6,5},{7,4},{8,11},{9,10},{10,... | collective-permute-start | bytes 3538952 | tf_op jit(solution)/shard_map/ppermute | solution.py:45
  138.6 24.6 %all-to-all-start.1 = ((bf16[8,256,192]{1,2,0:T(8,128)(2,1)}), bf16[8,256,192]{1,2,0:T(8,128)(2,1)}, u32[]{:S(2)}, u32[]{:S(2)}) async-start(bf16[8,256,192]{1,2,0:T(8,128)(2,1)} %copy.24), calls=%async_computation.1 | async-start | bytes 1572864 | tf_op jit(solution)/shard_map/all_to_all | solution.py:894
  144.7 340.7 %reduce-scatter.2.cloned.1.call-start = ((), (), s32[]{:S(2)}) async-start(), calls=%async_computation.5 | async-start | bytes 10616832 | tf_op jit(solution)/shard_map/reduce_scatter | solution.py:921
  145.2 20.2 %collective-permute-start.17 = (bf16[384,1536]{1,0:T(8,128)(2,1)S(1)}, bf16[384,1536]{1,0:T(8,128)(2,1)S(1)}, u32[]{:S(2)}, u32[]{:S(2)}) collective-permute-start(bf16[384,1536]{1,0:T(8,128)(2,1)S(1)} %copy-done.8), channel_id=1, source_target_pairs={{0,1},{1,0},{2,3},{3,2},{4,5},{5,4},{6,7},{7,6},{8,9},{9,8},{10,11... | collective-permute-start | bytes 3538952 | tf_op jit(solution)/shard_map/ppermute | solution.py:45
  145.3 20.2 %collective-permute-start.18 = (bf16[384,768]{1,0:T(8,128)(2,1)}, bf16[384,768]{1,0:T(8,128)(2,1)}, u32[]{:S(2)}, u32[]{:S(2)}) collective-permute-start(bf16[384,768]{1,0:T(8,128)(2,1)} %copy-done.22), channel_id=1, source_target_pairs={{0,1},{1,0},{2,3},{3,2},{4,5},{5,4},{6,7},{7,6},{8,9},{9,8},{10,11... | collective-permute-start | bytes 1769480 | tf_op jit(solution)/shard_map/ppermute | solution.py:45
  145.8 19.7 %collective-permute-start.19 = (bf16[384,768]{1,0:T(8,128)(2,1)}, bf16[384,768]{1,0:T(8,128)(2,1)}, u32[]{:S(2)}, u32[]{:S(2)}) collective-permute-start(bf16[384,768]{1,0:T(8,128)(2,1)} %collective-permute-done.13.refs_7_), channel_id=1, source_target_pairs={{0,1},{1,0},{2,3},{3,2},{4,5},{5,4},{6,7},{7,6},{8,9},{9,8},{10,11... | collective-permute-start | bytes 1769480 | tf_op jit(solution)/shard_map/ppermute | solution.py:45
  159.7 28.7 %collective-permute-start.21 = (bf16[3,384,512]{2,1,0:T(8,128)(2,1)}, bf16[3,384,512]{2,1,0:T(8,128)(2,1)}, u32[]{:S(2)}, u32[]{:S(2)}) collective-permute-start(bf16[3,384,512]{2,1,0:T(8,128)(2,1)} %collective-permute-done.14.refs_4_), channel_id=1, source_target_pairs={{0,8},{4,12},{8,0},{12,4},{16,24},{20,28},{24,16},{28,20},{1,9},{5... | collective-permute-start | bytes 3538952 | tf_op jit(solution)/shard_map/ppermute | solution.py:45
  173.3 20.2 %collective-permute-start.20 = (bf16[256,1536]{1,0:T(8,128)(2,1)}, bf16[256,1536]{1,0:T(8,128)(2,1)S(1)}, u32[]{:S(2)}, u32[]{:S(2)}) collective-permute-start(bf16[256,1536]{1,0:T(8,128)(2,1)} %get-tuple-element.85), channel_id=1, source_target_pairs={{0,2},{1,3},{2,0},{3,1},{4,6},{5,7},{6,4},{7,5},{8,10},{9,11},{10,... | collective-permute-start | bytes 2359304 | tf_op jit(solution)/shard_map/ppermute | solution.py:45
  174.0 24.3 %collective-permute-start.23 = (bf16[3,384,1024]{2,1,0:T(8,128)(2,1)S(1)}, bf16[3,384,1024]{2,1,0:T(8,128)(2,1)}, u32[]{:S(2)}, u32[]{:S(2)}) collective-permute-start(bf16[3,384,1024]{2,1,0:T(8,128)(2,1)S(1)} %copy-done.24), channel_id=1, source_target_pairs={{0,1},{1,0},{2,3},{3,2},{4,5},{5,4},{6,7},{7,6},{8,9},{9,8},{10,11... | collective-permute-start | bytes 7077896 | tf_op jit(solution)/shard_map/ppermute | solution.py:45
  234.4 25.0 %collective-permute-start.25 = (bf16[256,1536]{1,0:T(8,128)(2,1)S(1)}, bf16[256,1536]{1,0:T(8,128)(2,1)S(1)}, u32[]{:S(2)}, u32[]{:S(2)}) collective-permute-start(bf16[256,1536]{1,0:T(8,128)(2,1)S(1)} %add_convert_fusion.3), channel_id=1, source_target_pairs={{0,2},{1,3},{2,0},{3,1},{4,6},{5,7},{6,4},{7,5},{8,10},{9,11},{10,... | collective-permute-start | bytes 2359304 | tf_op jit(solution)/shard_map/ppermute | solution.py:45
  272.0 45.3 %all-to-all-start.2 = ((bf16[8,256,192]{1,2,0:T(8,128)(2,1)}), bf16[8,256,192]{1,2,0:T(8,128)(2,1)S(1)}, u32[]{:S(2)}, u32[]{:S(2)}) async-start(bf16[8,256,192]{1,2,0:T(8,128)(2,1)} %copy.26), calls=%async_computation.2 | async-start | bytes 1572864 | tf_op jit(solution)/shard_map/all_to_all | solution.py:924
  276.3 70.4 %collective-permute-start.37 = (bf16[256,1536]{1,0:T(8,128)(2,1)}, bf16[256,1536]{1,0:T(8,128)(2,1)}, u32[]{:S(2)}, u32[]{:S(2)}) collective-permute-start(bf16[256,1536]{1,0:T(8,128)(2,1)} %get-tuple-element.103), channel_id=1, source_target_pairs={{0,2},{1,3},{2,0},{3,1},{4,6},{5,7},{6,4},{7,5},{8,10},{9,11},{10,... | collective-permute-start | bytes 2359304 | tf_op jit(solution)/shard_map/ppermute | solution.py:45
  342.7 55.7 %all-to-all-start.3 = ((bf16[8,256,384]{2,1,0:T(8,128)(2,1)}), bf16[8,256,384]{2,1,0:T(8,128)(2,1)S(1)}, u32[]{:S(2)}, u32[]{:S(2)}) async-start(bf16[8,256,384]{2,1,0:T(8,128)(2,1)} %attention_backward.1), calls=%async_computation.3 | async-start | bytes 3145728 | tf_op jit(solution)/shard_map/all_to_all | solution.py:927
  349.5 28.5 %collective-permute-start.38 = (bf16[512,1536]{1,0:T(8,128)(2,1)}, bf16[512,1536]{1,0:T(8,128)(2,1)}, u32[]{:S(2)}, u32[]{:S(2)}) collective-permute-start(bf16[512,1536]{1,0:T(8,128)(2,1)} %pad_maximum_fusion.7), channel_id=1, source_target_pairs={{0,1},{1,0},{2,3},{3,2},{4,5},{5,4},{6,7},{7,6},{8,9},{9,8},{10,11... | collective-permute-start | bytes 4718600 | tf_op jit(solution)/shard_map/ppermute | solution.py:45
  349.5 20.4 %collective-permute-start.32 = (bf16[256,1536]{1,0:T(8,128)(2,1)S(1)}, bf16[256,1536]{1,0:T(8,128)(2,1)}, u32[]{:S(2)}, u32[]{:S(2)}) collective-permute-start(bf16[256,1536]{1,0:T(8,128)(2,1)S(1)} %copy-done.45), channel_id=1, source_target_pairs={{0,2},{1,3},{2,0},{3,1},{4,6},{5,7},{6,4},{7,5},{8,10},{9,11},{10,... | collective-permute-start | bytes 2359304 | tf_op jit(solution)/shard_map/ppermute | solution.py:45
  351.8 21.7 %collective-permute-start.41 = (bf16[256,384]{1,0:T(8,128)(2,1)}, bf16[256,384]{1,0:T(8,128)(2,1)}, u32[]{:S(2)}, u32[]{:S(2)}) collective-permute-start(bf16[256,384]{1,0:T(8,128)(2,1)} %get-tuple-element.163), channel_id=1, source_target_pairs={{0,3},{1,2},{2,1},{3,0},{4,7},{5,6},{6,5},{7,4},{8,11},{9,10},{10,... | collective-permute-start | bytes 589832 | tf_op jit(solution)/shard_map/ppermute | solution.py:45
  352.2 21.2 %collective-permute-start.40 = (bf16[256,384]{1,0:T(8,128)(2,1)}, bf16[256,384]{1,0:T(8,128)(2,1)}, u32[]{:S(2)}, u32[]{:S(2)}) collective-permute-start(bf16[256,384]{1,0:T(8,128)(2,1)} %get-tuple-element.164), channel_id=1, source_target_pairs={{0,1},{1,0},{2,3},{3,2},{4,5},{5,4},{6,7},{7,6},{8,9},{9,8},{10,11... | collective-permute-start | bytes 589832 | tf_op jit(solution)/shard_map/ppermute | solution.py:45
  352.5 25.5 %collective-permute-start.39 = (bf16[256,384]{1,0:T(8,128)(2,1)S(1)}, bf16[256,384]{1,0:T(8,128)(2,1)}, u32[]{:S(2)}, u32[]{:S(2)}) collective-permute-start(bf16[256,384]{1,0:T(8,128)(2,1)S(1)} %get-tuple-element.165), channel_id=1, source_target_pairs={{0,2},{1,3},{2,0},{3,1},{4,6},{5,7},{6,4},{7,5},{8,10},{9,11},{10,... | collective-permute-start | bytes 589832 | tf_op jit(solution)/shard_map/ppermute | solution.py:45
  371.5 62.9 %collective-permute-start.33 = (bf16[512,1536]{1,0:T(8,128)(2,1)S(1)}, bf16[512,1536]{1,0:T(8,128)(2,1)}, u32[]{:S(2)}, u32[]{:S(2)}) collective-permute-start(bf16[512,1536]{1,0:T(8,128)(2,1)S(1)} %pad_maximum_fusion.5), channel_id=1, source_target_pairs={{0,1},{1,0},{2,3},{3,2},{4,5},{5,4},{6,7},{7,6},{8,9},{9,8},{10,11... | collective-permute-start | bytes 4718600 | tf_op jit(solution)/shard_map/ppermute | solution.py:45
  383.1 51.3 %collective-permute-start.42 = (bf16[4,192,384]{2,1,0:T(8,128)(2,1)}, bf16[4,192,384]{2,1,0:T(8,128)(2,1)}, u32[]{:S(2)}, u32[]{:S(2)}) collective-permute-start(bf16[4,192,384]{2,1,0:T(8,128)(2,1)} %constant_dynamic-slice_fusion.14), channel_id=1, source_target_pairs={{0,4},{4,0},{8,12},{12,8},{16,20},{20,16},{24,28},{28,24},{1,5},{5... | collective-permute-start | bytes 1769480 | tf_op jit(solution)/shard_map/ppermute | solution.py:45
  414.3 11.2 %collective-permute-start.36 = (bf16[256,768]{1,0:T(8,128)(2,1)S(1)}, bf16[256,768]{1,0:T(8,128)(2,1)S(1)}, u32[]{:S(2)}, u32[]{:S(2)}) collective-permute-start(bf16[256,768]{1,0:T(8,128)(2,1)S(1)} %get-tuple-element.152), channel_id=1, source_target_pairs={{0,3},{1,2},{2,1},{3,0},{4,7},{5,6},{6,5},{7,4},{8,11},{9,10},{10,... | collective-permute-start | bytes 1179656 | tf_op jit(solution)/shard_map/ppermute | solution.py:45
  415.8 9.8 %collective-permute-start.35 = (bf16[256,768]{1,0:T(8,128)(2,1)S(1)}, bf16[256,768]{1,0:T(8,128)(2,1)S(1)}, u32[]{:S(2)}, u32[]{:S(2)}) collective-permute-start(bf16[256,768]{1,0:T(8,128)(2,1)S(1)} %get-tuple-element.153), channel_id=1, source_target_pairs={{0,1},{1,0},{2,3},{3,2},{4,5},{5,4},{6,7},{7,6},{8,9},{9,8},{10,11... | collective-permute-start | bytes 1179656 | tf_op jit(solution)/shard_map/ppermute | solution.py:45
  416.1 18.2 %collective-permute-start.34 = (bf16[256,768]{1,0:T(8,128)(2,1)S(1)}, bf16[256,768]{1,0:T(8,128)(2,1)S(1)}, u32[]{:S(2)}, u32[]{:S(2)}) collective-permute-start(bf16[256,768]{1,0:T(8,128)(2,1)S(1)} %get-tuple-element.154), channel_id=1, source_target_pairs={{0,2},{1,3},{2,0},{3,1},{4,6},{5,7},{6,4},{7,5},{8,10},{9,11},{10,... | collective-permute-start | bytes 1179656 | tf_op jit(solution)/shard_map/ppermute | solution.py:45
  439.8 30.7 %collective-permute-start.43 = (bf16[4,192,768]{2,1,0:T(8,128)(2,1)S(1)}, bf16[4,192,768]{2,1,0:T(8,128)(2,1)}, u32[]{:S(2)}, u32[]{:S(2)}) collective-permute-start(bf16[4,192,768]{2,1,0:T(8,128)(2,1)S(1)} %constant_dynamic-slice_fusion.13), channel_id=1, source_target_pairs={{0,4},{4,0},{8,12},{12,8},{16,20},{20,16},{24,28},{28,24},{1,5},{5... | collective-permute-start | bytes 3538952 | tf_op jit(solution)/shard_map/ppermute | solution.py:45
  443.0 15.7 %collective-permute-start.44 = (bf16[4,48,384]{2,1,0:T(8,128)(2,1)S(1)}, bf16[4,48,384]{2,1,0:T(8,128)(2,1)S(1)}, u32[]{:S(2)}, u32[]{:S(2)}) collective-permute-start(bf16[4,48,384]{2,1,0:T(8,128)(2,1)S(1)} %get-tuple-element.168), channel_id=1, source_target_pairs={{0,8},{4,12},{8,0},{12,4},{16,24},{20,28},{24,16},{28,20},{1,9},{5... | collective-permute-start | bytes 442376 | tf_op jit(solution)/shard_map/ppermute | solution.py:45
  443.1 22.0 %collective-permute-start.45 = (bf16[4,48,384]{2,1,0:T(8,128)(2,1)S(1)}, bf16[4,48,384]{2,1,0:T(8,128)(2,1)S(1)}, u32[]{:S(2)}, u32[]{:S(2)}) collective-permute-start(bf16[4,48,384]{2,1,0:T(8,128)(2,1)S(1)} %get-tuple-element.167), channel_id=1, source_target_pairs={{0,16},{4,20},{8,24},{12,28},{16,0},{20,4},{24,8},{28,12},{1,17},{... | collective-permute-start | bytes 442376 | tf_op jit(solution)/shard_map/ppermute | solution.py:45
  445.1 19.9 %collective-permute-start.46 = (bf16[4,48,384]{2,1,0:T(8,128)(2,1)S(1)}, bf16[4,48,384]{2,1,0:T(8,128)(2,1)S(1)}, u32[]{:S(2)}, u32[]{:S(2)}) collective-permute-start(bf16[4,48,384]{2,1,0:T(8,128)(2,1)S(1)} %get-tuple-element.166), channel_id=1, source_target_pairs={{0,24},{4,28},{8,16},{12,20},{16,8},{20,12},{24,0},{28,4},{1,25},{... | collective-permute-start | bytes 442376 | tf_op jit(solution)/shard_map/ppermute | solution.py:45
  487.8 14.7 %collective-permute-start.52 = (bf16[384,384]{1,0:T(8,128)(2,1)S(1)}, bf16[384,384]{1,0:T(8,128)(2,1)S(1)}, u32[]{:S(2)}, u32[]{:S(2)}) collective-permute-start(bf16[384,384]{1,0:T(8,128)(2,1)S(1)} %get-tuple-element.157), channel_id=1, source_target_pairs={{0,2},{1,3},{2,0},{3,1},{4,6},{5,7},{6,4},{7,5},{8,10},{9,11},{10,... | collective-permute-start | bytes 884744 | tf_op jit(solution)/shard_map/ppermute | solution.py:45
  488.4 14.1 %collective-permute-start.51 = (bf16[384,384]{1,0:T(8,128)(2,1)S(1)}, bf16[384,384]{1,0:T(8,128)(2,1)S(1)}, u32[]{:S(2)}, u32[]{:S(2)}) collective-permute-start(bf16[384,384]{1,0:T(8,128)(2,1)S(1)} %get-tuple-element.158), channel_id=1, source_target_pairs={{0,1},{1,0},{2,3},{3,2},{4,5},{5,4},{6,7},{7,6},{8,9},{9,8},{10,11... | collective-permute-start | bytes 884744 | tf_op jit(solution)/shard_map/ppermute | solution.py:45
  488.8 14.3 %collective-permute-start.48 = (bf16[4,48,768]{2,1,0:T(8,128)(2,1)S(1)}, bf16[4,48,768]{2,1,0:T(8,128)(2,1)S(1)}, u32[]{:S(2)}, u32[]{:S(2)}) collective-permute-start(bf16[4,48,768]{2,1,0:T(8,128)(2,1)S(1)} %get-tuple-element.161), channel_id=1, source_target_pairs={{0,8},{4,12},{8,0},{12,4},{16,24},{20,28},{24,16},{28,20},{1,9},{5... | collective-permute-start | bytes 884744 | tf_op jit(solution)/shard_map/ppermute | solution.py:45
  488.9 23.5 %collective-permute-start.49 = (bf16[4,48,768]{2,1,0:T(8,128)(2,1)S(1)}, bf16[4,48,768]{2,1,0:T(8,128)(2,1)S(1)}, u32[]{:S(2)}, u32[]{:S(2)}) collective-permute-start(bf16[4,48,768]{2,1,0:T(8,128)(2,1)S(1)} %get-tuple-element.160), channel_id=1, source_target_pairs={{0,16},{4,20},{8,24},{12,28},{16,0},{20,4},{24,8},{28,12},{1,17},{... | collective-permute-start | bytes 884744 | tf_op jit(solution)/shard_map/ppermute | solution.py:45
  496.1 16.3 %collective-permute-start.50 = (bf16[4,48,768]{2,1,0:T(8,128)(2,1)S(1)}, bf16[4,48,768]{2,1,0:T(8,128)(2,1)S(1)}, u32[]{:S(2)}, u32[]{:S(2)}) collective-permute-start(bf16[4,48,768]{2,1,0:T(8,128)(2,1)S(1)} %get-tuple-element.159), channel_id=1, source_target_pairs={{0,24},{4,28},{8,16},{12,20},{16,8},{20,12},{24,0},{28,4},{1,25},{... | collective-permute-start | bytes 884744 | tf_op jit(solution)/shard_map/ppermute | solution.py:45
  520.6 24.3 %collective-permute-start.59 = (bf16[4,272,384]{2,1,0:T(8,128)(2,1)S(1)}, bf16[4,272,384]{2,1,0:T(8,128)(2,1)S(1)}, u32[]{:S(2)}, u32[]{:S(2)}) collective-permute-start(bf16[4,272,384]{2,1,0:T(8,128)(2,1)S(1)} %pad_maximum_fusion.11.refs_0_), channel_id=1, source_target_pairs={{0,8},{8,16},{16,24},{24,28},{28,20},{20,12},{12,4},{4,0},{1,9},{9... | collective-permute-start | bytes 2506760 | tf_op jit(solution)/shard_map/ppermute | solution.py:695
  526.9 20.5 %collective-permute-start.66 = (bf16[4,256,384]{2,1,0:T(8,128)(2,1)S(1)}, bf16[4,256,384]{2,1,0:T(8,128)(2,1)S(1)}, u32[]{:S(2)}, u32[]{:S(2)}) collective-permute-start(bf16[4,256,384]{2,1,0:T(8,128)(2,1)S(1)} %pad_maximum_fusion.13.refs_8_), channel_id=1, source_target_pairs={{0,4},{8,0},{16,8},{24,16},{28,24},{20,28},{12,20},{4,12},{1,5},{9... | collective-permute-start | bytes 2359304 | tf_op jit(solution)/shard_map/ppermute | solution.py:695
  545.0 20.5 %collective-permute-start.60 = (bf16[4,272,384]{2,1,0:T(8,128)(2,1)S(1)}, bf16[4,272,384]{2,1,0:T(8,128)(2,1)S(1)}, u32[]{:S(2)}, u32[]{:S(2)}) collective-permute-start(bf16[4,272,384]{2,1,0:T(8,128)(2,1)S(1)} %collective-permute-done.59.refs_1_), channel_id=1, source_target_pairs={{0,8},{8,16},{16,24},{24,28},{28,20},{20,12},{12,4},{4,0},{1,9},{9... | collective-permute-start | bytes 2506760 | tf_op jit(solution)/shard_map/ppermute | solution.py:695
  547.5 19.8 %collective-permute-start.67 = (bf16[4,256,384]{2,1,0:T(8,128)(2,1)S(1)}, bf16[4,256,384]{2,1,0:T(8,128)(2,1)S(1)}, u32[]{:S(2)}, u32[]{:S(2)}) collective-permute-start(bf16[4,256,384]{2,1,0:T(8,128)(2,1)S(1)} %collective-permute-done.66.refs_9_), channel_id=1, source_target_pairs={{0,4},{8,0},{16,8},{24,16},{28,24},{20,28},{12,20},{4,12},{1,5},{9... | collective-permute-start | bytes 2359304 | tf_op jit(solution)/shard_map/ppermute | solution.py:695
  565.5 19.5 %collective-permute-start.61 = (bf16[4,272,384]{2,1,0:T(8,128)(2,1)S(1)}, bf16[4,272,384]{2,1,0:T(8,128)(2,1)S(1)}, u32[]{:S(2)}, u32[]{:S(2)}) collective-permute-start(bf16[4,272,384]{2,1,0:T(8,128)(2,1)S(1)} %collective-permute-done.60.refs_2_), channel_id=1, source_target_pairs={{0,8},{8,16},{16,24},{24,28},{28,20},{20,12},{12,4},{4,0},{1,9},{9... | collective-permute-start | bytes 2506760 | tf_op jit(solution)/shard_map/ppermute | solution.py:695
  567.2 18.9 %collective-permute-start.68 = (bf16[4,256,384]{2,1,0:T(8,128)(2,1)S(1)}, bf16[4,256,384]{2,1,0:T(8,128)(2,1)S(1)}, u32[]{:S(2)}, u32[]{:S(2)}) collective-permute-start(bf16[4,256,384]{2,1,0:T(8,128)(2,1)S(1)} %collective-permute-done.67.refs_10_), channel_id=1, source_target_pairs={{0,4},{8,0},{16,8},{24,16},{28,24},{20,28},{12,20},{4,12},{1,5},{9... | collective-permute-start | bytes 2359304 | tf_op jit(solution)/shard_map/ppermute | solution.py:695
  568.1 37.7 %collective-permute-start.26 = (bf16[512,1536]{1,0:T(8,128)(2,1)S(1)}, bf16[512,1536]{1,0:T(8,128)(2,1)S(1)}, u32[]{:S(2)}, u32[]{:S(2)}) collective-permute-start(bf16[512,1536]{1,0:T(8,128)(2,1)S(1)} %slice.72), channel_id=1, source_target_pairs={{0,1},{1,0},{2,3},{3,2},{4,5},{5,4},{6,7},{7,6},{8,9},{9,8},{10,11... | collective-permute-start | bytes 4718600 | tf_op jit(solution)/shard_map/ppermute | solution.py:45
  585.0 18.8 %collective-permute-start.62 = (bf16[4,272,384]{2,1,0:T(8,128)(2,1)S(1)}, bf16[4,272,384]{2,1,0:T(8,128)(2,1)S(1)}, u32[]{:S(2)}, u32[]{:S(2)}) collective-permute-start(bf16[4,272,384]{2,1,0:T(8,128)(2,1)S(1)} %collective-permute-done.61.refs_3_), channel_id=1, source_target_pairs={{0,8},{8,16},{16,24},{24,28},{28,20},{20,12},{12,4},{4,0},{1,9},{9... | collective-permute-start | bytes 2506760 | tf_op jit(solution)/shard_map/ppermute | solution.py:695
  586.1 18.2 %collective-permute-start.69 = (bf16[4,256,384]{2,1,0:T(8,128)(2,1)S(1)}, bf16[4,256,384]{2,1,0:T(8,128)(2,1)S(1)}, u32[]{:S(2)}, u32[]{:S(2)}) collective-permute-start(bf16[4,256,384]{2,1,0:T(8,128)(2,1)S(1)} %collective-permute-done.68.refs_11_), channel_id=1, source_target_pairs={{0,4},{8,0},{16,8},{24,16},{28,24},{20,28},{12,20},{4,12},{1,5},{9... | collective-permute-start | bytes 2359304 | tf_op jit(solution)/shard_map/ppermute | solution.py:695
  603.8 18.6 %collective-permute-start.63 = (bf16[4,272,384]{2,1,0:T(8,128)(2,1)S(1)}, bf16[4,272,384]{2,1,0:T(8,128)(2,1)S(1)}, u32[]{:S(2)}, u32[]{:S(2)}) collective-permute-start(bf16[4,272,384]{2,1,0:T(8,128)(2,1)S(1)} %collective-permute-done.62.refs_4_), channel_id=1, source_target_pairs={{0,8},{8,16},{16,24},{24,28},{28,20},{20,12},{12,4},{4,0},{1,9},{9... | collective-permute-start | bytes 2506760 | tf_op jit(solution)/shard_map/ppermute | solution.py:695
  604.3 19.3 %collective-permute-start.70 = (bf16[4,256,384]{2,1,0:T(8,128)(2,1)S(1)}, bf16[4,256,384]{2,1,0:T(8,128)(2,1)}, u32[]{:S(2)}, u32[]{:S(2)}) collective-permute-start(bf16[4,256,384]{2,1,0:T(8,128)(2,1)S(1)} %collective-permute-done.69.refs_12_), channel_id=1, source_target_pairs={{0,4},{8,0},{16,8},{24,16},{28,24},{20,28},{12,20},{4,12},{1,5},{9... | collective-permute-start | bytes 2359304 | tf_op jit(solution)/shard_map/ppermute | solution.py:695
  607.2 25.2 %collective-permute-start.27 = (bf16[256,1536]{1,0:T(8,128)(2,1)}, bf16[256,1536]{1,0:T(8,128)(2,1)}, u32[]{:S(2)}, u32[]{:S(2)}) collective-permute-start(bf16[256,1536]{1,0:T(8,128)(2,1)} %add_convert_fusion.2), channel_id=1, source_target_pairs={{0,2},{1,3},{2,0},{3,1},{4,6},{5,7},{6,4},{7,5},{8,10},{9,11},{10,... | collective-permute-start | bytes 2359304 | tf_op jit(solution)/shard_map/ppermute | solution.py:45
  622.4 22.1 %collective-permute-start.64 = (bf16[4,272,384]{2,1,0:T(8,128)(2,1)S(1)}, bf16[4,272,384]{2,1,0:T(8,128)(2,1)}, u32[]{:S(2)}, u32[]{:S(2)}) collective-permute-start(bf16[4,272,384]{2,1,0:T(8,128)(2,1)S(1)} %collective-permute-done.63.refs_5_), channel_id=1, source_target_pairs={{0,8},{8,16},{16,24},{24,28},{28,20},{20,12},{12,4},{4,0},{1,9},{9... | collective-permute-start | bytes 2506760 | tf_op jit(solution)/shard_map/ppermute | solution.py:695
  623.6 20.3 %collective-permute-start.71 = (bf16[4,256,384]{2,1,0:T(8,128)(2,1)}, bf16[4,256,384]{2,1,0:T(8,128)(2,1)}, u32[]{:S(2)}, u32[]{:S(2)}) collective-permute-start(bf16[4,256,384]{2,1,0:T(8,128)(2,1)} %collective-permute-done.70.refs_13_), channel_id=1, source_target_pairs={{0,4},{8,0},{16,8},{24,16},{28,24},{20,28},{12,20},{4,12},{1,5},{9... | collective-permute-start | bytes 2359304 | tf_op jit(solution)/shard_map/ppermute | solution.py:695
  639.6 9.4 %collective-permute-start.58 = (f32[2,384]{1,0:T(2,128)S(1)}, f32[2,384]{1,0:T(2,128)S(1)}, u32[]{:S(2)}, u32[]{:S(2)}) collective-permute-start(f32[2,384]{1,0:T(2,128)S(1)} %add.265), channel_id=1, source_target_pairs={{0,24},{4,28},{8,16},{12,20},{16,8},{20,12},{24,0},{28,4},{1,25},{... | collective-permute-start | bytes 9224 | tf_op jit(solution)/shard_map/ppermute | solution.py:45
  644.0 14.5 %collective-permute-start.72 = (bf16[4,256,384]{2,1,0:T(8,128)(2,1)}, bf16[4,256,384]{2,1,0:T(8,128)(2,1)S(1)}, u32[]{:S(2)}, u32[]{:S(2)}) collective-permute-start(bf16[4,256,384]{2,1,0:T(8,128)(2,1)} %collective-permute-done.71.refs_14_), channel_id=1, source_target_pairs={{0,4},{8,0},{16,8},{24,16},{28,24},{20,28},{12,20},{4,12},{1,5},{9... | collective-permute-start | bytes 2359304 | tf_op jit(solution)/shard_map/ppermute | solution.py:695
  644.6 14.9 %collective-permute-start.65 = (bf16[4,272,384]{2,1,0:T(8,128)(2,1)}, bf16[4,272,384]{2,1,0:T(8,128)(2,1)S(1)}, u32[]{:S(2)}, u32[]{:S(2)}) collective-permute-start(bf16[4,272,384]{2,1,0:T(8,128)(2,1)} %collective-permute-done.64.refs_6_), channel_id=1, source_target_pairs={{0,8},{8,16},{16,24},{24,28},{28,20},{20,12},{12,4},{4,0},{1,9},{9... | collective-permute-start | bytes 2506760 | tf_op jit(solution)/shard_map/ppermute | solution.py:695
  (77 other events, 1038.7 us)
Sparse Core Ops, SparseCore 0:
  262.1 223.2 reduce-scatter.1

commit v4 on v3

--- a/solution.py
+++ b/solution.py
@@ -303,48 +303,53 @@
     )
 
 
-def heads_back_kernel(
-    code_ref, load_ref, rows_ref, grad_middle_ref, cosine_ref, sine_ref, *refs
-):
-    gains, pieces = refs[:4], refs[4:12]
-    raw_ref, input_grad_ref, gain_grad_ref, gain, weight, raw = refs[12:]
-    gained(code_ref, gains, 0, gain)
-    fill_weight(code_ref, heads_plan, pieces, weight)
+def turn_back_kernel(code_ref, load_ref, cosine_ref, sine_ref, raw_ref, parts_ref):
     cosine, sine = cosine_ref[...], sine_ref[...]
     for head in range(HQ + 2 * HK):
         group, place = slot_of_head(head)
         part = load_ref[group, :, place * HD : (place + 1) * HD]
         if head < HQ + HK:
             part = turned(part.astype(wide), cosine, -sine).astype(low)
-        raw[:, head * HD : (head + 1) * HD] = part
-    quarter = raw_ref.shape[2] // 2
+        raw_ref[:, head * HD : (head + 1) * HD] = part
+    quarter = parts_ref.shape[2] // 2
     for k in range(4):
         for i in range(2):
             first = (4 * i + k) * quarter
-            raw_ref[k, :, i * quarter : (i + 1) * quarter] = raw[:, first : first + quarter]
-    grad = contract_last(raw[...], weight[...])
+            parts_ref[k, :, i * quarter : (i + 1) * quarter] = raw_ref[:, first : first + quarter]
+
+
+def turn_back_call(code, load, cosine, sine):
+    count, total = load.shape[1], load.shape[0] * load.shape[2]
+    outs = [
+        jax.ShapeDtypeStruct((count, total), low),
+        jax.ShapeDtypeStruct((4, count, total // 4), low),
+    ]
+    return whole_call(turn_back_kernel, code, (load, cosine, sine), outs, [], 0, "turn_back")
+
+
+def heads_back_kernel(code_ref, raw_ref, rows_ref, grad_middle_ref, *refs):
+    gains, pieces = refs[:4], refs[4:12]
+    input_grad_ref, gain_grad_ref, gain, weight = refs[12:]
+    gained(code_ref, gains, 0, gain)
+    fill_weight(code_ref, heads_plan, pieces, weight)
+    grad = contract_last(raw_ref[...], weight[...])
     back, gain_grad_ref[...] = norm_back(rows_ref[...].astype(wide), gain[...], grad)
     input_grad_ref[...] = grad_middle_ref[...] + back
 
 
-def heads_back_call(code, load, rows_in, grad_middle, cosine, sine, gains, pieces):
+def heads_back_call(code, raw, rows_in, grad_middle, gains, pieces):
     count, width = rows_in.shape
     total = pieces[0].shape[1]
     outs = [
-        jax.ShapeDtypeStruct((4, count, total // 4), low),
         jax.ShapeDtypeStruct((count, width), wide),
         jax.ShapeDtypeStruct((1, width), wide),
     ]
     return whole_call(
         heads_back_kernel,
         code,
-        (load, rows_in, grad_middle, cosine, sine, *gains, *pieces),
+        (raw, rows_in, grad_middle, *gains, *pieces),
         outs,
-        [
-            pltpu.VMEM((1, width), wide),
-            pltpu.VMEM((width, total), low),
-            pltpu.VMEM((count, total), low),
-        ],
+        [pltpu.VMEM((1, width), wide), pltpu.VMEM((width, total), low)],
         2 * count * width * total,
         "query_key_value_back",
     )
@@ -878,7 +883,7 @@
     sine = jnp.concatenate([-sine[:, 0], sine[:, 0]], axis=1)
 
     own, near, far, both = deal_weights((w_gate, w_up, w_down))
-    heads = gather_thirds(jnp.concatenate([w_query, w_key, w_value], axis=1), near, far, both)
+    heads = gather_thirds(jnp.concatenate([w_query, w_key, w_value], axis=1), near, far, both, *gains[1:])
     normed_one, load = heads_call(code, rows_in, cosine, sine, gains, heads)
     outward = gather_halves(w_out)
     load, near, far, both, _ = lax.optimization_barrier((load, near, far, both, outward[2]))
@@ -958,8 +963,9 @@
     branch_terms = terms_of(branch_all, mixed_part)
     if size == HK:
         out_got = over_ctx(side_of(branch_terms, 1), 1)
-    grad_raw, input_grad, grad_gain_one = heads_back_call(
-        code, grad_load, rows_in, grad_middle, cosine, sine, gains, heads
+    grad_whole, grad_raw = turn_back_call(code, grad_load, cosine, sine)
+    input_grad, grad_gain_one = heads_back_call(
+        code, grad_whole, rows_in, grad_middle, gains, heads
     )
     result, _ = scatter_fsdp(after(out_terms, grad_normed_two), mid)
     result = (middle + result).astype(low)

time: 691 us -> 699 us (1.012)
    pallas_call x4 -> x5, Pallas kernels: 39.5 us -> 44.7 us  [whole_call(): pl.pallas_call(kernel, grid_spec=pltpu.PrefetchScalarGridSpec(num_scalar_...]
    unnamed x126 -> x128, local copies, waits for them, and re-layouts: 17.6 us -> 16.7 us
  transfers between devices with their start and end apart: 78 -> 78, of which waited for: 40 -> 41; matrix products, arithmetic and copies ran while one was open for 9% -> 9% of each run, Pallas kernels for 14% -> 15%
where the time goes in v4:
time: 699 us; the launch traced here: 691 us
  waiting for transfers between devices  361 us (52%)
  Pallas kernels  144 us (21%)
  starting transfers between devices  85.5 us (12%)
  local copies, waits for them, and re-layouts  44.1 us (6%)
  other arithmetic  33.4 us (5%)
  between operations  15.1 us (2%)
  matrix products  7.91 us (1%)
    ppermute x59, waiting for transfers between devices, swap(): return lax.ppermute(array, axis, [(i, i ^ bits) for i in range(size)])  194 us
    ppermute x14, waiting for transfers between devices, turn_ring(): lax.ppermute(array, 'ctx', [(ring[i], ring[(i + step) % count]) for i in...  97.5 us
    ppermute x59, starting transfers between devices, swap(): return lax.ppermute(array, axis, [(i, i ^ bits) for i in range(size)])  47.3 us
    pallas_call x5, Pallas kernels, whole_call(): pl.pallas_call(kernel, grid_spec=pltpu.PrefetchScalarGridSpec(num_scalar_...  44.7 us
    all_to_all x1, waiting for transfers between devices, body(): grad_mixed = lax.all_to_all(grad_mixed, 'ctx', 0, 0, tiled=True)  41.4 us
    pallas_call x2, Pallas kernels, attention_call(): pl.pallas_call(kernel, grid_spec=pltpu.PrefetchScalarGridSpec(num_scalar_...  36.6 us
    pallas_call x1, Pallas kernels, units_call(): pl.pallas_call(units_kernel, grid_spec=pltpu.PrefetchScalarGridSpec(num_s...  28 us
    pallas_call x1, Pallas kernels, unit_grads(): pl.pallas_call(unit_grads_kernel, grid=(size,), in_specs=[whole, whole] +...  19.2 us
  transfers between devices with their start and end apart: 78, of which 41 were waited for; matrix products, arithmetic and copies ran while one was open for 9% of the time, Pallas kernels for 15%

profile of v4, /device:TPU:0, one launch (start us, length us, event | category | flops | bytes accessed | tf_op | source)
XLA Modules:
  0.0 690.8 jit_solution(3327548263178268605)
XLA Ops:
  9.2 2.6 collective-permute-start.1
  28.5 6.5 collective-permute-done.4.refs_6_
  38.2 16.2 %collective-permute-done.5.refs_7_ = bf16[384,1024]{1,0:T(8,128)(2,1)} collective-permute-done((bf16[384,1024]{1,0:T(8,128)(2,1)}, bf16[384,1024]{1,0:T(8,128)(2,1)}, u32[]{:S(2)}, u32[]{:S(2)}) %collective-permute-start.5) | collective-permute-done | bytes 786464 | tf_op jit(solution)/shard_map/ppermute | solution.py:45
  60.5 11.5 %query_key_value.1 = (bf16[256,1536]{1,0:T(8,128)(2,1)}, bf16[8,256,384]{2,1,0:T(8,128)(2,1)}) custom-call(s32[3]{0:T(128)} %pad_add_fusion.code_ref, bf16[256,1536]{1,0:T(8,128)(2,1)} %bitcast.67, f32[256,96]{1,0:T(8,128)} %get-tuple-element.186.cosine_ref, f32[256,96]{1,0:T(8,128)} %get-tuple-element.187.sine_ref, bf16[2,384]{1,0:T(2,128)(2,1)} %copy-done.57, ...), custom_call_target="tpu_custom_call" | custom-call | flops 2415919104 | bytes 12785664 | tf_op jit(solution)/shard_map/query_key_value/pallas_call | solution.py:153
  72.3 5.2 all-to-all-start
  81.0 2.0 collective-permute-start.13
  83.0 23.8 %collective-permute-done.11.refs_2_ = bf16[3,384,512]{2,1,0:T(8,128)(2,1)} collective-permute-done((bf16[3,384,512]{2,1,0:T(8,128)(2,1)}, bf16[3,384,512]{2,1,0:T(8,128)(2,1)}, u32[]{:S(2)}, u32[]{:S(2)}) %collective-permute-start.11) | collective-permute-done | bytes 1179680 | tf_op jit(solution)/shard_map/ppermute | solution.py:45
  106.8 2.1 collective-permute-start.12
  108.9 5.9 all-to-all-done.load_ref
  114.8 12.3 %attention_forward.1 = bf16[8,256,192]{2,1,0:T(8,128)(2,1)} custom-call(s32[16]{0:T(128)} %and_select_fusion.2.order_ref, bf16[8,256,384]{2,1,0:T(8,128)(2,1)} %all-to-all-done.load_ref), custom_call_target="tpu_custom_call" | custom-call | flops 4294967296 | bytes 3145728 | tf_op jit(solution)/shard_map/attention_forward/pallas_call | solution.py:546
  129.9 4.1 collective-permute-done.12.refs_3_
  134.1 2.2 copy.24
  136.3 6.3 all-to-all-start.1
  143.6 12.9 %collective-permute-done.14.refs_4_ = bf16[3,384,512]{2,1,0:T(8,128)(2,1)} collective-permute-done((bf16[3,384,512]{2,1,0:T(8,128)(2,1)}, bf16[3,384,512]{2,1,0:T(8,128)(2,1)}, u32[]{:S(2)}, u32[]{:S(2)}) %collective-permute-start.14) | collective-permute-done | bytes 1179680 | tf_op jit(solution)/shard_map/ppermute | solution.py:45
  156.5 3.5 pad_maximum_fusion.grad_ref
  161.5 2.2 copy.25.mixed_ref
  164.7 6.8 attention_output.1
  171.8 14.9 %collective-permute-done.21.refs_5_ = bf16[3,384,512]{2,1,0:T(8,128)(2,1)} collective-permute-done((bf16[3,384,512]{2,1,0:T(8,128)(2,1)}, bf16[3,384,512]{2,1,0:T(8,128)(2,1)}, u32[]{:S(2)}, u32[]{:S(2)}) %collective-permute-start.21) | collective-permute-done | bytes 1179680 | tf_op jit(solution)/shard_map/ppermute | solution.py:45
  186.7 3.9 collective-permute-done.20
  197.0 28.0 %feed_forward.1 = (bf16[1024,1536]{1,0:T(8,128)(2,1)}, bf16[1024,1536]{1,0:T(8,128)(2,1)}, bf16[1024,1024]{1,0:T(8,128)(2,1)}, bf16[1024,1024]{1,0:T(8,128)(2,1)}, bf16[1024,1024]{1,0:T(8,128)(2,1)}) custom-call(s32[3]{0:T(128)} %pad_add_fusion.code_ref, bf16[1024,1536]{1,0:T(8,128)(2,1)} %copy-done.1, bf16[1024,1536]{1,0:T(8,128)(2,1)} %pad_maximum_fusion.grad_ref, ...), custom_call_target="tpu_custom_call" | custom-call | flops 19327352832 | bytes 22020096 | tf_op jit(solution)/shard_map/feed_forward/pallas_call | solution.py:392
  226.9 3.3 collective-permute-done.24
  237.6 19.2 %unit_grads.1 = bf16[12288,384]{1,0:T(8,128)(2,1)} custom-call(bf16[1024,1536]{1,0:T(8,128)(2,1)S(1)} %copy-done.2, bf16[1024,1536]{1,0:T(8,128)(2,1)S(1)} %copy-done, bf16[1024,1024]{1,0:T(8,128)(2,1)S(1)} %copy-done.4, bf16[1024,1024]{1,0:T(8,128)(2,1)S(1)} %copy-done.5, bf16[1024,1024]{1,0:T(8,128)(2,1)S(1)} %copy-done.3), custom_call_target="tpu_custom_call" | custom-call | flops 99999997952 | tf_op jit(solution)/shard_map/unit_grads/pallas_call | solution.py:832
  256.9 2.6 convert_add_fusion.grad_ref
  259.4 7.8 %attention_output_back.1 = (f32[256,1536]{1,0:T(8,128)}, bf16[256,1536]{1,0:T(8,128)(2,1)}, bf16[8,256,192]{2,1,0:T(8,128)(2,1)}, f32[1,1536]{1,0:T(1,128)}) custom-call(s32[3]{0:T(128)} %pad_add_fusion.code_ref, f32[256,1536]{1,0:T(8,128)} %get-tuple-element.85.middle_ref, f32[256,1536]{1,0:T(8,128)} %convert_add_fusion.grad_ref, ...), custom_call_target="tpu_custom_call" | custom-call | flops 1207959552 | bytes 11808768 | tf_op jit(solution)/shard_map/attention_output_back/pallas_call | solution.py:153
  267.2 2.3 copy.26
  269.5 4.0 all-to-all-start.2
  274.4 41.4 %all-to-all-done.2 = bf16[8,256,192]{1,2,0:T(8,128)(2,1)S(1)} async-done(((bf16[8,256,192]{1,2,0:T(8,128)(2,1)}), bf16[8,256,192]{1,2,0:T(8,128)(2,1)S(1)}, u32[]{:S(2)}, u32[]{:S(2)}) %all-to-all-start.2) | async-done | bytes 786464 | tf_op jit(solution)/shard_map/all_to_all | solution.py:929
  317.1 24.3 %attention_backward.1 = bf16[8,256,384]{2,1,0:T(8,128)(2,1)} custom-call(s32[16]{0:T(128)} %and_select_fusion.2.order_ref, bf16[8,256,384]{2,1,0:T(8,128)(2,1)} %all-to-all-done.load_ref, bf16[8,256,192]{2,1,0:T(8,128)(2,1)} %copy.27.grad_ref), custom_call_target="tpu_custom_call" | custom-call | flops 10737418240 | bytes 6291456 | tf_op jit(solution)/shard_map/attention_backward/pallas_call | solution.py:546
  341.4 3.8 all-to-all-start.3
  346.8 19.7 %collective-permute-done.32 = bf16[256,1536]{1,0:T(8,128)(2,1)S(1)} collective-permute-done((bf16[256,1536]{1,0:T(8,128)(2,1)S(1)}, bf16[256,1536]{1,0:T(8,128)(2,1)S(1)}, u32[]{:S(2)}, u32[]{:S(2)}) %collective-permute-start.32) | collective-permute-done | bytes 786464 | tf_op jit(solution)/shard_map/ppermute | solution.py:45
  367.4 2.1 constant_dynamic-slice_fusion.18
  371.6 4.7 collective-permute-done.41
  376.4 4.9 collective-permute-done.39
  381.2 3.8 fusion.11
  388.2 6.8 all-to-all-done.3.load_ref
  396.1 7.8 %turn_back.1 = (bf16[256,3072]{1,0:T(8,128)(2,1)}, bf16[4,256,768]{2,1,0:T(8,128)(2,1)}) custom-call(s32[3]{0:T(128)} %pad_add_fusion.code_ref, bf16[8,256,384]{2,1,0:T(8,128)(2,1)} %copy-done.11, f32[256,96]{1,0:T(8,128)} %get-tuple-element.186.cosine_ref, f32[256,96]{1,0:T(8,128)} %get-tuple-element.187.sine_ref), custom_call_target="tpu_custom_call" | custom-call | bytes 4915200 | tf_op jit(solution)/shard_map/turn_back/pallas_call | solution.py:153
  407.6 9.3 %collective-permute-done.36 = bf16[256,768]{1,0:T(8,128)(2,1)S(1)} collective-permute-done((bf16[256,768]{1,0:T(8,128)(2,1)S(1)}, bf16[256,768]{1,0:T(8,128)(2,1)S(1)}, u32[]{:S(2)}, u32[]{:S(2)}) %collective-permute-start.36) | collective-permute-done | bytes 393248 | tf_op jit(solution)/shard_map/ppermute | solution.py:45
  416.9 8.4 %collective-permute-done.34 = bf16[256,768]{1,0:T(8,128)(2,1)S(1)} collective-permute-done((bf16[256,768]{1,0:T(8,128)(2,1)S(1)}, bf16[256,768]{1,0:T(8,128)(2,1)S(1)}, u32[]{:S(2)}, u32[]{:S(2)}) %collective-permute-start.34) | collective-permute-done | bytes 393248 | tf_op jit(solution)/shard_map/ppermute | solution.py:45
  426.7 4.1 convolution_convert_fusion
  433.8 2.1 collective-permute-start.45
  435.9 2.3 collective-permute-start.46
  438.2 11.3 %collective-permute-done.44 = bf16[4,48,384]{2,1,0:T(8,128)(2,1)S(1)} collective-permute-done((bf16[4,48,384]{2,1,0:T(8,128)(2,1)S(1)}, bf16[4,48,384]{2,1,0:T(8,128)(2,1)S(1)}, u32[]{:S(2)}, u32[]{:S(2)}) %collective-permute-start.44) | collective-permute-done | bytes 147488 | tf_op jit(solution)/shard_map/ppermute | solution.py:45
  449.5 4.0 collective-permute-done.45
  453.5 2.0 collective-permute-done.46
  456.2 12.8 %collective-permute-done.43 = bf16[4,192,768]{2,1,0:T(8,128)(2,1)} collective-permute-done((bf16[4,192,768]{2,1,0:T(8,128)(2,1)S(1)}, bf16[4,192,768]{2,1,0:T(8,128)(2,1)}, u32[]{:S(2)}, u32[]{:S(2)}) %collective-permute-start.43) | collective-permute-done | bytes 1179680 | tf_op jit(solution)/shard_map/ppermute | solution.py:45
  470.6 13.3 %reduce-scatter.2.cloned.1.call-done = bf16[1536,384]{1,0:T(8,128)(2,1)} async-done(((bf16[12288,384]{1,0:T(8,128)(2,1)}), bf16[1536,384]{1,0:T(8,128)(2,1)}) %reduce-scatter.2.cloned.1.call-update) | async-done | bytes 1179664 | tf_op jit(solution)/shard_map/reduce_scatter | solution.py:926
  489.0 5.5 collective-permute-done.53
  496.5 4.4 collective-permute-done.52
  501.5 9.3 %collective-permute-done.49 = bf16[4,48,768]{2,1,0:T(8,128)(2,1)S(1)} collective-permute-done((bf16[4,48,768]{2,1,0:T(8,128)(2,1)S(1)}, bf16[4,48,768]{2,1,0:T(8,128)(2,1)S(1)}, u32[]{:S(2)}, u32[]{:S(2)}) %collective-permute-start.49) | collective-permute-done | bytes 294944 | tf_op jit(solution)/shard_map/ppermute | solution.py:45
  512.9 3.5 collective-permute-done.56
  516.4 2.3 collective-permute-done.55
  519.0 6.2 collective-permute-start.59
  525.6 17.8 %collective-permute-done.59.refs_1_ = bf16[4,272,384]{2,1,0:T(8,128)(2,1)S(1)} collective-permute-done((bf16[4,272,384]{2,1,0:T(8,128)(2,1)S(1)}, bf16[4,272,384]{2,1,0:T(8,128)(2,1)S(1)}, u32[]{:S(2)}, u32[]{:S(2)}) %collective-permute-start.59) | collective-permute-done | bytes 835616 | tf_op jit(solution)/shard_map/ppermute | solution.py:700
  543.3 2.5 collective-permute-start.60
  545.8 18.1 %collective-permute-done.60.refs_2_ = bf16[4,272,384]{2,1,0:T(8,128)(2,1)S(1)} collective-permute-done((bf16[4,272,384]{2,1,0:T(8,128)(2,1)S(1)}, bf16[4,272,384]{2,1,0:T(8,128)(2,1)S(1)}, u32[]{:S(2)}, u32[]{:S(2)}) %collective-permute-start.60) | collective-permute-done | bytes 835616 | tf_op jit(solution)/shard_map/ppermute | solution.py:700
  566.5 16.9 %collective-permute-done.61.refs_3_ = bf16[4,272,384]{2,1,0:T(8,128)(2,1)S(1)} collective-permute-done((bf16[4,272,384]{2,1,0:T(8,128)(2,1)S(1)}, bf16[4,272,384]{2,1,0:T(8,128)(2,1)S(1)}, u32[]{:S(2)}, u32[]{:S(2)}) %collective-permute-start.61) | collective-permute-done | bytes 835616 | tf_op jit(solution)/shard_map/ppermute | solution.py:700
  585.5 16.7 %collective-permute-done.69.refs_12_ = bf16[4,256,384]{2,1,0:T(8,128)(2,1)S(1)} collective-permute-done((bf16[4,256,384]{2,1,0:T(8,128)(2,1)S(1)}, bf16[4,256,384]{2,1,0:T(8,128)(2,1)S(1)}, u32[]{:S(2)}, u32[]{:S(2)}) %collective-permute-start.69) | collective-permute-done | bytes 786464 | tf_op jit(solution)/shard_map/ppermute | solution.py:700
  607.8 11.9 %collective-permute-done.70.refs_13_ = bf16[4,256,384]{2,1,0:T(8,128)(2,1)} collective-permute-done((bf16[4,256,384]{2,1,0:T(8,128)(2,1)S(1)}, bf16[4,256,384]{2,1,0:T(8,128)(2,1)}, u32[]{:S(2)}, u32[]{:S(2)}) %collective-permute-start.70) | collective-permute-done | bytes 786464 | tf_op jit(solution)/shard_map/ppermute | solution.py:700
  622.2 10.8 %query_key_value_back.1 = (f32[256,1536]{1,0:T(8,128)}, f32[1,1536]{1,0:T(1,128)}) custom-call(s32[3]{0:T(128)} %pad_add_fusion.code_ref, bf16[256,3072]{1,0:T(8,128)(2,1)} %get-tuple-element.99.raw_ref, bf16[256,1536]{1,0:T(8,128)(2,1)} %bitcast.69, f32[256,1536]{1,0:T(8,128)} %get-tuple-element.100.grad_middle_ref, bf16[2,384]{1,0:T(2,128)(2,1)} %copy-done.57, ...), custom_call_target="tpu_custom_call" | custom-call | flops 2415919104 | bytes 14954496 | tf_op jit(solution)/shard_map/query_key_value_back/pallas_call | solution.py:153
  644.6 2.3 collective-permute-start.57
  649.0 2.7 fusion.14
  652.3 12.8 %collective-permute-done.72.refs_15_ = bf16[4,256,384]{2,1,0:T(8,128)(2,1)S(1)} collective-permute-done((bf16[4,256,384]{2,1,0:T(8,128)(2,1)}, bf16[4,256,384]{2,1,0:T(8,128)(2,1)S(1)}, u32[]{:S(2)}, u32[]{:S(2)}) %collective-permute-start.72) | collective-permute-done | bytes 786464 | tf_op jit(solution)/shard_map/ppermute | solution.py:700
  665.2 2.3 collective-permute-done.65.refs_7_
  668.4 15.3 %deal_gradients.1 = (f32[384,4096]{1,0:T(8,128)}, f32[384,4096]{1,0:T(8,128)}, f32[384,4096]{1,0:T(8,128)}, f32[384,1536]{1,0:T(8,128)}, f32[384,1536]{1,0:T(8,1...) custom-call(s32[17]{0:T(128)} %pad_add_fusion.1.code_ref, bf16[4,272,384]{2,1,0:T(8,128)(2,1)} %copy-done.14, ...), custom_call_target="tpu_custom_call" | custom-call | tf_op jit(solution)/shard_map/deal_gradients/pallas_call | solution.py:781
  (305 shorter events, 113.4 us)
Async XLA Ops:
  8.7 19.8 %collective-permute-start = (bf16[2,384]{1,0:T(2,128)(2,1)S(1)}, bf16[2,384]{1,0:T(2,128)(2,1)S(1)}, u32[]{:S(2)}, u32[]{:S(2)}) collective-permute-start(bf16[2,384]{1,0:T(2,128)(2,1)S(1)} %pad_maximum_fusion.17.refs_0_), channel_id=1, source_target_pairs={{0,1},{1,0},{2,3},{3,2},{4,5},{5,4},{6,7},{7,6},{8,9},{9,8},{10,11... | collective-permute-start | bytes 4616 | tf_op jit(solution)/shard_map/ppermute | solution.py:45
  9.2 19.3 %collective-permute-start.1 = (bf16[2,384]{1,0:T(2,128)(2,1)S(1)}, bf16[2,384]{1,0:T(2,128)(2,1)S(1)}, u32[]{:S(2)}, u32[]{:S(2)}) collective-permute-start(bf16[2,384]{1,0:T(2,128)(2,1)S(1)} %pad_maximum_fusion.17.refs_0_), channel_id=1, source_target_pairs={{0,2},{1,3},{2,0},{3,1},{4,6},{5,7},{6,4},{7,5},{8,10},{9,11},{10,... | collective-permute-start | bytes 4616 | tf_op jit(solution)/shard_map/ppermute | solution.py:45
  11.7 16.8 %collective-permute-start.2 = (bf16[2,384]{1,0:T(2,128)(2,1)S(1)}, bf16[2,384]{1,0:T(2,128)(2,1)S(1)}, u32[]{:S(2)}, u32[]{:S(2)}) collective-permute-start(bf16[2,384]{1,0:T(2,128)(2,1)S(1)} %pad_maximum_fusion.17.refs_0_), channel_id=1, source_target_pairs={{0,3},{1,2},{2,1},{3,0},{4,7},{5,6},{6,5},{7,4},{8,11},{9,10},{10,... | collective-permute-start | bytes 4616 | tf_op jit(solution)/shard_map/ppermute | solution.py:45
  13.4 47.1 %collective-permute-start.3 = (bf16[384,3072]{1,0:T(8,128)(2,1)S(1)}, bf16[384,3072]{1,0:T(8,128)(2,1)}, u32[]{:S(2)}, u32[]{:S(2)}) collective-permute-start(bf16[384,3072]{1,0:T(8,128)(2,1)S(1)} %constant_dynamic-update-slice_fusion.refs_4_), channel_id=1, source_target_pairs={{0,1},{1,0},{2,3},{3,2},{4,5},{5,4},{6,7},{7,6},{8,9},{9,8},{10,11... | collective-permute-start | bytes 7077896 | tf_op jit(solution)/shard_map/ppermute | solution.py:45
  14.8 20.2 %collective-permute-start.4 = (bf16[384,1024]{1,0:T(8,128)(2,1)}, bf16[384,1024]{1,0:T(8,128)(2,1)}, u32[]{:S(2)}, u32[]{:S(2)}) collective-permute-start(bf16[384,1024]{1,0:T(8,128)(2,1)} %constant_dynamic-slice_fusion.24), channel_id=1, source_target_pairs={{0,2},{1,3},{2,0},{3,1},{4,6},{5,7},{6,4},{7,5},{8,10},{9,11},{10,... | collective-permute-start | bytes 2359304 | tf_op jit(solution)/shard_map/ppermute | solution.py:45
  35.0 19.4 %collective-permute-start.5 = (bf16[384,1024]{1,0:T(8,128)(2,1)}, bf16[384,1024]{1,0:T(8,128)(2,1)}, u32[]{:S(2)}, u32[]{:S(2)}) collective-permute-start(bf16[384,1024]{1,0:T(8,128)(2,1)} %collective-permute-done.4.refs_6_), channel_id=1, source_target_pairs={{0,4},{4,0},{8,12},{12,8},{16,20},{20,16},{24,28},{28,24},{1,5},{5... | collective-permute-start | bytes 2359304 | tf_op jit(solution)/shard_map/ppermute | solution.py:45
  36.7 18.7 %collective-permute-start.6 = (bf16[384,1024]{1,0:T(8,128)(2,1)}, bf16[384,1024]{1,0:T(8,128)(2,1)}, u32[]{:S(2)}, u32[]{:S(2)}) collective-permute-start(bf16[384,1024]{1,0:T(8,128)(2,1)} %pad_maximum_fusion.12), channel_id=1, source_target_pairs={{0,2},{1,3},{2,0},{3,1},{4,6},{5,7},{6,4},{7,5},{8,10},{9,11},{10,... | collective-permute-start | bytes 2359304 | tf_op jit(solution)/shard_map/ppermute | solution.py:45
  38.2 22.3 %collective-permute-start.7 = (bf16[384,1024]{1,0:T(8,128)(2,1)}, bf16[384,1024]{1,0:T(8,128)(2,1)}, u32[]{:S(2)}, u32[]{:S(2)}) collective-permute-start(bf16[384,1024]{1,0:T(8,128)(2,1)} %collective-permute-done.4.refs_6_), channel_id=1, source_target_pairs={{0,1},{1,0},{2,3},{3,2},{4,5},{5,4},{6,7},{7,6},{8,9},{9,8},{10,11... | collective-permute-start | bytes 2359304 | tf_op jit(solution)/shard_map/ppermute | solution.py:45
  56.3 16.1 %collective-permute-start.10 = (bf16[384,768]{1,0:T(8,128)(2,1)}, bf16[384,768]{1,0:T(8,128)(2,1)}, u32[]{:S(2)}, u32[]{:S(2)}) collective-permute-start(bf16[384,768]{1,0:T(8,128)(2,1)} %constant_dynamic-slice_fusion.23), channel_id=1, source_target_pairs={{0,2},{1,3},{2,0},{3,1},{4,6},{5,7},{6,4},{7,5},{8,10},{9,11},{10,... | collective-permute-start | bytes 1769480 | tf_op jit(solution)/shard_map/ppermute | solution.py:45
  72.3 42.5 %all-to-all-start = ((bf16[8,256,384]{2,1,0:T(8,128)(2,1)}), bf16[8,256,384]{2,1,0:T(8,128)(2,1)}, u32[]{:S(2)}, u32[]{:S(2)}) async-start(bf16[8,256,384]{2,1,0:T(8,128)(2,1)} %get-tuple-element.78), calls=%async_computation | async-start | bytes 3145728 | tf_op jit(solution)/shard_map/all_to_all | solution.py:895
  77.6 29.3 %collective-permute-start.11 = (bf16[3,384,512]{2,1,0:T(8,128)(2,1)}, bf16[3,384,512]{2,1,0:T(8,128)(2,1)}, u32[]{:S(2)}, u32[]{:S(2)}) collective-permute-start(bf16[3,384,512]{2,1,0:T(8,128)(2,1)} %pad_maximum_fusion.8), channel_id=1, source_target_pairs={{0,2},{1,3},{2,0},{3,1},{4,6},{5,7},{6,4},{7,5},{8,10},{9,11},{10,... | collective-permute-start | bytes 3538952 | tf_op jit(solution)/shard_map/ppermute | solution.py:45
  79.1 48.0 %collective-permute-start.15 = (bf16[256,1536]{1,0:T(8,128)(2,1)S(1)}, bf16[256,1536]{1,0:T(8,128)(2,1)S(1)}, u32[]{:S(2)}, u32[]{:S(2)}) collective-permute-start(bf16[256,1536]{1,0:T(8,128)(2,1)S(1)} %bitcast.64), channel_id=1, source_target_pairs={{0,2},{1,3},{2,0},{3,1},{4,6},{5,7},{6,4},{7,5},{8,10},{9,11},{10,... | collective-permute-start | bytes 2359304 | tf_op jit(solution)/shard_map/ppermute | solution.py:45
  81.0 48.9 %collective-permute-start.13 = (bf16[384,768]{1,0:T(8,128)(2,1)}, bf16[384,768]{1,0:T(8,128)(2,1)S(1)}, u32[]{:S(2)}, u32[]{:S(2)}) collective-permute-start(bf16[384,768]{1,0:T(8,128)(2,1)} %collective-permute-done.10.refs_6_), channel_id=1, source_target_pairs={{0,8},{4,12},{8,0},{12,4},{16,24},{20,28},{24,16},{28,20},{1,9},{5... | collective-permute-start | bytes 1769480 | tf_op jit(solution)/shard_map/ppermute | solution.py:45
  106.8 27.2 %collective-permute-start.12 = (bf16[3,384,512]{2,1,0:T(8,128)(2,1)}, bf16[3,384,512]{2,1,0:T(8,128)(2,1)}, u32[]{:S(2)}, u32[]{:S(2)}) collective-permute-start(bf16[3,384,512]{2,1,0:T(8,128)(2,1)} %collective-permute-done.11.refs_2_), channel_id=1, source_target_pairs={{0,4},{4,0},{8,12},{12,8},{16,20},{20,16},{24,28},{28,24},{1,5},{5... | collective-permute-start | bytes 3538952 | tf_op jit(solution)/shard_map/ppermute | solution.py:45
  128.6 27.9 %collective-permute-start.16 = (bf16[512,1536]{1,0:T(8,128)(2,1)}, bf16[512,1536]{1,0:T(8,128)(2,1)}, u32[]{:S(2)}, u32[]{:S(2)}) collective-permute-start(bf16[512,1536]{1,0:T(8,128)(2,1)} %pad_maximum_fusion.3), channel_id=1, source_target_pairs={{0,1},{1,0},{2,3},{3,2},{4,5},{5,4},{6,7},{7,6},{8,9},{9,8},{10,11... | collective-permute-start | bytes 4718600 | tf_op jit(solution)/shard_map/ppermute | solution.py:45
  128.6 27.9 %collective-permute-start.14 = (bf16[3,384,512]{2,1,0:T(8,128)(2,1)}, bf16[3,384,512]{2,1,0:T(8,128)(2,1)}, u32[]{:S(2)}, u32[]{:S(2)}) collective-permute-start(bf16[3,384,512]{2,1,0:T(8,128)(2,1)} %pad_maximum_fusion.9), channel_id=1, source_target_pairs={{0,3},{1,2},{2,1},{3,0},{4,7},{5,6},{6,5},{7,4},{8,11},{9,10},{10,... | collective-permute-start | bytes 3538952 | tf_op jit(solution)/shard_map/ppermute | solution.py:45
  136.3 25.2 %all-to-all-start.1 = ((bf16[8,256,192]{1,2,0:T(8,128)(2,1)}), bf16[8,256,192]{1,2,0:T(8,128)(2,1)}, u32[]{:S(2)}, u32[]{:S(2)}) async-start(bf16[8,256,192]{1,2,0:T(8,128)(2,1)} %copy.24), calls=%async_computation.1 | async-start | bytes 1572864 | tf_op jit(solution)/shard_map/all_to_all | solution.py:899
  142.5 341.3 %reduce-scatter.2.cloned.1.call-start = ((), (), s32[]{:S(2)}) async-start(), calls=%async_computation.5 | async-start | bytes 10616832 | tf_op jit(solution)/shard_map/reduce_scatter | solution.py:926
  143.0 20.7 %collective-permute-start.17 = (bf16[384,1536]{1,0:T(8,128)(2,1)S(1)}, bf16[384,1536]{1,0:T(8,128)(2,1)S(1)}, u32[]{:S(2)}, u32[]{:S(2)}) collective-permute-start(bf16[384,1536]{1,0:T(8,128)(2,1)S(1)} %copy-done.8), channel_id=1, source_target_pairs={{0,1},{1,0},{2,3},{3,2},{4,5},{5,4},{6,7},{7,6},{8,9},{9,8},{10,11... | collective-permute-start | bytes 3538952 | tf_op jit(solution)/shard_map/ppermute | solution.py:45
  143.1 20.6 %collective-permute-start.18 = (bf16[384,768]{1,0:T(8,128)(2,1)}, bf16[384,768]{1,0:T(8,128)(2,1)}, u32[]{:S(2)}, u32[]{:S(2)}) collective-permute-start(bf16[384,768]{1,0:T(8,128)(2,1)} %collective-permute-done.10.refs_6_), channel_id=1, source_target_pairs={{0,1},{1,0},{2,3},{3,2},{4,5},{5,4},{6,7},{7,6},{8,9},{9,8},{10,11... | collective-permute-start | bytes 1769480 | tf_op jit(solution)/shard_map/ppermute | solution.py:45
  143.6 20.2 %collective-permute-start.19 = (bf16[384,768]{1,0:T(8,128)(2,1)}, bf16[384,768]{1,0:T(8,128)(2,1)}, u32[]{:S(2)}, u32[]{:S(2)}) collective-permute-start(bf16[384,768]{1,0:T(8,128)(2,1)} %copy-done.22), channel_id=1, source_target_pairs={{0,1},{1,0},{2,3},{3,2},{4,5},{5,4},{6,7},{7,6},{8,9},{9,8},{10,11... | collective-permute-start | bytes 1769480 | tf_op jit(solution)/shard_map/ppermute | solution.py:45
  156.5 30.2 %collective-permute-start.21 = (bf16[3,384,512]{2,1,0:T(8,128)(2,1)}, bf16[3,384,512]{2,1,0:T(8,128)(2,1)}, u32[]{:S(2)}, u32[]{:S(2)}) collective-permute-start(bf16[3,384,512]{2,1,0:T(8,128)(2,1)} %collective-permute-done.14.refs_4_), channel_id=1, source_target_pairs={{0,8},{4,12},{8,0},{12,4},{16,24},{20,28},{24,16},{28,20},{1,9},{5... | collective-permute-start | bytes 3538952 | tf_op jit(solution)/shard_map/ppermute | solution.py:45
  171.6 19.0 %collective-permute-start.20 = (bf16[256,1536]{1,0:T(8,128)(2,1)}, bf16[256,1536]{1,0:T(8,128)(2,1)S(1)}, u32[]{:S(2)}, u32[]{:S(2)}) collective-permute-start(bf16[256,1536]{1,0:T(8,128)(2,1)} %get-tuple-element.86), channel_id=1, source_target_pairs={{0,2},{1,3},{2,0},{3,1},{4,6},{5,7},{6,4},{7,5},{8,10},{9,11},{10,... | collective-permute-start | bytes 2359304 | tf_op jit(solution)/shard_map/ppermute | solution.py:45
  171.7 23.6 %collective-permute-start.23 = (bf16[3,384,1024]{2,1,0:T(8,128)(2,1)S(1)}, bf16[3,384,1024]{2,1,0:T(8,128)(2,1)}, u32[]{:S(2)}, u32[]{:S(2)}) collective-permute-start(bf16[3,384,1024]{2,1,0:T(8,128)(2,1)S(1)} %copy-done.23), channel_id=1, source_target_pairs={{0,1},{1,0},{2,3},{3,2},{4,5},{5,4},{6,7},{7,6},{8,9},{9,8},{10,11... | collective-permute-start | bytes 7077896 | tf_op jit(solution)/shard_map/ppermute | solution.py:45
  231.5 25.3 %collective-permute-start.25 = (bf16[256,1536]{1,0:T(8,128)(2,1)S(1)}, bf16[256,1536]{1,0:T(8,128)(2,1)S(1)}, u32[]{:S(2)}, u32[]{:S(2)}) collective-permute-start(bf16[256,1536]{1,0:T(8,128)(2,1)S(1)} %add_convert_fusion.3), channel_id=1, source_target_pairs={{0,2},{1,3},{2,0},{3,1},{4,6},{5,7},{6,4},{7,5},{8,10},{9,11},{10,... | collective-permute-start | bytes 2359304 | tf_op jit(solution)/shard_map/ppermute | solution.py:45
  269.5 46.3 %all-to-all-start.2 = ((bf16[8,256,192]{1,2,0:T(8,128)(2,1)}), bf16[8,256,192]{1,2,0:T(8,128)(2,1)S(1)}, u32[]{:S(2)}, u32[]{:S(2)}) async-start(bf16[8,256,192]{1,2,0:T(8,128)(2,1)} %copy.26), calls=%async_computation.2 | async-start | bytes 1572864 | tf_op jit(solution)/shard_map/all_to_all | solution.py:929
  273.5 71.7 %collective-permute-start.37 = (bf16[256,1536]{1,0:T(8,128)(2,1)S(1)}, bf16[256,1536]{1,0:T(8,128)(2,1)S(1)}, u32[]{:S(2)}, u32[]{:S(2)}) collective-permute-start(bf16[256,1536]{1,0:T(8,128)(2,1)S(1)} %copy-done.49), channel_id=1, source_target_pairs={{0,2},{1,3},{2,0},{3,1},{4,6},{5,7},{6,4},{7,5},{8,10},{9,11},{10,... | collective-permute-start | bytes 2359304 | tf_op jit(solution)/shard_map/ppermute | solution.py:45
  341.4 53.6 %all-to-all-start.3 = ((bf16[8,256,384]{2,1,0:T(8,128)(2,1)}), bf16[8,256,384]{2,1,0:T(8,128)(2,1)S(1)}, u32[]{:S(2)}, u32[]{:S(2)}) async-start(bf16[8,256,384]{2,1,0:T(8,128)(2,1)} %attention_backward.1), calls=%async_computation.3 | async-start | bytes 3145728 | tf_op jit(solution)/shard_map/all_to_all | solution.py:932
  346.6 34.6 %collective-permute-start.38 = (bf16[512,1536]{1,0:T(8,128)(2,1)}, bf16[512,1536]{1,0:T(8,128)(2,1)}, u32[]{:S(2)}, u32[]{:S(2)}) collective-permute-start(bf16[512,1536]{1,0:T(8,128)(2,1)} %pad_maximum_fusion.7), channel_id=1, source_target_pairs={{0,1},{1,0},{2,3},{3,2},{4,5},{5,4},{6,7},{7,6},{8,9},{9,8},{10,11... | collective-permute-start | bytes 4718600 | tf_op jit(solution)/shard_map/ppermute | solution.py:45
  346.8 19.7 %collective-permute-start.32 = (bf16[256,1536]{1,0:T(8,128)(2,1)S(1)}, bf16[256,1536]{1,0:T(8,128)(2,1)S(1)}, u32[]{:S(2)}, u32[]{:S(2)}) collective-permute-start(bf16[256,1536]{1,0:T(8,128)(2,1)S(1)} %copy-done.45), channel_id=1, source_target_pairs={{0,2},{1,3},{2,0},{3,1},{4,6},{5,7},{6,4},{7,5},{8,10},{9,11},{10,... | collective-permute-start | bytes 2359304 | tf_op jit(solution)/shard_map/ppermute | solution.py:45
  367.4 58.0 %collective-permute-start.33 = (bf16[512,1536]{1,0:T(8,128)(2,1)S(1)}, bf16[512,1536]{1,0:T(8,128)(2,1)}, u32[]{:S(2)}, u32[]{:S(2)}) collective-permute-start(bf16[512,1536]{1,0:T(8,128)(2,1)S(1)} %pad_maximum_fusion.5), channel_id=1, source_target_pairs={{0,1},{1,0},{2,3},{3,2},{4,5},{5,4},{6,7},{7,6},{8,9},{9,8},{10,11... | collective-permute-start | bytes 4718600 | tf_op jit(solution)/shard_map/ppermute | solution.py:45
  370.0 11.2 %collective-permute-start.39 = (bf16[256,384]{1,0:T(8,128)(2,1)S(1)}, bf16[256,384]{1,0:T(8,128)(2,1)}, u32[]{:S(2)}, u32[]{:S(2)}) collective-permute-start(bf16[256,384]{1,0:T(8,128)(2,1)S(1)} %get-tuple-element.167), channel_id=1, source_target_pairs={{0,2},{1,3},{2,0},{3,1},{4,6},{5,7},{6,4},{7,5},{8,10},{9,11},{10,... | collective-permute-start | bytes 589832 | tf_op jit(solution)/shard_map/ppermute | solution.py:45
  386.3 39.1 %collective-permute-start.42 = (bf16[4,192,384]{2,1,0:T(8,128)(2,1)}, bf16[4,192,384]{2,1,0:T(8,128)(2,1)}, u32[]{:S(2)}, u32[]{:S(2)}) collective-permute-start(bf16[4,192,384]{2,1,0:T(8,128)(2,1)} %constant_dynamic-slice_fusion.14), channel_id=1, source_target_pairs={{0,4},{4,0},{8,12},{12,8},{16,20},{20,16},{24,28},{28,24},{1,5},{5... | collective-permute-start | bytes 1769480 | tf_op jit(solution)/shard_map/ppermute | solution.py:45
  405.4 11.5 %collective-permute-start.36 = (bf16[256,768]{1,0:T(8,128)(2,1)S(1)}, bf16[256,768]{1,0:T(8,128)(2,1)S(1)}, u32[]{:S(2)}, u32[]{:S(2)}) collective-permute-start(bf16[256,768]{1,0:T(8,128)(2,1)S(1)} %get-tuple-element.154), channel_id=1, source_target_pairs={{0,3},{1,2},{2,1},{3,0},{4,7},{5,6},{6,5},{7,4},{8,11},{9,10},{10,... | collective-permute-start | bytes 1179656 | tf_op jit(solution)/shard_map/ppermute | solution.py:45
  406.5 10.3 %collective-permute-start.35 = (bf16[256,768]{1,0:T(8,128)(2,1)S(1)}, bf16[256,768]{1,0:T(8,128)(2,1)S(1)}, u32[]{:S(2)}, u32[]{:S(2)}) collective-permute-start(bf16[256,768]{1,0:T(8,128)(2,1)S(1)} %get-tuple-element.155), channel_id=1, source_target_pairs={{0,1},{1,0},{2,3},{3,2},{4,5},{5,4},{6,7},{7,6},{8,9},{9,8},{10,11... | collective-permute-start | bytes 1179656 | tf_op jit(solution)/shard_map/ppermute | solution.py:45
  407.0 18.3 %collective-permute-start.34 = (bf16[256,768]{1,0:T(8,128)(2,1)S(1)}, bf16[256,768]{1,0:T(8,128)(2,1)S(1)}, u32[]{:S(2)}, u32[]{:S(2)}) collective-permute-start(bf16[256,768]{1,0:T(8,128)(2,1)S(1)} %get-tuple-element.156), channel_id=1, source_target_pairs={{0,2},{1,3},{2,0},{3,1},{4,6},{5,7},{6,4},{7,5},{8,10},{9,11},{10,... | collective-permute-start | bytes 1179656 | tf_op jit(solution)/shard_map/ppermute | solution.py:45
  430.8 38.1 %collective-permute-start.43 = (bf16[4,192,768]{2,1,0:T(8,128)(2,1)S(1)}, bf16[4,192,768]{2,1,0:T(8,128)(2,1)}, u32[]{:S(2)}, u32[]{:S(2)}) collective-permute-start(bf16[4,192,768]{2,1,0:T(8,128)(2,1)S(1)} %constant_dynamic-slice_fusion.13), channel_id=1, source_target_pairs={{0,4},{4,0},{8,12},{12,8},{16,20},{20,16},{24,28},{28,24},{1,5},{5... | collective-permute-start | bytes 3538952 | tf_op jit(solution)/shard_map/ppermute | solution.py:45
  433.7 15.8 %collective-permute-start.44 = (bf16[4,48,384]{2,1,0:T(8,128)(2,1)S(1)}, bf16[4,48,384]{2,1,0:T(8,128)(2,1)S(1)}, u32[]{:S(2)}, u32[]{:S(2)}) collective-permute-start(bf16[4,48,384]{2,1,0:T(8,128)(2,1)S(1)} %get-tuple-element.170), channel_id=1, source_target_pairs={{0,8},{4,12},{8,0},{12,4},{16,24},{20,28},{24,16},{28,20},{1,9},{5... | collective-permute-start | bytes 442376 | tf_op jit(solution)/shard_map/ppermute | solution.py:45
  433.8 19.7 %collective-permute-start.45 = (bf16[4,48,384]{2,1,0:T(8,128)(2,1)S(1)}, bf16[4,48,384]{2,1,0:T(8,128)(2,1)S(1)}, u32[]{:S(2)}, u32[]{:S(2)}) collective-permute-start(bf16[4,48,384]{2,1,0:T(8,128)(2,1)S(1)} %get-tuple-element.169), channel_id=1, source_target_pairs={{0,16},{4,20},{8,24},{12,28},{16,0},{20,4},{24,8},{28,12},{1,17},{... | collective-permute-start | bytes 442376 | tf_op jit(solution)/shard_map/ppermute | solution.py:45
  435.9 19.6 %collective-permute-start.46 = (bf16[4,48,384]{2,1,0:T(8,128)(2,1)S(1)}, bf16[4,48,384]{2,1,0:T(8,128)(2,1)S(1)}, u32[]{:S(2)}, u32[]{:S(2)}) collective-permute-start(bf16[4,48,384]{2,1,0:T(8,128)(2,1)S(1)} %get-tuple-element.168), channel_id=1, source_target_pairs={{0,24},{4,28},{8,16},{12,20},{16,8},{20,12},{24,0},{28,4},{1,25},{... | collective-permute-start | bytes 442376 | tf_op jit(solution)/shard_map/ppermute | solution.py:45
  485.2 9.3 %collective-permute-start.53 = (bf16[384,384]{1,0:T(8,128)(2,1)S(1)}, bf16[384,384]{1,0:T(8,128)(2,1)S(1)}, u32[]{:S(2)}, u32[]{:S(2)}) collective-permute-start(bf16[384,384]{1,0:T(8,128)(2,1)S(1)} %get-tuple-element.158), channel_id=1, source_target_pairs={{0,3},{1,2},{2,1},{3,0},{4,7},{5,6},{6,5},{7,4},{8,11},{9,10},{10,... | collective-permute-start | bytes 884744 | tf_op jit(solution)/shard_map/ppermute | solution.py:45
  486.2 14.7 %collective-permute-start.52 = (bf16[384,384]{1,0:T(8,128)(2,1)S(1)}, bf16[384,384]{1,0:T(8,128)(2,1)S(1)}, u32[]{:S(2)}, u32[]{:S(2)}) collective-permute-start(bf16[384,384]{1,0:T(8,128)(2,1)S(1)} %get-tuple-element.159), channel_id=1, source_target_pairs={{0,2},{1,3},{2,0},{3,1},{4,6},{5,7},{6,4},{7,5},{8,10},{9,11},{10,... | collective-permute-start | bytes 884744 | tf_op jit(solution)/shard_map/ppermute | solution.py:45
  486.8 14.1 %collective-permute-start.51 = (bf16[384,384]{1,0:T(8,128)(2,1)S(1)}, bf16[384,384]{1,0:T(8,128)(2,1)S(1)}, u32[]{:S(2)}, u32[]{:S(2)}) collective-permute-start(bf16[384,384]{1,0:T(8,128)(2,1)S(1)} %get-tuple-element.160), channel_id=1, source_target_pairs={{0,1},{1,0},{2,3},{3,2},{4,5},{5,4},{6,7},{7,6},{8,9},{9,8},{10,11... | collective-permute-start | bytes 884744 | tf_op jit(solution)/shard_map/ppermute | solution.py:45
  487.2 14.2 %collective-permute-start.48 = (bf16[4,48,768]{2,1,0:T(8,128)(2,1)S(1)}, bf16[4,48,768]{2,1,0:T(8,128)(2,1)S(1)}, u32[]{:S(2)}, u32[]{:S(2)}) collective-permute-start(bf16[4,48,768]{2,1,0:T(8,128)(2,1)S(1)} %get-tuple-element.163), channel_id=1, source_target_pairs={{0,8},{4,12},{8,0},{12,4},{16,24},{20,28},{24,16},{28,20},{1,9},{5... | collective-permute-start | bytes 884744 | tf_op jit(solution)/shard_map/ppermute | solution.py:45
  487.3 23.5 %collective-permute-start.49 = (bf16[4,48,768]{2,1,0:T(8,128)(2,1)S(1)}, bf16[4,48,768]{2,1,0:T(8,128)(2,1)S(1)}, u32[]{:S(2)}, u32[]{:S(2)}) collective-permute-start(bf16[4,48,768]{2,1,0:T(8,128)(2,1)S(1)} %get-tuple-element.162), channel_id=1, source_target_pairs={{0,16},{4,20},{8,24},{12,28},{16,0},{20,4},{24,8},{28,12},{1,17},{... | collective-permute-start | bytes 884744 | tf_op jit(solution)/shard_map/ppermute | solution.py:45
  494.5 16.3 %collective-permute-start.50 = (bf16[4,48,768]{2,1,0:T(8,128)(2,1)S(1)}, bf16[4,48,768]{2,1,0:T(8,128)(2,1)S(1)}, u32[]{:S(2)}, u32[]{:S(2)}) collective-permute-start(bf16[4,48,768]{2,1,0:T(8,128)(2,1)S(1)} %get-tuple-element.161), channel_id=1, source_target_pairs={{0,24},{4,28},{8,16},{12,20},{16,8},{20,12},{24,0},{28,4},{1,25},{... | collective-permute-start | bytes 884744 | tf_op jit(solution)/shard_map/ppermute | solution.py:45
  511.1 7.7 %collective-permute-start.55 = (bf16[48,1152]{1,0:T(8,128)(2,1)S(1)}, bf16[48,1152]{1,0:T(8,128)(2,1)S(1)}, u32[]{:S(2)}, u32[]{:S(2)}) collective-permute-start(bf16[48,1152]{1,0:T(8,128)(2,1)S(1)} %get-tuple-element.176), channel_id=1, source_target_pairs={{0,2},{1,3},{2,0},{3,1},{4,6},{5,7},{6,4},{7,5},{8,10},{9,11},{10,... | collective-permute-start | bytes 331784 | tf_op jit(solution)/shard_map/ppermute | solution.py:45
  519.0 24.3 %collective-permute-start.59 = (bf16[4,272,384]{2,1,0:T(8,128)(2,1)S(1)}, bf16[4,272,384]{2,1,0:T(8,128)(2,1)S(1)}, u32[]{:S(2)}, u32[]{:S(2)}) collective-permute-start(bf16[4,272,384]{2,1,0:T(8,128)(2,1)S(1)} %pad_maximum_fusion.11.refs_0_), channel_id=1, source_target_pairs={{0,8},{8,16},{16,24},{24,28},{28,20},{20,12},{12,4},{4,0},{1,9},{9... | collective-permute-start | bytes 2506760 | tf_op jit(solution)/shard_map/ppermute | solution.py:700
  525.3 20.5 %collective-permute-start.66 = (bf16[4,256,384]{2,1,0:T(8,128)(2,1)S(1)}, bf16[4,256,384]{2,1,0:T(8,128)(2,1)S(1)}, u32[]{:S(2)}, u32[]{:S(2)}) collective-permute-start(bf16[4,256,384]{2,1,0:T(8,128)(2,1)S(1)} %pad_maximum_fusion.13.refs_8_), channel_id=1, source_target_pairs={{0,4},{8,0},{16,8},{24,16},{28,24},{20,28},{12,20},{4,12},{1,5},{9... | collective-permute-start | bytes 2359304 | tf_op jit(solution)/shard_map/ppermute | solution.py:700
  543.3 20.6 %collective-permute-start.60 = (bf16[4,272,384]{2,1,0:T(8,128)(2,1)S(1)}, bf16[4,272,384]{2,1,0:T(8,128)(2,1)S(1)}, u32[]{:S(2)}, u32[]{:S(2)}) collective-permute-start(bf16[4,272,384]{2,1,0:T(8,128)(2,1)S(1)} %collective-permute-done.59.refs_1_), channel_id=1, source_target_pairs={{0,8},{8,16},{16,24},{24,28},{28,20},{20,12},{12,4},{4,0},{1,9},{9... | collective-permute-start | bytes 2506760 | tf_op jit(solution)/shard_map/ppermute | solution.py:700
  545.8 19.8 %collective-permute-start.67 = (bf16[4,256,384]{2,1,0:T(8,128)(2,1)S(1)}, bf16[4,256,384]{2,1,0:T(8,128)(2,1)S(1)}, u32[]{:S(2)}, u32[]{:S(2)}) collective-permute-start(bf16[4,256,384]{2,1,0:T(8,128)(2,1)S(1)} %collective-permute-done.66.refs_9_), channel_id=1, source_target_pairs={{0,4},{8,0},{16,8},{24,16},{28,24},{20,28},{12,20},{4,12},{1,5},{9... | collective-permute-start | bytes 2359304 | tf_op jit(solution)/shard_map/ppermute | solution.py:700
  563.9 19.5 %collective-permute-start.61 = (bf16[4,272,384]{2,1,0:T(8,128)(2,1)S(1)}, bf16[4,272,384]{2,1,0:T(8,128)(2,1)S(1)}, u32[]{:S(2)}, u32[]{:S(2)}) collective-permute-start(bf16[4,272,384]{2,1,0:T(8,128)(2,1)S(1)} %collective-permute-done.60.refs_2_), channel_id=1, source_target_pairs={{0,8},{8,16},{16,24},{24,28},{28,20},{20,12},{12,4},{4,0},{1,9},{9... | collective-permute-start | bytes 2506760 | tf_op jit(solution)/shard_map/ppermute | solution.py:700
  565.6 18.9 %collective-permute-start.68 = (bf16[4,256,384]{2,1,0:T(8,128)(2,1)S(1)}, bf16[4,256,384]{2,1,0:T(8,128)(2,1)S(1)}, u32[]{:S(2)}, u32[]{:S(2)}) collective-permute-start(bf16[4,256,384]{2,1,0:T(8,128)(2,1)S(1)} %collective-permute-done.67.refs_10_), channel_id=1, source_target_pairs={{0,4},{8,0},{16,8},{24,16},{28,24},{20,28},{12,20},{4,12},{1,5},{9... | collective-permute-start | bytes 2359304 | tf_op jit(solution)/shard_map/ppermute | solution.py:700
  566.5 39.0 %collective-permute-start.26 = (bf16[512,1536]{1,0:T(8,128)(2,1)S(1)}, bf16[512,1536]{1,0:T(8,128)(2,1)S(1)}, u32[]{:S(2)}, u32[]{:S(2)}) collective-permute-start(bf16[512,1536]{1,0:T(8,128)(2,1)S(1)} %slice.72), channel_id=1, source_target_pairs={{0,1},{1,0},{2,3},{3,2},{4,5},{5,4},{6,7},{7,6},{8,9},{9,8},{10,11... | collective-permute-start | bytes 4718600 | tf_op jit(solution)/shard_map/ppermute | solution.py:45
  583.4 19.7 %collective-permute-start.62 = (bf16[4,272,384]{2,1,0:T(8,128)(2,1)S(1)}, bf16[4,272,384]{2,1,0:T(8,128)(2,1)S(1)}, u32[]{:S(2)}, u32[]{:S(2)}) collective-permute-start(bf16[4,272,384]{2,1,0:T(8,128)(2,1)S(1)} %collective-permute-done.61.refs_3_), channel_id=1, source_target_pairs={{0,8},{8,16},{16,24},{24,28},{28,20},{20,12},{12,4},{4,0},{1,9},{9... | collective-permute-start | bytes 2506760 | tf_op jit(solution)/shard_map/ppermute | solution.py:700
  584.5 17.7 %collective-permute-start.69 = (bf16[4,256,384]{2,1,0:T(8,128)(2,1)S(1)}, bf16[4,256,384]{2,1,0:T(8,128)(2,1)S(1)}, u32[]{:S(2)}, u32[]{:S(2)}) collective-permute-start(bf16[4,256,384]{2,1,0:T(8,128)(2,1)S(1)} %collective-permute-done.68.refs_11_), channel_id=1, source_target_pairs={{0,4},{8,0},{16,8},{24,16},{28,24},{20,28},{12,20},{4,12},{1,5},{9... | collective-permute-start | bytes 2359304 | tf_op jit(solution)/shard_map/ppermute | solution.py:700
  602.2 17.5 %collective-permute-start.70 = (bf16[4,256,384]{2,1,0:T(8,128)(2,1)S(1)}, bf16[4,256,384]{2,1,0:T(8,128)(2,1)}, u32[]{:S(2)}, u32[]{:S(2)}) collective-permute-start(bf16[4,256,384]{2,1,0:T(8,128)(2,1)S(1)} %collective-permute-done.69.refs_12_), channel_id=1, source_target_pairs={{0,4},{8,0},{16,8},{24,16},{28,24},{20,28},{12,20},{4,12},{1,5},{9... | collective-permute-start | bytes 2359304 | tf_op jit(solution)/shard_map/ppermute | solution.py:700
  603.2 18.5 %collective-permute-start.63 = (bf16[4,272,384]{2,1,0:T(8,128)(2,1)S(1)}, bf16[4,272,384]{2,1,0:T(8,128)(2,1)}, u32[]{:S(2)}, u32[]{:S(2)}) collective-permute-start(bf16[4,272,384]{2,1,0:T(8,128)(2,1)S(1)} %collective-permute-done.62.refs_4_), channel_id=1, source_target_pairs={{0,8},{8,16},{16,24},{24,28},{28,20},{20,12},{12,4},{4,0},{1,9},{9... | collective-permute-start | bytes 2506760 | tf_op jit(solution)/shard_map/ppermute | solution.py:700
  606.9 34.3 %collective-permute-start.27 = (bf16[256,1536]{1,0:T(8,128)(2,1)}, bf16[256,1536]{1,0:T(8,128)(2,1)}, u32[]{:S(2)}, u32[]{:S(2)}) collective-permute-start(bf16[256,1536]{1,0:T(8,128)(2,1)} %add_convert_fusion.2), channel_id=1, source_target_pairs={{0,2},{1,3},{2,0},{3,1},{4,6},{5,7},{6,4},{7,5},{8,10},{9,11},{10,... | collective-permute-start | bytes 2359304 | tf_op jit(solution)/shard_map/ppermute | solution.py:45
  619.7 27.3 %collective-permute-start.71 = (bf16[4,256,384]{2,1,0:T(8,128)(2,1)}, bf16[4,256,384]{2,1,0:T(8,128)(2,1)}, u32[]{:S(2)}, u32[]{:S(2)}) collective-permute-start(bf16[4,256,384]{2,1,0:T(8,128)(2,1)} %collective-permute-done.70.refs_13_), channel_id=1, source_target_pairs={{0,4},{8,0},{16,8},{24,16},{28,24},{20,28},{12,20},{4,12},{1,5},{9... | collective-permute-start | bytes 2359304 | tf_op jit(solution)/shard_map/ppermute | solution.py:700
  621.7 26.9 %collective-permute-start.64 = (bf16[4,272,384]{2,1,0:T(8,128)(2,1)}, bf16[4,272,384]{2,1,0:T(8,128)(2,1)}, u32[]{:S(2)}, u32[]{:S(2)}) collective-permute-start(bf16[4,272,384]{2,1,0:T(8,128)(2,1)} %collective-permute-done.63.refs_5_), channel_id=1, source_target_pairs={{0,8},{8,16},{16,24},{24,28},{28,20},{20,12},{12,4},{4,0},{1,9},{9... | collective-permute-start | bytes 2506760 | tf_op jit(solution)/shard_map/ppermute | solution.py:700
  642.6 9.1 %collective-permute-start.58 = (f32[2,384]{1,0:T(2,128)S(1)}, f32[2,384]{1,0:T(2,128)S(1)}, u32[]{:S(2)}, u32[]{:S(2)}) collective-permute-start(f32[2,384]{1,0:T(2,128)S(1)} %add.265), channel_id=1, source_target_pairs={{0,24},{4,28},{8,16},{12,20},{16,8},{20,12},{24,0},{28,4},{1,25},{... | collective-permute-start | bytes 9224 | tf_op jit(solution)/shard_map/ppermute | solution.py:45
  647.0 18.2 %collective-permute-start.72 = (bf16[4,256,384]{2,1,0:T(8,128)(2,1)}, bf16[4,256,384]{2,1,0:T(8,128)(2,1)S(1)}, u32[]{:S(2)}, u32[]{:S(2)}) collective-permute-start(bf16[4,256,384]{2,1,0:T(8,128)(2,1)} %collective-permute-done.71.refs_14_), channel_id=1, source_target_pairs={{0,4},{8,0},{16,8},{24,16},{28,24},{20,28},{12,20},{4,12},{1,5},{9... | collective-permute-start | bytes 2359304 | tf_op jit(solution)/shard_map/ppermute | solution.py:700
  648.5 18.9 %collective-permute-start.65 = (bf16[4,272,384]{2,1,0:T(8,128)(2,1)}, bf16[4,272,384]{2,1,0:T(8,128)(2,1)S(1)}, u32[]{:S(2)}, u32[]{:S(2)}) collective-permute-start(bf16[4,272,384]{2,1,0:T(8,128)(2,1)} %collective-permute-done.64.refs_6_), channel_id=1, source_target_pairs={{0,8},{8,16},{16,24},{24,28},{28,20},{20,12},{12,4},{4,0},{1,9},{9... | collective-permute-start | bytes 2506760 | tf_op jit(solution)/shard_map/ppermute | solution.py:700
  (78 other events, 893.2 us)
Sparse Core Ops, SparseCore 0:
  259.5 224.2 reduce-scatter.1

commit v5 on v4

--- a/solution.py
+++ b/solution.py
@@ -979,13 +979,12 @@
         raw_terms = terms_of(normed_one_all, raw_part)
         raw_got = over_ctx(side_of(raw_terms, 1), 1)
         out_got = exchange_levels(lambda k: level_of(out_kept, k))
-        raw_got, out_got = together(raw_got, out_got)
+        raw_got, out_got, input_grad = together(raw_got, out_got, input_grad)
         raw_kept = add_low(side_of(raw_terms, 0), raw_got)
         out_sums = add_low(level_of(out_kept, 0), *out_got)
-        raw_kept, unit_sums = together(raw_kept, unit_sums)
         raw_got = exchange_levels(lambda k: level_of(raw_kept, k))
+        raw_got, unit_sums = together(raw_got, unit_sums)
         unit_mine = deal_rows(unit_sums)
-        raw_got, unit_mine = together(raw_got, unit_mine)
         raw_sums = add_low(level_of(raw_kept, 0), *raw_got)
     else:
         raw_terms = terms_of(normed_one_all, raw_part)

time: 699 us -> 692 us (0.990)
  waiting for transfers between devices: 361 us -> 353 us
    reduce_scatter x1, waiting for transfers between devices: 13.3 us -> 0.01 us  [body(): lax.psum_scatter(unit_terms, 'ctx', scatter_dimension=0, tiled=True)]
    ppermute x59, waiting for transfers between devices: 194 us -> 204 us  [swap(): return lax.ppermute(array, axis, [(i, i ^ bits) for i in range(size)])]
    unnamed x128 -> x120, local copies, waits for them, and re-layouts: 16.7 us -> 16.8 us
  transfers between devices with their start and end apart: 78 -> 78, of which waited for: 41 -> 39; matrix products, arithmetic and copies ran while one was open for 9% -> 9% of each run, Pallas kernels for 15% -> 15%
where the time goes in v5:
time: 692 us; the launch traced here: 684 us
  waiting for transfers between devices  353 us (51%)
  Pallas kernels  144 us (21%)
  starting transfers between devices  89.8 us (13%)
  local copies, waits for them, and re-layouts  43 us (6%)
  other arithmetic  31.7 us (5%)
  between operations  15.1 us (2%)
  matrix products  7.9 us (1%)
    ppermute x59, waiting for transfers between devices, swap(): return lax.ppermute(array, axis, [(i, i ^ bits) for i in range(size)])  204 us
    ppermute x14, waiting for transfers between devices, turn_ring(): lax.ppermute(array, 'ctx', [(ring[i], ring[(i + step) % count]) for i in...  93.2 us
    ppermute x59, starting transfers between devices, swap(): return lax.ppermute(array, axis, [(i, i ^ bits) for i in range(size)])  50.6 us
    pallas_call x5, Pallas kernels, whole_call(): pl.pallas_call(kernel, grid_spec=pltpu.PrefetchScalarGridSpec(num_scalar_...  44.8 us
    all_to_all x1, waiting for transfers between devices, body(): grad_mixed = lax.all_to_all(grad_mixed, 'ctx', 0, 0, tiled=True)  41.4 us
    pallas_call x2, Pallas kernels, attention_call(): pl.pallas_call(kernel, grid_spec=pltpu.PrefetchScalarGridSpec(num_scalar_...  36.6 us
    pallas_call x1, Pallas kernels, units_call(): pl.pallas_call(units_kernel, grid_spec=pltpu.PrefetchScalarGridSpec(num_s...  28 us
    ppermute x14, starting transfers between devices, turn_ring(): lax.ppermute(array, 'ctx', [(ring[i], ring[(i + step) % count]) for i in...  19.5 us
  transfers between devices with their start and end apart: 78, of which 39 were waited for; matrix products, arithmetic and copies ran while one was open for 9% of the time, Pallas kernels for 15%

profile of v5, /device:TPU:0, one launch (start us, length us, event | category | flops | bytes accessed | tf_op | source)
XLA Modules:
  0.0 684.5 jit_solution(1987829079246291049)
XLA Ops:
  9.2 2.6 collective-permute-start.1
  14.8 2.0 collective-permute-start.4
  28.5 6.5 collective-permute-done.4.refs_6_
  38.2 16.2 %collective-permute-done.5.refs_7_ = bf16[384,1024]{1,0:T(8,128)(2,1)} collective-permute-done((bf16[384,1024]{1,0:T(8,128)(2,1)}, bf16[384,1024]{1,0:T(8,128)(2,1)}, u32[]{:S(2)}, u32[]{:S(2)}) %collective-permute-start.5) | collective-permute-done | bytes 786464 | tf_op jit(solution)/shard_map/ppermute | solution.py:45
  60.5 11.5 %query_key_value.1 = (bf16[256,1536]{1,0:T(8,128)(2,1)}, bf16[8,256,384]{2,1,0:T(8,128)(2,1)}) custom-call(s32[3]{0:T(128)} %pad_add_fusion.code_ref, bf16[256,1536]{1,0:T(8,128)(2,1)} %bitcast.67, f32[256,96]{1,0:T(8,128)} %get-tuple-element.184.cosine_ref, f32[256,96]{1,0:T(8,128)} %get-tuple-element.185.sine_ref, bf16[2,384]{1,0:T(2,128)(2,1)} %copy-done.52, ...), custom_call_target="tpu_custom_call" | custom-call | flops 2415919104 | bytes 12785664 | tf_op jit(solution)/shard_map/query_key_value/pallas_call | solution.py:153
  72.3 5.2 all-to-all-start
  81.0 2.0 collective-permute-start.13
  83.1 23.7 %collective-permute-done.11.refs_2_ = bf16[3,384,512]{2,1,0:T(8,128)(2,1)} collective-permute-done((bf16[3,384,512]{2,1,0:T(8,128)(2,1)}, bf16[3,384,512]{2,1,0:T(8,128)(2,1)}, u32[]{:S(2)}, u32[]{:S(2)}) %collective-permute-start.11) | collective-permute-done | bytes 1179680 | tf_op jit(solution)/shard_map/ppermute | solution.py:45
  106.8 2.1 collective-permute-start.12
  108.9 5.9 all-to-all-done.load_ref
  114.8 12.3 %attention_forward.1 = bf16[8,256,192]{2,1,0:T(8,128)(2,1)} custom-call(s32[16]{0:T(128)} %and_select_fusion.2.order_ref, bf16[8,256,384]{2,1,0:T(8,128)(2,1)} %all-to-all-done.load_ref), custom_call_target="tpu_custom_call" | custom-call | flops 4294967296 | bytes 3145728 | tf_op jit(solution)/shard_map/attention_forward/pallas_call | solution.py:546
  129.9 4.1 collective-permute-done.12.refs_3_
  134.0 2.2 copy.24
  136.3 6.2 all-to-all-start.1
  143.6 12.9 %collective-permute-done.14.refs_4_ = bf16[3,384,512]{2,1,0:T(8,128)(2,1)} collective-permute-done((bf16[3,384,512]{2,1,0:T(8,128)(2,1)}, bf16[3,384,512]{2,1,0:T(8,128)(2,1)}, u32[]{:S(2)}, u32[]{:S(2)}) %collective-permute-start.14) | collective-permute-done | bytes 1179680 | tf_op jit(solution)/shard_map/ppermute | solution.py:45
  156.5 3.5 pad_maximum_fusion.grad_ref
  161.4 2.2 copy.25.mixed_ref
  164.7 6.8 attention_output.1
  171.8 14.8 %collective-permute-done.21.refs_5_ = bf16[3,384,512]{2,1,0:T(8,128)(2,1)} collective-permute-done((bf16[3,384,512]{2,1,0:T(8,128)(2,1)}, bf16[3,384,512]{2,1,0:T(8,128)(2,1)}, u32[]{:S(2)}, u32[]{:S(2)}) %collective-permute-start.21) | collective-permute-done | bytes 1179680 | tf_op jit(solution)/shard_map/ppermute | solution.py:45
  186.6 3.9 collective-permute-done.20
  197.0 28.0 %feed_forward.1 = (bf16[1024,1536]{1,0:T(8,128)(2,1)}, bf16[1024,1536]{1,0:T(8,128)(2,1)}, bf16[1024,1024]{1,0:T(8,128)(2,1)}, bf16[1024,1024]{1,0:T(8,128)(2,1)}, bf16[1024,1024]{1,0:T(8,128)(2,1)}) custom-call(s32[3]{0:T(128)} %pad_add_fusion.code_ref, bf16[1024,1536]{1,0:T(8,128)(2,1)} %copy-done.1, bf16[1024,1536]{1,0:T(8,128)(2,1)} %pad_maximum_fusion.grad_ref, ...), custom_call_target="tpu_custom_call" | custom-call | flops 19327352832 | bytes 22020096 | tf_op jit(solution)/shard_map/feed_forward/pallas_call | solution.py:392
  226.9 3.3 collective-permute-done.24
  237.6 19.2 %unit_grads.1 = bf16[12288,384]{1,0:T(8,128)(2,1)} custom-call(bf16[1024,1536]{1,0:T(8,128)(2,1)S(1)} %copy-done.2, bf16[1024,1536]{1,0:T(8,128)(2,1)S(1)} %copy-done, bf16[1024,1024]{1,0:T(8,128)(2,1)S(1)} %copy-done.4, bf16[1024,1024]{1,0:T(8,128)(2,1)S(1)} %copy-done.5, bf16[1024,1024]{1,0:T(8,128)(2,1)S(1)} %copy-done.3), custom_call_target="tpu_custom_call" | custom-call | flops 99999997952 | tf_op jit(solution)/shard_map/unit_grads/pallas_call | solution.py:832
  256.9 2.6 convert_add_fusion.grad_ref
  259.4 7.8 %attention_output_back.1 = (f32[256,1536]{1,0:T(8,128)}, bf16[256,1536]{1,0:T(8,128)(2,1)}, bf16[8,256,192]{2,1,0:T(8,128)(2,1)}, f32[1,1536]{1,0:T(1,128)}) custom-call(s32[3]{0:T(128)} %pad_add_fusion.code_ref, f32[256,1536]{1,0:T(8,128)} %get-tuple-element.84.middle_ref, f32[256,1536]{1,0:T(8,128)} %convert_add_fusion.grad_ref, ...), custom_call_target="tpu_custom_call" | custom-call | flops 1207959552 | bytes 11808768 | tf_op jit(solution)/shard_map/attention_output_back/pallas_call | solution.py:153
  267.2 2.3 copy.26
  269.5 4.0 all-to-all-start.2
  274.4 41.4 %all-to-all-done.2 = bf16[8,256,192]{1,2,0:T(8,128)(2,1)S(1)} async-done(((bf16[8,256,192]{1,2,0:T(8,128)(2,1)}), bf16[8,256,192]{1,2,0:T(8,128)(2,1)S(1)}, u32[]{:S(2)}, u32[]{:S(2)}) %all-to-all-start.2) | async-done | bytes 786464 | tf_op jit(solution)/shard_map/all_to_all | solution.py:929
  317.1 24.3 %attention_backward.1 = bf16[8,256,384]{2,1,0:T(8,128)(2,1)} custom-call(s32[16]{0:T(128)} %and_select_fusion.2.order_ref, bf16[8,256,384]{2,1,0:T(8,128)(2,1)} %all-to-all-done.load_ref, bf16[8,256,192]{2,1,0:T(8,128)(2,1)} %copy.27.grad_ref), custom_call_target="tpu_custom_call" | custom-call | flops 10737418240 | bytes 6291456 | tf_op jit(solution)/shard_map/attention_backward/pallas_call | solution.py:546
  341.4 3.8 all-to-all-start.3
  346.8 19.7 %collective-permute-done.28 = bf16[256,1536]{1,0:T(8,128)(2,1)S(1)} collective-permute-done((bf16[256,1536]{1,0:T(8,128)(2,1)S(1)}, bf16[256,1536]{1,0:T(8,128)(2,1)S(1)}, u32[]{:S(2)}, u32[]{:S(2)}) %collective-permute-start.28) | collective-permute-done | bytes 786464 | tf_op jit(solution)/shard_map/ppermute | solution.py:45
  367.4 2.0 constant_dynamic-slice_fusion.22
  371.6 4.7 collective-permute-done.37
  376.3 4.9 collective-permute-done.35
  381.2 3.8 fusion.11
  388.1 6.8 all-to-all-done.3.load_ref
  396.1 7.8 %turn_back.1 = (bf16[256,3072]{1,0:T(8,128)(2,1)}, bf16[4,256,768]{2,1,0:T(8,128)(2,1)}) custom-call(s32[3]{0:T(128)} %pad_add_fusion.code_ref, bf16[8,256,384]{2,1,0:T(8,128)(2,1)} %copy-done.11, f32[256,96]{1,0:T(8,128)} %get-tuple-element.184.cosine_ref, f32[256,96]{1,0:T(8,128)} %get-tuple-element.185.sine_ref), custom_call_target="tpu_custom_call" | custom-call | bytes 4915200 | tf_op jit(solution)/shard_map/turn_back/pallas_call | solution.py:153
  407.6 9.3 %collective-permute-done.32 = bf16[256,768]{1,0:T(8,128)(2,1)S(1)} collective-permute-done((bf16[256,768]{1,0:T(8,128)(2,1)S(1)}, bf16[256,768]{1,0:T(8,128)(2,1)S(1)}, u32[]{:S(2)}, u32[]{:S(2)}) %collective-permute-start.32) | collective-permute-done | bytes 393248 | tf_op jit(solution)/shard_map/ppermute | solution.py:45
  416.8 8.4 %collective-permute-done.30 = bf16[256,768]{1,0:T(8,128)(2,1)S(1)} collective-permute-done((bf16[256,768]{1,0:T(8,128)(2,1)S(1)}, bf16[256,768]{1,0:T(8,128)(2,1)S(1)}, u32[]{:S(2)}, u32[]{:S(2)}) %collective-permute-start.30) | collective-permute-done | bytes 393248 | tf_op jit(solution)/shard_map/ppermute | solution.py:45
  426.6 4.1 convolution_convert_fusion
  434.6 2.1 collective-permute-start.41
  436.7 2.3 collective-permute-start.42
  439.0 10.9 %query_key_value_back.1 = (f32[256,1536]{1,0:T(8,128)}, f32[1,1536]{1,0:T(1,128)}) custom-call(s32[3]{0:T(128)} %pad_add_fusion.code_ref, bf16[256,3072]{1,0:T(8,128)(2,1)} %get-tuple-element.110.raw_ref, bf16[256,1536]{1,0:T(8,128)(2,1)} %bitcast.69, f32[256,1536]{1,0:T(8,128)} %get-tuple-element.111.grad_middle_ref, bf16[2,384]{1,0:T(2,128)(2,1)} %copy-done.52, ...), custom_call_target="tpu_custom_call" | custom-call | flops 2415919104 | bytes 14954496 | tf_op jit(solution)/shard_map/query_key_value_back/pallas_call | solution.py:153
  450.2 3.9 collective-permute-done.41
  454.1 2.2 collective-permute-done.42
  456.3 12.7 %collective-permute-done.39 = bf16[4,192,768]{2,1,0:T(8,128)(2,1)} collective-permute-done((bf16[4,192,768]{2,1,0:T(8,128)(2,1)S(1)}, bf16[4,192,768]{2,1,0:T(8,128)(2,1)}, u32[]{:S(2)}, u32[]{:S(2)}) %collective-permute-start.39) | collective-permute-done | bytes 1179680 | tf_op jit(solution)/shard_map/ppermute | solution.py:45
  471.8 2.8 collective-permute-start.49
  476.3 15.3 %collective-permute-done.48 = bf16[4,48,768]{2,1,0:T(8,128)(2,1)S(1)} collective-permute-done((bf16[4,48,768]{2,1,0:T(8,128)(2,1)S(1)}, bf16[4,48,768]{2,1,0:T(8,128)(2,1)S(1)}, u32[]{:S(2)}, u32[]{:S(2)}) %collective-permute-start.48) | collective-permute-done | bytes 294944 | tf_op jit(solution)/shard_map/ppermute | solution.py:45
  491.6 10.0 %collective-permute-done.49 = bf16[4,48,768]{2,1,0:T(8,128)(2,1)S(1)} collective-permute-done((bf16[4,48,768]{2,1,0:T(8,128)(2,1)S(1)}, bf16[4,48,768]{2,1,0:T(8,128)(2,1)S(1)}, u32[]{:S(2)}, u32[]{:S(2)}) %collective-permute-start.49) | collective-permute-done | bytes 294944 | tf_op jit(solution)/shard_map/ppermute | solution.py:45
  507.3 2.4 collective-permute-done.52
  509.8 6.1 collective-permute-done.58
  515.9 6.4 collective-permute-done.57
  522.4 6.8 collective-permute-start.59
  529.3 17.8 %collective-permute-done.59.refs_1_ = bf16[4,272,384]{2,1,0:T(8,128)(2,1)S(1)} collective-permute-done((bf16[4,272,384]{2,1,0:T(8,128)(2,1)S(1)}, bf16[4,272,384]{2,1,0:T(8,128)(2,1)S(1)}, u32[]{:S(2)}, u32[]{:S(2)}) %collective-permute-start.59) | collective-permute-done | bytes 835616 | tf_op jit(solution)/shard_map/ppermute | solution.py:700
  547.1 2.5 collective-permute-start.60
  549.6 18.0 %collective-permute-done.60.refs_2_ = bf16[4,272,384]{2,1,0:T(8,128)(2,1)S(1)} collective-permute-done((bf16[4,272,384]{2,1,0:T(8,128)(2,1)S(1)}, bf16[4,272,384]{2,1,0:T(8,128)(2,1)S(1)}, u32[]{:S(2)}, u32[]{:S(2)}) %collective-permute-start.60) | collective-permute-done | bytes 835616 | tf_op jit(solution)/shard_map/ppermute | solution.py:700
  570.2 16.7 %collective-permute-done.61.refs_3_ = bf16[4,272,384]{2,1,0:T(8,128)(2,1)S(1)} collective-permute-done((bf16[4,272,384]{2,1,0:T(8,128)(2,1)S(1)}, bf16[4,272,384]{2,1,0:T(8,128)(2,1)S(1)}, u32[]{:S(2)}, u32[]{:S(2)}) %collective-permute-start.61) | collective-permute-done | bytes 835616 | tf_op jit(solution)/shard_map/ppermute | solution.py:700
  589.0 16.7 %collective-permute-done.62.refs_4_ = bf16[4,272,384]{2,1,0:T(8,128)(2,1)S(1)} collective-permute-done((bf16[4,272,384]{2,1,0:T(8,128)(2,1)S(1)}, bf16[4,272,384]{2,1,0:T(8,128)(2,1)S(1)}, u32[]{:S(2)}, u32[]{:S(2)}) %collective-permute-start.62) | collective-permute-done | bytes 835616 | tf_op jit(solution)/shard_map/ppermute | solution.py:700
  610.4 13.9 %collective-permute-done.63.refs_5_ = bf16[4,272,384]{2,1,0:T(8,128)(2,1)} collective-permute-done((bf16[4,272,384]{2,1,0:T(8,128)(2,1)S(1)}, bf16[4,272,384]{2,1,0:T(8,128)(2,1)}, u32[]{:S(2)}, u32[]{:S(2)}) %collective-permute-start.63) | collective-permute-done | bytes 835616 | tf_op jit(solution)/shard_map/ppermute | solution.py:700
  634.6 6.7 collective-permute-done.46
  641.4 4.3 collective-permute-start.54
  647.7 2.7 fusion.19
  651.0 8.9 %collective-permute-done.72.refs_15_ = bf16[4,256,384]{2,1,0:T(8,128)(2,1)S(1)} collective-permute-done((bf16[4,256,384]{2,1,0:T(8,128)(2,1)}, bf16[4,256,384]{2,1,0:T(8,128)(2,1)S(1)}, u32[]{:S(2)}, u32[]{:S(2)}) %collective-permute-start.72) | collective-permute-done | bytes 786464 | tf_op jit(solution)/shard_map/ppermute | solution.py:700
  662.1 15.3 %deal_gradients.1 = (f32[384,4096]{1,0:T(8,128)}, f32[384,4096]{1,0:T(8,128)}, f32[384,4096]{1,0:T(8,128)}, f32[384,1536]{1,0:T(8,128)}, f32[384,1536]{1,0:T(8,1...) custom-call(s32[17]{0:T(128)} %pad_add_fusion.1.code_ref, bf16[4,272,384]{2,1,0:T(8,128)(2,1)} %copy-done.13, ...), custom_call_target="tpu_custom_call" | custom-call | tf_op jit(solution)/shard_map/deal_gradients/pallas_call | solution.py:781
  (292 shorter events, 107.1 us)
Async XLA Ops:
  8.7 19.8 %collective-permute-start = (bf16[2,384]{1,0:T(2,128)(2,1)S(1)}, bf16[2,384]{1,0:T(2,128)(2,1)S(1)}, u32[]{:S(2)}, u32[]{:S(2)}) collective-permute-start(bf16[2,384]{1,0:T(2,128)(2,1)S(1)} %pad_maximum_fusion.17.refs_0_), channel_id=1, source_target_pairs={{0,1},{1,0},{2,3},{3,2},{4,5},{5,4},{6,7},{7,6},{8,9},{9,8},{10,11... | collective-permute-start | bytes 4616 | tf_op jit(solution)/shard_map/ppermute | solution.py:45
  9.2 19.3 %collective-permute-start.1 = (bf16[2,384]{1,0:T(2,128)(2,1)S(1)}, bf16[2,384]{1,0:T(2,128)(2,1)S(1)}, u32[]{:S(2)}, u32[]{:S(2)}) collective-permute-start(bf16[2,384]{1,0:T(2,128)(2,1)S(1)} %pad_maximum_fusion.17.refs_0_), channel_id=1, source_target_pairs={{0,2},{1,3},{2,0},{3,1},{4,6},{5,7},{6,4},{7,5},{8,10},{9,11},{10,... | collective-permute-start | bytes 4616 | tf_op jit(solution)/shard_map/ppermute | solution.py:45
  11.7 16.8 %collective-permute-start.2 = (bf16[2,384]{1,0:T(2,128)(2,1)S(1)}, bf16[2,384]{1,0:T(2,128)(2,1)S(1)}, u32[]{:S(2)}, u32[]{:S(2)}) collective-permute-start(bf16[2,384]{1,0:T(2,128)(2,1)S(1)} %pad_maximum_fusion.17.refs_0_), channel_id=1, source_target_pairs={{0,3},{1,2},{2,1},{3,0},{4,7},{5,6},{6,5},{7,4},{8,11},{9,10},{10,... | collective-permute-start | bytes 4616 | tf_op jit(solution)/shard_map/ppermute | solution.py:45
  13.4 47.0 %collective-permute-start.3 = (bf16[384,3072]{1,0:T(8,128)(2,1)S(1)}, bf16[384,3072]{1,0:T(8,128)(2,1)}, u32[]{:S(2)}, u32[]{:S(2)}) collective-permute-start(bf16[384,3072]{1,0:T(8,128)(2,1)S(1)} %constant_dynamic-update-slice_fusion.refs_4_), channel_id=1, source_target_pairs={{0,1},{1,0},{2,3},{3,2},{4,5},{5,4},{6,7},{7,6},{8,9},{9,8},{10,11... | collective-permute-start | bytes 7077896 | tf_op jit(solution)/shard_map/ppermute | solution.py:45
  14.8 20.2 %collective-permute-start.4 = (bf16[384,1024]{1,0:T(8,128)(2,1)}, bf16[384,1024]{1,0:T(8,128)(2,1)}, u32[]{:S(2)}, u32[]{:S(2)}) collective-permute-start(bf16[384,1024]{1,0:T(8,128)(2,1)} %constant_dynamic-slice_fusion.24), channel_id=1, source_target_pairs={{0,2},{1,3},{2,0},{3,1},{4,6},{5,7},{6,4},{7,5},{8,10},{9,11},{10,... | collective-permute-start | bytes 2359304 | tf_op jit(solution)/shard_map/ppermute | solution.py:45
  35.0 19.4 %collective-permute-start.5 = (bf16[384,1024]{1,0:T(8,128)(2,1)}, bf16[384,1024]{1,0:T(8,128)(2,1)}, u32[]{:S(2)}, u32[]{:S(2)}) collective-permute-start(bf16[384,1024]{1,0:T(8,128)(2,1)} %collective-permute-done.4.refs_6_), channel_id=1, source_target_pairs={{0,4},{4,0},{8,12},{12,8},{16,20},{20,16},{24,28},{28,24},{1,5},{5... | collective-permute-start | bytes 2359304 | tf_op jit(solution)/shard_map/ppermute | solution.py:45
  36.7 18.7 %collective-permute-start.6 = (bf16[384,1024]{1,0:T(8,128)(2,1)}, bf16[384,1024]{1,0:T(8,128)(2,1)}, u32[]{:S(2)}, u32[]{:S(2)}) collective-permute-start(bf16[384,1024]{1,0:T(8,128)(2,1)} %pad_maximum_fusion.13), channel_id=1, source_target_pairs={{0,2},{1,3},{2,0},{3,1},{4,6},{5,7},{6,4},{7,5},{8,10},{9,11},{10,... | collective-permute-start | bytes 2359304 | tf_op jit(solution)/shard_map/ppermute | solution.py:45
  38.2 22.3 %collective-permute-start.7 = (bf16[384,1024]{1,0:T(8,128)(2,1)}, bf16[384,1024]{1,0:T(8,128)(2,1)}, u32[]{:S(2)}, u32[]{:S(2)}) collective-permute-start(bf16[384,1024]{1,0:T(8,128)(2,1)} %collective-permute-done.4.refs_6_), channel_id=1, source_target_pairs={{0,1},{1,0},{2,3},{3,2},{4,5},{5,4},{6,7},{7,6},{8,9},{9,8},{10,11... | collective-permute-start | bytes 2359304 | tf_op jit(solution)/shard_map/ppermute | solution.py:45
  56.3 16.1 %collective-permute-start.10 = (bf16[384,768]{1,0:T(8,128)(2,1)}, bf16[384,768]{1,0:T(8,128)(2,1)}, u32[]{:S(2)}, u32[]{:S(2)}) collective-permute-start(bf16[384,768]{1,0:T(8,128)(2,1)} %constant_dynamic-slice_fusion.23), channel_id=1, source_target_pairs={{0,2},{1,3},{2,0},{3,1},{4,6},{5,7},{6,4},{7,5},{8,10},{9,11},{10,... | collective-permute-start | bytes 1769480 | tf_op jit(solution)/shard_map/ppermute | solution.py:45
  72.3 42.5 %all-to-all-start = ((bf16[8,256,384]{2,1,0:T(8,128)(2,1)}), bf16[8,256,384]{2,1,0:T(8,128)(2,1)}, u32[]{:S(2)}, u32[]{:S(2)}) async-start(bf16[8,256,384]{2,1,0:T(8,128)(2,1)} %get-tuple-element.77), calls=%async_computation | async-start | bytes 3145728 | tf_op jit(solution)/shard_map/all_to_all | solution.py:895
  77.6 29.3 %collective-permute-start.11 = (bf16[3,384,512]{2,1,0:T(8,128)(2,1)}, bf16[3,384,512]{2,1,0:T(8,128)(2,1)}, u32[]{:S(2)}, u32[]{:S(2)}) collective-permute-start(bf16[3,384,512]{2,1,0:T(8,128)(2,1)} %pad_maximum_fusion.8), channel_id=1, source_target_pairs={{0,2},{1,3},{2,0},{3,1},{4,6},{5,7},{6,4},{7,5},{8,10},{9,11},{10,... | collective-permute-start | bytes 3538952 | tf_op jit(solution)/shard_map/ppermute | solution.py:45
  79.1 48.0 %collective-permute-start.15 = (bf16[256,1536]{1,0:T(8,128)(2,1)S(1)}, bf16[256,1536]{1,0:T(8,128)(2,1)S(1)}, u32[]{:S(2)}, u32[]{:S(2)}) collective-permute-start(bf16[256,1536]{1,0:T(8,128)(2,1)S(1)} %bitcast.64), channel_id=1, source_target_pairs={{0,2},{1,3},{2,0},{3,1},{4,6},{5,7},{6,4},{7,5},{8,10},{9,11},{10,... | collective-permute-start | bytes 2359304 | tf_op jit(solution)/shard_map/ppermute | solution.py:45
  81.0 48.9 %collective-permute-start.13 = (bf16[384,768]{1,0:T(8,128)(2,1)}, bf16[384,768]{1,0:T(8,128)(2,1)S(1)}, u32[]{:S(2)}, u32[]{:S(2)}) collective-permute-start(bf16[384,768]{1,0:T(8,128)(2,1)} %collective-permute-done.10.refs_6_), channel_id=1, source_target_pairs={{0,8},{4,12},{8,0},{12,4},{16,24},{20,28},{24,16},{28,20},{1,9},{5... | collective-permute-start | bytes 1769480 | tf_op jit(solution)/shard_map/ppermute | solution.py:45
  106.8 27.2 %collective-permute-start.12 = (bf16[3,384,512]{2,1,0:T(8,128)(2,1)}, bf16[3,384,512]{2,1,0:T(8,128)(2,1)}, u32[]{:S(2)}, u32[]{:S(2)}) collective-permute-start(bf16[3,384,512]{2,1,0:T(8,128)(2,1)} %collective-permute-done.11.refs_2_), channel_id=1, source_target_pairs={{0,4},{4,0},{8,12},{12,8},{16,20},{20,16},{24,28},{28,24},{1,5},{5... | collective-permute-start | bytes 3538952 | tf_op jit(solution)/shard_map/ppermute | solution.py:45
  128.5 27.9 %collective-permute-start.16 = (bf16[512,1536]{1,0:T(8,128)(2,1)}, bf16[512,1536]{1,0:T(8,128)(2,1)}, u32[]{:S(2)}, u32[]{:S(2)}) collective-permute-start(bf16[512,1536]{1,0:T(8,128)(2,1)} %pad_maximum_fusion.3), channel_id=1, source_target_pairs={{0,1},{1,0},{2,3},{3,2},{4,5},{5,4},{6,7},{7,6},{8,9},{9,8},{10,11... | collective-permute-start | bytes 4718600 | tf_op jit(solution)/shard_map/ppermute | solution.py:45
  128.5 27.9 %collective-permute-start.14 = (bf16[3,384,512]{2,1,0:T(8,128)(2,1)}, bf16[3,384,512]{2,1,0:T(8,128)(2,1)}, u32[]{:S(2)}, u32[]{:S(2)}) collective-permute-start(bf16[3,384,512]{2,1,0:T(8,128)(2,1)} %pad_maximum_fusion.9), channel_id=1, source_target_pairs={{0,3},{1,2},{2,1},{3,0},{4,7},{5,6},{6,5},{7,4},{8,11},{9,10},{10,... | collective-permute-start | bytes 3538952 | tf_op jit(solution)/shard_map/ppermute | solution.py:45
  136.3 25.2 %all-to-all-start.1 = ((bf16[8,256,192]{1,2,0:T(8,128)(2,1)}), bf16[8,256,192]{1,2,0:T(8,128)(2,1)}, u32[]{:S(2)}, u32[]{:S(2)}) async-start(bf16[8,256,192]{1,2,0:T(8,128)(2,1)} %copy.24), calls=%async_computation.1 | async-start | bytes 1572864 | tf_op jit(solution)/shard_map/all_to_all | solution.py:899
  142.5 359.1 %reduce-scatter.2.cloned.1.call-start = ((), (), s32[]{:S(2)}) async-start(), calls=%async_computation.5 | async-start | bytes 10616832 | tf_op jit(solution)/shard_map/reduce_scatter | solution.py:926
  142.9 20.7 %collective-permute-start.17 = (bf16[384,1536]{1,0:T(8,128)(2,1)S(1)}, bf16[384,1536]{1,0:T(8,128)(2,1)S(1)}, u32[]{:S(2)}, u32[]{:S(2)}) collective-permute-start(bf16[384,1536]{1,0:T(8,128)(2,1)S(1)} %copy-done.8), channel_id=1, source_target_pairs={{0,1},{1,0},{2,3},{3,2},{4,5},{5,4},{6,7},{7,6},{8,9},{9,8},{10,11... | collective-permute-start | bytes 3538952 | tf_op jit(solution)/shard_map/ppermute | solution.py:45
  143.0 20.6 %collective-permute-start.18 = (bf16[384,768]{1,0:T(8,128)(2,1)}, bf16[384,768]{1,0:T(8,128)(2,1)}, u32[]{:S(2)}, u32[]{:S(2)}) collective-permute-start(bf16[384,768]{1,0:T(8,128)(2,1)} %collective-permute-done.10.refs_6_), channel_id=1, source_target_pairs={{0,1},{1,0},{2,3},{3,2},{4,5},{5,4},{6,7},{7,6},{8,9},{9,8},{10,11... | collective-permute-start | bytes 1769480 | tf_op jit(solution)/shard_map/ppermute | solution.py:45
  143.5 20.1 %collective-permute-start.19 = (bf16[384,768]{1,0:T(8,128)(2,1)}, bf16[384,768]{1,0:T(8,128)(2,1)}, u32[]{:S(2)}, u32[]{:S(2)}) collective-permute-start(bf16[384,768]{1,0:T(8,128)(2,1)} %copy-done.21), channel_id=1, source_target_pairs={{0,1},{1,0},{2,3},{3,2},{4,5},{5,4},{6,7},{7,6},{8,9},{9,8},{10,11... | collective-permute-start | bytes 1769480 | tf_op jit(solution)/shard_map/ppermute | solution.py:45
  156.5 30.1 %collective-permute-start.21 = (bf16[3,384,512]{2,1,0:T(8,128)(2,1)}, bf16[3,384,512]{2,1,0:T(8,128)(2,1)}, u32[]{:S(2)}, u32[]{:S(2)}) collective-permute-start(bf16[3,384,512]{2,1,0:T(8,128)(2,1)} %collective-permute-done.14.refs_4_), channel_id=1, source_target_pairs={{0,8},{4,12},{8,0},{12,4},{16,24},{20,28},{24,16},{28,20},{1,9},{5... | collective-permute-start | bytes 3538952 | tf_op jit(solution)/shard_map/ppermute | solution.py:45
  171.5 19.0 %collective-permute-start.20 = (bf16[256,1536]{1,0:T(8,128)(2,1)}, bf16[256,1536]{1,0:T(8,128)(2,1)S(1)}, u32[]{:S(2)}, u32[]{:S(2)}) collective-permute-start(bf16[256,1536]{1,0:T(8,128)(2,1)} %get-tuple-element.85), channel_id=1, source_target_pairs={{0,2},{1,3},{2,0},{3,1},{4,6},{5,7},{6,4},{7,5},{8,10},{9,11},{10,... | collective-permute-start | bytes 2359304 | tf_op jit(solution)/shard_map/ppermute | solution.py:45
  171.7 23.6 %collective-permute-start.23 = (bf16[3,384,1024]{2,1,0:T(8,128)(2,1)S(1)}, bf16[3,384,1024]{2,1,0:T(8,128)(2,1)}, u32[]{:S(2)}, u32[]{:S(2)}) collective-permute-start(bf16[3,384,1024]{2,1,0:T(8,128)(2,1)S(1)} %copy-done.22), channel_id=1, source_target_pairs={{0,1},{1,0},{2,3},{3,2},{4,5},{5,4},{6,7},{7,6},{8,9},{9,8},{10,11... | collective-permute-start | bytes 7077896 | tf_op jit(solution)/shard_map/ppermute | solution.py:45
  231.5 25.4 %collective-permute-start.25 = (bf16[256,1536]{1,0:T(8,128)(2,1)S(1)}, bf16[256,1536]{1,0:T(8,128)(2,1)S(1)}, u32[]{:S(2)}, u32[]{:S(2)}) collective-permute-start(bf16[256,1536]{1,0:T(8,128)(2,1)S(1)} %add_convert_fusion.3), channel_id=1, source_target_pairs={{0,2},{1,3},{2,0},{3,1},{4,6},{5,7},{6,4},{7,5},{8,10},{9,11},{10,... | collective-permute-start | bytes 2359304 | tf_op jit(solution)/shard_map/ppermute | solution.py:45
  269.5 46.3 %all-to-all-start.2 = ((bf16[8,256,192]{1,2,0:T(8,128)(2,1)}), bf16[8,256,192]{1,2,0:T(8,128)(2,1)S(1)}, u32[]{:S(2)}, u32[]{:S(2)}) async-start(bf16[8,256,192]{1,2,0:T(8,128)(2,1)} %copy.26), calls=%async_computation.2 | async-start | bytes 1572864 | tf_op jit(solution)/shard_map/all_to_all | solution.py:929
  273.5 71.7 %collective-permute-start.33 = (bf16[256,1536]{1,0:T(8,128)(2,1)S(1)}, bf16[256,1536]{1,0:T(8,128)(2,1)S(1)}, u32[]{:S(2)}, u32[]{:S(2)}) collective-permute-start(bf16[256,1536]{1,0:T(8,128)(2,1)S(1)} %copy-done.47), channel_id=1, source_target_pairs={{0,2},{1,3},{2,0},{3,1},{4,6},{5,7},{6,4},{7,5},{8,10},{9,11},{10,... | collective-permute-start | bytes 2359304 | tf_op jit(solution)/shard_map/ppermute | solution.py:45
  341.4 53.6 %all-to-all-start.3 = ((bf16[8,256,384]{2,1,0:T(8,128)(2,1)}), bf16[8,256,384]{2,1,0:T(8,128)(2,1)S(1)}, u32[]{:S(2)}, u32[]{:S(2)}) async-start(bf16[8,256,384]{2,1,0:T(8,128)(2,1)} %attention_backward.1), calls=%async_computation.3 | async-start | bytes 3145728 | tf_op jit(solution)/shard_map/all_to_all | solution.py:932
  346.6 34.6 %collective-permute-start.34 = (bf16[512,1536]{1,0:T(8,128)(2,1)}, bf16[512,1536]{1,0:T(8,128)(2,1)}, u32[]{:S(2)}, u32[]{:S(2)}) collective-permute-start(bf16[512,1536]{1,0:T(8,128)(2,1)} %pad_maximum_fusion.7), channel_id=1, source_target_pairs={{0,1},{1,0},{2,3},{3,2},{4,5},{5,4},{6,7},{7,6},{8,9},{9,8},{10,11... | collective-permute-start | bytes 4718600 | tf_op jit(solution)/shard_map/ppermute | solution.py:45
  346.8 19.7 %collective-permute-start.28 = (bf16[256,1536]{1,0:T(8,128)(2,1)S(1)}, bf16[256,1536]{1,0:T(8,128)(2,1)S(1)}, u32[]{:S(2)}, u32[]{:S(2)}) collective-permute-start(bf16[256,1536]{1,0:T(8,128)(2,1)S(1)} %copy-done.43), channel_id=1, source_target_pairs={{0,2},{1,3},{2,0},{3,1},{4,6},{5,7},{6,4},{7,5},{8,10},{9,11},{10,... | collective-permute-start | bytes 2359304 | tf_op jit(solution)/shard_map/ppermute | solution.py:45
  367.4 58.0 %collective-permute-start.29 = (bf16[512,1536]{1,0:T(8,128)(2,1)S(1)}, bf16[512,1536]{1,0:T(8,128)(2,1)}, u32[]{:S(2)}, u32[]{:S(2)}) collective-permute-start(bf16[512,1536]{1,0:T(8,128)(2,1)S(1)} %pad_maximum_fusion.5), channel_id=1, source_target_pairs={{0,1},{1,0},{2,3},{3,2},{4,5},{5,4},{6,7},{7,6},{8,9},{9,8},{10,11... | collective-permute-start | bytes 4718600 | tf_op jit(solution)/shard_map/ppermute | solution.py:45
  370.0 11.2 %collective-permute-start.35 = (bf16[256,384]{1,0:T(8,128)(2,1)S(1)}, bf16[256,384]{1,0:T(8,128)(2,1)}, u32[]{:S(2)}, u32[]{:S(2)}) collective-permute-start(bf16[256,384]{1,0:T(8,128)(2,1)S(1)} %get-tuple-element.165), channel_id=1, source_target_pairs={{0,2},{1,3},{2,0},{3,1},{4,6},{5,7},{6,4},{7,5},{8,10},{9,11},{10,... | collective-permute-start | bytes 589832 | tf_op jit(solution)/shard_map/ppermute | solution.py:45
  386.2 39.1 %collective-permute-start.38 = (bf16[4,192,384]{2,1,0:T(8,128)(2,1)}, bf16[4,192,384]{2,1,0:T(8,128)(2,1)}, u32[]{:S(2)}, u32[]{:S(2)}) collective-permute-start(bf16[4,192,384]{2,1,0:T(8,128)(2,1)} %constant_dynamic-slice_fusion.18), channel_id=1, source_target_pairs={{0,4},{4,0},{8,12},{12,8},{16,20},{20,16},{24,28},{28,24},{1,5},{5... | collective-permute-start | bytes 1769480 | tf_op jit(solution)/shard_map/ppermute | solution.py:45
  405.4 11.5 %collective-permute-start.32 = (bf16[256,768]{1,0:T(8,128)(2,1)S(1)}, bf16[256,768]{1,0:T(8,128)(2,1)S(1)}, u32[]{:S(2)}, u32[]{:S(2)}) collective-permute-start(bf16[256,768]{1,0:T(8,128)(2,1)S(1)} %get-tuple-element.152), channel_id=1, source_target_pairs={{0,3},{1,2},{2,1},{3,0},{4,7},{5,6},{6,5},{7,4},{8,11},{9,10},{10,... | collective-permute-start | bytes 1179656 | tf_op jit(solution)/shard_map/ppermute | solution.py:45
  406.5 10.3 %collective-permute-start.31 = (bf16[256,768]{1,0:T(8,128)(2,1)S(1)}, bf16[256,768]{1,0:T(8,128)(2,1)S(1)}, u32[]{:S(2)}, u32[]{:S(2)}) collective-permute-start(bf16[256,768]{1,0:T(8,128)(2,1)S(1)} %get-tuple-element.153), channel_id=1, source_target_pairs={{0,1},{1,0},{2,3},{3,2},{4,5},{5,4},{6,7},{7,6},{8,9},{9,8},{10,11... | collective-permute-start | bytes 1179656 | tf_op jit(solution)/shard_map/ppermute | solution.py:45
  407.0 18.3 %collective-permute-start.30 = (bf16[256,768]{1,0:T(8,128)(2,1)S(1)}, bf16[256,768]{1,0:T(8,128)(2,1)S(1)}, u32[]{:S(2)}, u32[]{:S(2)}) collective-permute-start(bf16[256,768]{1,0:T(8,128)(2,1)S(1)} %get-tuple-element.154), channel_id=1, source_target_pairs={{0,2},{1,3},{2,0},{3,1},{4,6},{5,7},{6,4},{7,5},{8,10},{9,11},{10,... | collective-permute-start | bytes 1179656 | tf_op jit(solution)/shard_map/ppermute | solution.py:45
  430.8 38.2 %collective-permute-start.39 = (bf16[4,192,768]{2,1,0:T(8,128)(2,1)S(1)}, bf16[4,192,768]{2,1,0:T(8,128)(2,1)}, u32[]{:S(2)}, u32[]{:S(2)}) collective-permute-start(bf16[4,192,768]{2,1,0:T(8,128)(2,1)S(1)} %constant_dynamic-slice_fusion.17), channel_id=1, source_target_pairs={{0,4},{4,0},{8,12},{12,8},{16,20},{20,16},{24,28},{28,24},{1,5},{5... | collective-permute-start | bytes 3538952 | tf_op jit(solution)/shard_map/ppermute | solution.py:45
  434.6 15.6 %collective-permute-start.40 = (bf16[4,48,384]{2,1,0:T(8,128)(2,1)S(1)}, bf16[4,48,384]{2,1,0:T(8,128)(2,1)S(1)}, u32[]{:S(2)}, u32[]{:S(2)}) collective-permute-start(bf16[4,48,384]{2,1,0:T(8,128)(2,1)S(1)} %get-tuple-element.168), channel_id=1, source_target_pairs={{0,8},{4,12},{8,0},{12,4},{16,24},{20,28},{24,16},{28,20},{1,9},{5... | collective-permute-start | bytes 442376 | tf_op jit(solution)/shard_map/ppermute | solution.py:45
  434.6 19.5 %collective-permute-start.41 = (bf16[4,48,384]{2,1,0:T(8,128)(2,1)S(1)}, bf16[4,48,384]{2,1,0:T(8,128)(2,1)S(1)}, u32[]{:S(2)}, u32[]{:S(2)}) collective-permute-start(bf16[4,48,384]{2,1,0:T(8,128)(2,1)S(1)} %get-tuple-element.167), channel_id=1, source_target_pairs={{0,16},{4,20},{8,24},{12,28},{16,0},{20,4},{24,8},{28,12},{1,17},{... | collective-permute-start | bytes 442376 | tf_op jit(solution)/shard_map/ppermute | solution.py:45
  436.7 19.6 %collective-permute-start.42 = (bf16[4,48,384]{2,1,0:T(8,128)(2,1)S(1)}, bf16[4,48,384]{2,1,0:T(8,128)(2,1)S(1)}, u32[]{:S(2)}, u32[]{:S(2)}) collective-permute-start(bf16[4,48,384]{2,1,0:T(8,128)(2,1)S(1)} %get-tuple-element.166), channel_id=1, source_target_pairs={{0,24},{4,28},{8,16},{12,20},{16,8},{20,12},{24,0},{28,4},{1,25},{... | collective-permute-start | bytes 442376 | tf_op jit(solution)/shard_map/ppermute | solution.py:45
  470.6 20.9 %collective-permute-start.48 = (bf16[4,48,768]{2,1,0:T(8,128)(2,1)S(1)}, bf16[4,48,768]{2,1,0:T(8,128)(2,1)S(1)}, u32[]{:S(2)}, u32[]{:S(2)}) collective-permute-start(bf16[4,48,768]{2,1,0:T(8,128)(2,1)S(1)} %get-tuple-element.161), channel_id=1, source_target_pairs={{0,8},{4,12},{8,0},{12,4},{16,24},{20,28},{24,16},{28,20},{1,9},{5... | collective-permute-start | bytes 884744 | tf_op jit(solution)/shard_map/ppermute | solution.py:45
  471.8 29.8 %collective-permute-start.49 = (bf16[4,48,768]{2,1,0:T(8,128)(2,1)S(1)}, bf16[4,48,768]{2,1,0:T(8,128)(2,1)S(1)}, u32[]{:S(2)}, u32[]{:S(2)}) collective-permute-start(bf16[4,48,768]{2,1,0:T(8,128)(2,1)S(1)} %get-tuple-element.160), channel_id=1, source_target_pairs={{0,16},{4,20},{8,24},{12,28},{16,0},{20,4},{24,8},{28,12},{1,17},{... | collective-permute-start | bytes 884744 | tf_op jit(solution)/shard_map/ppermute | solution.py:45
  474.6 27.0 %collective-permute-start.50 = (bf16[4,48,768]{2,1,0:T(8,128)(2,1)S(1)}, bf16[4,48,768]{2,1,0:T(8,128)(2,1)S(1)}, u32[]{:S(2)}, u32[]{:S(2)}) collective-permute-start(bf16[4,48,768]{2,1,0:T(8,128)(2,1)S(1)} %get-tuple-element.159), channel_id=1, source_target_pairs={{0,24},{4,28},{8,16},{12,20},{16,8},{20,12},{24,0},{28,4},{1,25},{... | collective-permute-start | bytes 884744 | tf_op jit(solution)/shard_map/ppermute | solution.py:45
  503.9 12.0 %collective-permute-start.58 = (bf16[384,384]{1,0:T(8,128)(2,1)S(1)}, bf16[384,384]{1,0:T(8,128)(2,1)S(1)}, u32[]{:S(2)}, u32[]{:S(2)}) collective-permute-start(bf16[384,384]{1,0:T(8,128)(2,1)S(1)} %get-tuple-element.156), channel_id=1, source_target_pairs={{0,3},{1,2},{2,1},{3,0},{4,7},{5,6},{6,5},{7,4},{8,11},{9,10},{10,... | collective-permute-start | bytes 884744 | tf_op jit(solution)/shard_map/ppermute | solution.py:45
  505.1 17.1 %collective-permute-start.57 = (bf16[384,384]{1,0:T(8,128)(2,1)S(1)}, bf16[384,384]{1,0:T(8,128)(2,1)S(1)}, u32[]{:S(2)}, u32[]{:S(2)}) collective-permute-start(bf16[384,384]{1,0:T(8,128)(2,1)S(1)} %get-tuple-element.157), channel_id=1, source_target_pairs={{0,2},{1,3},{2,0},{3,1},{4,6},{5,7},{6,4},{7,5},{8,10},{9,11},{10,... | collective-permute-start | bytes 884744 | tf_op jit(solution)/shard_map/ppermute | solution.py:45
  507.2 15.1 %collective-permute-start.56 = (bf16[384,384]{1,0:T(8,128)(2,1)S(1)}, bf16[384,384]{1,0:T(8,128)(2,1)S(1)}, u32[]{:S(2)}, u32[]{:S(2)}) collective-permute-start(bf16[384,384]{1,0:T(8,128)(2,1)S(1)} %get-tuple-element.158), channel_id=1, source_target_pairs={{0,1},{1,0},{2,3},{3,2},{4,5},{5,4},{6,7},{7,6},{8,9},{9,8},{10,11... | collective-permute-start | bytes 884744 | tf_op jit(solution)/shard_map/ppermute | solution.py:45
  522.4 24.8 %collective-permute-start.59 = (bf16[4,272,384]{2,1,0:T(8,128)(2,1)S(1)}, bf16[4,272,384]{2,1,0:T(8,128)(2,1)S(1)}, u32[]{:S(2)}, u32[]{:S(2)}) collective-permute-start(bf16[4,272,384]{2,1,0:T(8,128)(2,1)S(1)} %fusion.18.refs_0_), channel_id=1, source_target_pairs={{0,8},{8,16},{16,24},{24,28},{28,20},{20,12},{12,4},{4,0},{1,9},{9... | collective-permute-start | bytes 2506760 | tf_op jit(solution)/shard_map/ppermute | solution.py:700
  529.3 20.3 %collective-permute-start.66 = (bf16[4,256,384]{2,1,0:T(8,128)(2,1)S(1)}, bf16[4,256,384]{2,1,0:T(8,128)(2,1)S(1)}, u32[]{:S(2)}, u32[]{:S(2)}) collective-permute-start(bf16[4,256,384]{2,1,0:T(8,128)(2,1)S(1)} %fusion.23.refs_8_), channel_id=1, source_target_pairs={{0,4},{8,0},{16,8},{24,16},{28,24},{20,28},{12,20},{4,12},{1,5},{9... | collective-permute-start | bytes 2359304 | tf_op jit(solution)/shard_map/ppermute | solution.py:700
  547.1 20.5 %collective-permute-start.60 = (bf16[4,272,384]{2,1,0:T(8,128)(2,1)S(1)}, bf16[4,272,384]{2,1,0:T(8,128)(2,1)S(1)}, u32[]{:S(2)}, u32[]{:S(2)}) collective-permute-start(bf16[4,272,384]{2,1,0:T(8,128)(2,1)S(1)} %collective-permute-done.59.refs_1_), channel_id=1, source_target_pairs={{0,8},{8,16},{16,24},{24,28},{28,20},{20,12},{12,4},{4,0},{1,9},{9... | collective-permute-start | bytes 2506760 | tf_op jit(solution)/shard_map/ppermute | solution.py:700
  549.6 19.6 %collective-permute-start.67 = (bf16[4,256,384]{2,1,0:T(8,128)(2,1)S(1)}, bf16[4,256,384]{2,1,0:T(8,128)(2,1)S(1)}, u32[]{:S(2)}, u32[]{:S(2)}) collective-permute-start(bf16[4,256,384]{2,1,0:T(8,128)(2,1)S(1)} %collective-permute-done.66.refs_9_), channel_id=1, source_target_pairs={{0,4},{8,0},{16,8},{24,16},{28,24},{20,28},{12,20},{4,12},{1,5},{9... | collective-permute-start | bytes 2359304 | tf_op jit(solution)/shard_map/ppermute | solution.py:700
  567.6 19.3 %collective-permute-start.61 = (bf16[4,272,384]{2,1,0:T(8,128)(2,1)S(1)}, bf16[4,272,384]{2,1,0:T(8,128)(2,1)S(1)}, u32[]{:S(2)}, u32[]{:S(2)}) collective-permute-start(bf16[4,272,384]{2,1,0:T(8,128)(2,1)S(1)} %collective-permute-done.60.refs_2_), channel_id=1, source_target_pairs={{0,8},{8,16},{16,24},{24,28},{28,20},{20,12},{12,4},{4,0},{1,9},{9... | collective-permute-start | bytes 2506760 | tf_op jit(solution)/shard_map/ppermute | solution.py:700
  569.2 18.7 %collective-permute-start.68 = (bf16[4,256,384]{2,1,0:T(8,128)(2,1)S(1)}, bf16[4,256,384]{2,1,0:T(8,128)(2,1)S(1)}, u32[]{:S(2)}, u32[]{:S(2)}) collective-permute-start(bf16[4,256,384]{2,1,0:T(8,128)(2,1)S(1)} %collective-permute-done.67.refs_10_), channel_id=1, source_target_pairs={{0,4},{8,0},{16,8},{24,16},{28,24},{20,28},{12,20},{4,12},{1,5},{9... | collective-permute-start | bytes 2359304 | tf_op jit(solution)/shard_map/ppermute | solution.py:700
  570.1 37.6 %collective-permute-start.26 = (bf16[512,1536]{1,0:T(8,128)(2,1)S(1)}, bf16[512,1536]{1,0:T(8,128)(2,1)S(1)}, u32[]{:S(2)}, u32[]{:S(2)}) collective-permute-start(bf16[512,1536]{1,0:T(8,128)(2,1)S(1)} %slice.72), channel_id=1, source_target_pairs={{0,1},{1,0},{2,3},{3,2},{4,5},{5,4},{6,7},{7,6},{8,9},{9,8},{10,11... | collective-permute-start | bytes 4718600 | tf_op jit(solution)/shard_map/ppermute | solution.py:45
  586.9 18.8 %collective-permute-start.62 = (bf16[4,272,384]{2,1,0:T(8,128)(2,1)S(1)}, bf16[4,272,384]{2,1,0:T(8,128)(2,1)S(1)}, u32[]{:S(2)}, u32[]{:S(2)}) collective-permute-start(bf16[4,272,384]{2,1,0:T(8,128)(2,1)S(1)} %collective-permute-done.61.refs_3_), channel_id=1, source_target_pairs={{0,8},{8,16},{16,24},{24,28},{28,20},{20,12},{12,4},{4,0},{1,9},{9... | collective-permute-start | bytes 2506760 | tf_op jit(solution)/shard_map/ppermute | solution.py:700
  587.9 18.3 %collective-permute-start.69 = (bf16[4,256,384]{2,1,0:T(8,128)(2,1)S(1)}, bf16[4,256,384]{2,1,0:T(8,128)(2,1)S(1)}, u32[]{:S(2)}, u32[]{:S(2)}) collective-permute-start(bf16[4,256,384]{2,1,0:T(8,128)(2,1)S(1)} %collective-permute-done.68.refs_11_), channel_id=1, source_target_pairs={{0,4},{8,0},{16,8},{24,16},{28,24},{20,28},{12,20},{4,12},{1,5},{9... | collective-permute-start | bytes 2359304 | tf_op jit(solution)/shard_map/ppermute | solution.py:700
  605.7 18.5 %collective-permute-start.63 = (bf16[4,272,384]{2,1,0:T(8,128)(2,1)S(1)}, bf16[4,272,384]{2,1,0:T(8,128)(2,1)}, u32[]{:S(2)}, u32[]{:S(2)}) collective-permute-start(bf16[4,272,384]{2,1,0:T(8,128)(2,1)S(1)} %collective-permute-done.62.refs_4_), channel_id=1, source_target_pairs={{0,8},{8,16},{16,24},{24,28},{28,20},{20,12},{12,4},{4,0},{1,9},{9... | collective-permute-start | bytes 2506760 | tf_op jit(solution)/shard_map/ppermute | solution.py:700
  606.3 19.2 %collective-permute-start.70 = (bf16[4,256,384]{2,1,0:T(8,128)(2,1)S(1)}, bf16[4,256,384]{2,1,0:T(8,128)(2,1)}, u32[]{:S(2)}, u32[]{:S(2)}) collective-permute-start(bf16[4,256,384]{2,1,0:T(8,128)(2,1)S(1)} %collective-permute-done.69.refs_12_), channel_id=1, source_target_pairs={{0,4},{8,0},{16,8},{24,16},{28,24},{20,28},{12,20},{4,12},{1,5},{9... | collective-permute-start | bytes 2359304 | tf_op jit(solution)/shard_map/ppermute | solution.py:700
  608.8 25.7 %collective-permute-start.27 = (bf16[256,1536]{1,0:T(8,128)(2,1)}, bf16[256,1536]{1,0:T(8,128)(2,1)}, u32[]{:S(2)}, u32[]{:S(2)}) collective-permute-start(bf16[256,1536]{1,0:T(8,128)(2,1)} %add_convert_fusion.2), channel_id=1, source_target_pairs={{0,2},{1,3},{2,0},{3,1},{4,6},{5,7},{6,4},{7,5},{8,10},{9,11},{10,... | collective-permute-start | bytes 2359304 | tf_op jit(solution)/shard_map/ppermute | solution.py:45
  624.2 21.9 %collective-permute-start.64 = (bf16[4,272,384]{2,1,0:T(8,128)(2,1)}, bf16[4,272,384]{2,1,0:T(8,128)(2,1)}, u32[]{:S(2)}, u32[]{:S(2)}) collective-permute-start(bf16[4,272,384]{2,1,0:T(8,128)(2,1)} %collective-permute-done.63.refs_5_), channel_id=1, source_target_pairs={{0,8},{8,16},{16,24},{24,28},{28,20},{20,12},{12,4},{4,0},{1,9},{9... | collective-permute-start | bytes 2506760 | tf_op jit(solution)/shard_map/ppermute | solution.py:700
  625.5 20.2 %collective-permute-start.71 = (bf16[4,256,384]{2,1,0:T(8,128)(2,1)}, bf16[4,256,384]{2,1,0:T(8,128)(2,1)}, u32[]{:S(2)}, u32[]{:S(2)}) collective-permute-start(bf16[4,256,384]{2,1,0:T(8,128)(2,1)} %collective-permute-done.70.refs_13_), channel_id=1, source_target_pairs={{0,4},{8,0},{16,8},{24,16},{28,24},{20,28},{12,20},{4,12},{1,5},{9... | collective-permute-start | bytes 2359304 | tf_op jit(solution)/shard_map/ppermute | solution.py:700
  641.3 9.1 %collective-permute-start.55 = (f32[2,384]{1,0:T(2,128)S(1)}, f32[2,384]{1,0:T(2,128)S(1)}, u32[]{:S(2)}, u32[]{:S(2)}) collective-permute-start(f32[2,384]{1,0:T(2,128)S(1)} %add.265), channel_id=1, source_target_pairs={{0,24},{4,28},{8,16},{12,20},{16,8},{20,12},{24,0},{28,4},{1,25},{... | collective-permute-start | bytes 9224 | tf_op jit(solution)/shard_map/ppermute | solution.py:45
  641.4 9.0 %collective-permute-start.47 = (f32[2,384]{1,0:T(2,128)S(1)}, f32[2,384]{1,0:T(2,128)S(1)}, u32[]{:S(2)}, u32[]{:S(2)}) collective-permute-start(f32[2,384]{1,0:T(2,128)S(1)} %add.265), channel_id=1, source_target_pairs={{0,8},{4,12},{8,0},{12,4},{16,24},{20,28},{24,16},{28,20},{1,9},{5... | collective-permute-start | bytes 9224 | tf_op jit(solution)/shard_map/ppermute | solution.py:45
  645.7 14.2 %collective-permute-start.72 = (bf16[4,256,384]{2,1,0:T(8,128)(2,1)}, bf16[4,256,384]{2,1,0:T(8,128)(2,1)S(1)}, u32[]{:S(2)}, u32[]{:S(2)}) collective-permute-start(bf16[4,256,384]{2,1,0:T(8,128)(2,1)} %collective-permute-done.71.refs_14_), channel_id=1, source_target_pairs={{0,4},{8,0},{16,8},{24,16},{28,24},{20,28},{12,20},{4,12},{1,5},{9... | collective-permute-start | bytes 2359304 | tf_op jit(solution)/shard_map/ppermute | solution.py:700
  646.1 15.0 %collective-permute-start.65 = (bf16[4,272,384]{2,1,0:T(8,128)(2,1)}, bf16[4,272,384]{2,1,0:T(8,128)(2,1)S(1)}, u32[]{:S(2)}, u32[]{:S(2)}) collective-permute-start(bf16[4,272,384]{2,1,0:T(8,128)(2,1)} %collective-permute-done.64.refs_6_), channel_id=1, source_target_pairs={{0,8},{8,16},{16,24},{24,28},{28,20},{20,12},{12,4},{4,0},{1,9},{9... | collective-permute-start | bytes 2506760 | tf_op jit(solution)/shard_map/ppermute | solution.py:700
  (72 other events, 921.5 us)
Sparse Core Ops, SparseCore 0:
  259.6 241.9 reduce-scatter.1
